TPU v7x, 768 devices: a whole 4x8x12 slice. The times are simulated.
768 devices in a mesh: tile: 24 (over z_lo, x), head: 32 (over z_hi, y, core).
Axes of the slice: x: 4, y: 8, z: 12 (z_hi: 2, z_lo: 6; z = z_hi * 6 + z_lo), core: 2. Of those that a mesh axis runs over, the one named last changes fastest.
Arguments:
- embedded: bfloat16 [24, 1024, 16, 64], P('tile', 'head'), may hold values from -6 to 6
- cotangent: bfloat16 [24, 1024, 16, 64], P('tile', 'head'), may hold values from -6 to 6
- weights: bfloat16 [1024, 4, 8, 128], P('head'), may hold values from -0.1875 to 0.1875
Outputs:
- attention: bfloat16 [24, 1024, 16, 64], P('tile', 'head')
- token_grads: float32 [24, 1024, 16, 64], P('tile', 'head')
- weight_grads: float32 [1024, 4, 8, 128], P('head')
All inputs are finite; a program needn't handle non-finite values.
Results may differ from a plain program's by a relative error of at most 0.022.
Values may be sent and summed in bfloat16 or wider, within the bound.
No kernel may reach another device: no remote copies, remote signals or barrier semaphores. Data moves between devices by JAX's collectives and lax.ppermute only.
A program may use at most 32 MiB of HBM per device.

v0:
```python
import jax
import jax.numpy as jnp
from jax import lax
from jax.sharding import PartitionSpec as P

D = 1024
HEADS = 8
HEAD_DIM = 128
TILE_ROWS = 16
TILE_COLS = 16
RIM = 4
PAD_ROWS = 24
PAD_COLS = 24
TILE_TOKENS = 256
PAD_TOKENS = 576


def passed_along(value, axis, steps):
    count = lax.axis_size(axis)
    leading, last = (max(0, -steps), min(count, count - steps))
    return lax.ppermute(value, axis, [(source, source + steps) for source in range(leading, last)])


def contract(first_op, second_op, first_dim, second_dim):
    return lax.dot_general(
        first_op,
        second_op,
        (((first_dim,), (second_dim,)), ((), ())),
        preferred_element_type=jnp.float32,
    )


def rim_move(piece, shift_by):
    return passed_along(piece.astype(jnp.bfloat16), "tile", shift_by).astype(piece.dtype)


def local(embedded, cotangent, weights):
    score_scale = HEAD_DIM ** (-0.5)
    n_head = lax.axis_size("head")
    n_tile = lax.axis_size("tile")
    tile_group = n_head // HEADS
    strip_cols = embedded.shape[3]
    width_part = embedded.shape[1]
    tile_id = lax.axis_index("tile")
    head_id = lax.axis_index("head")
    parity = tile_id % 2
    tile_slot = head_id // HEADS
    own_block = embedded[0].astype(jnp.float32)
    from_left = rim_move(own_block[:, :, strip_cols - RIM :], 1)
    from_right = rim_move(own_block[:, :, :RIM], -1)
    from_left = jnp.where(parity == 1, from_left, 0.0)
    from_right = jnp.where(parity == 0, from_right, 0.0)
    widened = jnp.concatenate([from_left, own_block, from_right], 2)
    from_above = rim_move(widened[:, TILE_ROWS - RIM :, :], 2)
    from_below = rim_move(widened[:, :RIM, :], -2)
    padded = jnp.concatenate([from_above, widened, from_below], 1).astype(jnp.bfloat16)
    tile_stack = jnp.stack(
        [
            padded[:, :, member * TILE_COLS : member * TILE_COLS + PAD_COLS]
            for member in range(tile_group)
        ]
    )
    token_send = jnp.repeat(tile_stack.reshape(tile_group, width_part, PAD_TOKENS), HEADS, axis=0)
    grad_tiles = (
        cotangent[0].reshape(width_part, TILE_ROWS, tile_group, TILE_COLS).transpose(2, 0, 1, 3)
    )
    grad_send = jnp.repeat(grad_tiles.reshape(tile_group, width_part, TILE_TOKENS), HEADS, axis=0)
    weight_send = jnp.tile(
        weights.transpose(2, 0, 1, 3).reshape(HEADS, width_part, 4 * HEAD_DIM), (tile_group, 1, 1)
    )
    tokens_in, grads_in, weights_in = (
        lax.all_to_all(token_send, "head", split_axis=0, concat_axis=1, tiled=True),
        lax.all_to_all(grad_send, "head", split_axis=0, concat_axis=1, tiled=True),
        lax.all_to_all(weight_send, "head", split_axis=0, concat_axis=1, tiled=True),
    )
    tokens_all = tokens_in[0]
    grads_all = grads_in[0]
    weight_head = weights_in[0]
    row_pos = tile_id // 2 * TILE_ROWS + jnp.arange(PAD_ROWS) - RIM
    col_pos = (parity * tile_group + tile_slot) * TILE_COLS + jnp.arange(PAD_COLS) - RIM
    height = n_tile // 2 * TILE_ROWS
    breadth = 2 * tile_group * TILE_COLS
    key_valid = (
        ((row_pos >= 0) & (row_pos < height))[:, None]
        & ((col_pos >= 0) & (col_pos < breadth))[None, :]
    ).reshape(PAD_TOKENS)
    interior = tokens_all.reshape(D, PAD_ROWS, PAD_COLS)[
        :, RIM : RIM + TILE_ROWS, RIM : RIM + TILE_COLS
    ].reshape(D, TILE_TOKENS)
    w_query = weight_head[:, :HEAD_DIM]
    w_keyval = weight_head[:, HEAD_DIM : 3 * HEAD_DIM]
    w_out = weight_head[:, 3 * HEAD_DIM :]
    queries = contract(interior, w_query, 0, 0).astype(jnp.bfloat16)
    keyval = contract(tokens_all, w_keyval, 0, 0).astype(jnp.bfloat16)
    keys = keyval[:, :HEAD_DIM]
    values = keyval[:, HEAD_DIM:]
    scores = contract(queries, keys, 1, 1) * score_scale
    scores = jnp.where(key_valid[None, :], scores, -jnp.inf)
    top_score = jnp.max(scores, axis=-1, keepdims=True)
    expo = jnp.exp(scores - top_score)
    probs = expo / jnp.sum(expo, axis=-1, keepdims=True)
    probs_low = probs.astype(jnp.bfloat16)
    attended = jnp.dot(probs_low, values, preferred_element_type=jnp.float32).astype(jnp.bfloat16)
    partial_value = contract(w_out, attended, 1, 1).astype(jnp.bfloat16)
    part_send = partial_value.reshape(n_head, width_part, TILE_TOKENS)
    d_attended = contract(grads_all, w_out, 0, 0).astype(jnp.bfloat16)
    grad_out_w = contract(grads_all, attended, 1, 0)
    d_probs = contract(d_attended, values, 1, 1)
    d_scores = (
        probs * (d_probs - jnp.sum(d_probs * probs, axis=-1, keepdims=True)) * score_scale
    ).astype(jnp.bfloat16)
    d_queries = jnp.dot(d_scores, keys, preferred_element_type=jnp.float32).astype(jnp.bfloat16)
    d_keys = contract(d_scores, queries, 0, 0).astype(jnp.bfloat16)
    d_values = contract(probs_low, d_attended, 0, 0).astype(jnp.bfloat16)
    d_keyval = jnp.concatenate([d_keys, d_values], 1)
    grad_query_w = jnp.dot(interior, d_queries, preferred_element_type=jnp.float32)
    grad_keyval_w = jnp.dot(tokens_all, d_keyval, preferred_element_type=jnp.float32)
    d_tokens = contract(w_keyval, d_keyval, 1, 1)
    d_inner = contract(w_query, d_queries, 1, 1)
    d_tokens = (
        d_tokens.reshape(D, PAD_ROWS, PAD_COLS)
        .at[:, RIM : RIM + TILE_ROWS, RIM : RIM + TILE_COLS]
        .add(d_inner.reshape(D, TILE_ROWS, TILE_COLS))
    )
    d_tokens = d_tokens.reshape(D, PAD_TOKENS).astype(jnp.bfloat16)
    weight_term = jnp.concatenate([grad_query_w, grad_keyval_w, grad_out_w], 1)
    weight_total = lax.psum(weight_term.astype(jnp.bfloat16), "tile")
    weight_send_back = weight_total.reshape(n_head, width_part, 4 * HEAD_DIM)
    grad_send_back = d_tokens.reshape(n_head, width_part, PAD_TOKENS)
    parts_back, grads_back, weights_back = (
        lax.all_to_all(part_send, "head", split_axis=0, concat_axis=0, tiled=True),
        lax.all_to_all(grad_send_back, "head", split_axis=0, concat_axis=0, tiled=True),
        lax.all_to_all(weight_send_back, "head", split_axis=0, concat_axis=0, tiled=True),
    )
    out_sum = jnp.sum(
        parts_back.reshape(tile_group, HEADS, width_part, TILE_TOKENS).astype(jnp.float32), axis=1
    ).astype(jnp.bfloat16)
    attention = (
        out_sum.reshape(tile_group, width_part, TILE_ROWS, TILE_COLS)
        .transpose(1, 2, 0, 3)
        .reshape(1, width_part, TILE_ROWS, strip_cols)
    )
    window_grads = jnp.sum(
        grads_back.reshape(tile_group, HEADS, width_part, PAD_TOKENS).astype(jnp.float32), axis=1
    )
    window_grads = window_grads.reshape(tile_group, width_part, PAD_ROWS, PAD_COLS)
    grad_field = jnp.zeros((width_part, PAD_ROWS, strip_cols + 2 * RIM), jnp.float32)
    for member in range(tile_group):
        grad_field = grad_field.at[:, :, member * TILE_COLS : member * TILE_COLS + PAD_COLS].add(
            window_grads[member]
        )
    to_above = rim_move(grad_field[:, :RIM, :], -2)
    to_below = rim_move(grad_field[:, RIM + TILE_ROWS :, :], 2)
    grad_core = grad_field[:, RIM : RIM + TILE_ROWS, :]
    grad_core = grad_core.at[:, TILE_ROWS - RIM :, :].add(to_above).at[:, :RIM, :].add(to_below)
    back_left = rim_move(grad_core[:, :, :RIM], -1)
    back_right = rim_move(grad_core[:, :, RIM + strip_cols :], 1)
    grad_inner = grad_core[:, :, RIM : RIM + strip_cols]
    grad_inner = grad_inner.at[:, :, strip_cols - RIM :].add(jnp.where(parity == 0, back_left, 0.0))
    grad_inner = grad_inner.at[:, :, :RIM].add(jnp.where(parity == 1, back_right, 0.0))
    token_grads = grad_inner[None]
    weight_parts = weights_back.reshape(tile_group, HEADS, width_part, 4, HEAD_DIM).astype(
        jnp.float32
    )
    weight_grads = jnp.sum(weight_parts, axis=0).transpose(1, 2, 0, 3)
    return (attention, token_grads, weight_grads)


def solution(mesh):
    placed = (
        P("tile", "head", None, None),
        P("tile", "head", None, None),
        P("head", None, None, None),
    )
    return jax.shard_map(
        local,
        mesh=mesh,
        in_specs=placed,
        out_specs=(
            P("tile", "head", None, None),
            P("tile", "head", None, None),
            P("head", None, None, None),
        ),
        check_vma=False,
    )
```

profile of v0, /device:TPU:22, one launch (start us, length us, event | category | flops | bytes accessed | tf_op | source)
XLA Modules:
  0.0 633.0 jit_solution(9002930955256587944)
XLA Ops:
  9.3 20.3 %all-to-all-start.3 = ((bf16[32,32,256]{2,1,0:T(8,128)(2,1)}), bf16[32,32,256]{2,1,0:T(8,128)(2,1)S(1)}, u32[]{:S(2)}, u32[]{:S(2)}) async-start(bf16[32,32,256]{2,1,0:T(8,128)(2,1)} %bitcast.16), calls=%async_computation.3 | async-start | bytes 1048576 | tf_op jit(solution)/shard_map/all_to_all | solution.py:73
  29.8 17.6 %all-to-all-done.3 = bf16[32,32,256]{2,1,0:T(8,128)(2,1)S(1)} async-done(((bf16[32,32,256]{2,1,0:T(8,128)(2,1)}), bf16[32,32,256]{2,1,0:T(8,128)(2,1)S(1)}, u32[]{:S(2)}, u32[]{:S(2)}) %all-to-all-start.3) | async-done | bytes 524320 | tf_op jit(solution)/shard_map/all_to_all | solution.py:73
  48.7 9.6 %all-to-all-start.1 = ((bf16[32,32,512]{2,1,0:T(8,128)(2,1)}), bf16[32,32,512]{2,1,0:T(8,128)(2,1)S(1)}, u32[]{:S(2)}, u32[]{:S(2)}) async-start(bf16[32,32,512]{2,1,0:T(8,128)(2,1)} %bitcast.4), calls=%async_computation.1 | async-start | bytes 2097152 | tf_op jit(solution)/shard_map/all_to_all | solution.py:74
  58.5 10.5 %collective-permute-start = (bf16[32,16,4]{2,1,0:T(8,128)(2,1)S(1)}, bf16[32,16,4]{2,1,0:T(8,128)(2,1)S(1)}, u32[]{:S(2)}, u32[]{:S(2)}) collective-permute-start(bf16[32,16,4]{2,1,0:T(8,128)(2,1)S(1)} %get-tuple-element.134), channel_id=1, source_target_pairs={{0,32},{32,64},{64,96},{96,128},{128,160},{160,192},{192,224},{224... | collective-permute-start | bytes 12296 | tf_op jit(solution)/shard_map/ppermute | solution.py:21
  69.0 1.9 collective-permute-start.1
  71.0 2.5 collective-permute-done
  73.4 28.3 %collective-permute-done.1 = bf16[32,16,4]{2,1,0:T(8,128)(2,1)S(1)} collective-permute-done((bf16[32,16,4]{2,1,0:T(8,128)(2,1)S(1)}, bf16[32,16,4]{2,1,0:T(8,128)(2,1)S(1)}, u32[]{:S(2)}, u32[]{:S(2)}) %collective-permute-start.1) | collective-permute-done | bytes 4128 | tf_op jit(solution)/shard_map/ppermute | solution.py:21
  101.9 1.9 collective-permute-start.2
  103.9 5.4 collective-permute-start.3
  109.3 2.8 collective-permute-done.3
  114.3 14.8 %all-to-all-start = ((bf16[32,32,576]{2,1,0:T(8,128)(2,1)}), bf16[32,32,576]{2,1,0:T(8,128)(2,1)S(1)}, u32[]{:S(2)}, u32[]{:S(2)}) async-start(bf16[32,32,576]{2,1,0:T(8,128)(2,1)} %bitcast.1), calls=%async_computation | async-start | bytes 2621440 | tf_op jit(solution)/shard_map/all_to_all | solution.py:72
  129.7 45.7 %all-to-all-done = bf16[32,32,576]{2,1,0:T(8,128)(2,1)S(1)} async-done(((bf16[32,32,576]{2,1,0:T(8,128)(2,1)}), bf16[32,32,576]{2,1,0:T(8,128)(2,1)S(1)}, u32[]{:S(2)}, u32[]{:S(2)}) %all-to-all-start) | async-done | bytes 1179680 | tf_op jit(solution)/shard_map/all_to_all | solution.py:72
  175.5 4.5 copy.24
  180.0 7.6 %reshape_squeeze.6 = bf16[1024,24,24]{0,2,1:T(8,128)(2,1)} reshape(bf16[32,32,576]{1,0,2:T(8,128)(2,1)} %copy.24) | data formatting | bytes 2359296 | tf_op jit(solution)/shard_map/reshape;squeeze | solution.py:87
  187.6 1.3 slice.343
  192.2 11.0 %all-to-all-start.2 = ((bf16[32,32,256]{2,1,0:T(8,128)(2,1)}), bf16[32,32,256]{2,1,0:T(8,128)(2,1)}, u32[]{:S(2)}, u32[]{:S(2)}) async-start(bf16[32,32,256]{2,1,0:T(8,128)(2,1)} %bitcast.8), calls=%async_computation.2 | async-start | bytes 1048576 | tf_op jit(solution)/shard_map/all_to_all | solution.py:131
  207.1 4.8 convert_element_type.106
  211.9 5.4 copy.32
  217.3 7.0 %all-to-all-done.2 = bf16[32,32,256]{2,1,0:T(8,128)(2,1)} async-done(((bf16[32,32,256]{2,1,0:T(8,128)(2,1)}), bf16[32,32,256]{2,1,0:T(8,128)(2,1)}, u32[]{:S(2)}, u32[]{:S(2)}) %all-to-all-start.2) | async-done | bytes 524320 | tf_op jit(solution)/shard_map/all_to_all | solution.py:131
  224.3 11.0 %all-to-all-start.4 = ((bf16[32,32,576]{2,1,0:T(8,128)(2,1)}), bf16[32,32,576]{2,1,0:T(8,128)(2,1)S(1)}, u32[]{:S(2)}, u32[]{:S(2)}) async-start(bf16[32,32,576]{2,1,0:T(8,128)(2,1)} %copy.32), calls=%async_computation.4 | async-start | bytes 2621440 | tf_op jit(solution)/shard_map/all_to_all | solution.py:132
  237.1 1.5 convolution_convert_fusion
  240.1 306.0 %all-reduce.3.cloned.1.call-done = bf16[32,32,512]{2,1,0:T(8,128)(2,1)} async-done(((bf16[32,32,512]{2,1,0:T(8,128)(2,1)}), bf16[32,32,512]{2,1,0:T(8,128)(2,1)}) %all-reduce.3.cloned.1.call-update) | async-done | bytes 1048592 | tf_op jit(solution)/shard_map/psum | solution.py:127
  546.1 15.6 %all-to-all-start.5 = ((bf16[32,32,512]{2,1,0:T(8,128)(2,1)}), bf16[32,32,512]{2,1,0:T(8,128)(2,1)S(1)}, u32[]{:S(2)}, u32[]{:S(2)}) async-start(bf16[32,32,512]{2,1,0:T(8,128)(2,1)} %all-reduce.3.cloned.1.call-done), calls=%async_computation.5 | async-start | bytes 2097152 | tf_op jit(solution)/shard_map/all_to_all | solution.py:133
  563.6 8.6 %scatter-add.34 = f32[32,24,72]{2,1,0:T(8,128)S(1)} dynamic-update-slice(f32[32,24,72]{2,1,0:T(8,128)S(1)} %scatter-add.31, f32[32,24,24]{2,1,0:T(8,128)S(1)} %slice_add_fusion.3, s32[]{:T(128)} %constant.290.clone.1, s32[]{:T(128)} %constant.290.clone.1, s32[]{:T(128)} %constant.292.clone.1) | dynamic-update-slice | bytes 147460 | tf_op jit(solution)/shard_map/scatter-add | solution.py:149
  572.5 8.6 %scatter-add.35 = f32[32,24,72]{2,1,0:T(8,128)S(1)} dynamic-update-slice(f32[32,24,72]{2,1,0:T(8,128)S(1)} %scatter-add.34, f32[32,24,24]{2,1,0:T(8,128)S(1)} %slice_add_fusion.2, s32[]{:T(128)} %constant.290.clone.1, s32[]{:T(128)} %constant.290.clone.1, s32[]{:T(128)} %constant.305.clone.1) | dynamic-update-slice | bytes 147460 | tf_op jit(solution)/shard_map/scatter-add | solution.py:149
  581.3 8.6 %scatter-add.36 = f32[32,24,72]{2,1,0:T(8,128)S(1)} dynamic-update-slice(f32[32,24,72]{2,1,0:T(8,128)S(1)} %scatter-add.35, f32[32,24,24]{2,1,0:T(8,128)S(1)} %slice_add_fusion.1, s32[]{:T(128)} %constant.290.clone.1, s32[]{:T(128)} %constant.290.clone.1, s32[]{:T(128)} %constant.306.clone.1) | dynamic-update-slice | bytes 147460 | tf_op jit(solution)/shard_map/scatter-add | solution.py:149
  590.0 10.1 %collective-permute-start.4 = (bf16[32,4,72]{2,1,0:T(4,128)(2,1)S(1)}, bf16[32,4,72]{2,1,0:T(4,128)(2,1)S(1)}, u32[]{:S(2)}, u32[]{:S(2)}) collective-permute-start(bf16[32,4,72]{2,1,0:T(4,128)(2,1)S(1)} %get-tuple-element.125), channel_id=1, source_target_pairs={{64,0},{96,32},{128,64},{160,96},{192,128},{224,160},{256,192},{28... | collective-permute-start | bytes 55304 | tf_op jit(solution)/shard_map/ppermute | solution.py:21
  600.2 1.9 collective-permute-start.5
  602.2 5.3 collective-permute-done.5
  607.7 3.9 collective-permute-start.6
  613.9 4.3 collective-permute-start.7
  618.3 4.8 scatter-add.41
  (116 shorter events, 24.6 us)
Async XLA Ops:
  7.2 22.4 %copy-start.11 = (bf16[32,4,8,128]{3,2,1,0:T(8,128)(2,1)S(1)}, bf16[32,4,8,128]{3,2,1,0:T(8,128)(2,1)}, u32[]{:S(2)}) copy-start(bf16[32,4,8,128]{3,2,1,0:T(8,128)(2,1)} %param.23) | copy-start | bytes 786436
  9.3 38.1 %all-to-all-start.3 = ((bf16[32,32,256]{2,1,0:T(8,128)(2,1)}), bf16[32,32,256]{2,1,0:T(8,128)(2,1)S(1)}, u32[]{:S(2)}, u32[]{:S(2)}) async-start(bf16[32,32,256]{2,1,0:T(8,128)(2,1)} %bitcast.16), calls=%async_computation.3 | async-start | bytes 1048576 | tf_op jit(solution)/shard_map/all_to_all | solution.py:73
  29.7 28.6 %copy-start.5 = (bf16[1,32,16,64]{3,2,1,0:T(8,128)(2,1)S(1)}, bf16[1,32,16,64]{3,2,1,0:T(8,128)(2,1)}, u32[]{:S(2)}) copy-start(bf16[1,32,16,64]{3,2,1,0:T(8,128)(2,1)} %param.21) | copy-start | bytes 196612
  47.5 81.9 %copy-start.2 = (bf16[32,32,256]{2,1,0:T(8,128)(2,1)}, bf16[32,32,256]{2,1,0:T(8,128)(2,1)S(1)}, u32[]{:S(2)}) copy-start(bf16[32,32,256]{2,1,0:T(8,128)(2,1)S(1)} %all-to-all-done.3) | copy-start | bytes 1572868
  48.7 64.4 %all-to-all-start.1 = ((bf16[32,32,512]{2,1,0:T(8,128)(2,1)}), bf16[32,32,512]{2,1,0:T(8,128)(2,1)S(1)}, u32[]{:S(2)}, u32[]{:S(2)}) async-start(bf16[32,32,512]{2,1,0:T(8,128)(2,1)} %bitcast.4), calls=%async_computation.1 | async-start | bytes 2097152 | tf_op jit(solution)/shard_map/all_to_all | solution.py:74
  58.5 15.0 %collective-permute-start = (bf16[32,16,4]{2,1,0:T(8,128)(2,1)S(1)}, bf16[32,16,4]{2,1,0:T(8,128)(2,1)S(1)}, u32[]{:S(2)}, u32[]{:S(2)}) collective-permute-start(bf16[32,16,4]{2,1,0:T(8,128)(2,1)S(1)} %get-tuple-element.134), channel_id=1, source_target_pairs={{0,32},{32,64},{64,96},{96,128},{128,160},{160,192},{192,224},{224... | collective-permute-start | bytes 12296 | tf_op jit(solution)/shard_map/ppermute | solution.py:21
  69.0 32.7 %collective-permute-start.1 = (bf16[32,16,4]{2,1,0:T(8,128)(2,1)S(1)}, bf16[32,16,4]{2,1,0:T(8,128)(2,1)S(1)}, u32[]{:S(2)}, u32[]{:S(2)}) collective-permute-start(bf16[32,16,4]{2,1,0:T(8,128)(2,1)S(1)} %get-tuple-element.135), channel_id=1, source_target_pairs={{32,0},{64,32},{96,64},{128,96},{160,128},{192,160},{224,192},{256... | collective-permute-start | bytes 12296 | tf_op jit(solution)/shard_map/ppermute | solution.py:21
  101.9 7.4 %collective-permute-start.2 = (bf16[32,4,72]{2,1,0:T(4,128)(2,1)S(1)}, bf16[32,4,72]{2,1,0:T(4,128)(2,1)S(1)}, u32[]{:S(2)}, u32[]{:S(2)}) collective-permute-start(bf16[32,4,72]{2,1,0:T(4,128)(2,1)S(1)} %get-tuple-element.132), channel_id=1, source_target_pairs={{0,64},{32,96},{64,128},{96,160},{128,192},{160,224},{192,256},{22... | collective-permute-start | bytes 55304 | tf_op jit(solution)/shard_map/ppermute | solution.py:21
  103.9 8.2 %collective-permute-start.3 = (bf16[32,4,72]{2,1,0:T(4,128)(2,1)S(1)}, bf16[32,4,72]{2,1,0:T(4,128)(2,1)S(1)}, u32[]{:S(2)}, u32[]{:S(2)}) collective-permute-start(bf16[32,4,72]{2,1,0:T(4,128)(2,1)S(1)} %get-tuple-element.133), channel_id=1, source_target_pairs={{64,0},{96,32},{128,64},{160,96},{192,128},{224,160},{256,192},{28... | collective-permute-start | bytes 55304 | tf_op jit(solution)/shard_map/ppermute | solution.py:21
  114.3 61.2 %all-to-all-start = ((bf16[32,32,576]{2,1,0:T(8,128)(2,1)}), bf16[32,32,576]{2,1,0:T(8,128)(2,1)S(1)}, u32[]{:S(2)}, u32[]{:S(2)}) async-start(bf16[32,32,576]{2,1,0:T(8,128)(2,1)} %bitcast.1), calls=%async_computation | async-start | bytes 2621440 | tf_op jit(solution)/shard_map/all_to_all | solution.py:72
  175.5 13.8 %copy-start = (bf16[32,32,576]{2,1,0:T(8,128)(2,1)}, bf16[32,32,576]{2,1,0:T(8,128)(2,1)S(1)}, u32[]{:S(2)}) copy-start(bf16[32,32,576]{2,1,0:T(8,128)(2,1)S(1)} %all-to-all-done) | copy-start | bytes 3538948
  189.0 1.2 copy-start.4
  190.6 1.6 copy-start.12
  192.2 32.1 %all-to-all-start.2 = ((bf16[32,32,256]{2,1,0:T(8,128)(2,1)}), bf16[32,32,256]{2,1,0:T(8,128)(2,1)}, u32[]{:S(2)}, u32[]{:S(2)}) async-start(bf16[32,32,256]{2,1,0:T(8,128)(2,1)} %bitcast.8), calls=%async_computation.2 | async-start | bytes 1048576 | tf_op jit(solution)/shard_map/all_to_all | solution.py:131
  203.6 1.2 copy-start.7
  203.9 0.6 copy-start.9
  204.5 0.8 copy-start.14
  217.3 18.1 %copy-start.10 = (bf16[256,128]{1,0:T(8,128)(2,1)S(1)}, bf16[256,128]{1,0:T(8,128)(2,1)}, u32[]{:S(2)}) copy-start(bf16[256,128]{1,0:T(8,128)(2,1)} %copy-done.9) | copy-start | bytes 196612
  217.3 19.5 %copy-start.3 = (bf16[32,32,256]{2,1,0:T(8,128)(2,1)S(1)}, bf16[32,32,256]{2,1,0:T(8,128)(2,1)}, u32[]{:S(2)}) copy-start(bf16[32,32,256]{2,1,0:T(8,128)(2,1)} %copy-done.2) | copy-start | bytes 1572868
  217.3 19.5 %copy-start.13 = (bf16[256,128]{1,0:T(8,128)(2,1)S(1)}, bf16[256,128]{1,0:T(8,128)(2,1)}, u32[]{:S(2)}) copy-start(bf16[256,128]{1,0:T(8,128)(2,1)} %copy-done.12) | copy-start | bytes 196612
  217.3 19.8 %copy-start.1 = (bf16[32,32,576]{2,1,0:T(8,128)(2,1)S(1)}, bf16[32,32,576]{2,1,0:T(8,128)(2,1)}, u32[]{:S(2)}) copy-start(bf16[32,32,576]{2,1,0:T(8,128)(2,1)} %copy-done) | copy-start | bytes 3538948
  217.3 19.8 %copy-start.8 = (bf16[576,128]{1,0:T(8,128)(2,1)S(1)}, bf16[576,128]{1,0:T(8,128)(2,1)}, u32[]{:S(2)}) copy-start(bf16[576,128]{1,0:T(8,128)(2,1)} %copy-done.7) | copy-start | bytes 442372
  224.3 321.8 %all-to-all-start.4 = ((bf16[32,32,576]{2,1,0:T(8,128)(2,1)}), bf16[32,32,576]{2,1,0:T(8,128)(2,1)S(1)}, u32[]{:S(2)}, u32[]{:S(2)}) async-start(bf16[32,32,576]{2,1,0:T(8,128)(2,1)} %copy.32), calls=%async_computation.4 | async-start | bytes 2621440 | tf_op jit(solution)/shard_map/all_to_all | solution.py:132
  235.4 310.7 %all-reduce.3.cloned.1.call-start = ((), (), s32[]{:S(2)}) async-start(), calls=%async_computation.6 | async-start | bytes 2097152 | tf_op jit(solution)/shard_map/psum | solution.py:127
  546.1 77.6 %all-to-all-start.5 = ((bf16[32,32,512]{2,1,0:T(8,128)(2,1)}), bf16[32,32,512]{2,1,0:T(8,128)(2,1)S(1)}, u32[]{:S(2)}, u32[]{:S(2)}) async-start(bf16[32,32,512]{2,1,0:T(8,128)(2,1)} %all-reduce.3.cloned.1.call-done), calls=%async_computation.5 | async-start | bytes 2097152 | tf_op jit(solution)/shard_map/all_to_all | solution.py:133
  590.0 12.1 %collective-permute-start.4 = (bf16[32,4,72]{2,1,0:T(4,128)(2,1)S(1)}, bf16[32,4,72]{2,1,0:T(4,128)(2,1)S(1)}, u32[]{:S(2)}, u32[]{:S(2)}) collective-permute-start(bf16[32,4,72]{2,1,0:T(4,128)(2,1)S(1)} %get-tuple-element.125), channel_id=1, source_target_pairs={{64,0},{96,32},{128,64},{160,96},{192,128},{224,160},{256,192},{28... | collective-permute-start | bytes 55304 | tf_op jit(solution)/shard_map/ppermute | solution.py:21
  600.2 7.3 %collective-permute-start.5 = (bf16[32,4,72]{2,1,0:T(4,128)(2,1)S(1)}, bf16[32,4,72]{2,1,0:T(4,128)(2,1)S(1)}, u32[]{:S(2)}, u32[]{:S(2)}) collective-permute-start(bf16[32,4,72]{2,1,0:T(4,128)(2,1)S(1)} %get-tuple-element.124), channel_id=1, source_target_pairs={{0,64},{32,96},{64,128},{96,160},{128,192},{160,224},{192,256},{22... | collective-permute-start | bytes 55304 | tf_op jit(solution)/shard_map/ppermute | solution.py:21
  607.7 10.5 %collective-permute-start.6 = (bf16[32,16,4]{2,1,0:T(8,128)(2,1)S(1)}, bf16[32,16,4]{2,1,0:T(8,128)(2,1)S(1)}, u32[]{:S(2)}, u32[]{:S(2)}) collective-permute-start(bf16[32,16,4]{2,1,0:T(8,128)(2,1)S(1)} %get-tuple-element.131), channel_id=1, source_target_pairs={{32,0},{64,32},{96,64},{128,96},{160,128},{192,160},{224,192},{256... | collective-permute-start | bytes 12296 | tf_op jit(solution)/shard_map/ppermute | solution.py:21
  613.9 9.3 %collective-permute-start.7 = (bf16[32,16,4]{2,1,0:T(8,128)(2,1)S(1)}, bf16[32,16,4]{2,1,0:T(8,128)(2,1)S(1)}, u32[]{:S(2)}, u32[]{:S(2)}) collective-permute-start(bf16[32,16,4]{2,1,0:T(8,128)(2,1)S(1)} %get-tuple-element.130), channel_id=1, source_target_pairs={{0,32},{32,64},{64,96},{96,128},{128,160},{160,192},{192,224},{224... | collective-permute-start | bytes 12296 | tf_op jit(solution)/shard_map/ppermute | solution.py:21
  623.7 1.4 copy-start.6
Sparse Core Ops, SparseCore 0:
  240.2 305.8 all-reduce.2
where the time goes:
time: 634 us; the launch traced here: 633 us
  waiting for transfers between devices  415 us (65%)
  starting transfers between devices  122 us (19%)
  local copies, waits for them, and re-layouts  69.5 us (11%)
  between operations  14.9 us (2%)
  matrix products  7.06 us (1%)
    psum x1, waiting for transfers between devices, local(): weight_total = lax.psum(weight_term.astype(jnp.bfloat16), 'tile')  306 us
    all_to_all x1, waiting for transfers between devices, local(): lax.all_to_all(token_send, 'head', split_axis=0, concat_axis=1, tiled=True)  45.7 us
    ppermute x8, starting transfers between devices, passed_along(): lax.ppermute(value, axis, [(source, source + steps) for source in range(l...  40 us
    ppermute x8, waiting for transfers between devices, passed_along(): lax.ppermute(value, axis, [(source, source + steps) for source in range(l...  38.8 us
    scatter-add x4, local copies, waits for them, and re-layouts, local(): grad_field.at[:, :, member * TILE_COLS:member * TILE_COLS + PAD_COLS]  25.9 us
    all_to_all x1, starting transfers between devices, local(): lax.all_to_all(grad_send, 'head', split_axis=0, concat_axis=1, tiled=True)  20.3 us
    all_to_all x1, waiting for transfers between devices, local(): lax.all_to_all(grad_send, 'head', split_axis=0, concat_axis=1, tiled=True)  17.6 us
    all_to_all x1, starting transfers between devices, local(): lax.all_to_all(weight_send_back, 'head', split_axis=0, concat_axis=0, til...  15.6 us
  transfers between devices with their start and end apart: 15, of which 8 were waited for; matrix products, arithmetic and copies ran while one was open for 9% of the time, Pallas kernels for 0%

commit v1 on v0

v1 whole, which is shorter than its diff:
```python
import jax
import jax.numpy as jnp
from jax import lax
from jax.sharding import Mesh, PartitionSpec as P

D = 1024
HEADS = 8
HEAD_DIM = 128
TILE_ROWS = 16
TILE_COLS = 16
RIM = 4
PAD_ROWS = 24
PAD_COLS = 24
TILE_TOKENS = 256
PAD_TOKENS = 576
WIDTH = 32
ROWS_TOTAL = 192
COLS_TOTAL = 128

AXES = ("zl", "x", "zh", "y", "c")
SIZES = (6, 4, 2, 8, 2)

bf16 = jnp.bfloat16
f32 = jnp.float32

SWAP2 = [(0, 1), (1, 0)]


def right_pairs():
    pairs = []
    for x in range(4):
        for y in range(8):
            for c in range(2):
                col = (x % 2) * 4 + (y % 2) * 2 + c + 1
                if col < 8:
                    k = col % 4
                    to = (x - x % 2 + col // 4, y - y % 2 + k // 2, k % 2)
                    pairs.append((x * 16 + y * 2 + c, to[0] * 16 + to[1] * 2 + to[2]))
    return pairs


RIGHT = right_pairs()
LEFT = [(b, a) for a, b in RIGHT]
DOWN = [(t, t + 2) for t in range(22)]
UP = [(t + 2, t) for t in range(22)]


def to_right(v):
    return lax.ppermute(v, ("x", "y", "c"), RIGHT)


def to_left(v):
    return lax.ppermute(v, ("x", "y", "c"), LEFT)


def to_down(v):
    return lax.ppermute(v, ("zl", "x"), DOWN)


def to_up(v):
    return lax.ppermute(v, ("zl", "x"), UP)


def a2a(v, axes):
    return lax.all_to_all(v, axes, 0, 0, tiled=True)


def dot(a, b, da, db):
    return lax.dot_general(a, b, (((da,), (db,)), ((), ())), preferred_element_type=f32)


def split_tiles(block):
    return (
        block.reshape(WIDTH, TILE_ROWS, 2, 2, TILE_COLS)
        .transpose(2, 3, 0, 1, 4)
        .reshape(2, 2, WIDTH, TILE_TOKENS)
    )


def join_tiles(tiles):
    return (
        tiles.reshape(2, 2, WIDTH, TILE_ROWS, TILE_COLS)
        .transpose(2, 3, 1, 0, 4)
        .reshape(1, WIDTH, TILE_ROWS, 64)
    )


def local(embedded, cotangent, weights):
    score_scale = HEAD_DIM ** (-0.5)
    zl = lax.axis_index("zl")
    x = lax.axis_index("x")
    zh = lax.axis_index("zh")
    y = lax.axis_index("y")
    c = lax.axis_index("c")

    w_mine = lax.dynamic_index_in_dim(weights, x, 1, keepdims=False).transpose(1, 0, 2)
    w_keep = lax.dynamic_slice_in_dim(w_mine, zh * 4, 4, 0)
    w_give = lax.dynamic_slice_in_dim(w_mine, (1 - zh) * 4, 4, 0)
    w_got = lax.ppermute(w_give, "zh", SWAP2)
    w_rows = jnp.concatenate([w_keep, w_got], 1)
    w_send = jnp.broadcast_to(w_rows[:, None], (4, 2, 64, HEAD_DIM)).reshape(8, 64, HEAD_DIM)
    w_x = a2a(w_send, "y").reshape(512, HEAD_DIM)

    own = jnp.stack([split_tiles(embedded[0]), split_tiles(cotangent[0])], 2)
    other = lax.ppermute(own, "zh", SWAP2)
    both = jnp.stack([own, other], 3)
    both = both.transpose(1, 0, 2, 3, 4, 5)
    mine = a2a(both, "c")
    mine = mine.transpose(1, 2, 0, 3, 4, 5).reshape(1, 2, 2, 2, 64, TILE_TOKENS)
    t_send = jnp.broadcast_to(mine, (4, 2, 2, 2, 64, TILE_TOKENS)).reshape(8, 2, 2, 64, TILE_TOKENS)
    t_in = a2a(t_send, "y")
    t_in = t_in.transpose(1, 2, 0, 3, 4).reshape(2, D, TILE_TOKENS)
    tokens = t_in[0]
    grads = t_in[1]

    w_all = lax.all_gather(w_x, "x")
    w_all = lax.all_gather(w_all, "c")
    w_all = w_all.transpose(0, 2, 1, 3).reshape(D, 4 * HEAD_DIM)
    w_qkv = w_all[:, : 3 * HEAD_DIM]
    w_out = w_all[:, 3 * HEAD_DIM :]

    qkv = dot(tokens, w_qkv, 0, 0).astype(bf16)
    queries = qkv[:, :HEAD_DIM]
    kv = qkv[:, HEAD_DIM:].reshape(TILE_ROWS, TILE_COLS, 2 * HEAD_DIM)
    from_left = to_right(kv[:, TILE_COLS - RIM :])
    from_right = to_left(kv[:, :RIM])
    wide = jnp.concatenate([from_left, kv, from_right], 1)
    from_above = to_down(wide[TILE_ROWS - RIM :])
    from_below = to_up(wide[:RIM])
    window = jnp.concatenate([from_above, wide, from_below], 0).reshape(PAD_TOKENS, 2 * HEAD_DIM)
    keys = window[:, :HEAD_DIM]
    values = window[:, HEAD_DIM:]

    row_pos = (zl * 2 + x // 2) * TILE_ROWS + jnp.arange(PAD_ROWS) - RIM
    col_pos = ((x % 2) * 4 + (y % 2) * 2 + c) * TILE_COLS + jnp.arange(PAD_COLS) - RIM
    key_valid = (
        ((row_pos >= 0) & (row_pos < ROWS_TOTAL))[:, None]
        & ((col_pos >= 0) & (col_pos < COLS_TOTAL))[None, :]
    ).reshape(PAD_TOKENS)

    scores = dot(queries, keys, 1, 1) * score_scale
    scores = jnp.where(key_valid[None, :], scores, -jnp.inf)
    top_score = jnp.max(scores, axis=-1, keepdims=True)
    expo = jnp.exp(scores - top_score)
    probs = expo / jnp.sum(expo, axis=-1, keepdims=True)
    probs_low = probs.astype(bf16)
    attended = dot(probs_low, values, 1, 0).astype(bf16)
    part = dot(w_out, attended, 1, 1).astype(bf16)
    d_attended = dot(grads, w_out, 0, 0).astype(bf16)
    d_probs = dot(d_attended, values, 1, 1)
    d_scores = (
        probs * (d_probs - jnp.sum(d_probs * probs, axis=-1, keepdims=True)) * score_scale
    ).astype(bf16)
    d_queries = dot(d_scores, keys, 1, 0).astype(bf16)
    d_keys = dot(d_scores, queries, 0, 0)
    d_values = dot(probs_low, d_attended, 0, 0)
    d_window = jnp.concatenate([d_keys, d_values], 1).astype(bf16)
    d_window = d_window.reshape(PAD_ROWS, PAD_COLS, 2 * HEAD_DIM)
    back_below = to_up(d_window[:RIM])
    back_above = to_down(d_window[RIM + TILE_ROWS :])
    d_mid = d_window[RIM : RIM + TILE_ROWS].astype(f32)
    d_mid = (
        d_mid
        + jnp.pad(back_below.astype(f32), ((TILE_ROWS - RIM, 0), (0, 0), (0, 0)))
        + jnp.pad(back_above.astype(f32), ((0, TILE_ROWS - RIM), (0, 0), (0, 0)))
    )
    back_right = to_left(d_mid[:, :RIM].astype(bf16))
    back_left = to_right(d_mid[:, RIM + TILE_COLS :].astype(bf16))
    d_kv = (
        d_mid[:, RIM : RIM + TILE_COLS]
        + jnp.pad(back_right.astype(f32), ((0, 0), (TILE_COLS - RIM, 0), (0, 0)))
        + jnp.pad(back_left.astype(f32), ((0, 0), (0, TILE_COLS - RIM), (0, 0)))
    )
    d_kv = d_kv.astype(bf16).reshape(TILE_TOKENS, 2 * HEAD_DIM)
    d_qkv = jnp.concatenate([d_queries, d_kv], 1)

    dw = jnp.concatenate([dot(tokens, d_qkv, 1, 0), dot(grads, attended, 1, 0)], 1).astype(bf16)
    dw = dw.reshape(2, 512, 4, HEAD_DIM).transpose(2, 0, 1, 3).reshape(8, 512, HEAD_DIM)
    dw = jnp.sum(a2a(dw, ("x", "c")).astype(f32), 0).astype(bf16)
    dw = a2a(dw.reshape(8, 64, HEAD_DIM), "y")
    dw = jnp.sum(dw.reshape(4, 2, 64, HEAD_DIM).astype(f32), 1).astype(bf16)
    dw = dw.reshape(4, 2, WIDTH, HEAD_DIM)
    dw_near, dw_far = dw[:, 0], dw[:, 1]
    first = zh == 0
    dw = jnp.stack([jnp.where(first, dw_near, dw_far), jnp.where(first, dw_far, dw_near)])
    dw = jnp.broadcast_to(dw[None], (6, 2, 4, WIDTH, HEAD_DIM)).reshape(12, 4, WIDTH, HEAD_DIM)
    dw = a2a(dw, ("zl", "zh")).reshape(6, HEADS, WIDTH, HEAD_DIM)
    dw = jnp.sum(dw.astype(f32), 0).astype(bf16)
    dw = lax.all_gather(dw, "x")
    weight_grads = dw.transpose(2, 0, 1, 3).astype(f32)

    d_tokens = dot(w_qkv, d_qkv, 1, 1).astype(bf16)
    back = jnp.stack([part, d_tokens]).reshape(2, 2, 8, 2, WIDTH, TILE_TOKENS)
    back = back.transpose(2, 0, 1, 3, 4, 5)
    back = a2a(back, "y").reshape(4, 2, 2, 2, 2, WIDTH, TILE_TOKENS).astype(f32)
    back = jnp.sum(back, 0)
    far = lax.ppermute(back[:, :, :, 1].astype(bf16), "zh", SWAP2)
    back = back[:, :, :, 0] + far.astype(f32)
    out = a2a(back[:, 0].astype(bf16).transpose(1, 0, 2, 3), "c")
    grad = a2a(back[:, 1].transpose(1, 0, 2, 3), "c")
    return join_tiles(out), join_tiles(grad), weight_grads


def solution(mesh):
    inner = Mesh(mesh.devices.reshape(SIZES), AXES)
    strips = P(("zl", "x"), ("zh", "y", "c"), None, None)
    rows = P(("zh", "y", "c"), None, None, None)
    return jax.shard_map(
        local,
        mesh=inner,
        in_specs=(strips, strips, rows),
        out_specs=(strips, strips, rows),
        check_vma=False,
    )
```

time: 634 us -> 318 us (0.50)
  the two profiles are of different devices: /device:TPU:22 before, /device:TPU:64 now
where the time goes in v1:
time: 318 us; the launch traced here: 317 us
  waiting for transfers between devices  150 us (47%)
  starting transfers between devices  94.1 us (30%)
  blocking collectives  38.1 us (12%)
  between operations  14.7 us (5%)
  local copies, waits for them, and re-layouts  13.9 us (4%)
  matrix products  3.87 us (1%)
  other arithmetic  3.29 us (1%)
    all_to_all x6, waiting for transfers between devices, a2a(): return lax.all_to_all(v, axes, 0, 0, tiled=True)  74.8 us
    all_to_all x6, starting transfers between devices, a2a(): return lax.all_to_all(v, axes, 0, 0, tiled=True)  44.1 us
    ppermute x1, waiting for transfers between devices, local(): other = lax.ppermute(own, 'zh', SWAP2)  42.1 us
    all_gather x1, waiting for transfers between devices, local(): w_all = lax.all_gather(w_all, 'c')  16.8 us
    ppermute x1, starting transfers between devices, local(): w_got = lax.ppermute(w_give, 'zh', SWAP2)  14.2 us
    all_gather x1, blocking collectives, local(): w_all = lax.all_gather(w_x, 'x')  14.2 us
    all_gather x1, blocking collectives, local(): dw = lax.all_gather(dw, 'x')  12.3 us
    all_to_all x3, blocking collectives, a2a(): return lax.all_to_all(v, axes, 0, 0, tiled=True)  11.6 us
  transfers between devices with their start and end apart: 18, of which 13 were waited for; matrix products, arithmetic and copies ran while one was open for 3% of the time, Pallas kernels for 0%

profile of v1, /device:TPU:64, one launch (start us, length us, event | category | flops | bytes accessed | tf_op | source)
XLA Modules:
  0.0 317.4 jit_solution(47530942253138719)
XLA Ops:
  8.2 14.2 %collective-permute-start = (bf16[4,32,128]{2,1,0:T(8,128)(2,1)S(1)}, bf16[4,32,128]{2,1,0:T(8,128)(2,1)S(1)}, u32[]{:S(2)}, u32[]{:S(2)}) collective-permute-start(bf16[4,32,128]{2,1,0:T(8,128)(2,1)S(1)} %bitcast.166), channel_id=1, source_target_pairs={{0,16},{16,0},{1,17},{17,1},{2,18},{18,2},{3,19},{19,3},{4,20},{20... | collective-permute-start | bytes 98312 | tf_op jit(solution)/shard_map/ppermute | solution.py:99
  25.9 42.1 %collective-permute-done.1 = bf16[2,2,2,32,256]{3,4,1,0,2:T(8,128)(2,1)S(1)} collective-permute-done((bf16[2,2,2,32,256]{3,4,1,0,2:T(8,128)(2,1)S(1)}, bf16[2,2,2,32,256]{3,4,1,0,2:T(8,128)(2,1)S(1)}, u32[]{:S(2)}, u32[]{:S(2)}) %collective-permute-start.1) | collective-permute-done | bytes 131104 | tf_op jit(solution)/shard_map/ppermute | solution.py:105
  68.5 3.9 %all_to_all.45 = bf16[2,2,2,2,32,256]{5,4,3,2,1,0:T(8,128)(2,1)S(1)} all-to-all(bf16[2,2,2,2,32,256]{5,4,3,2,1,0:T(8,128)(2,1)S(1)} %copy.146), channel_id=1, replica_groups=mesh['zl'=6,'x'=4,'zh'=2,'y'=8,'c'=2] {'c'}, dimensions={0} | all-to-all | bytes 524288 | tf_op jit(solution)/shard_map/all_to_all | solution.py:65
  73.2 7.1 %all-to-all-start = ((bf16[8,64,128]{2,1,0:T(8,128)(2,1)}), bf16[8,64,128]{2,1,0:T(8,128)(2,1)S(1)}, u32[]{:S(2)}, u32[]{:S(2)}) async-start(bf16[8,64,128]{2,1,0:T(8,128)(2,1)} %bitcast.4), calls=%async_computation | async-start | bytes 262144 | tf_op jit(solution)/shard_map/all_to_all | solution.py:65
  80.3 9.4 %all-to-all-done = bf16[8,64,128]{2,1,0:T(8,128)(2,1)S(1)} async-done(((bf16[8,64,128]{2,1,0:T(8,128)(2,1)}), bf16[8,64,128]{2,1,0:T(8,128)(2,1)S(1)}, u32[]{:S(2)}, u32[]{:S(2)}) %all-to-all-start) | async-done | bytes 131104 | tf_op jit(solution)/shard_map/all_to_all | solution.py:65
  90.8 3.6 %all-to-all-start.2 = ((bf16[8,2,2,64,256]{4,3,2,1,0:T(8,128)(2,1)}), bf16[8,2,2,64,256]{4,3,2,1,0:T(8,128)(2,1)S(1)}, u32[]{:S(2)}, u32[]{:S(2)}) async-start(bf16[8,2,2,64,256]{4,3,2,1,0:T(8,128)(2,1)} %bitcast.19), calls=%async_computation.2 | async-start | bytes 2097152 | tf_op jit(solution)/shard_map/all_to_all | solution.py:65
  94.4 14.2 %all_gather.15 = bf16[4,512,128]{2,1,0:T(8,128)(2,1)} all-gather(bf16[1,512,128]{2,1,0:T(8,128)(2,1)S(1)} %bitcast.159), channel_id=1, replica_groups=mesh['zl'=6,'x'=4,'zh'=2,'y'=8,'c'=2] {'x'}, dimensions={0}, use_global_device_ids=true | all-gather | bytes 655360 | tf_op jit(solution)/shard_map/all_gather | solution.py:116
  108.7 16.8 %all-gather.4.cloned.1.call-done = bf16[8,512,128]{2,1,0:T(8,128)(2,1)} async-done(((bf16[4,512,128]{2,1,0:T(8,128)(2,1)}), bf16[8,512,128]{2,1,0:T(8,128)(2,1)}) %all-gather.4.cloned.1.call-update) | async-done | bytes 1048592 | tf_op jit(solution)/shard_map/all_gather | solution.py:117
  125.5 2.0 copy.141
  128.5 2.2 collective-permute-start.2
  132.2 2.4 collective-permute-done.3
  134.7 4.9 %collective-permute-start.4 = (bf16[4,24,256]{2,1,0:T(8,128)(2,1)S(1)}, bf16[4,24,256]{2,1,0:T(8,128)(2,1)S(1)}, u32[]{:S(2)}, u32[]{:S(2)}) collective-permute-start(bf16[4,24,256]{2,1,0:T(8,128)(2,1)S(1)} %get-tuple-element.33), channel_id=1, source_target_pairs={{0,64},{32,96},{64,128},{96,160},{128,192},{160,224},{192,256},{22... | collective-permute-start | bytes 147464 | tf_op jit(solution)/shard_map/ppermute | solution.py:57
  139.6 3.4 %collective-permute-start.5 = (bf16[4,24,256]{2,1,0:T(8,128)(2,1)S(1)}, bf16[4,24,256]{2,1,0:T(8,128)(2,1)S(1)}, u32[]{:S(2)}, u32[]{:S(2)}) collective-permute-start(bf16[4,24,256]{2,1,0:T(8,128)(2,1)S(1)} %get-tuple-element.34), channel_id=1, source_target_pairs={{64,0},{96,32},{128,64},{160,96},{192,128},{224,160},{256,192},{28... | collective-permute-start | bytes 147464 | tf_op jit(solution)/shard_map/ppermute | solution.py:61
  143.3 3.8 %collective-permute-done.5 = bf16[4,24,256]{2,1,0:T(8,128)(2,1)S(1)} collective-permute-done((bf16[4,24,256]{2,1,0:T(8,128)(2,1)S(1)}, bf16[4,24,256]{2,1,0:T(8,128)(2,1)S(1)}, u32[]{:S(2)}, u32[]{:S(2)}) %collective-permute-start.5) | collective-permute-done | bytes 49184 | tf_op jit(solution)/shard_map/ppermute | solution.py:61
  148.9 4.3 %collective-permute-start.6 = (bf16[4,24,256]{2,1,0:T(8,128)(2,1)S(1)}, bf16[4,24,256]{2,1,0:T(8,128)(2,1)S(1)}, u32[]{:S(2)}, u32[]{:S(2)}) collective-permute-start(bf16[4,24,256]{2,1,0:T(8,128)(2,1)S(1)} %bitcast.165), channel_id=1, source_target_pairs={{64,0},{96,32},{128,64},{160,96},{192,128},{224,160},{256,192},{28... | collective-permute-start | bytes 147464 | tf_op jit(solution)/shard_map/ppermute | solution.py:61
  153.1 3.1 collective-permute-start.7
  156.6 5.4 %collective-permute-done.7 = bf16[4,24,256]{2,1,0:T(8,128)(2,1)S(1)} collective-permute-done((bf16[4,24,256]{2,1,0:T(8,128)(2,1)S(1)}, bf16[4,24,256]{2,1,0:T(8,128)(2,1)S(1)}, u32[]{:S(2)}, u32[]{:S(2)}) %collective-permute-start.7) | collective-permute-done | bytes 49184 | tf_op jit(solution)/shard_map/ppermute | solution.py:57
  163.4 3.0 collective-permute-start.9
  168.6 2.0 copy.158
  170.6 7.6 %all-to-all-start.6 = ((bf16[8,512,128]{2,1,0:T(8,128)(2,1)}), bf16[8,512,128]{2,1,0:T(8,128)(2,1)S(1)}, u32[]{:S(2)}, u32[]{:S(2)}) async-start(bf16[8,512,128]{2,1,0:T(8,128)(2,1)} %bitcast.46), calls=%async_computation.6 | async-start | bytes 2097152 | tf_op jit(solution)/shard_map/all_to_all | solution.py:65
  178.5 15.6 %all-to-all-done.6 = bf16[8,512,128]{2,1,0:T(8,128)(2,1)S(1)} async-done(((bf16[8,512,128]{2,1,0:T(8,128)(2,1)}), bf16[8,512,128]{2,1,0:T(8,128)(2,1)S(1)}, u32[]{:S(2)}, u32[]{:S(2)}) %all-to-all-start.6) | async-done | bytes 1048608 | tf_op jit(solution)/shard_map/all_to_all | solution.py:65
  195.0 6.4 %all-to-all-start.7 = ((bf16[8,64,128]{2,1,0:T(8,128)(2,1)}), bf16[8,64,128]{2,1,0:T(8,128)(2,1)S(1)}, u32[]{:S(2)}, u32[]{:S(2)}) async-start(bf16[8,64,128]{2,1,0:T(8,128)(2,1)} %bitcast.47), calls=%async_computation.7 | async-start | bytes 262144 | tf_op jit(solution)/shard_map/all_to_all | solution.py:65
  202.9 7.6 %all-to-all-done.7 = bf16[8,64,128]{2,1,0:T(8,128)(2,1)S(1)} async-done(((bf16[8,64,128]{2,1,0:T(8,128)(2,1)}), bf16[8,64,128]{2,1,0:T(8,128)(2,1)S(1)}, u32[]{:S(2)}, u32[]{:S(2)}) %all-to-all-start.7) | async-done | bytes 131104 | tf_op jit(solution)/shard_map/all_to_all | solution.py:65
  210.4 3.6 %all-to-all-start.3 = ((bf16[8,2,2,2,32,256]{5,4,3,2,1,0:T(8,128)(2,1)}), bf16[8,2,2,2,32,256]{5,4,3,2,1,0:T(8,128)(2,1)S(1)}, u32[]{:S(2)}, u32[]{:S(2)}) async-start(bf16[8,2,2,2,32,256]{5,4,3,2,1,0:T(8,128)(2,1)} %copy_bitcast_fusion.1), calls=%async_computation.3 | async-start | bytes 2097152 | tf_op jit(solution)/shard_map/all_to_all | solution.py:65
  214.0 27.2 %all-to-all-done.3 = bf16[8,2,2,2,32,256]{5,4,3,2,1,0:T(8,128)(2,1)S(1)} async-done(((bf16[8,2,2,2,32,256]{5,4,3,2,1,0:T(8,128)(2,1)}), bf16[8,2,2,2,32,256]{5,4,3,2,1,0:T(8,128)(2,1)S(1)}, u32[]{:S(2)}, u32[]{:S(2)}) %all-to-all-start.3) | async-done | bytes 1048608 | tf_op jit(solution)/shard_map/all_to_all | solution.py:65
  241.5 10.4 %collective-permute-start.10 = (bf16[2,2,2,32,256]{4,3,0,2,1:T(8,128)(2,1)S(1)}, bf16[2,2,2,32,256]{4,3,0,2,1:T(8,128)(2,1)S(1)}, u32[]{:S(2)}, u32[]{:S(2)}) collective-permute-start(bf16[2,2,2,32,256]{4,3,0,2,1:T(8,128)(2,1)S(1)} %fusion.14), channel_id=1, source_target_pairs={{0,16},{16,0},{1,17},{17,1},{2,18},{18,2},{3,19},{19,3},{4,20},{20... | collective-permute-start | bytes 393224 | tf_op jit(solution)/shard_map/ppermute | solution.py:197
  252.0 3.7 %collective-permute-done.10 = bf16[2,2,2,32,256]{4,3,0,2,1:T(8,128)(2,1)S(1)} collective-permute-done((bf16[2,2,2,32,256]{4,3,0,2,1:T(8,128)(2,1)S(1)}, bf16[2,2,2,32,256]{4,3,0,2,1:T(8,128)(2,1)S(1)}, u32[]{:S(2)}, u32[]{:S(2)}) %collective-permute-start.10) | collective-permute-done | bytes 131104 | tf_op jit(solution)/shard_map/ppermute | solution.py:197
  255.8 3.8 %all_to_all.46 = f32[2,2,32,256]{3,2,1,0:T(8,128)S(1)} all-to-all(f32[2,2,32,256]{3,2,1,0:T(8,128)S(1)} %slice_bitcast_fusion), channel_id=1, replica_groups=mesh['zl'=6,'x'=4,'zh'=2,'y'=8,'c'=2] {'c'}, dimensions={0} | all-to-all | bytes 262144 | tf_op jit(solution)/shard_map/all_to_all | solution.py:65
  259.6 3.8 %all_to_all.47 = bf16[2,2,32,256]{3,2,1,0:T(8,128)(2,1)S(1)} all-to-all(bf16[2,2,32,256]{3,2,1,0:T(8,128)(2,1)S(1)} %fusion.20), channel_id=1, replica_groups=mesh['zl'=6,'x'=4,'zh'=2,'y'=8,'c'=2] {'c'}, dimensions={0} | all-to-all | bytes 131072 | tf_op jit(solution)/shard_map/all_to_all | solution.py:65
  264.2 15.9 %all-to-all-start.8 = ((bf16[12,4,32,128]{3,2,1,0:T(8,128)(2,1)}), bf16[12,4,32,128]{3,2,1,0:T(8,128)(2,1)S(1)}, u32[]{:S(2)}, u32[]{:S(2)}) async-start(bf16[12,4,32,128]{3,2,1,0:T(8,128)(2,1)} %bitcast.55), calls=%async_computation.8 | async-start | bytes 786432 | tf_op jit(solution)/shard_map/all_to_all | solution.py:65
  282.3 15.0 %all-to-all-done.8 = bf16[12,4,32,128]{3,2,1,0:T(8,128)(2,1)S(1)} async-done(((bf16[12,4,32,128]{3,2,1,0:T(8,128)(2,1)}), bf16[12,4,32,128]{3,2,1,0:T(8,128)(2,1)S(1)}, u32[]{:S(2)}, u32[]{:S(2)}) %all-to-all-start.8) | async-done | bytes 393248 | tf_op jit(solution)/shard_map/all_to_all | solution.py:65
  297.4 12.3 %all-gather.1 = bf16[32,32,128]{2,1,0:T(8,128)(2,1)S(1)} all-gather(bf16[8,32,128]{2,1,0:T(8,128)(2,1)S(1)} %bitcast_reduce_fusion), channel_id=3, replica_groups=mesh['zl'=6,'x'=4,'zh'=2,'y'=8,'c'=2] {'x'}, dimensions={0}, use_global_device_ids=true | all-gather | bytes 327680 | tf_op jit(solution)/shard_map/all_gather | solution.py:189
  (88 shorter events, 22.1 us)
Async XLA Ops:
  7.2 16.4 %copy-start.4 = (bf16[1,32,16,64]{3,2,1,0:T(8,128)(2,1)S(1)}, bf16[1,32,16,64]{3,2,1,0:T(8,128)(2,1)}, u32[]{:S(2)}) copy-start(bf16[1,32,16,64]{3,2,1,0:T(8,128)(2,1)} %param.4) | copy-start | bytes 196612
  8.2 17.7 %collective-permute-start = (bf16[4,32,128]{2,1,0:T(8,128)(2,1)S(1)}, bf16[4,32,128]{2,1,0:T(8,128)(2,1)S(1)}, u32[]{:S(2)}, u32[]{:S(2)}) collective-permute-start(bf16[4,32,128]{2,1,0:T(8,128)(2,1)S(1)} %bitcast.166), channel_id=1, source_target_pairs={{0,16},{16,0},{1,17},{17,1},{2,18},{18,2},{3,19},{19,3},{4,20},{20... | collective-permute-start | bytes 98312 | tf_op jit(solution)/shard_map/ppermute | solution.py:99
  23.9 44.0 %collective-permute-start.1 = (bf16[2,2,2,32,256]{3,4,1,0,2:T(8,128)(2,1)S(1)}, bf16[2,2,2,32,256]{3,4,1,0,2:T(8,128)(2,1)S(1)}, u32[]{:S(2)}, u32[]{:S(2)}) collective-permute-start(bf16[2,2,2,32,256]{3,4,1,0,2:T(8,128)(2,1)S(1)} %get-tuple-element.24), channel_id=1, source_target_pairs={{0,16},{16,0},{1,17},{17,1},{2,18},{18,2},{3,19},{19,3},{4,20},{20... | collective-permute-start | bytes 393224 | tf_op jit(solution)/shard_map/ppermute | solution.py:105
  73.2 16.5 %all-to-all-start = ((bf16[8,64,128]{2,1,0:T(8,128)(2,1)}), bf16[8,64,128]{2,1,0:T(8,128)(2,1)S(1)}, u32[]{:S(2)}, u32[]{:S(2)}) async-start(bf16[8,64,128]{2,1,0:T(8,128)(2,1)} %bitcast.4), calls=%async_computation | async-start | bytes 262144 | tf_op jit(solution)/shard_map/all_to_all | solution.py:65
  90.8 37.0 %all-to-all-start.2 = ((bf16[8,2,2,64,256]{4,3,2,1,0:T(8,128)(2,1)}), bf16[8,2,2,64,256]{4,3,2,1,0:T(8,128)(2,1)S(1)}, u32[]{:S(2)}, u32[]{:S(2)}) async-start(bf16[8,2,2,64,256]{4,3,2,1,0:T(8,128)(2,1)} %bitcast.19), calls=%async_computation.2 | async-start | bytes 2097152 | tf_op jit(solution)/shard_map/all_to_all | solution.py:65
  94.3 31.2 %all-gather.4.cloned.1.call-start = ((), (), s32[]{:S(2)}) async-start(), calls=%async_computation.9 | async-start | bytes 1572864 | tf_op jit(solution)/shard_map/all_gather | solution.py:117
  128.5 3.7 %collective-permute-start.2 = (bf16[16,4,256]{2,1,0:T(4,128)(2,1)S(1)}, bf16[16,4,256]{2,1,0:T(4,128)(2,1)S(1)}, u32[]{:S(2)}, u32[]{:S(2)}) collective-permute-start(bf16[16,4,256]{2,1,0:T(4,128)(2,1)S(1)} %get-tuple-element.35), channel_id=1, source_target_pairs={{0,1},{1,2},{2,3},{3,32},{4,5},{5,6},{6,7},{7,36},{8,9},{9,10},{10... | collective-permute-start | bytes 98312 | tf_op jit(solution)/shard_map/ppermute | solution.py:49
  130.7 3.9 %collective-permute-start.3 = (bf16[16,4,256]{2,1,0:T(4,128)(2,1)S(1)}, bf16[16,4,256]{2,1,0:T(4,128)(2,1)S(1)}, u32[]{:S(2)}, u32[]{:S(2)}) collective-permute-start(bf16[16,4,256]{2,1,0:T(4,128)(2,1)S(1)} %get-tuple-element.36), channel_id=1, source_target_pairs={{1,0},{2,1},{3,2},{32,3},{5,4},{6,5},{7,6},{36,7},{9,8},{10,9},{11... | collective-permute-start | bytes 98312 | tf_op jit(solution)/shard_map/ppermute | solution.py:53
  134.7 8.6 %collective-permute-start.4 = (bf16[4,24,256]{2,1,0:T(8,128)(2,1)S(1)}, bf16[4,24,256]{2,1,0:T(8,128)(2,1)S(1)}, u32[]{:S(2)}, u32[]{:S(2)}) collective-permute-start(bf16[4,24,256]{2,1,0:T(8,128)(2,1)S(1)} %get-tuple-element.33), channel_id=1, source_target_pairs={{0,64},{32,96},{64,128},{96,160},{128,192},{160,224},{192,256},{22... | collective-permute-start | bytes 147464 | tf_op jit(solution)/shard_map/ppermute | solution.py:57
  139.6 7.5 %collective-permute-start.5 = (bf16[4,24,256]{2,1,0:T(8,128)(2,1)S(1)}, bf16[4,24,256]{2,1,0:T(8,128)(2,1)S(1)}, u32[]{:S(2)}, u32[]{:S(2)}) collective-permute-start(bf16[4,24,256]{2,1,0:T(8,128)(2,1)S(1)} %get-tuple-element.34), channel_id=1, source_target_pairs={{64,0},{96,32},{128,64},{160,96},{192,128},{224,160},{256,192},{28... | collective-permute-start | bytes 147464 | tf_op jit(solution)/shard_map/ppermute | solution.py:61
  148.4 7.8 %copy-start.2 = (bf16[256,128]{1,0:T(8,128)(2,1)}, bf16[256,128]{1,0:T(8,128)(2,1)S(1)}, u32[]{:S(2)}) copy-start(bf16[256,128]{1,0:T(8,128)(2,1)S(1)} %convolution_convert_fusion.9) | copy-start | bytes 196612
  148.9 7.8 %collective-permute-start.6 = (bf16[4,24,256]{2,1,0:T(8,128)(2,1)S(1)}, bf16[4,24,256]{2,1,0:T(8,128)(2,1)S(1)}, u32[]{:S(2)}, u32[]{:S(2)}) collective-permute-start(bf16[4,24,256]{2,1,0:T(8,128)(2,1)S(1)} %bitcast.165), channel_id=1, source_target_pairs={{64,0},{96,32},{128,64},{160,96},{192,128},{224,160},{256,192},{28... | collective-permute-start | bytes 147464 | tf_op jit(solution)/shard_map/ppermute | solution.py:61
  153.1 8.9 %collective-permute-start.7 = (bf16[4,24,256]{2,1,0:T(8,128)(2,1)S(1)}, bf16[4,24,256]{2,1,0:T(8,128)(2,1)S(1)}, u32[]{:S(2)}, u32[]{:S(2)}) collective-permute-start(bf16[4,24,256]{2,1,0:T(8,128)(2,1)S(1)} %bitcast.164), channel_id=1, source_target_pairs={{0,64},{32,96},{64,128},{96,160},{128,192},{160,224},{192,256},{22... | collective-permute-start | bytes 147464 | tf_op jit(solution)/shard_map/ppermute | solution.py:57
  162.1 4.7 %collective-permute-start.8 = (bf16[16,4,256]{2,1,0:T(4,128)(2,1)S(1)}, bf16[16,4,256]{2,1,0:T(4,128)(2,1)S(1)}, u32[]{:S(2)}, u32[]{:S(2)}) collective-permute-start(bf16[16,4,256]{2,1,0:T(4,128)(2,1)S(1)} %get-tuple-element.31), channel_id=1, source_target_pairs={{1,0},{2,1},{3,2},{32,3},{5,4},{6,5},{7,6},{36,7},{9,8},{10,9},{11... | collective-permute-start | bytes 98312 | tf_op jit(solution)/shard_map/ppermute | solution.py:53
  163.4 3.9 %collective-permute-start.9 = (bf16[16,4,256]{2,1,0:T(4,128)(2,1)S(1)}, bf16[16,4,256]{2,1,0:T(4,128)(2,1)S(1)}, u32[]{:S(2)}, u32[]{:S(2)}) collective-permute-start(bf16[16,4,256]{2,1,0:T(4,128)(2,1)S(1)} %get-tuple-element.32), channel_id=1, source_target_pairs={{0,1},{1,2},{2,3},{3,32},{4,5},{5,6},{6,7},{7,36},{8,9},{9,10},{10... | collective-permute-start | bytes 98312 | tf_op jit(solution)/shard_map/ppermute | solution.py:49
  166.8 0.9 copy-start
  170.6 7.6 %copy-start.3 = (bf16[256,128]{1,0:T(8,128)(2,1)S(1)}, bf16[256,128]{1,0:T(8,128)(2,1)}, u32[]{:S(2)}) copy-start(bf16[256,128]{1,0:T(8,128)(2,1)} %copy-done.2) | copy-start | bytes 196612
  170.6 23.5 %all-to-all-start.6 = ((bf16[8,512,128]{2,1,0:T(8,128)(2,1)}), bf16[8,512,128]{2,1,0:T(8,128)(2,1)S(1)}, u32[]{:S(2)}, u32[]{:S(2)}) async-start(bf16[8,512,128]{2,1,0:T(8,128)(2,1)} %bitcast.46), calls=%async_computation.6 | async-start | bytes 2097152 | tf_op jit(solution)/shard_map/all_to_all | solution.py:65
  178.2 23.1 %copy-start.1 = (bf16[256,128]{1,0:T(8,128)(2,1)S(1)}, bf16[256,128]{1,0:T(8,128)(2,1)}, u32[]{:S(2)}) copy-start(bf16[256,128]{1,0:T(8,128)(2,1)} %copy-done) | copy-start | bytes 196612
  195.0 15.4 %all-to-all-start.7 = ((bf16[8,64,128]{2,1,0:T(8,128)(2,1)}), bf16[8,64,128]{2,1,0:T(8,128)(2,1)S(1)}, u32[]{:S(2)}, u32[]{:S(2)}) async-start(bf16[8,64,128]{2,1,0:T(8,128)(2,1)} %bitcast.47), calls=%async_computation.7 | async-start | bytes 262144 | tf_op jit(solution)/shard_map/all_to_all | solution.py:65
  210.4 30.9 %all-to-all-start.3 = ((bf16[8,2,2,2,32,256]{5,4,3,2,1,0:T(8,128)(2,1)}), bf16[8,2,2,2,32,256]{5,4,3,2,1,0:T(8,128)(2,1)S(1)}, u32[]{:S(2)}, u32[]{:S(2)}) async-start(bf16[8,2,2,2,32,256]{5,4,3,2,1,0:T(8,128)(2,1)} %copy_bitcast_fusion.1), calls=%async_computation.3 | async-start | bytes 2097152 | tf_op jit(solution)/shard_map/all_to_all | solution.py:65
  241.5 14.2 %collective-permute-start.10 = (bf16[2,2,2,32,256]{4,3,0,2,1:T(8,128)(2,1)S(1)}, bf16[2,2,2,32,256]{4,3,0,2,1:T(8,128)(2,1)S(1)}, u32[]{:S(2)}, u32[]{:S(2)}) collective-permute-start(bf16[2,2,2,32,256]{4,3,0,2,1:T(8,128)(2,1)S(1)} %fusion.14), channel_id=1, source_target_pairs={{0,16},{16,0},{1,17},{17,1},{2,18},{18,2},{3,19},{19,3},{4,20},{20... | collective-permute-start | bytes 393224 | tf_op jit(solution)/shard_map/ppermute | solution.py:197
  264.2 33.1 %all-to-all-start.8 = ((bf16[12,4,32,128]{3,2,1,0:T(8,128)(2,1)}), bf16[12,4,32,128]{3,2,1,0:T(8,128)(2,1)S(1)}, u32[]{:S(2)}, u32[]{:S(2)}) async-start(bf16[12,4,32,128]{3,2,1,0:T(8,128)(2,1)} %bitcast.55), calls=%async_computation.8 | async-start | bytes 786432 | tf_op jit(solution)/shard_map/all_to_all | solution.py:65
Sparse Core Ops, SparseCore 0:
  108.8 16.7 all-gather.3

commit v2 on v1

--- a/solution.py
+++ b/solution.py
@@ -3,8 +3,8 @@
 from jax import lax
 from jax.sharding import Mesh, PartitionSpec as P
 
+
 D = 1024
-HEADS = 8
 HEAD_DIM = 128
 TILE_ROWS = 16
 TILE_COLS = 16
@@ -23,8 +23,6 @@
 bf16 = jnp.bfloat16
 f32 = jnp.float32
 
-SWAP2 = [(0, 1), (1, 0)]
-
 
 def right_pairs():
     pairs = []
@@ -69,6 +67,37 @@
     return lax.dot_general(a, b, (((da,), (db,)), ((), ())), preferred_element_type=f32)
 
 
+def shift(v, axis, count, step, by):
+    size = lax.axis_size(axis)
+    ring = count * step
+    pairs = []
+    for i in range(size):
+        base = i - i % ring
+        pairs.append((i, base + (i % ring - by * step) % ring))
+    return lax.ppermute(v, axis, pairs)
+
+
+def swap(v, axis):
+    return lax.ppermute(v, axis, [(i, i ^ 1) for i in range(lax.axis_size(axis))])
+
+
+def swap_diag(v):
+    return lax.ppermute(v, ("zh", "y", "c"), [(i, (i ^ 1) ^ 16) for i in range(32)])
+
+
+def pick(v, index, axis=0):
+    return lax.dynamic_index_in_dim(v, index, axis, keepdims=False)
+
+
+def unroll(parts, me):
+    return lax.dynamic_slice_in_dim(jnp.stack(parts + parts), (4 - me) % 4, 4, 0)
+
+
+def in_order(mine, other, bit):
+    first = bit == 0
+    return jnp.where(first, mine, other), jnp.where(first, other, mine)
+
+
 def split_tiles(block):
     return (
         block.reshape(WIDTH, TILE_ROWS, 2, 2, TILE_COLS)
@@ -85,7 +114,7 @@
     )
 
 
-def local(embedded, cotangent, weights):
+def work(embedded, cotangent, weights):
     score_scale = HEAD_DIM ** (-0.5)
     zl = lax.axis_index("zl")
     x = lax.axis_index("x")
@@ -93,31 +122,38 @@
     y = lax.axis_index("y")
     c = lax.axis_index("c")
 
-    w_mine = lax.dynamic_index_in_dim(weights, x, 1, keepdims=False).transpose(1, 0, 2)
+    y2 = y // 2
+    b = y % 2
+
+    w_mine = pick(weights, x, 1).transpose(1, 0, 2)
     w_keep = lax.dynamic_slice_in_dim(w_mine, zh * 4, 4, 0)
     w_give = lax.dynamic_slice_in_dim(w_mine, (1 - zh) * 4, 4, 0)
-    w_got = lax.ppermute(w_give, "zh", SWAP2)
-    w_rows = jnp.concatenate([w_keep, w_got], 1)
-    w_send = jnp.broadcast_to(w_rows[:, None], (4, 2, 64, HEAD_DIM)).reshape(8, 64, HEAD_DIM)
-    w_x = a2a(w_send, "y").reshape(512, HEAD_DIM)
-
-    own = jnp.stack([split_tiles(embedded[0]), split_tiles(cotangent[0])], 2)
-    other = lax.ppermute(own, "zh", SWAP2)
-    both = jnp.stack([own, other], 3)
-    both = both.transpose(1, 0, 2, 3, 4, 5)
-    mine = a2a(both, "c")
-    mine = mine.transpose(1, 2, 0, 3, 4, 5).reshape(1, 2, 2, 2, 64, TILE_TOKENS)
-    t_send = jnp.broadcast_to(mine, (4, 2, 2, 2, 64, TILE_TOKENS)).reshape(8, 2, 2, 64, TILE_TOKENS)
-    t_in = a2a(t_send, "y")
-    t_in = t_in.transpose(1, 2, 0, 3, 4).reshape(2, D, TILE_TOKENS)
-    tokens = t_in[0]
-    grads = t_in[1]
-
-    w_all = lax.all_gather(w_x, "x")
-    w_all = lax.all_gather(w_all, "c")
-    w_all = w_all.transpose(0, 2, 1, 3).reshape(D, 4 * HEAD_DIM)
-    w_qkv = w_all[:, : 3 * HEAD_DIM]
-    w_out = w_all[:, 3 * HEAD_DIM :]
+    w_zh = swap(w_give, "zh")
+    w_zc = swap_diag(w_give)
+    w_c = swap(w_keep, "c")
+    w_rows = jnp.stack([w_keep, w_zh, w_c, w_zc], 1).reshape(4, 128, HEAD_DIM)
+    w_near = [pick(w_rows, y2)] + [
+        shift(pick(w_rows, (y2 - s) % 4), "y", 4, 2, s) for s in (1, 2, 3)
+    ]
+    w_near = unroll(w_near, y2)
+    w_even, w_odd = in_order(w_near, swap(w_near, "y"), b)
+    w_x = jnp.stack([w_even, w_odd], 1).reshape(D, HEAD_DIM)
+
+    def gather_tiles(block):
+        own = split_tiles(block)
+        keep = pick(own, c, 1)
+        give = pick(own, 1 - c, 1)
+        mine = jnp.stack([keep, swap(keep, "zh"), swap(give, "c"), swap_diag(give)], 1)
+        mine = mine.reshape(1, 2, 128, TILE_TOKENS)
+        send = jnp.broadcast_to(mine, (4, 2, 128, TILE_TOKENS)).reshape(8, 128, TILE_TOKENS)
+        return a2a(send, "y").reshape(D, TILE_TOKENS)
+
+    tokens = gather_tiles(embedded[0])
+    grads = gather_tiles(cotangent[0])
+
+    w_list = jnp.stack([w_x] + [shift(w_x, "x", 4, 1, s) for s in (1, 2, 3)])
+    w_qkv = jnp.concatenate([pick(w_list, (m - x) % 4) for m in range(3)], 1)
+    w_out = pick(w_list, (3 - x) % 4)
 
     qkv = dot(tokens, w_qkv, 0, 0).astype(bf16)
     queries = qkv[:, :HEAD_DIM]
@@ -174,31 +210,48 @@
     d_kv = d_kv.astype(bf16).reshape(TILE_TOKENS, 2 * HEAD_DIM)
     d_qkv = jnp.concatenate([d_queries, d_kv], 1)
 
-    dw = jnp.concatenate([dot(tokens, d_qkv, 1, 0), dot(grads, attended, 1, 0)], 1).astype(bf16)
-    dw = dw.reshape(2, 512, 4, HEAD_DIM).transpose(2, 0, 1, 3).reshape(8, 512, HEAD_DIM)
-    dw = jnp.sum(a2a(dw, ("x", "c")).astype(f32), 0).astype(bf16)
-    dw = a2a(dw.reshape(8, 64, HEAD_DIM), "y")
-    dw = jnp.sum(dw.reshape(4, 2, 64, HEAD_DIM).astype(f32), 1).astype(bf16)
-    dw = dw.reshape(4, 2, WIDTH, HEAD_DIM)
-    dw_near, dw_far = dw[:, 0], dw[:, 1]
-    first = zh == 0
-    dw = jnp.stack([jnp.where(first, dw_near, dw_far), jnp.where(first, dw_far, dw_near)])
-    dw = jnp.broadcast_to(dw[None], (6, 2, 4, WIDTH, HEAD_DIM)).reshape(12, 4, WIDTH, HEAD_DIM)
-    dw = a2a(dw, ("zl", "zh")).reshape(6, HEADS, WIDTH, HEAD_DIM)
-    dw = jnp.sum(dw.astype(f32), 0).astype(bf16)
-    dw = lax.all_gather(dw, "x")
-    weight_grads = dw.transpose(2, 0, 1, 3).astype(f32)
-
     d_tokens = dot(w_qkv, d_qkv, 1, 1).astype(bf16)
-    back = jnp.stack([part, d_tokens]).reshape(2, 2, 8, 2, WIDTH, TILE_TOKENS)
-    back = back.transpose(2, 0, 1, 3, 4, 5)
-    back = a2a(back, "y").reshape(4, 2, 2, 2, 2, WIDTH, TILE_TOKENS).astype(f32)
+    back = jnp.stack([part.reshape(8, 128, TILE_TOKENS), d_tokens.reshape(8, 128, TILE_TOKENS)], 1)
+    back = a2a(back, "y")
+    back = back.reshape(4, 2, 2, 2, 2, WIDTH, TILE_TOKENS).astype(f32)
     back = jnp.sum(back, 0)
-    far = lax.ppermute(back[:, :, :, 1].astype(bf16), "zh", SWAP2)
-    back = back[:, :, :, 0] + far.astype(f32)
-    out = a2a(back[:, 0].astype(bf16).transpose(1, 0, 2, 3), "c")
-    grad = a2a(back[:, 1].transpose(1, 0, 2, 3), "c")
-    return join_tiles(out), join_tiles(grad), weight_grads
+    low = back.astype(bf16)
+    own_tile = back[:, :, 0, 0] + swap(low[:, :, 0, 1], "zh").astype(f32)
+    other_tile = swap(back[:, :, 1, 0], "c") + swap_diag(low[:, :, 1, 1]).astype(f32)
+    left, right = in_order(own_tile, other_tile, c)
+    back = jnp.stack([left, right])
+    attention = join_tiles(back[:, :, 0].astype(bf16))
+    token_grads = join_tiles(back[:, :, 1])
+
+    def core_sum(mats):
+        mats = mats.reshape(8, 2, 64, -1)
+        return mats[:, 0] + swap(mats[:, 1].astype(bf16), "c").astype(f32)
+
+    dw_q = core_sum(dot(tokens, d_queries, 1, 0))
+    dw_o = core_sum(dot(grads, attended, 1, 0))
+    dw_kv = core_sum(dot(tokens, d_kv, 1, 0))
+    dw = jnp.stack([dw_q, dw_kv[:, :, :HEAD_DIM], dw_kv[:, :, HEAD_DIM:], dw_o])
+    dw_low = dw.astype(bf16)
+    total = pick(dw, x)
+    for s in (1, 2, 3):
+        got = shift(pick(dw_low, (x - s) % 4), "x", 4, 1, s)
+        total = total + got.astype(f32)
+    total = total.reshape(4, 2, 64, HEAD_DIM)
+    total = pick(total, b, 1) + swap(pick(total.astype(bf16), 1 - b, 1), "y").astype(f32)
+    low = total.astype(bf16)
+    heads = [pick(low, y2)] + [shift(pick(low, (y2 - s) % 4), "y", 4, 2, s) for s in (1, 2, 3)]
+    heads = unroll(heads, y2).reshape(4, 2, WIDTH, HEAD_DIM)
+    low_heads, high_heads = in_order(heads[:, 0], swap(heads[:, 1], "zh"), zh)
+    total = jnp.concatenate([low_heads, high_heads])
+    total = (total.astype(f32) + swap(total, "zl").astype(f32)).astype(bf16)
+    total = (
+        total.astype(f32)
+        + shift(total, "zl", 3, 2, 1).astype(f32)
+        + shift(total, "zl", 3, 2, 2).astype(f32)
+    ).astype(bf16)
+    total = unroll([total] + [shift(total, "x", 4, 1, s) for s in (1, 2, 3)], x)
+    weight_grads = total.transpose(2, 0, 1, 3).astype(f32)
+    return attention, token_grads, weight_grads
 
 
 def solution(mesh):
@@ -206,7 +259,7 @@
     strips = P(("zl", "x"), ("zh", "y", "c"), None, None)
     rows = P(("zh", "y", "c"), None, None, None)
     return jax.shard_map(
-        local,
+        work,
         mesh=inner,
         in_specs=(strips, strips, rows),
         out_specs=(strips, strips, rows),

time: 318 us -> 284 us (0.89)
  the two profiles are of different devices: /device:TPU:64 before, /device:TPU:1 now
where the time goes in v2:
time: 284 us; the launch traced here: 282 us
  starting transfers between devices  207 us (73%)
  waiting for transfers between devices  57.6 us (20%)
  local copies, waits for them, and re-layouts  8.67 us (3%)
  matrix products  4.02 us (1%)
    ppermute x15, starting transfers between devices, swap(): lax.ppermute(v, axis, [(i, i ^ 1) for i in range(lax.axis_size(axis))])  65.6 us
    ppermute x17, starting transfers between devices, shift(): return lax.ppermute(v, axis, pairs)  62.1 us
    ppermute x4, starting transfers between devices, swap_diag(): lax.ppermute(v, ('zh', 'y', 'c'), [(i, i ^ 1 ^ 16) for i in range(32)])  40.3 us
    all_to_all x3, starting transfers between devices, a2a(): return lax.all_to_all(v, axes, 0, 0, tiled=True)  16.2 us
    ppermute x15, waiting for transfers between devices, swap(): lax.ppermute(v, axis, [(i, i ^ 1) for i in range(lax.axis_size(axis))])  12 us
    ppermute x2, waiting for transfers between devices, to_up(): return lax.ppermute(v, ('zl', 'x'), UP)  10.1 us
    all_to_all x3, waiting for transfers between devices, a2a(): return lax.all_to_all(v, axes, 0, 0, tiled=True)  9.73 us
    ppermute x4, waiting for transfers between devices, swap_diag(): lax.ppermute(v, ('zh', 'y', 'c'), [(i, i ^ 1 ^ 16) for i in range(32)])  9.11 us
  transfers between devices with their start and end apart: 47, of which 19 were waited for; matrix products, arithmetic and copies ran while one was open for 3% of the time, Pallas kernels for 0%

profile of v2, /device:TPU:1, one launch (start us, length us, event | category | flops | bytes accessed | tf_op | source)
XLA Modules:
  0.0 282.3 jit_solution(15312041082362014775)
XLA Ops:
  1.6 16.2 %collective-permute-start.2 = (bf16[4,32,128]{2,1,0:T(8,128)(2,1)S(1)}, bf16[4,32,128]{2,1,0:T(8,128)(2,1)S(1)}, u32[]{:S(2)}, u32[]{:S(2)}) collective-permute-start(bf16[4,32,128]{2,1,0:T(8,128)(2,1)S(1)} %bitcast.290), channel_id=1, source_target_pairs={{0,17},{1,16},{2,19},{3,18},{4,21},{5,20},{6,23},{7,22},{8,25},{9,... | collective-permute-start | bytes 98312 | tf_op jit(solution)/shard_map/ppermute | solution.py:85
  17.9 5.7 %collective-permute-start = (bf16[4,32,128]{2,1,0:T(8,128)(2,1)S(1)}, bf16[4,32,128]{2,1,0:T(8,128)(2,1)S(1)}, u32[]{:S(2)}, u32[]{:S(2)}) collective-permute-start(bf16[4,32,128]{2,1,0:T(8,128)(2,1)S(1)} %bitcast.291), channel_id=1, source_target_pairs={{0,16},{16,0},{1,17},{17,1},{2,18},{18,2},{3,19},{19,3},{4,20},{20... | collective-permute-start | bytes 98312 | tf_op jit(solution)/shard_map/ppermute | solution.py:81
  27.1 6.3 %collective-permute-start.12 = (bf16[2,32,256]{2,1,0:T(8,128)(2,1)S(1)}, bf16[2,32,256]{2,1,0:T(8,128)(2,1)S(1)}, u32[]{:S(2)}, u32[]{:S(2)}) collective-permute-start(bf16[2,32,256]{2,1,0:T(8,128)(2,1)S(1)} %bitcast.284), channel_id=1, source_target_pairs={{0,17},{1,16},{2,19},{3,18},{4,21},{5,20},{6,23},{7,22},{8,25},{9,... | collective-permute-start | bytes 98312 | tf_op jit(solution)/shard_map/ppermute | solution.py:85
  35.7 5.6 %collective-permute-start.10 = (bf16[2,32,256]{2,1,0:T(8,128)(2,1)S(1)}, bf16[2,32,256]{2,1,0:T(8,128)(2,1)S(1)}, u32[]{:S(2)}, u32[]{:S(2)}) collective-permute-start(bf16[2,32,256]{2,1,0:T(8,128)(2,1)S(1)} %bitcast.289), channel_id=1, source_target_pairs={{0,16},{16,0},{1,17},{17,1},{2,18},{18,2},{3,19},{19,3},{4,20},{20... | collective-permute-start | bytes 98312 | tf_op jit(solution)/shard_map/ppermute | solution.py:81
  43.3 4.5 %collective-permute-start.4 = (bf16[128,128]{1,0:T(8,128)(2,1)S(1)}, bf16[128,128]{1,0:T(8,128)(2,1)S(1)}, u32[]{:S(2)}, u32[]{:S(2)}) collective-permute-start(bf16[128,128]{1,0:T(8,128)(2,1)S(1)} %get-tuple-element.55), channel_id=1, source_target_pairs={{0,8},{2,10},{4,12},{6,14},{8,0},{10,2},{12,4},{14,6},{1,9},{3,11}... | collective-permute-start | bytes 98312 | tf_op jit(solution)/shard_map/ppermute | solution.py:77
  48.0 4.8 %collective-permute-start.3 = (bf16[128,128]{1,0:T(8,128)(2,1)S(1)}, bf16[128,128]{1,0:T(8,128)(2,1)S(1)}, u32[]{:S(2)}, u32[]{:S(2)}) collective-permute-start(bf16[128,128]{1,0:T(8,128)(2,1)S(1)} %get-tuple-element.56), channel_id=1, source_target_pairs={{0,12},{2,14},{4,0},{6,2},{8,4},{10,6},{12,8},{14,10},{1,13},{3,15... | collective-permute-start | bytes 98312 | tf_op jit(solution)/shard_map/ppermute | solution.py:77
  53.7 4.5 %all-to-all-start = ((bf16[8,128,256]{2,1,0:T(8,128)(2,1)}), bf16[8,128,256]{2,1,0:T(8,128)(2,1)S(1)}, u32[]{:S(2)}, u32[]{:S(2)}) async-start(bf16[8,128,256]{2,1,0:T(8,128)(2,1)} %bitcast.37), calls=%async_computation | async-start | bytes 1048576 | tf_op jit(solution)/shard_map/all_to_all | solution.py:63
  61.9 8.3 %collective-permute-start.17 = (bf16[2,32,256]{2,1,0:T(8,128)(2,1)S(1)}, bf16[2,32,256]{2,1,0:T(8,128)(2,1)S(1)}, u32[]{:S(2)}, u32[]{:S(2)}) collective-permute-start(bf16[2,32,256]{2,1,0:T(8,128)(2,1)S(1)} %bitcast.288), channel_id=1, source_target_pairs={{0,16},{16,0},{1,17},{17,1},{2,18},{18,2},{3,19},{19,3},{4,20},{20... | collective-permute-start | bytes 98312 | tf_op jit(solution)/shard_map/ppermute | solution.py:81
  74.4 4.3 %collective-permute-start.8 = (bf16[1024,128]{1,0:T(8,128)(2,1)S(1)}, bf16[1024,128]{1,0:T(8,128)(2,1)S(1)}, u32[]{:S(2)}, u32[]{:S(2)}) collective-permute-start(bf16[1024,128]{1,0:T(8,128)(2,1)S(1)} %bitcast.258), channel_id=1, source_target_pairs={{0,64},{32,96},{64,0},{96,32},{1,65},{33,97},{65,1},{97,33},{2,66}... | collective-permute-start | bytes 786440 | tf_op jit(solution)/shard_map/ppermute | solution.py:77
  81.8 13.5 %collective-permute-start.19 = (bf16[2,32,256]{2,1,0:T(8,128)(2,1)S(1)}, bf16[2,32,256]{2,1,0:T(8,128)(2,1)S(1)}, u32[]{:S(2)}, u32[]{:S(2)}) collective-permute-start(bf16[2,32,256]{2,1,0:T(8,128)(2,1)S(1)} %bitcast.286), channel_id=1, source_target_pairs={{0,17},{1,16},{2,19},{3,18},{4,21},{5,20},{6,23},{7,22},{8,25},{9,... | collective-permute-start | bytes 98312 | tf_op jit(solution)/shard_map/ppermute | solution.py:85
  99.5 5.5 %all-to-all-start.1 = ((bf16[8,128,256]{2,1,0:T(8,128)(2,1)}), bf16[8,128,256]{2,1,0:T(8,128)(2,1)S(1)}, u32[]{:S(2)}, u32[]{:S(2)}) async-start(bf16[8,128,256]{2,1,0:T(8,128)(2,1)} %bitcast.58), calls=%async_computation.1 | async-start | bytes 1048576 | tf_op jit(solution)/shard_map/all_to_all | solution.py:63
  105.6 4.0 %collective-permute-start.13 = (bf16[16,4,256]{2,1,0:T(4,128)(2,1)S(1)}, bf16[16,4,256]{2,1,0:T(4,128)(2,1)S(1)}, u32[]{:S(2)}, u32[]{:S(2)}) collective-permute-start(bf16[16,4,256]{2,1,0:T(4,128)(2,1)S(1)} %get-tuple-element.51), channel_id=1, source_target_pairs={{0,1},{1,2},{2,3},{3,32},{4,5},{5,6},{6,7},{7,36},{8,9},{9,10},{10... | collective-permute-start | bytes 98312 | tf_op jit(solution)/shard_map/ppermute | solution.py:47
  111.8 3.8 %collective-permute-done.13 = bf16[16,4,256]{2,1,0:T(4,128)(2,1)S(1)} collective-permute-done((bf16[16,4,256]{2,1,0:T(4,128)(2,1)S(1)}, bf16[16,4,256]{2,1,0:T(4,128)(2,1)S(1)}, u32[]{:S(2)}, u32[]{:S(2)}) %collective-permute-start.13) | collective-permute-done | bytes 32800 | tf_op jit(solution)/shard_map/ppermute | solution.py:47
  115.6 4.0 %collective-permute-done.14 = bf16[16,4,256]{2,1,0:T(4,128)(2,1)S(1)} collective-permute-done((bf16[16,4,256]{2,1,0:T(4,128)(2,1)S(1)}, bf16[16,4,256]{2,1,0:T(4,128)(2,1)S(1)}, u32[]{:S(2)}, u32[]{:S(2)}) %collective-permute-start.14) | collective-permute-done | bytes 32800 | tf_op jit(solution)/shard_map/ppermute | solution.py:51
  123.7 5.4 %collective-permute-done.16 = bf16[4,24,256]{2,1,0:T(8,128)(2,1)S(1)} collective-permute-done((bf16[4,24,256]{2,1,0:T(8,128)(2,1)S(1)}, bf16[4,24,256]{2,1,0:T(8,128)(2,1)S(1)}, u32[]{:S(2)}, u32[]{:S(2)}) %collective-permute-start.16) | collective-permute-done | bytes 49184 | tf_op jit(solution)/shard_map/ppermute | solution.py:59
  133.4 5.8 %collective-permute-start.21 = (bf16[4,24,256]{2,1,0:T(8,128)(2,1)S(1)}, bf16[4,24,256]{2,1,0:T(8,128)(2,1)S(1)}, u32[]{:S(2)}, u32[]{:S(2)}) collective-permute-start(bf16[4,24,256]{2,1,0:T(8,128)(2,1)S(1)} %bitcast.283), channel_id=1, source_target_pairs={{0,64},{32,96},{64,128},{96,160},{128,192},{160,224},{192,256},{22... | collective-permute-start | bytes 147464 | tf_op jit(solution)/shard_map/ppermute | solution.py:55
  140.8 4.7 %collective-permute-done.20 = bf16[4,24,256]{2,1,0:T(8,128)(2,1)S(1)} collective-permute-done((bf16[4,24,256]{2,1,0:T(8,128)(2,1)S(1)}, bf16[4,24,256]{2,1,0:T(8,128)(2,1)S(1)}, u32[]{:S(2)}, u32[]{:S(2)}) %collective-permute-start.20) | collective-permute-done | bytes 49184 | tf_op jit(solution)/shard_map/ppermute | solution.py:59
  145.6 3.8 %collective-permute-start.22 = (bf16[16,4,256]{2,1,0:T(4,128)(2,1)S(1)}, bf16[16,4,256]{2,1,0:T(4,128)(2,1)S(1)}, u32[]{:S(2)}, u32[]{:S(2)}) collective-permute-start(bf16[16,4,256]{2,1,0:T(4,128)(2,1)S(1)} %get-tuple-element.47), channel_id=1, source_target_pairs={{1,0},{2,1},{3,2},{32,3},{5,4},{6,5},{7,6},{36,7},{9,8},{10,9},{11... | collective-permute-start | bytes 98312 | tf_op jit(solution)/shard_map/ppermute | solution.py:51
  158.0 4.6 %collective-permute-start.30 = (bf16[8,64,128]{2,1,0:T(8,128)(2,1)S(1)}, bf16[8,64,128]{2,1,0:T(8,128)(2,1)S(1)}, u32[]{:S(2)}, u32[]{:S(2)}) collective-permute-start(bf16[8,64,128]{2,1,0:T(8,128)(2,1)S(1)} %get-tuple-element.28), channel_id=1, source_target_pairs={{0,96},{32,0},{64,32},{96,64},{1,97},{33,1},{65,33},{97,65},{2,98}... | collective-permute-start | bytes 393224 | tf_op jit(solution)/shard_map/ppermute | solution.py:77
  164.5 3.6 %collective-permute-start.31 = (bf16[8,64,128]{2,1,0:T(8,128)(2,1)S(1)}, bf16[8,64,128]{2,1,0:T(8,128)(2,1)S(1)}, u32[]{:S(2)}, u32[]{:S(2)}) collective-permute-start(bf16[8,64,128]{2,1,0:T(8,128)(2,1)S(1)} %get-tuple-element.30), channel_id=1, source_target_pairs={{0,64},{32,96},{64,0},{96,32},{1,65},{33,97},{65,1},{97,33},{2,66}... | collective-permute-start | bytes 393224 | tf_op jit(solution)/shard_map/ppermute | solution.py:77
  183.8 7.1 %collective-permute-start.35 = (bf16[64,128]{1,0:T(8,128)(2,1)S(1)}, bf16[64,128]{1,0:T(8,128)(2,1)S(1)}, u32[]{:S(2)}, u32[]{:S(2)}) collective-permute-start(bf16[64,128]{1,0:T(8,128)(2,1)S(1)} %get-tuple-element.61), channel_id=1, source_target_pairs={{0,8},{2,10},{4,12},{6,14},{8,0},{10,2},{12,4},{14,6},{1,9},{3,11}... | collective-permute-start | bytes 49160 | tf_op jit(solution)/shard_map/ppermute | solution.py:77
  192.3 8.0 %collective-permute-start.37 = (bf16[4,32,128]{2,1,0:T(8,128)(2,1)S(1)}, bf16[4,32,128]{2,1,0:T(8,128)(2,1)S(1)}, u32[]{:S(2)}, u32[]{:S(2)}) collective-permute-start(bf16[4,32,128]{2,1,0:T(8,128)(2,1)S(1)} %slice_bitcast_fusion.8), channel_id=1, source_target_pairs={{0,16},{16,0},{1,17},{17,1},{2,18},{18,2},{3,19},{19,3},{4,20},{20... | collective-permute-start | bytes 98312 | tf_op jit(solution)/shard_map/ppermute | solution.py:81
  203.3 3.5 %collective-permute-start.38 = (bf16[8,32,128]{2,1,0:T(8,128)(2,1)S(1)}, bf16[8,32,128]{2,1,0:T(8,128)(2,1)S(1)}, u32[]{:S(2)}, u32[]{:S(2)}) collective-permute-start(bf16[8,32,128]{2,1,0:T(8,128)(2,1)S(1)} %pad_maximum_fusion.12), channel_id=1, source_target_pairs={{0,128},{128,0},{256,384},{384,256},{512,640},{640,512},{1,129},{1... | collective-permute-start | bytes 196616 | tf_op jit(solution)/shard_map/ppermute | solution.py:81
  209.1 6.3 %collective-permute-start.40 = (bf16[8,32,128]{2,1,0:T(8,128)(2,1)S(1)}, bf16[8,32,128]{2,1,0:T(8,128)(2,1)S(1)}, u32[]{:S(2)}, u32[]{:S(2)}) collective-permute-start(bf16[8,32,128]{2,1,0:T(8,128)(2,1)S(1)} %add_convert_fusion.1), channel_id=1, source_target_pairs={{0,256},{128,384},{256,512},{384,640},{512,0},{640,128},{1,257},{1... | collective-permute-start | bytes 196616 | tf_op jit(solution)/shard_map/ppermute | solution.py:77
  219.5 6.2 %all-to-all-start.2 = ((bf16[8,2,128,256]{3,2,1,0:T(8,128)(2,1)}), bf16[8,2,128,256]{3,2,1,0:T(8,128)(2,1)S(1)}, u32[]{:S(2)}, u32[]{:S(2)}) async-start(bf16[8,2,128,256]{3,2,1,0:T(8,128)(2,1)} %pad_maximum_fusion.1), calls=%async_computation.2 | async-start | bytes 2097152 | tf_op jit(solution)/shard_map/all_to_all | solution.py:63
  225.7 4.0 %collective-permute-start.41 = (bf16[8,32,128]{2,1,0:T(8,128)(2,1)S(1)}, bf16[8,32,128]{2,1,0:T(8,128)(2,1)S(1)}, u32[]{:S(2)}, u32[]{:S(2)}) collective-permute-start(bf16[8,32,128]{2,1,0:T(8,128)(2,1)S(1)} %get-tuple-element.22), channel_id=1, source_target_pairs={{0,96},{32,0},{64,32},{96,64},{1,97},{33,1},{65,33},{97,65},{2,98}... | collective-permute-start | bytes 196616 | tf_op jit(solution)/shard_map/ppermute | solution.py:77
  234.8 3.4 %collective-permute-done.42 = bf16[8,32,128]{2,1,0:T(8,128)(2,1)S(1)} collective-permute-done((bf16[8,32,128]{2,1,0:T(8,128)(2,1)S(1)}, bf16[8,32,128]{2,1,0:T(8,128)(2,1)S(1)}, u32[]{:S(2)}, u32[]{:S(2)}) %collective-permute-start.42) | collective-permute-done | bytes 65568 | tf_op jit(solution)/shard_map/ppermute | solution.py:77
  238.3 9.7 %all-to-all-done.2 = bf16[8,2,128,256]{3,2,1,0:T(8,128)(2,1)S(1)} async-done(((bf16[8,2,128,256]{3,2,1,0:T(8,128)(2,1)}), bf16[8,2,128,256]{3,2,1,0:T(8,128)(2,1)S(1)}, u32[]{:S(2)}, u32[]{:S(2)}) %all-to-all-start.2) | async-done | bytes 1048608 | tf_op jit(solution)/shard_map/all_to_all | solution.py:63
  248.3 9.3 %collective-permute-start.25 = (f32[2,2,32,256]{3,2,0,1:T(8,128)S(1)}, f32[2,2,32,256]{3,2,0,1:T(8,128)S(1)}, u32[]{:S(2)}, u32[]{:S(2)}) collective-permute-start(f32[2,2,32,256]{3,2,0,1:T(8,128)S(1)} %copy_bitcast_fusion), channel_id=1, source_target_pairs={{0,1},{1,0},{2,3},{3,2},{4,5},{5,4},{6,7},{7,6},{8,9},{9,8},{10,11... | collective-permute-start | bytes 393224 | tf_op jit(solution)/shard_map/ppermute | solution.py:81
  257.6 7.5 %collective-permute-start.24 = (bf16[2,2,32,256]{3,2,0,1:T(8,128)(2,1)S(1)}, bf16[2,2,32,256]{3,2,0,1:T(8,128)(2,1)S(1)}, u32[]{:S(2)}, u32[]{:S(2)}) collective-permute-start(bf16[2,2,32,256]{3,2,0,1:T(8,128)(2,1)S(1)} %get-tuple-element.37), channel_id=1, source_target_pairs={{0,16},{16,0},{1,17},{17,1},{2,18},{18,2},{3,19},{19,3},{4,20},{20... | collective-permute-start | bytes 196616 | tf_op jit(solution)/shard_map/ppermute | solution.py:81
  265.1 4.2 %collective-permute-start.26 = (bf16[2,2,32,256]{3,2,0,1:T(8,128)(2,1)S(1)}, bf16[2,2,32,256]{3,2,0,1:T(8,128)(2,1)S(1)}, u32[]{:S(2)}, u32[]{:S(2)}) collective-permute-start(bf16[2,2,32,256]{3,2,0,1:T(8,128)(2,1)S(1)} %get-tuple-element.38), channel_id=1, source_target_pairs={{0,17},{1,16},{2,19},{3,18},{4,21},{5,20},{6,23},{7,22},{8,25},{9,... | collective-permute-start | bytes 196616 | tf_op jit(solution)/shard_map/ppermute | solution.py:85
  271.0 9.1 %collective-permute-done.26 = bf16[2,2,32,256]{3,2,0,1:T(8,128)(2,1)S(1)} collective-permute-done((bf16[2,2,32,256]{3,2,0,1:T(8,128)(2,1)S(1)}, bf16[2,2,32,256]{3,2,0,1:T(8,128)(2,1)S(1)}, u32[]{:S(2)}, u32[]{:S(2)}) %collective-permute-start.26) | collective-permute-done | bytes 65568 | tf_op jit(solution)/shard_map/ppermute | solution.py:85
  (175 shorter events, 82.9 us)
Async XLA Ops:
  1.6 34.0 %collective-permute-start.2 = (bf16[4,32,128]{2,1,0:T(8,128)(2,1)S(1)}, bf16[4,32,128]{2,1,0:T(8,128)(2,1)S(1)}, u32[]{:S(2)}, u32[]{:S(2)}) collective-permute-start(bf16[4,32,128]{2,1,0:T(8,128)(2,1)S(1)} %bitcast.290), channel_id=1, source_target_pairs={{0,17},{1,16},{2,19},{3,18},{4,21},{5,20},{6,23},{7,22},{8,25},{9,... | collective-permute-start | bytes 98312 | tf_op jit(solution)/shard_map/ppermute | solution.py:85
  17.9 23.4 %collective-permute-start = (bf16[4,32,128]{2,1,0:T(8,128)(2,1)S(1)}, bf16[4,32,128]{2,1,0:T(8,128)(2,1)S(1)}, u32[]{:S(2)}, u32[]{:S(2)}) collective-permute-start(bf16[4,32,128]{2,1,0:T(8,128)(2,1)S(1)} %bitcast.291), channel_id=1, source_target_pairs={{0,16},{16,0},{1,17},{17,1},{2,18},{18,2},{3,19},{19,3},{4,20},{20... | collective-permute-start | bytes 98312 | tf_op jit(solution)/shard_map/ppermute | solution.py:81
  23.6 17.7 %collective-permute-start.1 = (bf16[4,32,128]{2,1,0:T(8,128)(2,1)S(1)}, bf16[4,32,128]{2,1,0:T(8,128)(2,1)S(1)}, u32[]{:S(2)}, u32[]{:S(2)}) collective-permute-start(bf16[4,32,128]{2,1,0:T(8,128)(2,1)S(1)} %bitcast.280), channel_id=1, source_target_pairs={{0,1},{1,0},{2,3},{3,2},{4,5},{5,4},{6,7},{7,6},{8,9},{9,8},{10,11... | collective-permute-start | bytes 98312 | tf_op jit(solution)/shard_map/ppermute | solution.py:81
  27.1 25.8 %collective-permute-start.12 = (bf16[2,32,256]{2,1,0:T(8,128)(2,1)S(1)}, bf16[2,32,256]{2,1,0:T(8,128)(2,1)S(1)}, u32[]{:S(2)}, u32[]{:S(2)}) collective-permute-start(bf16[2,32,256]{2,1,0:T(8,128)(2,1)S(1)} %bitcast.284), channel_id=1, source_target_pairs={{0,17},{1,16},{2,19},{3,18},{4,21},{5,20},{6,23},{7,22},{8,25},{9,... | collective-permute-start | bytes 98312 | tf_op jit(solution)/shard_map/ppermute | solution.py:85
  33.3 19.5 %collective-permute-start.11 = (bf16[2,32,256]{2,1,0:T(8,128)(2,1)S(1)}, bf16[2,32,256]{2,1,0:T(8,128)(2,1)S(1)}, u32[]{:S(2)}, u32[]{:S(2)}) collective-permute-start(bf16[2,32,256]{2,1,0:T(8,128)(2,1)S(1)} %bitcast.285), channel_id=1, source_target_pairs={{0,1},{1,0},{2,3},{3,2},{4,5},{5,4},{6,7},{7,6},{8,9},{9,8},{10,11... | collective-permute-start | bytes 98312 | tf_op jit(solution)/shard_map/ppermute | solution.py:81
  35.7 12.4 %collective-permute-start.10 = (bf16[2,32,256]{2,1,0:T(8,128)(2,1)S(1)}, bf16[2,32,256]{2,1,0:T(8,128)(2,1)S(1)}, u32[]{:S(2)}, u32[]{:S(2)}) collective-permute-start(bf16[2,32,256]{2,1,0:T(8,128)(2,1)S(1)} %bitcast.289), channel_id=1, source_target_pairs={{0,16},{16,0},{1,17},{17,1},{2,18},{18,2},{3,19},{19,3},{4,20},{20... | collective-permute-start | bytes 98312 | tf_op jit(solution)/shard_map/ppermute | solution.py:81
  41.4 16.9 %collective-permute-start.5 = (bf16[128,128]{1,0:T(8,128)(2,1)S(1)}, bf16[128,128]{1,0:T(8,128)(2,1)S(1)}, u32[]{:S(2)}, u32[]{:S(2)}) collective-permute-start(bf16[128,128]{1,0:T(8,128)(2,1)S(1)} %get-tuple-element.53), channel_id=1, source_target_pairs={{0,4},{2,6},{4,8},{6,10},{8,12},{10,14},{12,0},{14,2},{1,5},{3,7},... | collective-permute-start | bytes 98312 | tf_op jit(solution)/shard_map/ppermute | solution.py:77
  43.3 15.0 %collective-permute-start.4 = (bf16[128,128]{1,0:T(8,128)(2,1)S(1)}, bf16[128,128]{1,0:T(8,128)(2,1)S(1)}, u32[]{:S(2)}, u32[]{:S(2)}) collective-permute-start(bf16[128,128]{1,0:T(8,128)(2,1)S(1)} %get-tuple-element.55), channel_id=1, source_target_pairs={{0,8},{2,10},{4,12},{6,14},{8,0},{10,2},{12,4},{14,6},{1,9},{3,11}... | collective-permute-start | bytes 98312 | tf_op jit(solution)/shard_map/ppermute | solution.py:77
  48.0 10.2 %collective-permute-start.3 = (bf16[128,128]{1,0:T(8,128)(2,1)S(1)}, bf16[128,128]{1,0:T(8,128)(2,1)S(1)}, u32[]{:S(2)}, u32[]{:S(2)}) collective-permute-start(bf16[128,128]{1,0:T(8,128)(2,1)S(1)} %get-tuple-element.56), channel_id=1, source_target_pairs={{0,12},{2,14},{4,0},{6,2},{8,4},{10,6},{12,8},{14,10},{1,13},{3,15... | collective-permute-start | bytes 98312 | tf_op jit(solution)/shard_map/ppermute | solution.py:77
  53.7 45.0 %all-to-all-start = ((bf16[8,128,256]{2,1,0:T(8,128)(2,1)}), bf16[8,128,256]{2,1,0:T(8,128)(2,1)S(1)}, u32[]{:S(2)}, u32[]{:S(2)}) async-start(bf16[8,128,256]{2,1,0:T(8,128)(2,1)} %bitcast.37), calls=%async_computation | async-start | bytes 1048576 | tf_op jit(solution)/shard_map/all_to_all | solution.py:63
  58.4 14.0 %collective-permute-start.6 = (bf16[4,128,128]{2,1,0:T(8,128)(2,1)S(1)}, bf16[4,128,128]{2,1,0:T(8,128)(2,1)S(1)}, u32[]{:S(2)}, u32[]{:S(2)}) collective-permute-start(bf16[4,128,128]{2,1,0:T(8,128)(2,1)S(1)} %constant_dynamic-slice_fusion.5), channel_id=1, source_target_pairs={{0,2},{2,0},{4,6},{6,4},{8,10},{10,8},{12,14},{14,12},{1,3},{3,1},... | collective-permute-start | bytes 393224 | tf_op jit(solution)/shard_map/ppermute | solution.py:81
  61.9 33.5 %collective-permute-start.17 = (bf16[2,32,256]{2,1,0:T(8,128)(2,1)S(1)}, bf16[2,32,256]{2,1,0:T(8,128)(2,1)S(1)}, u32[]{:S(2)}, u32[]{:S(2)}) collective-permute-start(bf16[2,32,256]{2,1,0:T(8,128)(2,1)S(1)} %bitcast.288), channel_id=1, source_target_pairs={{0,16},{16,0},{1,17},{17,1},{2,18},{18,2},{3,19},{19,3},{4,20},{20... | collective-permute-start | bytes 98312 | tf_op jit(solution)/shard_map/ppermute | solution.py:81
  72.5 26.0 %collective-permute-start.9 = (bf16[1024,128]{1,0:T(8,128)(2,1)S(1)}, bf16[1024,128]{1,0:T(8,128)(2,1)S(1)}, u32[]{:S(2)}, u32[]{:S(2)}) collective-permute-start(bf16[1024,128]{1,0:T(8,128)(2,1)S(1)} %bitcast.257), channel_id=1, source_target_pairs={{0,32},{32,64},{64,96},{96,0},{1,33},{33,65},{65,97},{97,1},{2,34}... | collective-permute-start | bytes 786440 | tf_op jit(solution)/shard_map/ppermute | solution.py:77
  74.4 24.1 %collective-permute-start.8 = (bf16[1024,128]{1,0:T(8,128)(2,1)S(1)}, bf16[1024,128]{1,0:T(8,128)(2,1)S(1)}, u32[]{:S(2)}, u32[]{:S(2)}) collective-permute-start(bf16[1024,128]{1,0:T(8,128)(2,1)S(1)} %bitcast.258), channel_id=1, source_target_pairs={{0,64},{32,96},{64,0},{96,32},{1,65},{33,97},{65,1},{97,33},{2,66}... | collective-permute-start | bytes 786440 | tf_op jit(solution)/shard_map/ppermute | solution.py:77
  78.7 19.9 %collective-permute-start.7 = (bf16[1024,128]{1,0:T(8,128)(2,1)S(1)}, bf16[1024,128]{1,0:T(8,128)(2,1)S(1)}, u32[]{:S(2)}, u32[]{:S(2)}) collective-permute-start(bf16[1024,128]{1,0:T(8,128)(2,1)S(1)} %bitcast.259), channel_id=1, source_target_pairs={{0,96},{32,0},{64,32},{96,64},{1,97},{33,1},{65,33},{97,65},{2,98}... | collective-permute-start | bytes 786440 | tf_op jit(solution)/shard_map/ppermute | solution.py:77
  81.8 15.7 %collective-permute-start.19 = (bf16[2,32,256]{2,1,0:T(8,128)(2,1)S(1)}, bf16[2,32,256]{2,1,0:T(8,128)(2,1)S(1)}, u32[]{:S(2)}, u32[]{:S(2)}) collective-permute-start(bf16[2,32,256]{2,1,0:T(8,128)(2,1)S(1)} %bitcast.286), channel_id=1, source_target_pairs={{0,17},{1,16},{2,19},{3,18},{4,21},{5,20},{6,23},{7,22},{8,25},{9,... | collective-permute-start | bytes 98312 | tf_op jit(solution)/shard_map/ppermute | solution.py:85
  99.5 23.8 %all-to-all-start.1 = ((bf16[8,128,256]{2,1,0:T(8,128)(2,1)}), bf16[8,128,256]{2,1,0:T(8,128)(2,1)S(1)}, u32[]{:S(2)}, u32[]{:S(2)}) async-start(bf16[8,128,256]{2,1,0:T(8,128)(2,1)} %bitcast.58), calls=%async_computation.1 | async-start | bytes 1048576 | tf_op jit(solution)/shard_map/all_to_all | solution.py:63
  105.6 9.9 %collective-permute-start.13 = (bf16[16,4,256]{2,1,0:T(4,128)(2,1)S(1)}, bf16[16,4,256]{2,1,0:T(4,128)(2,1)S(1)}, u32[]{:S(2)}, u32[]{:S(2)}) collective-permute-start(bf16[16,4,256]{2,1,0:T(4,128)(2,1)S(1)} %get-tuple-element.51), channel_id=1, source_target_pairs={{0,1},{1,2},{2,3},{3,32},{4,5},{5,6},{6,7},{7,36},{8,9},{9,10},{10... | collective-permute-start | bytes 98312 | tf_op jit(solution)/shard_map/ppermute | solution.py:47
  109.6 10.0 %collective-permute-start.14 = (bf16[16,4,256]{2,1,0:T(4,128)(2,1)S(1)}, bf16[16,4,256]{2,1,0:T(4,128)(2,1)S(1)}, u32[]{:S(2)}, u32[]{:S(2)}) collective-permute-start(bf16[16,4,256]{2,1,0:T(4,128)(2,1)S(1)} %get-tuple-element.52), channel_id=1, source_target_pairs={{1,0},{2,1},{3,2},{32,3},{5,4},{6,5},{7,6},{36,7},{9,8},{10,9},{11... | collective-permute-start | bytes 98312 | tf_op jit(solution)/shard_map/ppermute | solution.py:51
  131.5 25.1 %collective-permute-start.29 = (bf16[8,64,128]{2,1,0:T(8,128)(2,1)S(1)}, bf16[8,64,128]{2,1,0:T(8,128)(2,1)S(1)}, u32[]{:S(2)}, u32[]{:S(2)}) collective-permute-start(bf16[8,64,128]{2,1,0:T(8,128)(2,1)S(1)} %fusion.31), channel_id=1, source_target_pairs={{0,1},{1,0},{2,3},{3,2},{4,5},{5,4},{6,7},{7,6},{8,9},{9,8},{10,11... | collective-permute-start | bytes 393224 | tf_op jit(solution)/shard_map/ppermute | solution.py:81
  158.0 10.3 %collective-permute-start.30 = (bf16[8,64,128]{2,1,0:T(8,128)(2,1)S(1)}, bf16[8,64,128]{2,1,0:T(8,128)(2,1)S(1)}, u32[]{:S(2)}, u32[]{:S(2)}) collective-permute-start(bf16[8,64,128]{2,1,0:T(8,128)(2,1)S(1)} %get-tuple-element.28), channel_id=1, source_target_pairs={{0,96},{32,0},{64,32},{96,64},{1,97},{33,1},{65,33},{97,65},{2,98}... | collective-permute-start | bytes 393224 | tf_op jit(solution)/shard_map/ppermute | solution.py:77
  177.6 13.3 %collective-permute-start.34 = (bf16[64,128]{1,0:T(8,128)(2,1)S(1)}, bf16[64,128]{1,0:T(8,128)(2,1)S(1)}, u32[]{:S(2)}, u32[]{:S(2)}) collective-permute-start(bf16[64,128]{1,0:T(8,128)(2,1)S(1)} %get-tuple-element.62), channel_id=1, source_target_pairs={{0,12},{2,14},{4,0},{6,2},{8,4},{10,6},{12,8},{14,10},{1,13},{3,15... | collective-permute-start | bytes 49160 | tf_op jit(solution)/shard_map/ppermute | solution.py:77
  180.8 11.4 %collective-permute-start.36 = (bf16[64,128]{1,0:T(8,128)(2,1)S(1)}, bf16[64,128]{1,0:T(8,128)(2,1)S(1)}, u32[]{:S(2)}, u32[]{:S(2)}) collective-permute-start(bf16[64,128]{1,0:T(8,128)(2,1)S(1)} %get-tuple-element.59), channel_id=1, source_target_pairs={{0,4},{2,6},{4,8},{6,10},{8,12},{10,14},{12,0},{14,2},{1,5},{3,7},... | collective-permute-start | bytes 49160 | tf_op jit(solution)/shard_map/ppermute | solution.py:77
  192.3 11.0 %collective-permute-start.37 = (bf16[4,32,128]{2,1,0:T(8,128)(2,1)S(1)}, bf16[4,32,128]{2,1,0:T(8,128)(2,1)S(1)}, u32[]{:S(2)}, u32[]{:S(2)}) collective-permute-start(bf16[4,32,128]{2,1,0:T(8,128)(2,1)S(1)} %slice_bitcast_fusion.8), channel_id=1, source_target_pairs={{0,16},{16,0},{1,17},{17,1},{2,18},{18,2},{3,19},{19,3},{4,20},{20... | collective-permute-start | bytes 98312 | tf_op jit(solution)/shard_map/ppermute | solution.py:81
  209.1 16.6 %collective-permute-start.40 = (bf16[8,32,128]{2,1,0:T(8,128)(2,1)S(1)}, bf16[8,32,128]{2,1,0:T(8,128)(2,1)S(1)}, u32[]{:S(2)}, u32[]{:S(2)}) collective-permute-start(bf16[8,32,128]{2,1,0:T(8,128)(2,1)S(1)} %add_convert_fusion.1), channel_id=1, source_target_pairs={{0,256},{128,384},{256,512},{384,640},{512,0},{640,128},{1,257},{1... | collective-permute-start | bytes 196616 | tf_op jit(solution)/shard_map/ppermute | solution.py:77
  215.4 10.3 %collective-permute-start.39 = (bf16[8,32,128]{2,1,0:T(8,128)(2,1)S(1)}, bf16[8,32,128]{2,1,0:T(8,128)(2,1)S(1)}, u32[]{:S(2)}, u32[]{:S(2)}) collective-permute-start(bf16[8,32,128]{2,1,0:T(8,128)(2,1)S(1)} %add_convert_fusion.1), channel_id=1, source_target_pairs={{0,512},{128,640},{256,0},{384,128},{512,256},{640,384},{1,513},{1... | collective-permute-start | bytes 196616 | tf_op jit(solution)/shard_map/ppermute | solution.py:77
  219.5 28.6 %all-to-all-start.2 = ((bf16[8,2,128,256]{3,2,1,0:T(8,128)(2,1)}), bf16[8,2,128,256]{3,2,1,0:T(8,128)(2,1)S(1)}, u32[]{:S(2)}, u32[]{:S(2)}) async-start(bf16[8,2,128,256]{3,2,1,0:T(8,128)(2,1)} %pad_maximum_fusion.1), calls=%async_computation.2 | async-start | bytes 2097152 | tf_op jit(solution)/shard_map/all_to_all | solution.py:63
  225.7 9.0 %collective-permute-start.41 = (bf16[8,32,128]{2,1,0:T(8,128)(2,1)S(1)}, bf16[8,32,128]{2,1,0:T(8,128)(2,1)S(1)}, u32[]{:S(2)}, u32[]{:S(2)}) collective-permute-start(bf16[8,32,128]{2,1,0:T(8,128)(2,1)S(1)} %get-tuple-element.22), channel_id=1, source_target_pairs={{0,96},{32,0},{64,32},{96,64},{1,97},{33,1},{65,33},{97,65},{2,98}... | collective-permute-start | bytes 196616 | tf_op jit(solution)/shard_map/ppermute | solution.py:77
  229.8 8.5 %collective-permute-start.43 = (bf16[8,32,128]{2,1,0:T(8,128)(2,1)S(1)}, bf16[8,32,128]{2,1,0:T(8,128)(2,1)S(1)}, u32[]{:S(2)}, u32[]{:S(2)}) collective-permute-start(bf16[8,32,128]{2,1,0:T(8,128)(2,1)S(1)} %get-tuple-element.22), channel_id=1, source_target_pairs={{0,32},{32,64},{64,96},{96,0},{1,33},{33,65},{65,97},{97,1},{2,34}... | collective-permute-start | bytes 196616 | tf_op jit(solution)/shard_map/ppermute | solution.py:77
  248.3 31.8 %collective-permute-start.25 = (f32[2,2,32,256]{3,2,0,1:T(8,128)S(1)}, f32[2,2,32,256]{3,2,0,1:T(8,128)S(1)}, u32[]{:S(2)}, u32[]{:S(2)}) collective-permute-start(f32[2,2,32,256]{3,2,0,1:T(8,128)S(1)} %copy_bitcast_fusion), channel_id=1, source_target_pairs={{0,1},{1,0},{2,3},{3,2},{4,5},{5,4},{6,7},{7,6},{8,9},{9,8},{10,11... | collective-permute-start | bytes 393224 | tf_op jit(solution)/shard_map/ppermute | solution.py:81
  257.6 13.4 %collective-permute-start.24 = (bf16[2,2,32,256]{3,2,0,1:T(8,128)(2,1)S(1)}, bf16[2,2,32,256]{3,2,0,1:T(8,128)(2,1)S(1)}, u32[]{:S(2)}, u32[]{:S(2)}) collective-permute-start(bf16[2,2,32,256]{3,2,0,1:T(8,128)(2,1)S(1)} %get-tuple-element.37), channel_id=1, source_target_pairs={{0,16},{16,0},{1,17},{17,1},{2,18},{18,2},{3,19},{19,3},{4,20},{20... | collective-permute-start | bytes 196616 | tf_op jit(solution)/shard_map/ppermute | solution.py:81
  265.1 14.9 %collective-permute-start.26 = (bf16[2,2,32,256]{3,2,0,1:T(8,128)(2,1)S(1)}, bf16[2,2,32,256]{3,2,0,1:T(8,128)(2,1)S(1)}, u32[]{:S(2)}, u32[]{:S(2)}) collective-permute-start(bf16[2,2,32,256]{3,2,0,1:T(8,128)(2,1)S(1)} %get-tuple-element.38), channel_id=1, source_target_pairs={{0,17},{1,16},{2,19},{3,18},{4,21},{5,20},{6,23},{7,22},{8,25},{9,... | collective-permute-start | bytes 196616 | tf_op jit(solution)/shard_map/ppermute | solution.py:85
  (16 other events, 116.1 us)

commit v3 on v2

--- a/solution.py
+++ b/solution.py
@@ -5,6 +5,7 @@
 
 
 D = 1024
+HEADS = 8
 HEAD_DIM = 128
 TILE_ROWS = 16
 TILE_COLS = 16
@@ -81,10 +82,6 @@
     return lax.ppermute(v, axis, [(i, i ^ 1) for i in range(lax.axis_size(axis))])
 
 
-def swap_diag(v):
-    return lax.ppermute(v, ("zh", "y", "c"), [(i, (i ^ 1) ^ 16) for i in range(32)])
-
-
 def pick(v, index, axis=0):
     return lax.dynamic_index_in_dim(v, index, axis, keepdims=False)
 
@@ -100,16 +97,16 @@
 
 def split_tiles(block):
     return (
-        block.reshape(WIDTH, TILE_ROWS, 2, 2, TILE_COLS)
-        .transpose(2, 3, 0, 1, 4)
-        .reshape(2, 2, WIDTH, TILE_TOKENS)
+        block.reshape(WIDTH, 2, 8, 2, 2, TILE_COLS)
+        .transpose(3, 4, 1, 0, 2, 5)
+        .reshape(2, 2, 2, WIDTH, 128)
     )
 
 
 def join_tiles(tiles):
     return (
-        tiles.reshape(2, 2, WIDTH, TILE_ROWS, TILE_COLS)
-        .transpose(2, 3, 1, 0, 4)
+        tiles.reshape(2, 2, 2, WIDTH, 8, TILE_COLS)
+        .transpose(3, 2, 4, 1, 0, 5)
         .reshape(1, WIDTH, TILE_ROWS, 64)
     )
 
@@ -122,34 +119,33 @@
     y = lax.axis_index("y")
     c = lax.axis_index("c")
 
-    y2 = y // 2
-    b = y % 2
-
     w_mine = pick(weights, x, 1).transpose(1, 0, 2)
     w_keep = lax.dynamic_slice_in_dim(w_mine, zh * 4, 4, 0)
     w_give = lax.dynamic_slice_in_dim(w_mine, (1 - zh) * 4, 4, 0)
-    w_zh = swap(w_give, "zh")
-    w_zc = swap_diag(w_give)
-    w_c = swap(w_keep, "c")
-    w_rows = jnp.stack([w_keep, w_zh, w_c, w_zc], 1).reshape(4, 128, HEAD_DIM)
-    w_near = [pick(w_rows, y2)] + [
-        shift(pick(w_rows, (y2 - s) % 4), "y", 4, 2, s) for s in (1, 2, 3)
-    ]
-    w_near = unroll(w_near, y2)
-    w_even, w_odd = in_order(w_near, swap(w_near, "y"), b)
-    w_x = jnp.stack([w_even, w_odd], 1).reshape(D, HEAD_DIM)
-
-    def gather_tiles(block):
-        own = split_tiles(block)
-        keep = pick(own, c, 1)
-        give = pick(own, 1 - c, 1)
-        mine = jnp.stack([keep, swap(keep, "zh"), swap(give, "c"), swap_diag(give)], 1)
-        mine = mine.reshape(1, 2, 128, TILE_TOKENS)
-        send = jnp.broadcast_to(mine, (4, 2, 128, TILE_TOKENS)).reshape(8, 128, TILE_TOKENS)
-        return a2a(send, "y").reshape(D, TILE_TOKENS)
-
-    tokens = gather_tiles(embedded[0])
-    grads = gather_tiles(cotangent[0])
+    tiles = jnp.concatenate([split_tiles(embedded[0]), split_tiles(cotangent[0])], 2)
+    mine = jnp.concatenate([tiles.reshape(16, WIDTH, 128), w_give])
+    got = swap(mine, "zh")
+    pairs = jnp.stack([tiles, got[:16].reshape(2, 2, 4, WIDTH, 128)], 3)
+    t_keep = pick(pairs, c, 1)
+    t_give = pick(pairs, 1 - c, 1)
+    w_keep = jnp.stack([w_keep, got[16:]], 1)
+    mine = jnp.concatenate([t_give.reshape(16, WIDTH, 128), w_keep.reshape(8, WIDTH, 128)])
+    got = swap(mine, "c")
+    t_mine = jnp.stack([t_keep, got[:16].reshape(2, 4, 2, WIDTH, 128)], 2)
+    t_mine = t_mine.reshape(2, 4, 128, 128)
+    w_mine = jnp.stack([w_keep, got[16:].reshape(4, 2, WIDTH, 128)], 1).reshape(4, 128, 128)
+    t_mine = t_mine.transpose(0, 2, 1, 3).reshape(1, 2, 128, 512)
+    send = jnp.concatenate(
+        [
+            jnp.broadcast_to(t_mine, (4, 2, 128, 512)),
+            jnp.broadcast_to(w_mine[:, None], (4, 2, 128, 128)),
+        ],
+        3,
+    )
+    got = a2a(send.reshape(8, 128, 640), "y").reshape(D, 640)
+    tokens = got[:, :TILE_TOKENS]
+    grads = got[:, TILE_TOKENS : 2 * TILE_TOKENS]
+    w_x = got[:, 2 * TILE_TOKENS :]
 
     w_list = jnp.stack([w_x] + [shift(w_x, "x", 4, 1, s) for s in (1, 2, 3)])
     w_qkv = jnp.concatenate([pick(w_list, (m - x) % 4) for m in range(3)], 1)
@@ -211,44 +207,39 @@
     d_qkv = jnp.concatenate([d_queries, d_kv], 1)
 
     d_tokens = dot(w_qkv, d_qkv, 1, 1).astype(bf16)
-    back = jnp.stack([part.reshape(8, 128, TILE_TOKENS), d_tokens.reshape(8, 128, TILE_TOKENS)], 1)
-    back = a2a(back, "y")
-    back = back.reshape(4, 2, 2, 2, 2, WIDTH, TILE_TOKENS).astype(f32)
-    back = jnp.sum(back, 0)
-    low = back.astype(bf16)
-    own_tile = back[:, :, 0, 0] + swap(low[:, :, 0, 1], "zh").astype(f32)
-    other_tile = swap(back[:, :, 1, 0], "c") + swap_diag(low[:, :, 1, 1]).astype(f32)
-    left, right = in_order(own_tile, other_tile, c)
-    back = jnp.stack([left, right])
-    attention = join_tiles(back[:, :, 0].astype(bf16))
-    token_grads = join_tiles(back[:, :, 1])
-
-    def core_sum(mats):
-        mats = mats.reshape(8, 2, 64, -1)
-        return mats[:, 0] + swap(mats[:, 1].astype(bf16), "c").astype(f32)
-
-    dw_q = core_sum(dot(tokens, d_queries, 1, 0))
-    dw_o = core_sum(dot(grads, attended, 1, 0))
-    dw_kv = core_sum(dot(tokens, d_kv, 1, 0))
-    dw = jnp.stack([dw_q, dw_kv[:, :, :HEAD_DIM], dw_kv[:, :, HEAD_DIM:], dw_o])
-    dw_low = dw.astype(bf16)
-    total = pick(dw, x)
+    dw_kv = dot(tokens, d_kv, 1, 0)
+    dw = jnp.stack(
+        [
+            dot(tokens, d_queries, 1, 0),
+            dw_kv[:, :HEAD_DIM],
+            dw_kv[:, HEAD_DIM:],
+            dot(grads, attended, 1, 0),
+        ]
+    ).astype(bf16)
+    total = pick(dw, x).astype(f32)
     for s in (1, 2, 3):
-        got = shift(pick(dw_low, (x - s) % 4), "x", 4, 1, s)
-        total = total + got.astype(f32)
-    total = total.reshape(4, 2, 64, HEAD_DIM)
-    total = pick(total, b, 1) + swap(pick(total.astype(bf16), 1 - b, 1), "y").astype(f32)
-    low = total.astype(bf16)
-    heads = [pick(low, y2)] + [shift(pick(low, (y2 - s) % 4), "y", 4, 2, s) for s in (1, 2, 3)]
-    heads = unroll(heads, y2).reshape(4, 2, WIDTH, HEAD_DIM)
-    low_heads, high_heads = in_order(heads[:, 0], swap(heads[:, 1], "zh"), zh)
-    total = jnp.concatenate([low_heads, high_heads])
-    total = (total.astype(f32) + swap(total, "zl").astype(f32)).astype(bf16)
-    total = (
-        total.astype(f32)
-        + shift(total, "zl", 3, 2, 1).astype(f32)
-        + shift(total, "zl", 3, 2, 2).astype(f32)
-    ).astype(bf16)
+        total = total + shift(pick(dw, (x - s) % 4), "x", 4, 1, s).astype(f32)
+    send = jnp.concatenate([part, d_tokens, total.astype(bf16)], 1).reshape(8, 128, 640)
+    got = a2a(send, "y").reshape(4, 2, 128, 640)
+    back = jnp.sum(got[..., :512].astype(f32), 0)
+    back = back.reshape(2, 2, 64, 4, 128).transpose(1, 0, 3, 2, 4)
+    dw = jnp.sum(got[..., 512:].astype(f32), 1).reshape(4, 2, 64, 128)
+    give = jnp.concatenate([back[1].reshape(8, 64, 128), dw[:, 1]]).astype(bf16)
+    got = swap(give, "c")
+    dw = (dw[:, 0] + got[8:].astype(f32)).astype(bf16).reshape(4, 2, WIDTH, 128)
+    dw = jnp.stack(in_order(dw[:, 0], dw[:, 1], zh))
+    dw = jnp.broadcast_to(dw, (6, 2, 4, WIDTH, 128)).reshape(12, 4, WIDTH, 128)
+    dw = a2a(dw, ("zl", "zh"))
+    total = jnp.sum(dw.reshape(6, HEADS, WIDTH, 128).astype(f32), 0).astype(bf16)
+
+    back = jnp.stack([back[0], got[:8].reshape(2, 4, 64, 128).astype(f32)])
+    back = back.reshape(2, 2, 4, 2, WIDTH, 128)
+    far = swap(back[:, :, :, 1].astype(bf16), "zh")
+    back = back[:, :, :, 0] + far.astype(f32)
+    back = jnp.stack(in_order(back[0], back[1], c))
+    attention = join_tiles(back[:, :, :2].astype(bf16))
+    token_grads = join_tiles(back[:, :, 2:])
+
     total = unroll([total] + [shift(total, "x", 4, 1, s) for s in (1, 2, 3)], x)
     weight_grads = total.transpose(2, 0, 1, 3).astype(f32)
     return attention, token_grads, weight_grads

time: 284 us -> 261 us (0.919)
  the two profiles are of different devices: /device:TPU:1 before, /device:TPU:64 now
where the time goes in v3:
time: 261 us; the launch traced here: 260 us
  starting transfers between devices  99 us (38%)
  blocking collectives  77.8 us (30%)
  waiting for transfers between devices  61.4 us (24%)
  local copies, waits for them, and re-layouts  10.9 us (4%)
  other arithmetic  4.84 us (2%)
  matrix products  4.12 us (2%)
    all_to_all x2, blocking collectives, a2a(): return lax.all_to_all(v, axes, 0, 0, tiled=True)  77.8 us
    ppermute x9, starting transfers between devices, shift(): return lax.ppermute(v, axis, pairs)  33.8 us
    ppermute x4, waiting for transfers between devices, swap(): lax.ppermute(v, axis, [(i, i ^ 1) for i in range(lax.axis_size(axis))])  32.7 us
    ppermute x4, starting transfers between devices, swap(): lax.ppermute(v, axis, [(i, i ^ 1) for i in range(lax.axis_size(axis))])  26.9 us
    ppermute x9, waiting for transfers between devices, shift(): return lax.ppermute(v, axis, pairs)  23.2 us
    all_to_all x1, starting transfers between devices, a2a(): return lax.all_to_all(v, axes, 0, 0, tiled=True)  14.2 us
    ppermute x2, starting transfers between devices, to_up(): return lax.ppermute(v, ('zl', 'x'), UP)  10.4 us
    ppermute x2, starting transfers between devices, to_down(): return lax.ppermute(v, ('zl', 'x'), DOWN)  6.2 us
  transfers between devices with their start and end apart: 22, of which 15 were waited for; matrix products, arithmetic and copies ran while one was open for 2% of the time, Pallas kernels for 0%

profile of v3, /device:TPU:64, one launch (start us, length us, event | category | flops | bytes accessed | tf_op | source)
XLA Modules:
  0.0 259.9 jit_solution(12552062060679587001)
XLA Ops:
  3.3 14.2 %collective-permute-start = (bf16[20,32,128]{2,1,0:T(8,128)(2,1)S(1)}, bf16[20,32,128]{2,1,0:T(8,128)(2,1)S(1)}, u32[]{:S(2)}, u32[]{:S(2)}) collective-permute-start(bf16[20,32,128]{2,1,0:T(8,128)(2,1)S(1)} %pad_maximum_fusion.11), channel_id=1, source_target_pairs={{0,16},{16,0},{1,17},{17,1},{2,18},{18,2},{3,19},{19,3},{4,20},{20... | collective-permute-start | bytes 491528 | tf_op jit(solution)/shard_map/ppermute | solution.py:82
  17.6 10.3 %collective-permute-done = bf16[20,32,128]{2,1,0:T(8,128)(2,1)S(1)} collective-permute-done((bf16[20,32,128]{2,1,0:T(8,128)(2,1)S(1)}, bf16[20,32,128]{2,1,0:T(8,128)(2,1)S(1)}, u32[]{:S(2)}, u32[]{:S(2)}) %collective-permute-start) | collective-permute-done | bytes 163872 | tf_op jit(solution)/shard_map/ppermute | solution.py:82
  28.0 1.9 collective-permute-start.1
  32.1 41.5 %all_to_all.15 = bf16[8,128,640]{2,1,0:T(8,128)(2,1)S(1)} all-to-all(bf16[8,128,640]{2,1,0:T(8,128)(2,1)S(1)} %bitcast.167), channel_id=1, replica_groups=mesh['zl'=6,'x'=4,'zh'=2,'y'=8,'c'=2] {'y'}, dimensions={0} | all-to-all | bytes 2621440 | tf_op jit(solution)/shard_map/all_to_all | solution.py:64
  73.7 4.7 %collective-permute-start.2 = (bf16[1024,128]{1,0:T(8,128)(2,1)S(1)}, bf16[1024,128]{1,0:T(8,128)(2,1)S(1)}, u32[]{:S(2)}, u32[]{:S(2)}) collective-permute-start(bf16[1024,128]{1,0:T(8,128)(2,1)S(1)} %get-tuple-element.22), channel_id=1, source_target_pairs={{0,96},{32,0},{64,32},{96,64},{1,97},{33,1},{65,33},{97,65},{2,98}... | collective-permute-start | bytes 786440 | tf_op jit(solution)/shard_map/ppermute | solution.py:78
  78.3 2.7 %collective-permute-start.3 = (bf16[1024,128]{1,0:T(8,128)(2,1)S(1)}, bf16[1024,128]{1,0:T(8,128)(2,1)S(1)}, u32[]{:S(2)}, u32[]{:S(2)}) collective-permute-start(bf16[1024,128]{1,0:T(8,128)(2,1)S(1)} %get-tuple-element.22), channel_id=1, source_target_pairs={{0,64},{32,96},{64,0},{96,32},{1,65},{33,97},{65,1},{97,33},{2,66}... | collective-permute-start | bytes 786440 | tf_op jit(solution)/shard_map/ppermute | solution.py:78
  81.0 2.8 %collective-permute-start.4 = (bf16[1024,128]{1,0:T(8,128)(2,1)S(1)}, bf16[1024,128]{1,0:T(8,128)(2,1)S(1)}, u32[]{:S(2)}, u32[]{:S(2)}) collective-permute-start(bf16[1024,128]{1,0:T(8,128)(2,1)S(1)} %get-tuple-element.22), channel_id=1, source_target_pairs={{0,32},{32,64},{64,96},{96,0},{1,33},{33,65},{65,97},{97,1},{2,34}... | collective-permute-start | bytes 786440 | tf_op jit(solution)/shard_map/ppermute | solution.py:78
  84.0 4.5 %collective-permute-done.2 = bf16[1024,128]{1,0:T(8,128)(2,1)S(1)} collective-permute-done((bf16[1024,128]{1,0:T(8,128)(2,1)S(1)}, bf16[1024,128]{1,0:T(8,128)(2,1)S(1)}, u32[]{:S(2)}, u32[]{:S(2)}) %collective-permute-start.2) | collective-permute-done | bytes 262176 | tf_op jit(solution)/shard_map/ppermute | solution.py:78
  88.5 2.4 collective-permute-done.3
  90.9 3.2 %collective-permute-done.4 = bf16[1024,128]{1,0:T(8,128)(2,1)S(1)} collective-permute-done((bf16[1024,128]{1,0:T(8,128)(2,1)S(1)}, bf16[1024,128]{1,0:T(8,128)(2,1)S(1)}, u32[]{:S(2)}, u32[]{:S(2)}) %collective-permute-start.4) | collective-permute-done | bytes 262176 | tf_op jit(solution)/shard_map/ppermute | solution.py:78
  99.6 2.7 %collective-permute-start.7 = (bf16[4,24,256]{2,1,0:T(8,128)(2,1)S(1)}, bf16[4,24,256]{2,1,0:T(8,128)(2,1)S(1)}, u32[]{:S(2)}, u32[]{:S(2)}) collective-permute-start(bf16[4,24,256]{2,1,0:T(8,128)(2,1)S(1)} %get-tuple-element.43), channel_id=1, source_target_pairs={{0,64},{32,96},{64,128},{96,160},{128,192},{160,224},{192,256},{22... | collective-permute-start | bytes 147464 | tf_op jit(solution)/shard_map/ppermute | solution.py:56
  102.3 5.5 %collective-permute-start.8 = (bf16[4,24,256]{2,1,0:T(8,128)(2,1)S(1)}, bf16[4,24,256]{2,1,0:T(8,128)(2,1)S(1)}, u32[]{:S(2)}, u32[]{:S(2)}) collective-permute-start(bf16[4,24,256]{2,1,0:T(8,128)(2,1)S(1)} %get-tuple-element.44), channel_id=1, source_target_pairs={{64,0},{96,32},{128,64},{160,96},{192,128},{224,160},{256,192},{28... | collective-permute-start | bytes 147464 | tf_op jit(solution)/shard_map/ppermute | solution.py:60
  108.2 1.6 collective-permute-done.8
  111.8 3.5 %collective-permute-start.10 = (bf16[4,24,256]{2,1,0:T(8,128)(2,1)S(1)}, bf16[4,24,256]{2,1,0:T(8,128)(2,1)S(1)}, u32[]{:S(2)}, u32[]{:S(2)}) collective-permute-start(bf16[4,24,256]{2,1,0:T(8,128)(2,1)S(1)} %bitcast.215), channel_id=1, source_target_pairs={{0,64},{32,96},{64,128},{96,160},{128,192},{160,224},{192,256},{22... | collective-permute-start | bytes 147464 | tf_op jit(solution)/shard_map/ppermute | solution.py:56
  115.3 4.9 %collective-permute-start.9 = (bf16[4,24,256]{2,1,0:T(8,128)(2,1)S(1)}, bf16[4,24,256]{2,1,0:T(8,128)(2,1)S(1)}, u32[]{:S(2)}, u32[]{:S(2)}) collective-permute-start(bf16[4,24,256]{2,1,0:T(8,128)(2,1)S(1)} %bitcast.214), channel_id=1, source_target_pairs={{64,0},{96,32},{128,64},{160,96},{192,128},{224,160},{256,192},{28... | collective-permute-start | bytes 147464 | tf_op jit(solution)/shard_map/ppermute | solution.py:60
  120.8 2.1 collective-permute-done.9
  124.9 3.6 %collective-permute-start.12 = (bf16[16,4,256]{2,1,0:T(4,128)(2,1)}, bf16[16,4,256]{2,1,0:T(4,128)(2,1)}, u32[]{:S(2)}, u32[]{:S(2)}) collective-permute-start(bf16[16,4,256]{2,1,0:T(4,128)(2,1)} %get-tuple-element.42), channel_id=1, source_target_pairs={{0,1},{1,2},{2,3},{3,32},{4,5},{5,6},{6,7},{7,36},{8,9},{9,10},{10... | collective-permute-start | bytes 98312 | tf_op jit(solution)/shard_map/ppermute | solution.py:48
  131.9 8.9 %collective-permute-start.13 = (bf16[1024,128]{0,1:T(8,128)(2,1)S(1)}, bf16[1024,128]{0,1:T(8,128)(2,1)S(1)}, u32[]{:S(2)}, u32[]{:S(2)}) collective-permute-start(bf16[1024,128]{0,1:T(8,128)(2,1)S(1)} %get-tuple-element.23), channel_id=1, source_target_pairs={{0,96},{32,0},{64,32},{96,64},{1,97},{33,1},{65,33},{97,65},{2,98}... | collective-permute-start | bytes 786440 | tf_op jit(solution)/shard_map/ppermute | solution.py:78
  140.8 3.2 %collective-permute-start.14 = (bf16[1024,128]{0,1:T(8,128)(2,1)S(1)}, bf16[1024,128]{0,1:T(8,128)(2,1)S(1)}, u32[]{:S(2)}, u32[]{:S(2)}) collective-permute-start(bf16[1024,128]{0,1:T(8,128)(2,1)S(1)} %get-tuple-element.25), channel_id=1, source_target_pairs={{0,64},{32,96},{64,0},{96,32},{1,65},{33,97},{65,1},{97,33},{2,66}... | collective-permute-start | bytes 786440 | tf_op jit(solution)/shard_map/ppermute | solution.py:78
  144.0 1.9 collective-permute-start.15
  146.8 3.2 %collective-permute-done.13 = bf16[1024,128]{0,1:T(8,128)(2,1)S(1)} collective-permute-done((bf16[1024,128]{0,1:T(8,128)(2,1)S(1)}, bf16[1024,128]{0,1:T(8,128)(2,1)S(1)}, u32[]{:S(2)}, u32[]{:S(2)}) %collective-permute-start.13) | collective-permute-done | bytes 262176 | tf_op jit(solution)/shard_map/ppermute | solution.py:78
  150.0 2.7 %collective-permute-done.14 = bf16[1024,128]{0,1:T(8,128)(2,1)S(1)} collective-permute-done((bf16[1024,128]{0,1:T(8,128)(2,1)S(1)}, bf16[1024,128]{0,1:T(8,128)(2,1)S(1)}, u32[]{:S(2)}, u32[]{:S(2)}) %collective-permute-start.14) | collective-permute-done | bytes 262176 | tf_op jit(solution)/shard_map/ppermute | solution.py:78
  152.7 2.8 %collective-permute-done.15 = bf16[1024,128]{0,1:T(8,128)(2,1)S(1)} collective-permute-done((bf16[1024,128]{0,1:T(8,128)(2,1)S(1)}, bf16[1024,128]{0,1:T(8,128)(2,1)S(1)}, u32[]{:S(2)}, u32[]{:S(2)}) %collective-permute-start.15) | collective-permute-done | bytes 262176 | tf_op jit(solution)/shard_map/ppermute | solution.py:78
  155.9 36.3 %all_to_all.16 = bf16[8,128,640]{1,2,0:T(8,128)(2,1)S(1)} all-to-all(bf16[8,128,640]{1,2,0:T(8,128)(2,1)S(1)} %copy_bitcast_fusion), channel_id=1, replica_groups=mesh['zl'=6,'x'=4,'zh'=2,'y'=8,'c'=2] {'y'}, dimensions={0} | all-to-all | bytes 2621440 | tf_op jit(solution)/shard_map/all_to_all | solution.py:64
  195.2 1.9 collective-permute-start.16
  199.4 14.2 %all-to-all-start.2 = ((bf16[12,4,32,128]{3,2,1,0:T(8,128)(2,1)}), bf16[12,4,32,128]{3,2,1,0:T(8,128)(2,1)S(1)}, u32[]{:S(2)}, u32[]{:S(2)}) async-start(bf16[12,4,32,128]{3,2,1,0:T(8,128)(2,1)} %bitcast.71), calls=%async_computation.2 | async-start | bytes 786432 | tf_op jit(solution)/shard_map/all_to_all | solution.py:64
  213.8 8.8 %collective-permute-start.17 = (bf16[2,2,4,32,128]{4,3,2,1,0:T(8,128)(2,1)S(1)}, bf16[2,2,4,32,128]{4,3,2,1,0:T(8,128)(2,1)S(1)}, u32[]{:S(2)}, u32[]{:S(2)}) collective-permute-start(bf16[2,2,4,32,128]{4,3,2,1,0:T(8,128)(2,1)S(1)} %fusion.32), channel_id=1, source_target_pairs={{0,16},{16,0},{1,17},{17,1},{2,18},{18,2},{3,19},{19,3},{4,20},{20... | collective-permute-start | bytes 393224 | tf_op jit(solution)/shard_map/ppermute | solution.py:82
  222.6 19.6 %collective-permute-done.17 = bf16[2,2,4,32,128]{4,3,2,1,0:T(8,128)(2,1)S(1)} collective-permute-done((bf16[2,2,4,32,128]{4,3,2,1,0:T(8,128)(2,1)S(1)}, bf16[2,2,4,32,128]{4,3,2,1,0:T(8,128)(2,1)S(1)}, u32[]{:S(2)}, u32[]{:S(2)}) %collective-permute-start.17) | collective-permute-done | bytes 131104 | tf_op jit(solution)/shard_map/ppermute | solution.py:82
  244.6 1.9 collective-permute-start.18
  246.5 4.8 %collective-permute-start.19 = (bf16[8,32,128]{2,1,0:T(8,128)(2,1)S(1)}, bf16[8,32,128]{2,1,0:T(8,128)(2,1)S(1)}, u32[]{:S(2)}, u32[]{:S(2)}) collective-permute-start(bf16[8,32,128]{2,1,0:T(8,128)(2,1)S(1)} %bitcast_reduce_fusion), channel_id=1, source_target_pairs={{0,64},{32,96},{64,0},{96,32},{1,65},{33,97},{65,1},{97,33},{2,66}... | collective-permute-start | bytes 196616 | tf_op jit(solution)/shard_map/ppermute | solution.py:78
  251.3 2.9 %collective-permute-start.20 = (bf16[8,32,128]{2,1,0:T(8,128)(2,1)S(1)}, bf16[8,32,128]{2,1,0:T(8,128)(2,1)S(1)}, u32[]{:S(2)}, u32[]{:S(2)}) collective-permute-start(bf16[8,32,128]{2,1,0:T(8,128)(2,1)S(1)} %bitcast_reduce_fusion), channel_id=1, source_target_pairs={{0,32},{32,64},{64,96},{96,0},{1,33},{33,65},{65,97},{97,1},{2,34}... | collective-permute-start | bytes 196616 | tf_op jit(solution)/shard_map/ppermute | solution.py:78
  254.3 4.4 %collective-permute-done.20 = bf16[8,32,128]{2,1,0:T(8,128)(2,1)S(1)} collective-permute-done((bf16[8,32,128]{2,1,0:T(8,128)(2,1)S(1)}, bf16[8,32,128]{2,1,0:T(8,128)(2,1)S(1)}, u32[]{:S(2)}, u32[]{:S(2)}) %collective-permute-start.20) | collective-permute-done | bytes 65568 | tf_op jit(solution)/shard_map/ppermute | solution.py:78
  (140 shorter events, 28.4 us)
Async XLA Ops:
  0.6 2.3 copy-start.7
  3.3 24.5 %collective-permute-start = (bf16[20,32,128]{2,1,0:T(8,128)(2,1)S(1)}, bf16[20,32,128]{2,1,0:T(8,128)(2,1)S(1)}, u32[]{:S(2)}, u32[]{:S(2)}) collective-permute-start(bf16[20,32,128]{2,1,0:T(8,128)(2,1)S(1)} %pad_maximum_fusion.11), channel_id=1, source_target_pairs={{0,16},{16,0},{1,17},{17,1},{2,18},{18,2},{3,19},{19,3},{4,20},{20... | collective-permute-start | bytes 491528 | tf_op jit(solution)/shard_map/ppermute | solution.py:82
  28.0 3.3 %collective-permute-start.1 = (bf16[24,32,128]{2,1,0:T(8,128)(2,1)S(1)}, bf16[24,32,128]{2,1,0:T(8,128)(2,1)S(1)}, u32[]{:S(2)}, u32[]{:S(2)}) collective-permute-start(bf16[24,32,128]{2,1,0:T(8,128)(2,1)S(1)} %pad_maximum_fusion.9), channel_id=1, source_target_pairs={{0,1},{1,0},{2,3},{3,2},{4,5},{5,4},{6,7},{7,6},{8,9},{9,8},{10,11... | collective-permute-start | bytes 589832 | tf_op jit(solution)/shard_map/ppermute | solution.py:82
  73.7 14.8 %collective-permute-start.2 = (bf16[1024,128]{1,0:T(8,128)(2,1)S(1)}, bf16[1024,128]{1,0:T(8,128)(2,1)S(1)}, u32[]{:S(2)}, u32[]{:S(2)}) collective-permute-start(bf16[1024,128]{1,0:T(8,128)(2,1)S(1)} %get-tuple-element.22), channel_id=1, source_target_pairs={{0,96},{32,0},{64,32},{96,64},{1,97},{33,1},{65,33},{97,65},{2,98}... | collective-permute-start | bytes 786440 | tf_op jit(solution)/shard_map/ppermute | solution.py:78
  78.3 12.6 %collective-permute-start.3 = (bf16[1024,128]{1,0:T(8,128)(2,1)S(1)}, bf16[1024,128]{1,0:T(8,128)(2,1)S(1)}, u32[]{:S(2)}, u32[]{:S(2)}) collective-permute-start(bf16[1024,128]{1,0:T(8,128)(2,1)S(1)} %get-tuple-element.22), channel_id=1, source_target_pairs={{0,64},{32,96},{64,0},{96,32},{1,65},{33,97},{65,1},{97,33},{2,66}... | collective-permute-start | bytes 786440 | tf_op jit(solution)/shard_map/ppermute | solution.py:78
  81.0 13.0 %collective-permute-start.4 = (bf16[1024,128]{1,0:T(8,128)(2,1)S(1)}, bf16[1024,128]{1,0:T(8,128)(2,1)S(1)}, u32[]{:S(2)}, u32[]{:S(2)}) collective-permute-start(bf16[1024,128]{1,0:T(8,128)(2,1)S(1)} %get-tuple-element.22), channel_id=1, source_target_pairs={{0,32},{32,64},{64,96},{96,0},{1,33},{33,65},{65,97},{97,1},{2,34}... | collective-permute-start | bytes 786440 | tf_op jit(solution)/shard_map/ppermute | solution.py:78
  94.3 0.7 copy-start
  94.3 0.8 copy-start.2
  95.1 2.8 %collective-permute-start.5 = (bf16[16,4,256]{2,1,0:T(4,128)(2,1)S(1)}, bf16[16,4,256]{2,1,0:T(4,128)(2,1)S(1)}, u32[]{:S(2)}, u32[]{:S(2)}) collective-permute-start(bf16[16,4,256]{2,1,0:T(4,128)(2,1)S(1)} %get-tuple-element.45), channel_id=1, source_target_pairs={{0,1},{1,2},{2,3},{3,32},{4,5},{5,6},{6,7},{7,36},{8,9},{9,10},{10... | collective-permute-start | bytes 98312 | tf_op jit(solution)/shard_map/ppermute | solution.py:48
  96.4 3.1 %collective-permute-start.6 = (bf16[16,4,256]{2,1,0:T(4,128)(2,1)S(1)}, bf16[16,4,256]{2,1,0:T(4,128)(2,1)S(1)}, u32[]{:S(2)}, u32[]{:S(2)}) collective-permute-start(bf16[16,4,256]{2,1,0:T(4,128)(2,1)S(1)} %get-tuple-element.46), channel_id=1, source_target_pairs={{1,0},{2,1},{3,2},{32,3},{5,4},{6,5},{7,6},{36,7},{9,8},{10,9},{11... | collective-permute-start | bytes 98312 | tf_op jit(solution)/shard_map/ppermute | solution.py:52
  99.6 8.6 %collective-permute-start.7 = (bf16[4,24,256]{2,1,0:T(8,128)(2,1)S(1)}, bf16[4,24,256]{2,1,0:T(8,128)(2,1)S(1)}, u32[]{:S(2)}, u32[]{:S(2)}) collective-permute-start(bf16[4,24,256]{2,1,0:T(8,128)(2,1)S(1)} %get-tuple-element.43), channel_id=1, source_target_pairs={{0,64},{32,96},{64,128},{96,160},{128,192},{160,224},{192,256},{22... | collective-permute-start | bytes 147464 | tf_op jit(solution)/shard_map/ppermute | solution.py:56
  102.3 7.5 %collective-permute-start.8 = (bf16[4,24,256]{2,1,0:T(8,128)(2,1)S(1)}, bf16[4,24,256]{2,1,0:T(8,128)(2,1)S(1)}, u32[]{:S(2)}, u32[]{:S(2)}) collective-permute-start(bf16[4,24,256]{2,1,0:T(8,128)(2,1)S(1)} %get-tuple-element.44), channel_id=1, source_target_pairs={{64,0},{96,32},{128,64},{160,96},{192,128},{224,160},{256,192},{28... | collective-permute-start | bytes 147464 | tf_op jit(solution)/shard_map/ppermute | solution.py:60
  110.6 17.9 %copy-start.4 = (bf16[256,128]{1,0:T(8,128)(2,1)}, bf16[256,128]{1,0:T(8,128)(2,1)S(1)}, u32[]{:S(2)}) copy-start(bf16[256,128]{1,0:T(8,128)(2,1)S(1)} %convolution_convert_fusion.10) | copy-start | bytes 196612
  111.6 11.4 %copy-start.6 = (bf16[256,128]{0,1:T(8,128)(2,1)}, bf16[256,128]{0,1:T(8,128)(2,1)S(1)}, u32[]{:S(2)}) copy-start(bf16[256,128]{0,1:T(8,128)(2,1)S(1)} %convolution_convert_fusion.8) | copy-start | bytes 196612
  111.8 8.9 %collective-permute-start.10 = (bf16[4,24,256]{2,1,0:T(8,128)(2,1)S(1)}, bf16[4,24,256]{2,1,0:T(8,128)(2,1)S(1)}, u32[]{:S(2)}, u32[]{:S(2)}) collective-permute-start(bf16[4,24,256]{2,1,0:T(8,128)(2,1)S(1)} %bitcast.215), channel_id=1, source_target_pairs={{0,64},{32,96},{64,128},{96,160},{128,192},{160,224},{192,256},{22... | collective-permute-start | bytes 147464 | tf_op jit(solution)/shard_map/ppermute | solution.py:56
  115.3 7.5 %collective-permute-start.9 = (bf16[4,24,256]{2,1,0:T(8,128)(2,1)S(1)}, bf16[4,24,256]{2,1,0:T(8,128)(2,1)S(1)}, u32[]{:S(2)}, u32[]{:S(2)}) collective-permute-start(bf16[4,24,256]{2,1,0:T(8,128)(2,1)S(1)} %bitcast.214), channel_id=1, source_target_pairs={{64,0},{96,32},{128,64},{160,96},{192,128},{224,160},{256,192},{28... | collective-permute-start | bytes 147464 | tf_op jit(solution)/shard_map/ppermute | solution.py:60
  123.6 6.8 %collective-permute-start.11 = (bf16[16,4,256]{2,1,0:T(4,128)(2,1)}, bf16[16,4,256]{2,1,0:T(4,128)(2,1)}, u32[]{:S(2)}, u32[]{:S(2)}) collective-permute-start(bf16[16,4,256]{2,1,0:T(4,128)(2,1)} %get-tuple-element.41), channel_id=1, source_target_pairs={{1,0},{2,1},{3,2},{32,3},{5,4},{6,5},{7,6},{36,7},{9,8},{10,9},{11... | collective-permute-start | bytes 98312 | tf_op jit(solution)/shard_map/ppermute | solution.py:52
  124.9 5.5 %collective-permute-start.12 = (bf16[16,4,256]{2,1,0:T(4,128)(2,1)}, bf16[16,4,256]{2,1,0:T(4,128)(2,1)}, u32[]{:S(2)}, u32[]{:S(2)}) collective-permute-start(bf16[16,4,256]{2,1,0:T(4,128)(2,1)} %get-tuple-element.42), channel_id=1, source_target_pairs={{0,1},{1,2},{2,3},{3,32},{4,5},{5,6},{6,7},{7,36},{8,9},{9,10},{10... | collective-permute-start | bytes 98312 | tf_op jit(solution)/shard_map/ppermute | solution.py:48
  131.8 14.2 %copy-start.5 = (bf16[256,128]{1,0:T(8,128)(2,1)S(1)}, bf16[256,128]{1,0:T(8,128)(2,1)}, u32[]{:S(2)}) copy-start(bf16[256,128]{1,0:T(8,128)(2,1)} %copy-done.4) | copy-start | bytes 196612
  131.8 14.5 %copy-start.1 = (bf16[1024,128]{1,0:T(8,128)(2,1)S(1)}, bf16[1024,128]{1,0:T(8,128)(2,1)}, u32[]{:S(2)}) copy-start(bf16[1024,128]{1,0:T(8,128)(2,1)} %copy-done) | copy-start | bytes 786436
  131.8 14.5 %copy-start.3 = (bf16[1024,128]{1,0:T(8,128)(2,1)S(1)}, bf16[1024,128]{1,0:T(8,128)(2,1)}, u32[]{:S(2)}) copy-start(bf16[1024,128]{1,0:T(8,128)(2,1)} %copy-done.2) | copy-start | bytes 786436
  131.8 14.5 %copy-start.8 = (bf16[256,128]{1,0:T(8,128)(2,1)S(1)}, bf16[256,128]{1,0:T(8,128)(2,1)}, u32[]{:S(2)}) copy-start(bf16[256,128]{1,0:T(8,128)(2,1)} %copy.218) | copy-start | bytes 196612
  131.9 18.1 %collective-permute-start.13 = (bf16[1024,128]{0,1:T(8,128)(2,1)S(1)}, bf16[1024,128]{0,1:T(8,128)(2,1)S(1)}, u32[]{:S(2)}, u32[]{:S(2)}) collective-permute-start(bf16[1024,128]{0,1:T(8,128)(2,1)S(1)} %get-tuple-element.23), channel_id=1, source_target_pairs={{0,96},{32,0},{64,32},{96,64},{1,97},{33,1},{65,33},{97,65},{2,98}... | collective-permute-start | bytes 786440 | tf_op jit(solution)/shard_map/ppermute | solution.py:78
  140.8 11.9 %collective-permute-start.14 = (bf16[1024,128]{0,1:T(8,128)(2,1)S(1)}, bf16[1024,128]{0,1:T(8,128)(2,1)S(1)}, u32[]{:S(2)}, u32[]{:S(2)}) collective-permute-start(bf16[1024,128]{0,1:T(8,128)(2,1)S(1)} %get-tuple-element.25), channel_id=1, source_target_pairs={{0,64},{32,96},{64,0},{96,32},{1,65},{33,97},{65,1},{97,33},{2,66}... | collective-permute-start | bytes 786440 | tf_op jit(solution)/shard_map/ppermute | solution.py:78
  144.0 11.5 %collective-permute-start.15 = (bf16[1024,128]{0,1:T(8,128)(2,1)S(1)}, bf16[1024,128]{0,1:T(8,128)(2,1)S(1)}, u32[]{:S(2)}, u32[]{:S(2)}) collective-permute-start(bf16[1024,128]{0,1:T(8,128)(2,1)S(1)} %get-tuple-element.24), channel_id=1, source_target_pairs={{0,32},{32,64},{64,96},{96,0},{1,33},{33,65},{65,97},{97,1},{2,34}... | collective-permute-start | bytes 786440 | tf_op jit(solution)/shard_map/ppermute | solution.py:78
  195.2 3.3 %collective-permute-start.16 = (bf16[12,64,128]{2,1,0:T(8,128)(2,1)S(1)}, bf16[12,64,128]{2,1,0:T(8,128)(2,1)S(1)}, u32[]{:S(2)}, u32[]{:S(2)}) collective-permute-start(bf16[12,64,128]{2,1,0:T(8,128)(2,1)S(1)} %pad_maximum_fusion.10), channel_id=1, source_target_pairs={{0,1},{1,0},{2,3},{3,2},{4,5},{5,4},{6,7},{7,6},{8,9},{9,8},{10,11... | collective-permute-start | bytes 589832 | tf_op jit(solution)/shard_map/ppermute | solution.py:82
  199.4 45.1 %all-to-all-start.2 = ((bf16[12,4,32,128]{3,2,1,0:T(8,128)(2,1)}), bf16[12,4,32,128]{3,2,1,0:T(8,128)(2,1)S(1)}, u32[]{:S(2)}, u32[]{:S(2)}) async-start(bf16[12,4,32,128]{3,2,1,0:T(8,128)(2,1)} %bitcast.71), calls=%async_computation.2 | async-start | bytes 786432 | tf_op jit(solution)/shard_map/all_to_all | solution.py:64
  213.8 28.5 %collective-permute-start.17 = (bf16[2,2,4,32,128]{4,3,2,1,0:T(8,128)(2,1)S(1)}, bf16[2,2,4,32,128]{4,3,2,1,0:T(8,128)(2,1)S(1)}, u32[]{:S(2)}, u32[]{:S(2)}) collective-permute-start(bf16[2,2,4,32,128]{4,3,2,1,0:T(8,128)(2,1)S(1)} %fusion.32), channel_id=1, source_target_pairs={{0,16},{16,0},{1,17},{17,1},{2,18},{18,2},{3,19},{19,3},{4,20},{20... | collective-permute-start | bytes 393224 | tf_op jit(solution)/shard_map/ppermute | solution.py:82
  244.6 9.7 %collective-permute-start.18 = (bf16[8,32,128]{2,1,0:T(8,128)(2,1)S(1)}, bf16[8,32,128]{2,1,0:T(8,128)(2,1)S(1)}, u32[]{:S(2)}, u32[]{:S(2)}) collective-permute-start(bf16[8,32,128]{2,1,0:T(8,128)(2,1)S(1)} %bitcast_reduce_fusion), channel_id=1, source_target_pairs={{0,96},{32,0},{64,32},{96,64},{1,97},{33,1},{65,33},{97,65},{2,98}... | collective-permute-start | bytes 196616 | tf_op jit(solution)/shard_map/ppermute | solution.py:78
  246.5 7.8 %collective-permute-start.19 = (bf16[8,32,128]{2,1,0:T(8,128)(2,1)S(1)}, bf16[8,32,128]{2,1,0:T(8,128)(2,1)S(1)}, u32[]{:S(2)}, u32[]{:S(2)}) collective-permute-start(bf16[8,32,128]{2,1,0:T(8,128)(2,1)S(1)} %bitcast_reduce_fusion), channel_id=1, source_target_pairs={{0,64},{32,96},{64,0},{96,32},{1,65},{33,97},{65,1},{97,33},{2,66}... | collective-permute-start | bytes 196616 | tf_op jit(solution)/shard_map/ppermute | solution.py:78
  251.3 7.4 %collective-permute-start.20 = (bf16[8,32,128]{2,1,0:T(8,128)(2,1)S(1)}, bf16[8,32,128]{2,1,0:T(8,128)(2,1)S(1)}, u32[]{:S(2)}, u32[]{:S(2)}) collective-permute-start(bf16[8,32,128]{2,1,0:T(8,128)(2,1)S(1)} %bitcast_reduce_fusion), channel_id=1, source_target_pairs={{0,32},{32,64},{64,96},{96,0},{1,33},{33,65},{65,97},{97,1},{2,34}... | collective-permute-start | bytes 196616 | tf_op jit(solution)/shard_map/ppermute | solution.py:78

commit v4 on v3

--- a/solution.py
+++ b/solution.py
@@ -134,19 +134,15 @@
     t_mine = jnp.stack([t_keep, got[:16].reshape(2, 4, 2, WIDTH, 128)], 2)
     t_mine = t_mine.reshape(2, 4, 128, 128)
     w_mine = jnp.stack([w_keep, got[16:].reshape(4, 2, WIDTH, 128)], 1).reshape(4, 128, 128)
-    t_mine = t_mine.transpose(0, 2, 1, 3).reshape(1, 2, 128, 512)
-    send = jnp.concatenate(
-        [
-            jnp.broadcast_to(t_mine, (4, 2, 128, 512)),
-            jnp.broadcast_to(w_mine[:, None], (4, 2, 128, 128)),
-        ],
-        3,
-    )
-    got = a2a(send.reshape(8, 128, 640), "y").reshape(D, 640)
-    tokens = got[:, :TILE_TOKENS]
-    grads = got[:, TILE_TOKENS : 2 * TILE_TOKENS]
-    w_x = got[:, 2 * TILE_TOKENS :]
-
+    t_mine = t_mine.transpose(0, 2, 1, 3)
+
+    def gather(v, lead):
+        send = jnp.broadcast_to(v, lead + v.shape[2:]).reshape(8, 128, -1)
+        return a2a(send, "y").reshape(D, -1)
+
+    w_x = gather(w_mine[:, None], (4, 2))
+    tokens = gather(t_mine[None, :, :, :2].reshape(1, 2, 128, TILE_TOKENS), (4, 2))
+    grads = gather(t_mine[None, :, :, 2:].reshape(1, 2, 128, TILE_TOKENS), (4, 2))
     w_list = jnp.stack([w_x] + [shift(w_x, "x", 4, 1, s) for s in (1, 2, 3)])
     w_qkv = jnp.concatenate([pick(w_list, (m - x) % 4) for m in range(3)], 1)
     w_out = pick(w_list, (3 - x) % 4)
@@ -218,21 +214,24 @@
     ).astype(bf16)
     total = pick(dw, x).astype(f32)
     for s in (1, 2, 3):
-        total = total + shift(pick(dw, (x - s) % 4), "x", 4, 1, s).astype(f32)
-    send = jnp.concatenate([part, d_tokens, total.astype(bf16)], 1).reshape(8, 128, 640)
-    got = a2a(send, "y").reshape(4, 2, 128, 640)
-    back = jnp.sum(got[..., :512].astype(f32), 0)
+        got = shift(pick(dw, (x - s) % 4), "x", 4, 1, s)
+        total = total + got.astype(f32)
+    send = jnp.concatenate([part, d_tokens], 1).reshape(8, 128, 512)
+    got = a2a(send, "y").reshape(4, 2, 128, 512)
+    back = jnp.sum(got.astype(f32), 0)
     back = back.reshape(2, 2, 64, 4, 128).transpose(1, 0, 3, 2, 4)
-    dw = jnp.sum(got[..., 512:].astype(f32), 1).reshape(4, 2, 64, 128)
-    give = jnp.concatenate([back[1].reshape(8, 64, 128), dw[:, 1]]).astype(bf16)
-    got = swap(give, "c")
-    dw = (dw[:, 0] + got[8:].astype(f32)).astype(bf16).reshape(4, 2, WIDTH, 128)
+    back_c = swap(back[1].astype(bf16), "c")
+    got = a2a(total.astype(bf16).reshape(8, 128, 128), "y")
+    dw = jnp.sum(got.reshape(4, 2, 128, 128).astype(f32), 1)
+    dw = dw.reshape(4, 2, 64, 128)
+    got = swap(dw[:, 1].astype(bf16), "c")
+    dw = (dw[:, 0] + got.astype(f32)).astype(bf16).reshape(4, 2, WIDTH, 128)
     dw = jnp.stack(in_order(dw[:, 0], dw[:, 1], zh))
     dw = jnp.broadcast_to(dw, (6, 2, 4, WIDTH, 128)).reshape(12, 4, WIDTH, 128)
     dw = a2a(dw, ("zl", "zh"))
     total = jnp.sum(dw.reshape(6, HEADS, WIDTH, 128).astype(f32), 0).astype(bf16)
 
-    back = jnp.stack([back[0], got[:8].reshape(2, 4, 64, 128).astype(f32)])
+    back = jnp.stack([back[0], back_c.astype(f32)])
     back = back.reshape(2, 2, 4, 2, WIDTH, 128)
     far = swap(back[:, :, :, 1].astype(bf16), "zh")
     back = back[:, :, :, 0] + far.astype(f32)

time: 261 us -> 257 us (0.985)
  the two profiles are of different devices: /device:TPU:64 before, /device:TPU:198 now
where the time goes in v4:
time: 257 us; the launch traced here: 256 us
  starting transfers between devices  121 us (47%)
  waiting for transfers between devices  113 us (44%)
  local copies, waits for them, and re-layouts  12.2 us (5%)
  other arithmetic  4.64 us (2%)
  matrix products  4.05 us (2%)
    all_to_all x6, waiting for transfers between devices, a2a(): return lax.all_to_all(v, axes, 0, 0, tiled=True)  52.3 us
    all_to_all x6, starting transfers between devices, a2a(): return lax.all_to_all(v, axes, 0, 0, tiled=True)  38.3 us
    ppermute x9, starting transfers between devices, shift(): return lax.ppermute(v, axis, pairs)  29.2 us
    ppermute x5, starting transfers between devices, swap(): lax.ppermute(v, axis, [(i, i ^ 1) for i in range(lax.axis_size(axis))])  25 us
    ppermute x9, waiting for transfers between devices, shift(): return lax.ppermute(v, axis, pairs)  22.4 us
    ppermute x5, waiting for transfers between devices, swap(): lax.ppermute(v, axis, [(i, i ^ 1) for i in range(lax.axis_size(axis))])  20.3 us
    ppermute x2, waiting for transfers between devices, to_up(): return lax.ppermute(v, ('zl', 'x'), UP)  11.3 us
    ppermute x2, starting transfers between devices, to_down(): return lax.ppermute(v, ('zl', 'x'), DOWN)  10.2 us
  transfers between devices with their start and end apart: 28, of which 20 were waited for; matrix products, arithmetic and copies ran while one was open for 3% of the time, Pallas kernels for 0%

profile of v4, /device:TPU:198, one launch (start us, length us, event | category | flops | bytes accessed | tf_op | source)
XLA Modules:
  0.0 255.9 jit_solution(5878463062545226670)
XLA Ops:
  3.3 12.4 %collective-permute-start = (bf16[20,32,128]{2,1,0:T(8,128)(2,1)S(1)}, bf16[20,32,128]{2,1,0:T(8,128)(2,1)S(1)}, u32[]{:S(2)}, u32[]{:S(2)}) collective-permute-start(bf16[20,32,128]{2,1,0:T(8,128)(2,1)S(1)} %pad_maximum_fusion.9), channel_id=1, source_target_pairs={{0,16},{16,0},{1,17},{17,1},{2,18},{18,2},{3,19},{19,3},{4,20},{20... | collective-permute-start | bytes 491528 | tf_op jit(solution)/shard_map/ppermute | solution.py:82
  15.8 9.6 %collective-permute-done = bf16[20,32,128]{2,1,0:T(8,128)(2,1)S(1)} collective-permute-done((bf16[20,32,128]{2,1,0:T(8,128)(2,1)S(1)}, bf16[20,32,128]{2,1,0:T(8,128)(2,1)S(1)}, u32[]{:S(2)}, u32[]{:S(2)}) %collective-permute-start) | collective-permute-done | bytes 163872 | tf_op jit(solution)/shard_map/ppermute | solution.py:82
  29.6 7.1 %all-to-all-start = ((bf16[8,128,128]{2,1,0:T(8,128)(2,1)}), bf16[8,128,128]{2,1,0:T(8,128)(2,1)S(1)}, u32[]{:S(2)}, u32[]{:S(2)}) async-start(bf16[8,128,128]{2,1,0:T(8,128)(2,1)} %bitcast.20), calls=%async_computation | async-start | bytes 524288 | tf_op jit(solution)/shard_map/all_to_all | solution.py:64
  37.1 11.8 %all-to-all-done = bf16[8,128,128]{2,1,0:T(8,128)(2,1)S(1)} async-done(((bf16[8,128,128]{2,1,0:T(8,128)(2,1)}), bf16[8,128,128]{2,1,0:T(8,128)(2,1)S(1)}, u32[]{:S(2)}, u32[]{:S(2)}) %all-to-all-start) | async-done | bytes 262176 | tf_op jit(solution)/shard_map/all_to_all | solution.py:64
  49.7 3.5 %all-to-all-start.1 = ((bf16[8,128,256]{2,1,0:T(8,128)(2,1)}), bf16[8,128,256]{2,1,0:T(8,128)(2,1)S(1)}, u32[]{:S(2)}, u32[]{:S(2)}) async-start(bf16[8,128,256]{2,1,0:T(8,128)(2,1)} %bitcast.32), calls=%async_computation.1 | async-start | bytes 1048576 | tf_op jit(solution)/shard_map/all_to_all | solution.py:64
  53.2 2.4 collective-permute-start.4
  55.6 4.3 %collective-permute-start.3 = (bf16[1024,128]{1,0:T(8,128)(2,1)S(1)}, bf16[1024,128]{1,0:T(8,128)(2,1)S(1)}, u32[]{:S(2)}, u32[]{:S(2)}) collective-permute-start(bf16[1024,128]{1,0:T(8,128)(2,1)S(1)} %bitcast.204), channel_id=1, source_target_pairs={{0,64},{32,96},{64,0},{96,32},{1,65},{33,97},{65,1},{97,33},{2,66}... | collective-permute-start | bytes 786440 | tf_op jit(solution)/shard_map/ppermute | solution.py:78
  64.3 3.3 %collective-permute-done.3 = bf16[1024,128]{1,0:T(8,128)(2,1)S(1)} collective-permute-done((bf16[1024,128]{1,0:T(8,128)(2,1)S(1)}, bf16[1024,128]{1,0:T(8,128)(2,1)S(1)}, u32[]{:S(2)}, u32[]{:S(2)}) %collective-permute-start.3) | collective-permute-done | bytes 262176 | tf_op jit(solution)/shard_map/ppermute | solution.py:78
  67.6 3.8 %collective-permute-done.2 = bf16[1024,128]{1,0:T(8,128)(2,1)S(1)} collective-permute-done((bf16[1024,128]{1,0:T(8,128)(2,1)S(1)}, bf16[1024,128]{1,0:T(8,128)(2,1)S(1)}, u32[]{:S(2)}, u32[]{:S(2)}) %collective-permute-start.2) | collective-permute-done | bytes 262176 | tf_op jit(solution)/shard_map/ppermute | solution.py:78
  72.3 6.8 %all-to-all-start.2 = ((bf16[8,128,256]{2,1,0:T(8,128)(2,1)}), bf16[8,128,256]{2,1,0:T(8,128)(2,1)S(1)}, u32[]{:S(2)}, u32[]{:S(2)}) async-start(bf16[8,128,256]{2,1,0:T(8,128)(2,1)} %bitcast.41), calls=%async_computation.2 | async-start | bytes 1048576 | tf_op jit(solution)/shard_map/all_to_all | solution.py:64
  81.7 4.5 %collective-permute-start.6 = (bf16[16,4,256]{2,1,0:T(4,128)(2,1)S(1)}, bf16[16,4,256]{2,1,0:T(4,128)(2,1)S(1)}, u32[]{:S(2)}, u32[]{:S(2)}) collective-permute-start(bf16[16,4,256]{2,1,0:T(4,128)(2,1)S(1)} %get-tuple-element.49), channel_id=1, source_target_pairs={{1,0},{2,1},{3,2},{32,3},{5,4},{6,5},{7,6},{36,7},{9,8},{10,9},{11... | collective-permute-start | bytes 98312 | tf_op jit(solution)/shard_map/ppermute | solution.py:52
  86.5 2.6 %collective-permute-done.5 = bf16[16,4,256]{2,1,0:T(4,128)(2,1)S(1)} collective-permute-done((bf16[16,4,256]{2,1,0:T(4,128)(2,1)S(1)}, bf16[16,4,256]{2,1,0:T(4,128)(2,1)S(1)}, u32[]{:S(2)}, u32[]{:S(2)}) %collective-permute-start.5) | collective-permute-done | bytes 32800 | tf_op jit(solution)/shard_map/ppermute | solution.py:48
  89.2 8.3 %collective-permute-start.7 = (bf16[4,24,256]{2,1,0:T(8,128)(2,1)S(1)}, bf16[4,24,256]{2,1,0:T(8,128)(2,1)S(1)}, u32[]{:S(2)}, u32[]{:S(2)}) collective-permute-start(bf16[4,24,256]{2,1,0:T(8,128)(2,1)S(1)} %get-tuple-element.46), channel_id=1, source_target_pairs={{0,64},{32,96},{64,128},{96,160},{128,192},{160,224},{192,256},{22... | collective-permute-start | bytes 147464 | tf_op jit(solution)/shard_map/ppermute | solution.py:56
  99.8 7.3 %collective-permute-done.8 = bf16[4,24,256]{2,1,0:T(8,128)(2,1)S(1)} collective-permute-done((bf16[4,24,256]{2,1,0:T(8,128)(2,1)S(1)}, bf16[4,24,256]{2,1,0:T(8,128)(2,1)S(1)}, u32[]{:S(2)}, u32[]{:S(2)}) %collective-permute-start.8) | collective-permute-done | bytes 49184 | tf_op jit(solution)/shard_map/ppermute | solution.py:60
  111.4 5.4 %collective-permute-start.9 = (bf16[4,24,256]{2,1,0:T(8,128)(2,1)S(1)}, bf16[4,24,256]{2,1,0:T(8,128)(2,1)S(1)}, u32[]{:S(2)}, u32[]{:S(2)}) collective-permute-start(bf16[4,24,256]{2,1,0:T(8,128)(2,1)S(1)} %bitcast.234), channel_id=1, source_target_pairs={{64,0},{96,32},{128,64},{160,96},{192,128},{224,160},{256,192},{28... | collective-permute-start | bytes 147464 | tf_op jit(solution)/shard_map/ppermute | solution.py:60
  117.1 4.0 %collective-permute-done.9 = bf16[4,24,256]{2,1,0:T(8,128)(2,1)S(1)} collective-permute-done((bf16[4,24,256]{2,1,0:T(8,128)(2,1)S(1)}, bf16[4,24,256]{2,1,0:T(8,128)(2,1)S(1)}, u32[]{:S(2)}, u32[]{:S(2)}) %collective-permute-start.9) | collective-permute-done | bytes 49184 | tf_op jit(solution)/shard_map/ppermute | solution.py:60
  123.1 2.4 collective-permute-start.12
  125.9 3.4 %collective-permute-done.12 = bf16[16,4,256]{2,1,0:T(4,128)(2,1)S(1)} collective-permute-done((bf16[16,4,256]{2,1,0:T(4,128)(2,1)S(1)}, bf16[16,4,256]{2,1,0:T(4,128)(2,1)S(1)}, u32[]{:S(2)}, u32[]{:S(2)}) %collective-permute-start.12) | collective-permute-done | bytes 32800 | tf_op jit(solution)/shard_map/ppermute | solution.py:48
  132.6 5.1 %collective-permute-start.17 = (bf16[1024,128]{1,0:T(8,128)(2,1)}, bf16[1024,128]{1,0:T(8,128)(2,1)}, u32[]{:S(2)}, u32[]{:S(2)}) collective-permute-start(bf16[1024,128]{1,0:T(8,128)(2,1)} %get-tuple-element.25), channel_id=1, source_target_pairs={{0,32},{32,64},{64,96},{96,0},{1,33},{33,65},{65,97},{97,1},{2,34}... | collective-permute-start | bytes 786440 | tf_op jit(solution)/shard_map/ppermute | solution.py:78
  137.7 2.6 %collective-permute-start.16 = (bf16[1024,128]{1,0:T(8,128)(2,1)S(1)}, bf16[1024,128]{1,0:T(8,128)(2,1)}, u32[]{:S(2)}, u32[]{:S(2)}) collective-permute-start(bf16[1024,128]{1,0:T(8,128)(2,1)S(1)} %get-tuple-element.26), channel_id=1, source_target_pairs={{0,64},{32,96},{64,0},{96,32},{1,65},{33,97},{65,1},{97,33},{2,66}... | collective-permute-start | bytes 786440 | tf_op jit(solution)/shard_map/ppermute | solution.py:78
  141.6 6.8 %collective-permute-done.17 = bf16[1024,128]{1,0:T(8,128)(2,1)} collective-permute-done((bf16[1024,128]{1,0:T(8,128)(2,1)}, bf16[1024,128]{1,0:T(8,128)(2,1)}, u32[]{:S(2)}, u32[]{:S(2)}) %collective-permute-start.17) | collective-permute-done | bytes 262176 | tf_op jit(solution)/shard_map/ppermute | solution.py:78
  150.3 7.6 %all-to-all-start.4 = ((bf16[8,128,128]{2,1,0:T(8,128)(2,1)}), bf16[8,128,128]{2,1,0:T(8,128)(2,1)S(1)}, u32[]{:S(2)}, u32[]{:S(2)}) async-start(bf16[8,128,128]{2,1,0:T(8,128)(2,1)} %bitcast.68), calls=%async_computation.4 | async-start | bytes 524288 | tf_op jit(solution)/shard_map/all_to_all | solution.py:64
  159.9 8.5 %all-to-all-done.4 = bf16[8,128,128]{2,1,0:T(8,128)(2,1)S(1)} async-done(((bf16[8,128,128]{2,1,0:T(8,128)(2,1)}), bf16[8,128,128]{2,1,0:T(8,128)(2,1)S(1)}, u32[]{:S(2)}, u32[]{:S(2)}) %all-to-all-start.4) | async-done | bytes 262176 | tf_op jit(solution)/shard_map/all_to_all | solution.py:64
  168.4 3.6 %all-to-all-start.3 = ((bf16[8,128,512]{1,2,0:T(8,128)(2,1)}), bf16[8,128,512]{1,2,0:T(8,128)(2,1)S(1)}, u32[]{:S(2)}, u32[]{:S(2)}) async-start(bf16[8,128,512]{1,2,0:T(8,128)(2,1)} %copy_bitcast_fusion), calls=%async_computation.3 | async-start | bytes 2097152 | tf_op jit(solution)/shard_map/all_to_all | solution.py:64
  175.3 21.9 %all-to-all-done.3 = bf16[8,128,512]{1,2,0:T(8,128)(2,1)S(1)} async-done(((bf16[8,128,512]{1,2,0:T(8,128)(2,1)}), bf16[8,128,512]{1,2,0:T(8,128)(2,1)S(1)}, u32[]{:S(2)}, u32[]{:S(2)}) %all-to-all-start.3) | async-done | bytes 1048608 | tf_op jit(solution)/shard_map/all_to_all | solution.py:64
  198.0 9.7 %all-to-all-start.5 = ((bf16[12,4,32,128]{3,2,1,0:T(8,128)(2,1)}), bf16[12,4,32,128]{3,2,1,0:T(8,128)(2,1)S(1)}, u32[]{:S(2)}, u32[]{:S(2)}) async-start(bf16[12,4,32,128]{3,2,1,0:T(8,128)(2,1)} %bitcast.79), calls=%async_computation.5 | async-start | bytes 786432 | tf_op jit(solution)/shard_map/all_to_all | solution.py:64
  210.9 10.1 %all-to-all-done.5 = bf16[12,4,32,128]{3,2,1,0:T(8,128)(2,1)S(1)} async-done(((bf16[12,4,32,128]{3,2,1,0:T(8,128)(2,1)}), bf16[12,4,32,128]{3,2,1,0:T(8,128)(2,1)S(1)}, u32[]{:S(2)}, u32[]{:S(2)}) %all-to-all-start.5) | async-done | bytes 393248 | tf_op jit(solution)/shard_map/all_to_all | solution.py:64
  221.0 4.5 %collective-permute-start.21 = (bf16[8,32,128]{2,1,0:T(8,128)(2,1)S(1)}, bf16[8,32,128]{2,1,0:T(8,128)(2,1)S(1)}, u32[]{:S(2)}, u32[]{:S(2)}) collective-permute-start(bf16[8,32,128]{2,1,0:T(8,128)(2,1)S(1)} %bitcast_reduce_fusion), channel_id=1, source_target_pairs={{0,32},{32,64},{64,96},{96,0},{1,33},{33,65},{65,97},{97,1},{2,34}... | collective-permute-start | bytes 196616 | tf_op jit(solution)/shard_map/ppermute | solution.py:78
  225.5 4.4 %collective-permute-start.20 = (bf16[8,32,128]{2,1,0:T(8,128)(2,1)S(1)}, bf16[8,32,128]{2,1,0:T(8,128)(2,1)S(1)}, u32[]{:S(2)}, u32[]{:S(2)}) collective-permute-start(bf16[8,32,128]{2,1,0:T(8,128)(2,1)S(1)} %bitcast_reduce_fusion), channel_id=1, source_target_pairs={{0,64},{32,96},{64,0},{96,32},{1,65},{33,97},{65,1},{97,33},{2,66}... | collective-permute-start | bytes 196616 | tf_op jit(solution)/shard_map/ppermute | solution.py:78
  231.9 5.4 %collective-permute-done.19 = bf16[8,32,128]{2,1,0:T(8,128)(2,1)S(1)} collective-permute-done((bf16[8,32,128]{2,1,0:T(8,128)(2,1)S(1)}, bf16[8,32,128]{2,1,0:T(8,128)(2,1)S(1)}, u32[]{:S(2)}, u32[]{:S(2)}) %collective-permute-start.19) | collective-permute-done | bytes 65568 | tf_op jit(solution)/shard_map/ppermute | solution.py:78
  237.5 6.8 %collective-permute-start.14 = (bf16[2,2,4,32,128]{4,3,2,1,0:T(8,128)(2,1)S(1)}, bf16[2,2,4,32,128]{4,3,2,1,0:T(8,128)(2,1)S(1)}, u32[]{:S(2)}, u32[]{:S(2)}) collective-permute-start(bf16[2,2,4,32,128]{4,3,2,1,0:T(8,128)(2,1)S(1)} %fusion.28), channel_id=1, source_target_pairs={{0,16},{16,0},{1,17},{17,1},{2,18},{18,2},{3,19},{19,3},{4,20},{20... | collective-permute-start | bytes 393224 | tf_op jit(solution)/shard_map/ppermute | solution.py:82
  245.5 8.2 %collective-permute-done.14 = bf16[2,2,4,32,128]{4,3,2,1,0:T(8,128)(2,1)S(1)} collective-permute-done((bf16[2,2,4,32,128]{4,3,2,1,0:T(8,128)(2,1)S(1)}, bf16[2,2,4,32,128]{4,3,2,1,0:T(8,128)(2,1)S(1)}, u32[]{:S(2)}, u32[]{:S(2)}) %collective-permute-start.14) | collective-permute-done | bytes 131104 | tf_op jit(solution)/shard_map/ppermute | solution.py:82
  (133 shorter events, 46.1 us)
Async XLA Ops:
  0.6 2.3 copy-start.2
  3.3 22.0 %collective-permute-start = (bf16[20,32,128]{2,1,0:T(8,128)(2,1)S(1)}, bf16[20,32,128]{2,1,0:T(8,128)(2,1)S(1)}, u32[]{:S(2)}, u32[]{:S(2)}) collective-permute-start(bf16[20,32,128]{2,1,0:T(8,128)(2,1)S(1)} %pad_maximum_fusion.9), channel_id=1, source_target_pairs={{0,16},{16,0},{1,17},{17,1},{2,18},{18,2},{3,19},{19,3},{4,20},{20... | collective-permute-start | bytes 491528 | tf_op jit(solution)/shard_map/ppermute | solution.py:82
  25.5 3.3 %collective-permute-start.1 = (bf16[24,32,128]{2,1,0:T(8,128)(2,1)S(1)}, bf16[24,32,128]{2,1,0:T(8,128)(2,1)S(1)}, u32[]{:S(2)}, u32[]{:S(2)}) collective-permute-start(bf16[24,32,128]{2,1,0:T(8,128)(2,1)S(1)} %pad_maximum_fusion.8), channel_id=1, source_target_pairs={{0,1},{1,0},{2,3},{3,2},{4,5},{5,4},{6,7},{7,6},{8,9},{9,8},{10,11... | collective-permute-start | bytes 589832 | tf_op jit(solution)/shard_map/ppermute | solution.py:82
  29.6 19.3 %all-to-all-start = ((bf16[8,128,128]{2,1,0:T(8,128)(2,1)}), bf16[8,128,128]{2,1,0:T(8,128)(2,1)S(1)}, u32[]{:S(2)}, u32[]{:S(2)}) async-start(bf16[8,128,128]{2,1,0:T(8,128)(2,1)} %bitcast.20), calls=%async_computation | async-start | bytes 524288 | tf_op jit(solution)/shard_map/all_to_all | solution.py:64
  49.7 21.8 %all-to-all-start.1 = ((bf16[8,128,256]{2,1,0:T(8,128)(2,1)}), bf16[8,128,256]{2,1,0:T(8,128)(2,1)S(1)}, u32[]{:S(2)}, u32[]{:S(2)}) async-start(bf16[8,128,256]{2,1,0:T(8,128)(2,1)} %bitcast.32), calls=%async_computation.1 | async-start | bytes 1048576 | tf_op jit(solution)/shard_map/all_to_all | solution.py:64
  53.2 11.1 %collective-permute-start.4 = (bf16[1024,128]{1,0:T(8,128)(2,1)S(1)}, bf16[1024,128]{1,0:T(8,128)(2,1)S(1)}, u32[]{:S(2)}, u32[]{:S(2)}) collective-permute-start(bf16[1024,128]{1,0:T(8,128)(2,1)S(1)} %bitcast.203), channel_id=1, source_target_pairs={{0,32},{32,64},{64,96},{96,0},{1,33},{33,65},{65,97},{97,1},{2,34}... | collective-permute-start | bytes 786440 | tf_op jit(solution)/shard_map/ppermute | solution.py:78
  55.6 12.0 %collective-permute-start.3 = (bf16[1024,128]{1,0:T(8,128)(2,1)S(1)}, bf16[1024,128]{1,0:T(8,128)(2,1)S(1)}, u32[]{:S(2)}, u32[]{:S(2)}) collective-permute-start(bf16[1024,128]{1,0:T(8,128)(2,1)S(1)} %bitcast.204), channel_id=1, source_target_pairs={{0,64},{32,96},{64,0},{96,32},{1,65},{33,97},{65,1},{97,33},{2,66}... | collective-permute-start | bytes 786440 | tf_op jit(solution)/shard_map/ppermute | solution.py:78
  59.9 11.4 %collective-permute-start.2 = (bf16[1024,128]{1,0:T(8,128)(2,1)S(1)}, bf16[1024,128]{1,0:T(8,128)(2,1)S(1)}, u32[]{:S(2)}, u32[]{:S(2)}) collective-permute-start(bf16[1024,128]{1,0:T(8,128)(2,1)S(1)} %bitcast.205), channel_id=1, source_target_pairs={{0,96},{32,0},{64,32},{96,64},{1,97},{33,1},{65,33},{97,65},{2,98}... | collective-permute-start | bytes 786440 | tf_op jit(solution)/shard_map/ppermute | solution.py:78
  72.3 27.1 %all-to-all-start.2 = ((bf16[8,128,256]{2,1,0:T(8,128)(2,1)}), bf16[8,128,256]{2,1,0:T(8,128)(2,1)S(1)}, u32[]{:S(2)}, u32[]{:S(2)}) async-start(bf16[8,128,256]{2,1,0:T(8,128)(2,1)} %bitcast.41), calls=%async_computation.2 | async-start | bytes 1048576 | tf_op jit(solution)/shard_map/all_to_all | solution.py:64
  79.8 9.3 %collective-permute-start.5 = (bf16[16,4,256]{2,1,0:T(4,128)(2,1)S(1)}, bf16[16,4,256]{2,1,0:T(4,128)(2,1)S(1)}, u32[]{:S(2)}, u32[]{:S(2)}) collective-permute-start(bf16[16,4,256]{2,1,0:T(4,128)(2,1)S(1)} %get-tuple-element.48), channel_id=1, source_target_pairs={{0,1},{1,2},{2,3},{3,32},{4,5},{5,6},{6,7},{7,36},{8,9},{9,10},{10... | collective-permute-start | bytes 98312 | tf_op jit(solution)/shard_map/ppermute | solution.py:48
  81.7 7.4 %collective-permute-start.6 = (bf16[16,4,256]{2,1,0:T(4,128)(2,1)S(1)}, bf16[16,4,256]{2,1,0:T(4,128)(2,1)S(1)}, u32[]{:S(2)}, u32[]{:S(2)}) collective-permute-start(bf16[16,4,256]{2,1,0:T(4,128)(2,1)S(1)} %get-tuple-element.49), channel_id=1, source_target_pairs={{1,0},{2,1},{3,2},{32,3},{5,4},{6,5},{7,6},{36,7},{9,8},{10,9},{11... | collective-permute-start | bytes 98312 | tf_op jit(solution)/shard_map/ppermute | solution.py:52
  89.2 10.6 %collective-permute-start.7 = (bf16[4,24,256]{2,1,0:T(8,128)(2,1)S(1)}, bf16[4,24,256]{2,1,0:T(8,128)(2,1)S(1)}, u32[]{:S(2)}, u32[]{:S(2)}) collective-permute-start(bf16[4,24,256]{2,1,0:T(8,128)(2,1)S(1)} %get-tuple-element.46), channel_id=1, source_target_pairs={{0,64},{32,96},{64,128},{96,160},{128,192},{160,224},{192,256},{22... | collective-permute-start | bytes 147464 | tf_op jit(solution)/shard_map/ppermute | solution.py:56
  97.5 9.6 %collective-permute-start.8 = (bf16[4,24,256]{2,1,0:T(8,128)(2,1)S(1)}, bf16[4,24,256]{2,1,0:T(8,128)(2,1)S(1)}, u32[]{:S(2)}, u32[]{:S(2)}) collective-permute-start(bf16[4,24,256]{2,1,0:T(8,128)(2,1)S(1)} %get-tuple-element.47), channel_id=1, source_target_pairs={{64,0},{96,32},{128,64},{160,96},{192,128},{224,160},{256,192},{28... | collective-permute-start | bytes 147464 | tf_op jit(solution)/shard_map/ppermute | solution.py:60
  108.9 16.7 %copy-start = (bf16[256,128]{0,1:T(8,128)(2,1)}, bf16[256,128]{0,1:T(8,128)(2,1)S(1)}, u32[]{:S(2)}) copy-start(bf16[256,128]{0,1:T(8,128)(2,1)S(1)} %convolution_convert_fusion.8) | copy-start | bytes 196612
  109.4 7.6 %collective-permute-start.10 = (bf16[4,24,256]{2,1,0:T(8,128)(2,1)S(1)}, bf16[4,24,256]{2,1,0:T(8,128)(2,1)S(1)}, u32[]{:S(2)}, u32[]{:S(2)}) collective-permute-start(bf16[4,24,256]{2,1,0:T(8,128)(2,1)S(1)} %bitcast.235), channel_id=1, source_target_pairs={{0,64},{32,96},{64,128},{96,160},{128,192},{160,224},{192,256},{22... | collective-permute-start | bytes 147464 | tf_op jit(solution)/shard_map/ppermute | solution.py:56
  111.4 9.7 %collective-permute-start.9 = (bf16[4,24,256]{2,1,0:T(8,128)(2,1)S(1)}, bf16[4,24,256]{2,1,0:T(8,128)(2,1)S(1)}, u32[]{:S(2)}, u32[]{:S(2)}) collective-permute-start(bf16[4,24,256]{2,1,0:T(8,128)(2,1)S(1)} %bitcast.234), channel_id=1, source_target_pairs={{64,0},{96,32},{128,64},{160,96},{192,128},{224,160},{256,192},{28... | collective-permute-start | bytes 147464 | tf_op jit(solution)/shard_map/ppermute | solution.py:60
  121.2 4.7 %collective-permute-start.11 = (bf16[16,4,256]{2,1,0:T(4,128)(2,1)S(1)}, bf16[16,4,256]{2,1,0:T(4,128)(2,1)S(1)}, u32[]{:S(2)}, u32[]{:S(2)}) collective-permute-start(bf16[16,4,256]{2,1,0:T(4,128)(2,1)S(1)} %get-tuple-element.44), channel_id=1, source_target_pairs={{1,0},{2,1},{3,2},{32,3},{5,4},{6,5},{7,6},{36,7},{9,8},{10,9},{11... | collective-permute-start | bytes 98312 | tf_op jit(solution)/shard_map/ppermute | solution.py:52
  123.1 6.1 %collective-permute-start.12 = (bf16[16,4,256]{2,1,0:T(4,128)(2,1)S(1)}, bf16[16,4,256]{2,1,0:T(4,128)(2,1)S(1)}, u32[]{:S(2)}, u32[]{:S(2)}) collective-permute-start(bf16[16,4,256]{2,1,0:T(4,128)(2,1)S(1)} %get-tuple-element.45), channel_id=1, source_target_pairs={{0,1},{1,2},{2,3},{3,32},{4,5},{5,6},{6,7},{7,36},{8,9},{9,10},{10... | collective-permute-start | bytes 98312 | tf_op jit(solution)/shard_map/ppermute | solution.py:48
  129.8 10.6 %copy-start.1 = (bf16[256,128]{0,1:T(8,128)(2,1)S(1)}, bf16[256,128]{0,1:T(8,128)(2,1)}, u32[]{:S(2)}) copy-start(bf16[256,128]{0,1:T(8,128)(2,1)} %copy-done) | copy-start | bytes 196612
  130.7 10.9 %collective-permute-start.15 = (bf16[1024,128]{1,0:T(8,128)(2,1)}, bf16[1024,128]{1,0:T(8,128)(2,1)}, u32[]{:S(2)}, u32[]{:S(2)}) collective-permute-start(bf16[1024,128]{1,0:T(8,128)(2,1)} %get-tuple-element.24), channel_id=1, source_target_pairs={{0,96},{32,0},{64,32},{96,64},{1,97},{33,1},{65,33},{97,65},{2,98}... | collective-permute-start | bytes 786440 | tf_op jit(solution)/shard_map/ppermute | solution.py:78
  132.6 15.8 %collective-permute-start.17 = (bf16[1024,128]{1,0:T(8,128)(2,1)}, bf16[1024,128]{1,0:T(8,128)(2,1)}, u32[]{:S(2)}, u32[]{:S(2)}) collective-permute-start(bf16[1024,128]{1,0:T(8,128)(2,1)} %get-tuple-element.25), channel_id=1, source_target_pairs={{0,32},{32,64},{64,96},{96,0},{1,33},{33,65},{65,97},{97,1},{2,34}... | collective-permute-start | bytes 786440 | tf_op jit(solution)/shard_map/ppermute | solution.py:78
  137.7 10.6 %collective-permute-start.16 = (bf16[1024,128]{1,0:T(8,128)(2,1)S(1)}, bf16[1024,128]{1,0:T(8,128)(2,1)}, u32[]{:S(2)}, u32[]{:S(2)}) collective-permute-start(bf16[1024,128]{1,0:T(8,128)(2,1)S(1)} %get-tuple-element.26), channel_id=1, source_target_pairs={{0,64},{32,96},{64,0},{96,32},{1,65},{33,97},{65,1},{97,33},{2,66}... | collective-permute-start | bytes 786440 | tf_op jit(solution)/shard_map/ppermute | solution.py:78
  150.3 18.1 %all-to-all-start.4 = ((bf16[8,128,128]{2,1,0:T(8,128)(2,1)}), bf16[8,128,128]{2,1,0:T(8,128)(2,1)S(1)}, u32[]{:S(2)}, u32[]{:S(2)}) async-start(bf16[8,128,128]{2,1,0:T(8,128)(2,1)} %bitcast.68), calls=%async_computation.4 | async-start | bytes 524288 | tf_op jit(solution)/shard_map/all_to_all | solution.py:64
  168.4 28.7 %all-to-all-start.3 = ((bf16[8,128,512]{1,2,0:T(8,128)(2,1)}), bf16[8,128,512]{1,2,0:T(8,128)(2,1)S(1)}, u32[]{:S(2)}, u32[]{:S(2)}) async-start(bf16[8,128,512]{1,2,0:T(8,128)(2,1)} %copy_bitcast_fusion), calls=%async_computation.3 | async-start | bytes 2097152 | tf_op jit(solution)/shard_map/all_to_all | solution.py:64
  172.0 3.1 %collective-permute-start.18 = (bf16[4,64,128]{2,1,0:T(8,128)(2,1)S(1)}, bf16[4,64,128]{2,1,0:T(8,128)(2,1)S(1)}, u32[]{:S(2)}, u32[]{:S(2)}) collective-permute-start(bf16[4,64,128]{2,1,0:T(8,128)(2,1)S(1)} %fusion.38), channel_id=1, source_target_pairs={{0,1},{1,0},{2,3},{3,2},{4,5},{5,4},{6,7},{7,6},{8,9},{9,8},{10,11... | collective-permute-start | bytes 196616 | tf_op jit(solution)/shard_map/ppermute | solution.py:82
  198.0 23.0 %all-to-all-start.5 = ((bf16[12,4,32,128]{3,2,1,0:T(8,128)(2,1)}), bf16[12,4,32,128]{3,2,1,0:T(8,128)(2,1)S(1)}, u32[]{:S(2)}, u32[]{:S(2)}) async-start(bf16[12,4,32,128]{3,2,1,0:T(8,128)(2,1)} %bitcast.79), calls=%async_computation.5 | async-start | bytes 786432 | tf_op jit(solution)/shard_map/all_to_all | solution.py:64
  208.9 28.5 %collective-permute-start.13 = (bf16[2,4,64,128]{3,2,1,0:T(8,128)(2,1)S(1)}, bf16[2,4,64,128]{3,2,1,0:T(8,128)(2,1)S(1)}, u32[]{:S(2)}, u32[]{:S(2)}) collective-permute-start(bf16[2,4,64,128]{3,2,1,0:T(8,128)(2,1)S(1)} %fusion.27), channel_id=1, source_target_pairs={{0,1},{1,0},{2,3},{3,2},{4,5},{5,4},{6,7},{7,6},{8,9},{9,8},{10,11... | collective-permute-start | bytes 393224 | tf_op jit(solution)/shard_map/ppermute | solution.py:82
  221.0 16.4 %collective-permute-start.21 = (bf16[8,32,128]{2,1,0:T(8,128)(2,1)S(1)}, bf16[8,32,128]{2,1,0:T(8,128)(2,1)S(1)}, u32[]{:S(2)}, u32[]{:S(2)}) collective-permute-start(bf16[8,32,128]{2,1,0:T(8,128)(2,1)S(1)} %bitcast_reduce_fusion), channel_id=1, source_target_pairs={{0,32},{32,64},{64,96},{96,0},{1,33},{33,65},{65,97},{97,1},{2,34}... | collective-permute-start | bytes 196616 | tf_op jit(solution)/shard_map/ppermute | solution.py:78
  225.5 11.8 %collective-permute-start.20 = (bf16[8,32,128]{2,1,0:T(8,128)(2,1)S(1)}, bf16[8,32,128]{2,1,0:T(8,128)(2,1)S(1)}, u32[]{:S(2)}, u32[]{:S(2)}) collective-permute-start(bf16[8,32,128]{2,1,0:T(8,128)(2,1)S(1)} %bitcast_reduce_fusion), channel_id=1, source_target_pairs={{0,64},{32,96},{64,0},{96,32},{1,65},{33,97},{65,1},{97,33},{2,66}... | collective-permute-start | bytes 196616 | tf_op jit(solution)/shard_map/ppermute | solution.py:78
  229.9 7.4 %collective-permute-start.19 = (bf16[8,32,128]{2,1,0:T(8,128)(2,1)S(1)}, bf16[8,32,128]{2,1,0:T(8,128)(2,1)S(1)}, u32[]{:S(2)}, u32[]{:S(2)}) collective-permute-start(bf16[8,32,128]{2,1,0:T(8,128)(2,1)S(1)} %bitcast_reduce_fusion), channel_id=1, source_target_pairs={{0,96},{32,0},{64,32},{96,64},{1,97},{33,1},{65,33},{97,65},{2,98}... | collective-permute-start | bytes 196616 | tf_op jit(solution)/shard_map/ppermute | solution.py:78
  237.5 16.1 %collective-permute-start.14 = (bf16[2,2,4,32,128]{4,3,2,1,0:T(8,128)(2,1)S(1)}, bf16[2,2,4,32,128]{4,3,2,1,0:T(8,128)(2,1)S(1)}, u32[]{:S(2)}, u32[]{:S(2)}) collective-permute-start(bf16[2,2,4,32,128]{4,3,2,1,0:T(8,128)(2,1)S(1)} %fusion.28), channel_id=1, source_target_pairs={{0,16},{16,0},{1,17},{17,1},{2,18},{18,2},{3,19},{19,3},{4,20},{20... | collective-permute-start | bytes 393224 | tf_op jit(solution)/shard_map/ppermute | solution.py:82

commit v5 on v4

--- a/solution.py
+++ b/solution.py
@@ -42,6 +42,7 @@
 LEFT = [(b, a) for a, b in RIGHT]
 DOWN = [(t, t + 2) for t in range(22)]
 UP = [(t + 2, t) for t in range(22)]
+SWAP_X2 = [(i, i ^ 2) for i in range(4)]
 
 
 def to_right(v):
@@ -84,10 +85,6 @@
 
 def pick(v, index, axis=0):
     return lax.dynamic_index_in_dim(v, index, axis, keepdims=False)
-
-
-def unroll(parts, me):
-    return lax.dynamic_slice_in_dim(jnp.stack(parts + parts), (4 - me) % 4, 4, 0)
 
 
 def in_order(mine, other, bit):
@@ -141,8 +138,8 @@
         return a2a(send, "y").reshape(D, -1)
 
     w_x = gather(w_mine[:, None], (4, 2))
-    tokens = gather(t_mine[None, :, :, :2].reshape(1, 2, 128, TILE_TOKENS), (4, 2))
-    grads = gather(t_mine[None, :, :, 2:].reshape(1, 2, 128, TILE_TOKENS), (4, 2))
+    both = gather(t_mine[None].reshape(1, 2, 128, 2 * TILE_TOKENS), (4, 2))
+    tokens, grads = both[:, :TILE_TOKENS], both[:, TILE_TOKENS:]
     w_list = jnp.stack([w_x] + [shift(w_x, "x", 4, 1, s) for s in (1, 2, 3)])
     w_qkv = jnp.concatenate([pick(w_list, (m - x) % 4) for m in range(3)], 1)
     w_out = pick(w_list, (3 - x) % 4)
@@ -219,27 +216,27 @@
     send = jnp.concatenate([part, d_tokens], 1).reshape(8, 128, 512)
     got = a2a(send, "y").reshape(4, 2, 128, 512)
     back = jnp.sum(got.astype(f32), 0)
-    back = back.reshape(2, 2, 64, 4, 128).transpose(1, 0, 3, 2, 4)
-    back_c = swap(back[1].astype(bf16), "c")
-    got = a2a(total.astype(bf16).reshape(8, 128, 128), "y")
-    dw = jnp.sum(got.reshape(4, 2, 128, 128).astype(f32), 1)
-    dw = dw.reshape(4, 2, 64, 128)
-    got = swap(dw[:, 1].astype(bf16), "c")
-    dw = (dw[:, 0] + got.astype(f32)).astype(bf16).reshape(4, 2, WIDTH, 128)
-    dw = jnp.stack(in_order(dw[:, 0], dw[:, 1], zh))
-    dw = jnp.broadcast_to(dw, (6, 2, 4, WIDTH, 128)).reshape(12, 4, WIDTH, 128)
-    dw = a2a(dw, ("zl", "zh"))
-    total = jnp.sum(dw.reshape(6, HEADS, WIDTH, 128).astype(f32), 0).astype(bf16)
-
-    back = jnp.stack([back[0], back_c.astype(f32)])
-    back = back.reshape(2, 2, 4, 2, WIDTH, 128)
-    far = swap(back[:, :, :, 1].astype(bf16), "zh")
-    back = back[:, :, :, 0] + far.astype(f32)
-    back = jnp.stack(in_order(back[0], back[1], c))
+    back = back.reshape(2, 2, 2, WIDTH, 4, 128).transpose(2, 1, 0, 4, 3, 5)
+    far = swap(back[1].astype(bf16), "zh")
+    back = back[0] + far.astype(f32)
+    other = swap(back[1], "c")
+    back = jnp.stack(in_order(back[0], other, c))
     attention = join_tiles(back[:, :, :2].astype(bf16))
     token_grads = join_tiles(back[:, :, 2:])
 
-    total = unroll([total] + [shift(total, "x", 4, 1, s) for s in (1, 2, 3)], x)
+    total = total.reshape(8, 2, 64, 128)
+    got = swap(total[:, 1].astype(bf16), "c")
+    total = (total[:, 0] + got.astype(f32)).astype(bf16).reshape(8, 2, WIDTH, 128)
+    got = swap(total[:, 1], "zh")
+    total = jnp.stack(in_order(total[:, 0], got, zh), 1)
+    total = a2a(total, "y")
+    total = jnp.sum(total.reshape(4, 2, 2, WIDTH, 128).astype(f32), 1).astype(bf16)
+    total = total.transpose(1, 0, 2, 3).reshape(1, HEADS, WIDTH, 128)
+    total = jnp.broadcast_to(total, (6, HEADS, WIDTH, 128))
+    total = a2a(total, "zl")
+    total = jnp.sum(total.astype(f32), 0).astype(bf16)
+    total = jnp.stack(in_order(total, swap(total, "x"), x % 2))
+    total = jnp.concatenate(in_order(total, lax.ppermute(total, "x", SWAP_X2), x // 2))
     weight_grads = total.transpose(2, 0, 1, 3).astype(f32)
     return attention, token_grads, weight_grads
 

time: 257 us -> 259 us (level)
  the two profiles are of different devices: /device:TPU:198 before, /device:TPU:1 now
where the time goes in v5:
time: 259 us; the launch traced here: 258 us
  starting transfers between devices  118 us (46%)
  waiting for transfers between devices  111 us (43%)
  blocking collectives  10.3 us (4%)
  local copies, waits for them, and re-layouts  9.83 us (4%)
  matrix products  4.04 us (2%)
  other arithmetic  3.06 us (1%)
    all_to_all x4, waiting for transfers between devices, a2a(): return lax.all_to_all(v, axes, 0, 0, tiled=True)  63.8 us
    ppermute x7, starting transfers between devices, swap(): lax.ppermute(v, axis, [(i, i ^ 1) for i in range(lax.axis_size(axis))])  54.7 us
    ppermute x6, starting transfers between devices, shift(): return lax.ppermute(v, axis, pairs)  20.8 us
    all_to_all x4, starting transfers between devices, a2a(): return lax.all_to_all(v, axes, 0, 0, tiled=True)  16.8 us
    ppermute x6, waiting for transfers between devices, shift(): return lax.ppermute(v, axis, pairs)  15.6 us
    ppermute x2, waiting for transfers between devices, to_up(): return lax.ppermute(v, ('zl', 'x'), UP)  14.5 us
    ppermute x7, waiting for transfers between devices, swap(): lax.ppermute(v, axis, [(i, i ^ 1) for i in range(lax.axis_size(axis))])  13.1 us
    ppermute x2, starting transfers between devices, to_down(): return lax.ppermute(v, ('zl', 'x'), DOWN)  10.4 us
  transfers between devices with their start and end apart: 26, of which 17 were waited for; matrix products, arithmetic and copies ran while one was open for 2% of the time, Pallas kernels for 0%

profile of v5, /device:TPU:1, one launch (start us, length us, event | category | flops | bytes accessed | tf_op | source)
XLA Modules:
  0.0 257.8 jit_solution(18141280560685855209)
XLA Ops:
  3.3 15.7 %collective-permute-start = (bf16[20,32,128]{2,1,0:T(8,128)(2,1)S(1)}, bf16[20,32,128]{2,1,0:T(8,128)(2,1)S(1)}, u32[]{:S(2)}, u32[]{:S(2)}) collective-permute-start(bf16[20,32,128]{2,1,0:T(8,128)(2,1)S(1)} %pad_maximum_fusion.8), channel_id=1, source_target_pairs={{0,16},{16,0},{1,17},{17,1},{2,18},{18,2},{3,19},{19,3},{4,20},{20... | collective-permute-start | bytes 491528 | tf_op jit(solution)/shard_map/ppermute | solution.py:83
  19.0 5.7 %collective-permute-done = bf16[20,32,128]{2,1,0:T(8,128)(2,1)S(1)} collective-permute-done((bf16[20,32,128]{2,1,0:T(8,128)(2,1)S(1)}, bf16[20,32,128]{2,1,0:T(8,128)(2,1)S(1)}, u32[]{:S(2)}, u32[]{:S(2)}) %collective-permute-start) | collective-permute-done | bytes 163872 | tf_op jit(solution)/shard_map/ppermute | solution.py:83
  24.9 4.5 %collective-permute-start.1 = (bf16[24,32,128]{2,1,0:T(8,128)(2,1)S(1)}, bf16[24,32,128]{2,1,0:T(8,128)(2,1)S(1)}, u32[]{:S(2)}, u32[]{:S(2)}) collective-permute-start(bf16[24,32,128]{2,1,0:T(8,128)(2,1)S(1)} %pad_maximum_fusion.7), channel_id=1, source_target_pairs={{0,1},{1,0},{2,3},{3,2},{4,5},{5,4},{6,7},{7,6},{8,9},{9,8},{10,11... | collective-permute-start | bytes 589832 | tf_op jit(solution)/shard_map/ppermute | solution.py:83
  31.3 3.8 %all-to-all-start = ((bf16[8,128,128]{2,1,0:T(8,128)(2,1)}), bf16[8,128,128]{2,1,0:T(8,128)(2,1)S(1)}, u32[]{:S(2)}, u32[]{:S(2)}) async-start(bf16[8,128,128]{2,1,0:T(8,128)(2,1)} %bitcast.20), calls=%async_computation | async-start | bytes 524288 | tf_op jit(solution)/shard_map/all_to_all | solution.py:65
  35.5 10.7 %all-to-all-done = bf16[8,128,128]{2,1,0:T(8,128)(2,1)S(1)} async-done(((bf16[8,128,128]{2,1,0:T(8,128)(2,1)}), bf16[8,128,128]{2,1,0:T(8,128)(2,1)S(1)}, u32[]{:S(2)}, u32[]{:S(2)}) %all-to-all-start) | async-done | bytes 262176 | tf_op jit(solution)/shard_map/all_to_all | solution.py:65
  47.3 3.6 %all-to-all-start.1 = ((bf16[8,128,512]{2,1,0:T(8,128)(2,1)}), bf16[8,128,512]{2,1,0:T(8,128)(2,1)S(1)}, u32[]{:S(2)}, u32[]{:S(2)}) async-start(bf16[8,128,512]{2,1,0:T(8,128)(2,1)} %bitcast.32), calls=%async_computation.1 | async-start | bytes 2097152 | tf_op jit(solution)/shard_map/all_to_all | solution.py:65
  50.8 3.1 %collective-permute-start.4 = (bf16[1024,128]{1,0:T(8,128)(2,1)S(1)}, bf16[1024,128]{1,0:T(8,128)(2,1)S(1)}, u32[]{:S(2)}, u32[]{:S(2)}) collective-permute-start(bf16[1024,128]{1,0:T(8,128)(2,1)S(1)} %bitcast.186), channel_id=1, source_target_pairs={{0,32},{32,64},{64,96},{96,0},{1,33},{33,65},{65,97},{97,1},{2,34}... | collective-permute-start | bytes 786440 | tf_op jit(solution)/shard_map/ppermute | solution.py:79
  53.9 4.4 %collective-permute-start.3 = (bf16[1024,128]{1,0:T(8,128)(2,1)S(1)}, bf16[1024,128]{1,0:T(8,128)(2,1)S(1)}, u32[]{:S(2)}, u32[]{:S(2)}) collective-permute-start(bf16[1024,128]{1,0:T(8,128)(2,1)S(1)} %bitcast.187), channel_id=1, source_target_pairs={{0,64},{32,96},{64,0},{96,32},{1,65},{33,97},{65,1},{97,33},{2,66}... | collective-permute-start | bytes 786440 | tf_op jit(solution)/shard_map/ppermute | solution.py:79
  58.3 3.1 %collective-permute-start.2 = (bf16[1024,128]{1,0:T(8,128)(2,1)S(1)}, bf16[1024,128]{1,0:T(8,128)(2,1)S(1)}, u32[]{:S(2)}, u32[]{:S(2)}) collective-permute-start(bf16[1024,128]{1,0:T(8,128)(2,1)S(1)} %bitcast.188), channel_id=1, source_target_pairs={{0,96},{32,0},{64,32},{96,64},{1,97},{33,1},{65,33},{97,65},{2,98}... | collective-permute-start | bytes 786440 | tf_op jit(solution)/shard_map/ppermute | solution.py:79
  61.5 5.2 %collective-permute-done.3 = bf16[1024,128]{1,0:T(8,128)(2,1)S(1)} collective-permute-done((bf16[1024,128]{1,0:T(8,128)(2,1)S(1)}, bf16[1024,128]{1,0:T(8,128)(2,1)S(1)}, u32[]{:S(2)}, u32[]{:S(2)}) %collective-permute-start.3) | collective-permute-done | bytes 262176 | tf_op jit(solution)/shard_map/ppermute | solution.py:79
  68.7 11.2 %all-to-all-done.1 = bf16[8,128,512]{2,1,0:T(8,128)(2,1)S(1)} async-done(((bf16[8,128,512]{2,1,0:T(8,128)(2,1)}), bf16[8,128,512]{2,1,0:T(8,128)(2,1)S(1)}, u32[]{:S(2)}, u32[]{:S(2)}) %all-to-all-start.1) | async-done | bytes 1048608 | tf_op jit(solution)/shard_map/all_to_all | solution.py:65
  80.5 2.6 %collective-permute-start.5 = (bf16[16,4,256]{2,1,0:T(4,128)(2,1)S(1)}, bf16[16,4,256]{2,1,0:T(4,128)(2,1)S(1)}, u32[]{:S(2)}, u32[]{:S(2)}) collective-permute-start(bf16[16,4,256]{2,1,0:T(4,128)(2,1)S(1)} %get-tuple-element.55), channel_id=1, source_target_pairs={{0,1},{1,2},{2,3},{3,32},{4,5},{5,6},{6,7},{7,36},{8,9},{9,10},{10... | collective-permute-start | bytes 98312 | tf_op jit(solution)/shard_map/ppermute | solution.py:49
  85.2 3.1 %collective-permute-done.6 = bf16[16,4,256]{2,1,0:T(4,128)(2,1)S(1)} collective-permute-done((bf16[16,4,256]{2,1,0:T(4,128)(2,1)S(1)}, bf16[16,4,256]{2,1,0:T(4,128)(2,1)S(1)}, u32[]{:S(2)}, u32[]{:S(2)}) %collective-permute-start.6) | collective-permute-done | bytes 32800 | tf_op jit(solution)/shard_map/ppermute | solution.py:53
  88.3 4.6 %collective-permute-start.7 = (bf16[4,24,256]{2,1,0:T(8,128)(2,1)S(1)}, bf16[4,24,256]{2,1,0:T(8,128)(2,1)S(1)}, u32[]{:S(2)}, u32[]{:S(2)}) collective-permute-start(bf16[4,24,256]{2,1,0:T(8,128)(2,1)S(1)} %get-tuple-element.51), channel_id=1, source_target_pairs={{0,64},{32,96},{64,128},{96,160},{128,192},{160,224},{192,256},{22... | collective-permute-start | bytes 147464 | tf_op jit(solution)/shard_map/ppermute | solution.py:57
  94.6 8.8 %collective-permute-done.8 = bf16[4,24,256]{2,1,0:T(8,128)(2,1)S(1)} collective-permute-done((bf16[4,24,256]{2,1,0:T(8,128)(2,1)S(1)}, bf16[4,24,256]{2,1,0:T(8,128)(2,1)S(1)}, u32[]{:S(2)}, u32[]{:S(2)}) %collective-permute-start.8) | collective-permute-done | bytes 49184 | tf_op jit(solution)/shard_map/ppermute | solution.py:61
  105.7 5.8 %collective-permute-start.10 = (bf16[4,24,256]{2,1,0:T(8,128)(2,1)S(1)}, bf16[4,24,256]{2,1,0:T(8,128)(2,1)S(1)}, u32[]{:S(2)}, u32[]{:S(2)}) collective-permute-start(bf16[4,24,256]{2,1,0:T(8,128)(2,1)S(1)} %bitcast.215), channel_id=1, source_target_pairs={{0,64},{32,96},{64,128},{96,160},{128,192},{160,224},{192,256},{22... | collective-permute-start | bytes 147464 | tf_op jit(solution)/shard_map/ppermute | solution.py:57
  112.9 5.8 %collective-permute-done.9 = bf16[4,24,256]{2,1,0:T(8,128)(2,1)S(1)} collective-permute-done((bf16[4,24,256]{2,1,0:T(8,128)(2,1)S(1)}, bf16[4,24,256]{2,1,0:T(8,128)(2,1)S(1)}, u32[]{:S(2)}, u32[]{:S(2)}) %collective-permute-start.9) | collective-permute-done | bytes 49184 | tf_op jit(solution)/shard_map/ppermute | solution.py:61
  121.1 3.6 %collective-permute-start.12 = (bf16[16,4,256]{2,1,0:T(4,128)(2,1)S(1)}, bf16[16,4,256]{2,1,0:T(4,128)(2,1)S(1)}, u32[]{:S(2)}, u32[]{:S(2)}) collective-permute-start(bf16[16,4,256]{2,1,0:T(4,128)(2,1)S(1)} %get-tuple-element.50), channel_id=1, source_target_pairs={{0,1},{1,2},{2,3},{3,32},{4,5},{5,6},{6,7},{7,36},{8,9},{9,10},{10... | collective-permute-start | bytes 98312 | tf_op jit(solution)/shard_map/ppermute | solution.py:49
  126.3 5.3 %collective-permute-start.15 = (bf16[1024,128]{1,0:T(8,128)(2,1)S(1)}, bf16[1024,128]{1,0:T(8,128)(2,1)S(1)}, u32[]{:S(2)}, u32[]{:S(2)}) collective-permute-start(bf16[1024,128]{1,0:T(8,128)(2,1)S(1)} %get-tuple-element.27), channel_id=1, source_target_pairs={{0,96},{32,0},{64,32},{96,64},{1,97},{33,1},{65,33},{97,65},{2,98}... | collective-permute-start | bytes 786440 | tf_op jit(solution)/shard_map/ppermute | solution.py:79
  133.5 3.1 %collective-permute-start.16 = (bf16[1024,128]{1,0:T(8,128)(2,1)S(1)}, bf16[1024,128]{1,0:T(8,128)(2,1)S(1)}, u32[]{:S(2)}, u32[]{:S(2)}) collective-permute-start(bf16[1024,128]{1,0:T(8,128)(2,1)S(1)} %get-tuple-element.29), channel_id=1, source_target_pairs={{0,64},{32,96},{64,0},{96,32},{1,65},{33,97},{65,1},{97,33},{2,66}... | collective-permute-start | bytes 786440 | tf_op jit(solution)/shard_map/ppermute | solution.py:79
  136.6 3.9 %collective-permute-done.17 = bf16[1024,128]{1,0:T(8,128)(2,1)S(1)} collective-permute-done((bf16[1024,128]{1,0:T(8,128)(2,1)S(1)}, bf16[1024,128]{1,0:T(8,128)(2,1)S(1)}, u32[]{:S(2)}, u32[]{:S(2)}) %collective-permute-start.17) | collective-permute-done | bytes 262176 | tf_op jit(solution)/shard_map/ppermute | solution.py:79
  140.5 4.7 %collective-permute-done.16 = bf16[1024,128]{1,0:T(8,128)(2,1)S(1)} collective-permute-done((bf16[1024,128]{1,0:T(8,128)(2,1)S(1)}, bf16[1024,128]{1,0:T(8,128)(2,1)S(1)}, u32[]{:S(2)}, u32[]{:S(2)}) %collective-permute-start.16) | collective-permute-done | bytes 262176 | tf_op jit(solution)/shard_map/ppermute | solution.py:79
  145.4 5.9 %collective-permute-start.18 = (bf16[8,64,128]{2,1,0:T(8,128)(2,1)S(1)}, bf16[8,64,128]{2,1,0:T(8,128)(2,1)S(1)}, u32[]{:S(2)}, u32[]{:S(2)}) collective-permute-start(bf16[8,64,128]{2,1,0:T(8,128)(2,1)S(1)} %fusion.31), channel_id=1, source_target_pairs={{0,1},{1,0},{2,3},{3,2},{4,5},{5,4},{6,7},{7,6},{8,9},{9,8},{10,11... | collective-permute-start | bytes 393224 | tf_op jit(solution)/shard_map/ppermute | solution.py:83
  152.3 11.2 %collective-permute-start.19 = (bf16[8,32,128]{2,1,0:T(8,128)(2,1)S(1)}, bf16[8,32,128]{2,1,0:T(8,128)(2,1)S(1)}, u32[]{:S(2)}, u32[]{:S(2)}) collective-permute-start(bf16[8,32,128]{2,1,0:T(8,128)(2,1)S(1)} %slice_bitcast_fusion.5), channel_id=1, source_target_pairs={{0,16},{16,0},{1,17},{17,1},{2,18},{18,2},{3,19},{19,3},{4,20},{20... | collective-permute-start | bytes 196616 | tf_op jit(solution)/shard_map/ppermute | solution.py:83
  165.7 10.3 %all_to_all.25 = bf16[8,2,32,128]{3,2,1,0:T(8,128)(2,1)S(1)} all-to-all(bf16[8,2,32,128]{3,2,1,0:T(8,128)(2,1)S(1)} %copy.253), channel_id=1, replica_groups=mesh['zl'=6,'x'=4,'zh'=2,'y'=8,'c'=2] {'y'}, dimensions={0} | all-to-all | bytes 262144 | tf_op jit(solution)/shard_map/all_to_all | solution.py:65
  176.9 5.9 %all-to-all-start.4 = ((bf16[6,8,32,128]{3,2,1,0:T(8,128)(2,1)}), bf16[6,8,32,128]{3,2,1,0:T(8,128)(2,1)S(1)}, u32[]{:S(2)}, u32[]{:S(2)}) async-start(bf16[6,8,32,128]{3,2,1,0:T(8,128)(2,1)} %broadcast_in_dim.45), calls=%async_computation.4 | async-start | bytes 786432 | tf_op jit(solution)/shard_map/all_to_all | solution.py:65
  184.8 14.8 %all-to-all-done.4 = bf16[6,8,32,128]{3,2,1,0:T(8,128)(2,1)S(1)} async-done(((bf16[6,8,32,128]{3,2,1,0:T(8,128)(2,1)}), bf16[6,8,32,128]{3,2,1,0:T(8,128)(2,1)S(1)}, u32[]{:S(2)}, u32[]{:S(2)}) %all-to-all-start.4) | async-done | bytes 393248 | tf_op jit(solution)/shard_map/all_to_all | solution.py:65
  199.6 3.6 %all-to-all-start.2 = ((bf16[8,128,512]{1,2,0:T(8,128)(2,1)}), bf16[8,128,512]{1,2,0:T(8,128)(2,1)S(1)}, u32[]{:S(2)}, u32[]{:S(2)}) async-start(bf16[8,128,512]{1,2,0:T(8,128)(2,1)} %copy_bitcast_fusion), calls=%async_computation.2 | async-start | bytes 2097152 | tf_op jit(solution)/shard_map/all_to_all | solution.py:65
  205.2 27.1 %all-to-all-done.2 = bf16[8,128,512]{1,2,0:T(8,128)(2,1)S(1)} async-done(((bf16[8,128,512]{1,2,0:T(8,128)(2,1)}), bf16[8,128,512]{1,2,0:T(8,128)(2,1)S(1)}, u32[]{:S(2)}, u32[]{:S(2)}) %all-to-all-start.2) | async-done | bytes 1048608 | tf_op jit(solution)/shard_map/all_to_all | solution.py:65
  232.9 8.6 %collective-permute-start.13 = (bf16[2,2,4,32,128]{4,2,3,0,1:T(4,128)(2,1)S(1)}, bf16[2,2,4,32,128]{4,2,3,0,1:T(4,128)(2,1)S(1)}, u32[]{:S(2)}, u32[]{:S(2)}) collective-permute-start(bf16[2,2,4,32,128]{4,2,3,0,1:T(4,128)(2,1)S(1)} %fusion.30), channel_id=1, source_target_pairs={{0,16},{16,0},{1,17},{17,1},{2,18},{18,2},{3,19},{19,3},{4,20},{20... | collective-permute-start | bytes 393224 | tf_op jit(solution)/shard_map/ppermute | solution.py:83
  243.9 3.3 %collective-permute-done.13 = bf16[2,2,4,32,128]{4,2,3,0,1:T(4,128)(2,1)S(1)} collective-permute-done((bf16[2,2,4,32,128]{4,2,3,0,1:T(4,128)(2,1)S(1)}, bf16[2,2,4,32,128]{4,2,3,0,1:T(4,128)(2,1)S(1)}, u32[]{:S(2)}, u32[]{:S(2)}) %collective-permute-start.13) | collective-permute-done | bytes 131104 | tf_op jit(solution)/shard_map/ppermute | solution.py:83
  247.2 6.9 %collective-permute-start.14 = (f32[2,4,32,128]{3,1,2,0:T(4,128)S(1)}, f32[2,4,32,128]{3,1,2,0:T(4,128)S(1)}, u32[]{:S(2)}, u32[]{:S(2)}) collective-permute-start(f32[2,4,32,128]{3,1,2,0:T(4,128)S(1)} %slice_bitcast_fusion.3), channel_id=1, source_target_pairs={{0,1},{1,0},{2,3},{3,2},{4,5},{5,4},{6,7},{7,6},{8,9},{9,8},{10,11... | collective-permute-start | bytes 393224 | tf_op jit(solution)/shard_map/ppermute | solution.py:83
  (117 shorter events, 36.6 us)
Async XLA Ops:
  0.6 2.3 copy-start
  3.3 21.4 %collective-permute-start = (bf16[20,32,128]{2,1,0:T(8,128)(2,1)S(1)}, bf16[20,32,128]{2,1,0:T(8,128)(2,1)S(1)}, u32[]{:S(2)}, u32[]{:S(2)}) collective-permute-start(bf16[20,32,128]{2,1,0:T(8,128)(2,1)S(1)} %pad_maximum_fusion.8), channel_id=1, source_target_pairs={{0,16},{16,0},{1,17},{17,1},{2,18},{18,2},{3,19},{19,3},{4,20},{20... | collective-permute-start | bytes 491528 | tf_op jit(solution)/shard_map/ppermute | solution.py:83
  24.9 5.6 %collective-permute-start.1 = (bf16[24,32,128]{2,1,0:T(8,128)(2,1)S(1)}, bf16[24,32,128]{2,1,0:T(8,128)(2,1)S(1)}, u32[]{:S(2)}, u32[]{:S(2)}) collective-permute-start(bf16[24,32,128]{2,1,0:T(8,128)(2,1)S(1)} %pad_maximum_fusion.7), channel_id=1, source_target_pairs={{0,1},{1,0},{2,3},{3,2},{4,5},{5,4},{6,7},{7,6},{8,9},{9,8},{10,11... | collective-permute-start | bytes 589832 | tf_op jit(solution)/shard_map/ppermute | solution.py:83
  31.3 14.9 %all-to-all-start = ((bf16[8,128,128]{2,1,0:T(8,128)(2,1)}), bf16[8,128,128]{2,1,0:T(8,128)(2,1)S(1)}, u32[]{:S(2)}, u32[]{:S(2)}) async-start(bf16[8,128,128]{2,1,0:T(8,128)(2,1)} %bitcast.20), calls=%async_computation | async-start | bytes 524288 | tf_op jit(solution)/shard_map/all_to_all | solution.py:65
  47.3 32.7 %all-to-all-start.1 = ((bf16[8,128,512]{2,1,0:T(8,128)(2,1)}), bf16[8,128,512]{2,1,0:T(8,128)(2,1)S(1)}, u32[]{:S(2)}, u32[]{:S(2)}) async-start(bf16[8,128,512]{2,1,0:T(8,128)(2,1)} %bitcast.32), calls=%async_computation.1 | async-start | bytes 2097152 | tf_op jit(solution)/shard_map/all_to_all | solution.py:65
  50.8 10.7 %collective-permute-start.4 = (bf16[1024,128]{1,0:T(8,128)(2,1)S(1)}, bf16[1024,128]{1,0:T(8,128)(2,1)S(1)}, u32[]{:S(2)}, u32[]{:S(2)}) collective-permute-start(bf16[1024,128]{1,0:T(8,128)(2,1)S(1)} %bitcast.186), channel_id=1, source_target_pairs={{0,32},{32,64},{64,96},{96,0},{1,33},{33,65},{65,97},{97,1},{2,34}... | collective-permute-start | bytes 786440 | tf_op jit(solution)/shard_map/ppermute | solution.py:79
  53.9 12.7 %collective-permute-start.3 = (bf16[1024,128]{1,0:T(8,128)(2,1)S(1)}, bf16[1024,128]{1,0:T(8,128)(2,1)S(1)}, u32[]{:S(2)}, u32[]{:S(2)}) collective-permute-start(bf16[1024,128]{1,0:T(8,128)(2,1)S(1)} %bitcast.187), channel_id=1, source_target_pairs={{0,64},{32,96},{64,0},{96,32},{1,65},{33,97},{65,1},{97,33},{2,66}... | collective-permute-start | bytes 786440 | tf_op jit(solution)/shard_map/ppermute | solution.py:79
  58.3 10.2 %collective-permute-start.2 = (bf16[1024,128]{1,0:T(8,128)(2,1)S(1)}, bf16[1024,128]{1,0:T(8,128)(2,1)S(1)}, u32[]{:S(2)}, u32[]{:S(2)}) collective-permute-start(bf16[1024,128]{1,0:T(8,128)(2,1)S(1)} %bitcast.188), channel_id=1, source_target_pairs={{0,96},{32,0},{64,32},{96,64},{1,97},{33,1},{65,33},{97,65},{2,98}... | collective-permute-start | bytes 786440 | tf_op jit(solution)/shard_map/ppermute | solution.py:79
  80.5 4.7 %collective-permute-start.5 = (bf16[16,4,256]{2,1,0:T(4,128)(2,1)S(1)}, bf16[16,4,256]{2,1,0:T(4,128)(2,1)S(1)}, u32[]{:S(2)}, u32[]{:S(2)}) collective-permute-start(bf16[16,4,256]{2,1,0:T(4,128)(2,1)S(1)} %get-tuple-element.55), channel_id=1, source_target_pairs={{0,1},{1,2},{2,3},{3,32},{4,5},{5,6},{6,7},{7,36},{8,9},{9,10},{10... | collective-permute-start | bytes 98312 | tf_op jit(solution)/shard_map/ppermute | solution.py:49
  83.1 5.2 %collective-permute-start.6 = (bf16[16,4,256]{2,1,0:T(4,128)(2,1)S(1)}, bf16[16,4,256]{2,1,0:T(4,128)(2,1)S(1)}, u32[]{:S(2)}, u32[]{:S(2)}) collective-permute-start(bf16[16,4,256]{2,1,0:T(4,128)(2,1)S(1)} %get-tuple-element.56), channel_id=1, source_target_pairs={{1,0},{2,1},{3,2},{32,3},{5,4},{6,5},{7,6},{36,7},{9,8},{10,9},{11... | collective-permute-start | bytes 98312 | tf_op jit(solution)/shard_map/ppermute | solution.py:53
  88.3 6.3 %collective-permute-start.7 = (bf16[4,24,256]{2,1,0:T(8,128)(2,1)S(1)}, bf16[4,24,256]{2,1,0:T(8,128)(2,1)S(1)}, u32[]{:S(2)}, u32[]{:S(2)}) collective-permute-start(bf16[4,24,256]{2,1,0:T(8,128)(2,1)S(1)} %get-tuple-element.51), channel_id=1, source_target_pairs={{0,64},{32,96},{64,128},{96,160},{128,192},{160,224},{192,256},{22... | collective-permute-start | bytes 147464 | tf_op jit(solution)/shard_map/ppermute | solution.py:57
  93.0 10.4 %collective-permute-start.8 = (bf16[4,24,256]{2,1,0:T(8,128)(2,1)S(1)}, bf16[4,24,256]{2,1,0:T(8,128)(2,1)S(1)}, u32[]{:S(2)}, u32[]{:S(2)}) collective-permute-start(bf16[4,24,256]{2,1,0:T(8,128)(2,1)S(1)} %get-tuple-element.52), channel_id=1, source_target_pairs={{64,0},{96,32},{128,64},{160,96},{192,128},{224,160},{256,192},{28... | collective-permute-start | bytes 147464 | tf_op jit(solution)/shard_map/ppermute | solution.py:61
  105.7 7.1 %collective-permute-start.10 = (bf16[4,24,256]{2,1,0:T(8,128)(2,1)S(1)}, bf16[4,24,256]{2,1,0:T(8,128)(2,1)S(1)}, u32[]{:S(2)}, u32[]{:S(2)}) collective-permute-start(bf16[4,24,256]{2,1,0:T(8,128)(2,1)S(1)} %bitcast.215), channel_id=1, source_target_pairs={{0,64},{32,96},{64,128},{96,160},{128,192},{160,224},{192,256},{22... | collective-permute-start | bytes 147464 | tf_op jit(solution)/shard_map/ppermute | solution.py:57
  111.5 7.1 %collective-permute-start.9 = (bf16[4,24,256]{2,1,0:T(8,128)(2,1)S(1)}, bf16[4,24,256]{2,1,0:T(8,128)(2,1)S(1)}, u32[]{:S(2)}, u32[]{:S(2)}) collective-permute-start(bf16[4,24,256]{2,1,0:T(8,128)(2,1)S(1)} %bitcast.214), channel_id=1, source_target_pairs={{64,0},{96,32},{128,64},{160,96},{192,128},{224,160},{256,192},{28... | collective-permute-start | bytes 147464 | tf_op jit(solution)/shard_map/ppermute | solution.py:61
  118.7 6.2 %collective-permute-start.11 = (bf16[16,4,256]{2,1,0:T(4,128)(2,1)S(1)}, bf16[16,4,256]{2,1,0:T(4,128)(2,1)S(1)}, u32[]{:S(2)}, u32[]{:S(2)}) collective-permute-start(bf16[16,4,256]{2,1,0:T(4,128)(2,1)S(1)} %get-tuple-element.49), channel_id=1, source_target_pairs={{1,0},{2,1},{3,2},{32,3},{5,4},{6,5},{7,6},{36,7},{9,8},{10,9},{11... | collective-permute-start | bytes 98312 | tf_op jit(solution)/shard_map/ppermute | solution.py:53
  121.1 4.6 %collective-permute-start.12 = (bf16[16,4,256]{2,1,0:T(4,128)(2,1)S(1)}, bf16[16,4,256]{2,1,0:T(4,128)(2,1)S(1)}, u32[]{:S(2)}, u32[]{:S(2)}) collective-permute-start(bf16[16,4,256]{2,1,0:T(4,128)(2,1)S(1)} %get-tuple-element.50), channel_id=1, source_target_pairs={{0,1},{1,2},{2,3},{3,32},{4,5},{5,6},{6,7},{7,36},{8,9},{9,10},{10... | collective-permute-start | bytes 98312 | tf_op jit(solution)/shard_map/ppermute | solution.py:49
  126.3 10.3 %collective-permute-start.15 = (bf16[1024,128]{1,0:T(8,128)(2,1)S(1)}, bf16[1024,128]{1,0:T(8,128)(2,1)S(1)}, u32[]{:S(2)}, u32[]{:S(2)}) collective-permute-start(bf16[1024,128]{1,0:T(8,128)(2,1)S(1)} %get-tuple-element.27), channel_id=1, source_target_pairs={{0,96},{32,0},{64,32},{96,64},{1,97},{33,1},{65,33},{97,65},{2,98}... | collective-permute-start | bytes 786440 | tf_op jit(solution)/shard_map/ppermute | solution.py:79
  131.6 8.9 %collective-permute-start.17 = (bf16[1024,128]{1,0:T(8,128)(2,1)S(1)}, bf16[1024,128]{1,0:T(8,128)(2,1)S(1)}, u32[]{:S(2)}, u32[]{:S(2)}) collective-permute-start(bf16[1024,128]{1,0:T(8,128)(2,1)S(1)} %get-tuple-element.28), channel_id=1, source_target_pairs={{0,32},{32,64},{64,96},{96,0},{1,33},{33,65},{65,97},{97,1},{2,34}... | collective-permute-start | bytes 786440 | tf_op jit(solution)/shard_map/ppermute | solution.py:79
  133.5 11.7 %collective-permute-start.16 = (bf16[1024,128]{1,0:T(8,128)(2,1)S(1)}, bf16[1024,128]{1,0:T(8,128)(2,1)S(1)}, u32[]{:S(2)}, u32[]{:S(2)}) collective-permute-start(bf16[1024,128]{1,0:T(8,128)(2,1)S(1)} %get-tuple-element.29), channel_id=1, source_target_pairs={{0,64},{32,96},{64,0},{96,32},{1,65},{33,97},{65,1},{97,33},{2,66}... | collective-permute-start | bytes 786440 | tf_op jit(solution)/shard_map/ppermute | solution.py:79
  145.4 6.9 %collective-permute-start.18 = (bf16[8,64,128]{2,1,0:T(8,128)(2,1)S(1)}, bf16[8,64,128]{2,1,0:T(8,128)(2,1)S(1)}, u32[]{:S(2)}, u32[]{:S(2)}) collective-permute-start(bf16[8,64,128]{2,1,0:T(8,128)(2,1)S(1)} %fusion.31), channel_id=1, source_target_pairs={{0,1},{1,0},{2,3},{3,2},{4,5},{5,4},{6,7},{7,6},{8,9},{9,8},{10,11... | collective-permute-start | bytes 393224 | tf_op jit(solution)/shard_map/ppermute | solution.py:83
  152.3 13.3 %collective-permute-start.19 = (bf16[8,32,128]{2,1,0:T(8,128)(2,1)S(1)}, bf16[8,32,128]{2,1,0:T(8,128)(2,1)S(1)}, u32[]{:S(2)}, u32[]{:S(2)}) collective-permute-start(bf16[8,32,128]{2,1,0:T(8,128)(2,1)S(1)} %slice_bitcast_fusion.5), channel_id=1, source_target_pairs={{0,16},{16,0},{1,17},{17,1},{2,18},{18,2},{3,19},{19,3},{4,20},{20... | collective-permute-start | bytes 196616 | tf_op jit(solution)/shard_map/ppermute | solution.py:83
  176.9 22.7 %all-to-all-start.4 = ((bf16[6,8,32,128]{3,2,1,0:T(8,128)(2,1)}), bf16[6,8,32,128]{3,2,1,0:T(8,128)(2,1)S(1)}, u32[]{:S(2)}, u32[]{:S(2)}) async-start(bf16[6,8,32,128]{3,2,1,0:T(8,128)(2,1)} %broadcast_in_dim.45), calls=%async_computation.4 | async-start | bytes 786432 | tf_op jit(solution)/shard_map/all_to_all | solution.py:65
  199.6 32.7 %all-to-all-start.2 = ((bf16[8,128,512]{1,2,0:T(8,128)(2,1)}), bf16[8,128,512]{1,2,0:T(8,128)(2,1)S(1)}, u32[]{:S(2)}, u32[]{:S(2)}) async-start(bf16[8,128,512]{1,2,0:T(8,128)(2,1)} %copy_bitcast_fusion), calls=%async_computation.2 | async-start | bytes 2097152 | tf_op jit(solution)/shard_map/all_to_all | solution.py:65
  203.3 38.2 %collective-permute-start.20 = (bf16[8,32,128]{2,1,0:T(8,128)(2,1)S(1)}, bf16[8,32,128]{2,1,0:T(8,128)(2,1)S(1)}, u32[]{:S(2)}, u32[]{:S(2)}) collective-permute-start(bf16[8,32,128]{2,1,0:T(8,128)(2,1)S(1)} %reduce_sum.55), channel_id=1, source_target_pairs={{0,32},{32,0},{64,96},{96,64},{1,33},{33,1},{65,97},{97,65},{2,34}... | collective-permute-start | bytes 196616 | tf_op jit(solution)/shard_map/ppermute | solution.py:83
  232.9 14.2 %collective-permute-start.13 = (bf16[2,2,4,32,128]{4,2,3,0,1:T(4,128)(2,1)S(1)}, bf16[2,2,4,32,128]{4,2,3,0,1:T(4,128)(2,1)S(1)}, u32[]{:S(2)}, u32[]{:S(2)}) collective-permute-start(bf16[2,2,4,32,128]{4,2,3,0,1:T(4,128)(2,1)S(1)} %fusion.30), channel_id=1, source_target_pairs={{0,16},{16,0},{1,17},{17,1},{2,18},{18,2},{3,19},{19,3},{4,20},{20... | collective-permute-start | bytes 393224 | tf_op jit(solution)/shard_map/ppermute | solution.py:83
  241.5 12.6 %collective-permute-start.21 = (bf16[2,8,32,128]{3,2,1,0:T(8,128)(2,1)S(1)}, bf16[2,8,32,128]{3,2,1,0:T(8,128)(2,1)S(1)}, u32[]{:S(2)}, u32[]{:S(2)}) collective-permute-start(bf16[2,8,32,128]{3,2,1,0:T(8,128)(2,1)S(1)} %pad_maximum_fusion.13), channel_id=1, source_target_pairs={{0,64},{32,96},{64,0},{96,32},{1,65},{33,97},{65,1},{97,33},{2,66}... | collective-permute-start | bytes 393224 | tf_op jit(solution)/shard_map/ppermute | solution.py:239
  247.2 8.1 %collective-permute-start.14 = (f32[2,4,32,128]{3,1,2,0:T(4,128)S(1)}, f32[2,4,32,128]{3,1,2,0:T(4,128)S(1)}, u32[]{:S(2)}, u32[]{:S(2)}) collective-permute-start(f32[2,4,32,128]{3,1,2,0:T(4,128)S(1)} %slice_bitcast_fusion.3), channel_id=1, source_target_pairs={{0,1},{1,0},{2,3},{3,2},{4,5},{5,4},{6,7},{7,6},{8,9},{9,8},{10,11... | collective-permute-start | bytes 393224 | tf_op jit(solution)/shard_map/ppermute | solution.py:83

commit v6 on v5

--- a/solution.py
+++ b/solution.py
@@ -116,30 +116,26 @@
     y = lax.axis_index("y")
     c = lax.axis_index("c")
 
-    w_mine = pick(weights, x, 1).transpose(1, 0, 2)
-    w_keep = lax.dynamic_slice_in_dim(w_mine, zh * 4, 4, 0)
-    w_give = lax.dynamic_slice_in_dim(w_mine, (1 - zh) * 4, 4, 0)
+    w_mine = pick(weights, x, 1).reshape(WIDTH, 2, 4, HEAD_DIM).transpose(2, 1, 0, 3)
+    w_send = jnp.broadcast_to(w_mine[:, None], (4, 2, 2, WIDTH, HEAD_DIM))
+    w_in = a2a(w_send.reshape(8, 2, WIDTH, HEAD_DIM), "y")
+
     tiles = jnp.concatenate([split_tiles(embedded[0]), split_tiles(cotangent[0])], 2)
-    mine = jnp.concatenate([tiles.reshape(16, WIDTH, 128), w_give])
-    got = swap(mine, "zh")
-    pairs = jnp.stack([tiles, got[:16].reshape(2, 2, 4, WIDTH, 128)], 3)
+    got = swap(tiles, "zh")
+    pairs = jnp.stack([tiles, got], 3)
     t_keep = pick(pairs, c, 1)
     t_give = pick(pairs, 1 - c, 1)
-    w_keep = jnp.stack([w_keep, got[16:]], 1)
-    mine = jnp.concatenate([t_give.reshape(16, WIDTH, 128), w_keep.reshape(8, WIDTH, 128)])
+    mine = jnp.concatenate([t_give.reshape(16, WIDTH, 128), w_in.reshape(16, WIDTH, 128)])
     got = swap(mine, "c")
     t_mine = jnp.stack([t_keep, got[:16].reshape(2, 4, 2, WIDTH, 128)], 2)
-    t_mine = t_mine.reshape(2, 4, 128, 128)
-    w_mine = jnp.stack([w_keep, got[16:].reshape(4, 2, WIDTH, 128)], 1).reshape(4, 128, 128)
-    t_mine = t_mine.transpose(0, 2, 1, 3)
-
-    def gather(v, lead):
-        send = jnp.broadcast_to(v, lead + v.shape[2:]).reshape(8, 128, -1)
-        return a2a(send, "y").reshape(D, -1)
-
-    w_x = gather(w_mine[:, None], (4, 2))
-    both = gather(t_mine[None].reshape(1, 2, 128, 2 * TILE_TOKENS), (4, 2))
+    t_mine = t_mine.reshape(2, 4, 128, 128).transpose(0, 2, 1, 3)
+    send = jnp.broadcast_to(t_mine.reshape(1, 2, 128, 512), (4, 2, 128, 512))
+    both = a2a(send.reshape(8, 128, 512), "y").reshape(D, 512)
     tokens, grads = both[:, :TILE_TOKENS], both[:, TILE_TOKENS:]
+
+    w_both = jnp.stack([w_in, got[16:].reshape(8, 2, WIDTH, HEAD_DIM)], 2)
+    w_far = swap(pick(w_both, 1 - zh, 1), "zh")
+    w_x = jnp.stack([pick(w_both, zh, 1), w_far], 2).reshape(D, HEAD_DIM)
     w_list = jnp.stack([w_x] + [shift(w_x, "x", 4, 1, s) for s in (1, 2, 3)])
     w_qkv = jnp.concatenate([pick(w_list, (m - x) % 4) for m in range(3)], 1)
     w_out = pick(w_list, (3 - x) % 4)
@@ -235,8 +231,10 @@
     total = jnp.broadcast_to(total, (6, HEADS, WIDTH, 128))
     total = a2a(total, "zl")
     total = jnp.sum(total.astype(f32), 0).astype(bf16)
-    total = jnp.stack(in_order(total, swap(total, "x"), x % 2))
-    total = jnp.concatenate(in_order(total, lax.ppermute(total, "x", SWAP_X2), x // 2))
+    got = swap(total, "x")
+    total = jnp.stack(in_order(total, got, x % 2))
+    got = lax.ppermute(total, "x", SWAP_X2)
+    total = jnp.concatenate(in_order(total, got, x // 2))
     weight_grads = total.transpose(2, 0, 1, 3).astype(f32)
     return attention, token_grads, weight_grads
 

time: 259 us -> 280 us (1.081)
  starting transfers between devices: 118 us -> 150 us
  waiting for transfers between devices: 111 us -> 95 us
  blocking collectives: 10.3 us -> 14.1 us
    ppermute x7 -> x8, starting transfers between devices: 54.7 us -> 77.9 us  [swap(): lax.ppermute(v, axis, [(i, i ^ 1) for i in range(lax.axis_size(axis))])]
    all_to_all x4, waiting for transfers between devices: 63.8 us -> 45.6 us  [a2a(): return lax.all_to_all(v, axes, 0, 0, tiled=True)]
    all_to_all x4, starting transfers between devices: 16.8 us -> 23.6 us  [a2a(): return lax.all_to_all(v, axes, 0, 0, tiled=True)]
    ppermute x7 -> x8, waiting for transfers between devices: 13.1 us -> 19.4 us  [swap(): lax.ppermute(v, axis, [(i, i ^ 1) for i in range(lax.axis_size(axis))])]
    all_to_all x1, blocking collectives: 10.3 us -> 14.1 us  [a2a(): return lax.all_to_all(v, axes, 0, 0, tiled=True)]
    ppermute x2, waiting for transfers between devices: 14.5 us -> 11.4 us  [to_up(): return lax.ppermute(v, ('zl', 'x'), UP)]
  transfers between devices with their start and end apart: 26 -> 27, of which waited for: 17 -> 17; matrix products, arithmetic and copies ran while one was open for 2% -> 2% of each run, Pallas kernels for 0% -> 0%
where the time goes in v6:
time: 280 us; the launch traced here: 279 us
  starting transfers between devices  150 us (54%)
  waiting for transfers between devices  95 us (34%)
  blocking collectives  14.1 us (5%)
  local copies, waits for them, and re-layouts  10.5 us (4%)
  matrix products  4.05 us (1%)
  other arithmetic  3.32 us (1%)
    ppermute x8, starting transfers between devices, swap(): lax.ppermute(v, axis, [(i, i ^ 1) for i in range(lax.axis_size(axis))])  77.9 us
    all_to_all x4, waiting for transfers between devices, a2a(): return lax.all_to_all(v, axes, 0, 0, tiled=True)  45.6 us
    all_to_all x4, starting transfers between devices, a2a(): return lax.all_to_all(v, axes, 0, 0, tiled=True)  23.6 us
    ppermute x6, starting transfers between devices, shift(): return lax.ppermute(v, axis, pairs)  20.5 us
    ppermute x8, waiting for transfers between devices, swap(): lax.ppermute(v, axis, [(i, i ^ 1) for i in range(lax.axis_size(axis))])  19.4 us
    ppermute x6, waiting for transfers between devices, shift(): return lax.ppermute(v, axis, pairs)  14.6 us
    all_to_all x1, blocking collectives, a2a(): return lax.all_to_all(v, axes, 0, 0, tiled=True)  14.1 us
    ppermute x2, waiting for transfers between devices, to_up(): return lax.ppermute(v, ('zl', 'x'), UP)  11.4 us
  transfers between devices with their start and end apart: 27, of which 17 were waited for; matrix products, arithmetic and copies ran while one was open for 2% of the time, Pallas kernels for 0%

profile of v6, /device:TPU:1, one launch (start us, length us, event | category | flops | bytes accessed | tf_op | source)
XLA Modules:
  0.0 279.1 jit_solution(7224330409167234105)
XLA Ops:
  3.1 15.7 %collective-permute-start = (bf16[2,2,4,32,128]{3,4,2,1,0:T(8,128)(2,1)S(1)}, bf16[2,2,4,32,128]{3,4,2,1,0:T(8,128)(2,1)S(1)}, u32[]{:S(2)}, u32[]{:S(2)}) collective-permute-start(bf16[2,2,4,32,128]{3,4,2,1,0:T(8,128)(2,1)S(1)} %get-tuple-element.37), channel_id=1, source_target_pairs={{0,16},{16,0},{1,17},{17,1},{2,18},{18,2},{3,19},{19,3},{4,20},{20... | collective-permute-start | bytes 393224 | tf_op jit(solution)/shard_map/ppermute | solution.py:83
  19.5 6.8 %all-to-all-start = ((bf16[8,2,32,128]{3,2,1,0:T(8,128)(2,1)}), bf16[8,2,32,128]{3,2,1,0:T(8,128)(2,1)S(1)}, u32[]{:S(2)}, u32[]{:S(2)}) async-start(bf16[8,2,32,128]{3,2,1,0:T(8,128)(2,1)} %bitcast.2), calls=%async_computation | async-start | bytes 262144 | tf_op jit(solution)/shard_map/all_to_all | solution.py:65
  26.3 3.8 %collective-permute-done = bf16[2,2,4,32,128]{3,4,2,1,0:T(8,128)(2,1)S(1)} collective-permute-done((bf16[2,2,4,32,128]{3,4,2,1,0:T(8,128)(2,1)S(1)}, bf16[2,2,4,32,128]{3,4,2,1,0:T(8,128)(2,1)S(1)}, u32[]{:S(2)}, u32[]{:S(2)}) %collective-permute-start) | collective-permute-done | bytes 131104 | tf_op jit(solution)/shard_map/ppermute | solution.py:83
  30.5 3.7 %all-to-all-done = bf16[8,2,32,128]{3,2,1,0:T(8,128)(2,1)S(1)} async-done(((bf16[8,2,32,128]{3,2,1,0:T(8,128)(2,1)}), bf16[8,2,32,128]{3,2,1,0:T(8,128)(2,1)S(1)}, u32[]{:S(2)}, u32[]{:S(2)}) %all-to-all-start) | async-done | bytes 131104 | tf_op jit(solution)/shard_map/all_to_all | solution.py:65
  34.3 4.3 %collective-permute-start.1 = (bf16[32,32,128]{2,1,0:T(8,128)(2,1)S(1)}, bf16[32,32,128]{2,1,0:T(8,128)(2,1)S(1)}, u32[]{:S(2)}, u32[]{:S(2)}) collective-permute-start(bf16[32,32,128]{2,1,0:T(8,128)(2,1)S(1)} %pad_maximum_fusion.7), channel_id=1, source_target_pairs={{0,1},{1,0},{2,3},{3,2},{4,5},{5,4},{6,7},{7,6},{8,9},{9,8},{10,11... | collective-permute-start | bytes 786440 | tf_op jit(solution)/shard_map/ppermute | solution.py:83
  41.2 3.6 %all-to-all-start.1 = ((bf16[8,128,512]{2,1,0:T(8,128)(2,1)}), bf16[8,128,512]{2,1,0:T(8,128)(2,1)S(1)}, u32[]{:S(2)}, u32[]{:S(2)}) async-start(bf16[8,128,512]{2,1,0:T(8,128)(2,1)} %bitcast.29), calls=%async_computation.1 | async-start | bytes 2097152 | tf_op jit(solution)/shard_map/all_to_all | solution.py:65
  44.8 30.2 %collective-permute-start.2 = (bf16[8,2,32,128]{3,2,1,0:T(8,128)(2,1)S(1)}, bf16[8,2,32,128]{3,2,1,0:T(8,128)(2,1)S(1)}, u32[]{:S(2)}, u32[]{:S(2)}) collective-permute-start(bf16[8,2,32,128]{3,2,1,0:T(8,128)(2,1)S(1)} %bitcast.204), channel_id=1, source_target_pairs={{0,16},{16,0},{1,17},{17,1},{2,18},{18,2},{3,19},{19,3},{4,20},{20... | collective-permute-start | bytes 393224 | tf_op jit(solution)/shard_map/ppermute | solution.py:83
  75.1 3.2 %collective-permute-done.2 = bf16[8,2,32,128]{3,2,1,0:T(8,128)(2,1)S(1)} collective-permute-done((bf16[8,2,32,128]{3,2,1,0:T(8,128)(2,1)S(1)}, bf16[8,2,32,128]{3,2,1,0:T(8,128)(2,1)S(1)}, u32[]{:S(2)}, u32[]{:S(2)}) %collective-permute-start.2) | collective-permute-done | bytes 131104 | tf_op jit(solution)/shard_map/ppermute | solution.py:83
  78.3 3.1 %collective-permute-start.5 = (bf16[1024,128]{1,0:T(8,128)(2,1)S(1)}, bf16[1024,128]{1,0:T(8,128)(2,1)S(1)}, u32[]{:S(2)}, u32[]{:S(2)}) collective-permute-start(bf16[1024,128]{1,0:T(8,128)(2,1)S(1)} %bitcast.179), channel_id=1, source_target_pairs={{0,32},{32,64},{64,96},{96,0},{1,33},{33,65},{65,97},{97,1},{2,34}... | collective-permute-start | bytes 786440 | tf_op jit(solution)/shard_map/ppermute | solution.py:79
  81.4 4.4 %collective-permute-start.4 = (bf16[1024,128]{1,0:T(8,128)(2,1)S(1)}, bf16[1024,128]{1,0:T(8,128)(2,1)S(1)}, u32[]{:S(2)}, u32[]{:S(2)}) collective-permute-start(bf16[1024,128]{1,0:T(8,128)(2,1)S(1)} %bitcast.180), channel_id=1, source_target_pairs={{0,64},{32,96},{64,0},{96,32},{1,65},{33,97},{65,1},{97,33},{2,66}... | collective-permute-start | bytes 786440 | tf_op jit(solution)/shard_map/ppermute | solution.py:79
  89.0 5.6 %collective-permute-done.4 = bf16[1024,128]{1,0:T(8,128)(2,1)S(1)} collective-permute-done((bf16[1024,128]{1,0:T(8,128)(2,1)S(1)}, bf16[1024,128]{1,0:T(8,128)(2,1)S(1)}, u32[]{:S(2)}, u32[]{:S(2)}) %collective-permute-start.4) | collective-permute-done | bytes 262176 | tf_op jit(solution)/shard_map/ppermute | solution.py:79
  97.4 5.2 %collective-permute-start.6 = (bf16[16,4,256]{2,1,0:T(4,128)(2,1)}, bf16[16,4,256]{2,1,0:T(4,128)(2,1)S(1)}, u32[]{:S(2)}, u32[]{:S(2)}) collective-permute-start(bf16[16,4,256]{2,1,0:T(4,128)(2,1)} %get-tuple-element.59), channel_id=1, source_target_pairs={{0,1},{1,2},{2,3},{3,32},{4,5},{5,6},{6,7},{7,36},{8,9},{9,10},{10... | collective-permute-start | bytes 98312 | tf_op jit(solution)/shard_map/ppermute | solution.py:49
  104.7 3.3 %collective-permute-done.7 = bf16[16,4,256]{2,1,0:T(4,128)(2,1)S(1)} collective-permute-done((bf16[16,4,256]{2,1,0:T(4,128)(2,1)}, bf16[16,4,256]{2,1,0:T(4,128)(2,1)S(1)}, u32[]{:S(2)}, u32[]{:S(2)}) %collective-permute-start.7) | collective-permute-done | bytes 32800 | tf_op jit(solution)/shard_map/ppermute | solution.py:53
  108.1 4.7 %collective-permute-start.8 = (bf16[4,24,256]{2,1,0:T(8,128)(2,1)S(1)}, bf16[4,24,256]{2,1,0:T(8,128)(2,1)S(1)}, u32[]{:S(2)}, u32[]{:S(2)}) collective-permute-start(bf16[4,24,256]{2,1,0:T(8,128)(2,1)S(1)} %get-tuple-element.55), channel_id=1, source_target_pairs={{0,64},{32,96},{64,128},{96,160},{128,192},{160,224},{192,256},{22... | collective-permute-start | bytes 147464 | tf_op jit(solution)/shard_map/ppermute | solution.py:57
  114.4 5.7 %collective-permute-done.9 = bf16[4,24,256]{2,1,0:T(8,128)(2,1)S(1)} collective-permute-done((bf16[4,24,256]{2,1,0:T(8,128)(2,1)S(1)}, bf16[4,24,256]{2,1,0:T(8,128)(2,1)S(1)}, u32[]{:S(2)}, u32[]{:S(2)}) %collective-permute-start.9) | collective-permute-done | bytes 49184 | tf_op jit(solution)/shard_map/ppermute | solution.py:61
  122.4 5.8 %collective-permute-start.11 = (bf16[4,24,256]{2,1,0:T(8,128)(2,1)S(1)}, bf16[4,24,256]{2,1,0:T(8,128)(2,1)S(1)}, u32[]{:S(2)}, u32[]{:S(2)}) collective-permute-start(bf16[4,24,256]{2,1,0:T(8,128)(2,1)S(1)} %bitcast.207), channel_id=1, source_target_pairs={{0,64},{32,96},{64,128},{96,160},{128,192},{160,224},{192,256},{22... | collective-permute-start | bytes 147464 | tf_op jit(solution)/shard_map/ppermute | solution.py:57
  129.6 5.8 %collective-permute-done.10 = bf16[4,24,256]{2,1,0:T(8,128)(2,1)S(1)} collective-permute-done((bf16[4,24,256]{2,1,0:T(8,128)(2,1)S(1)}, bf16[4,24,256]{2,1,0:T(8,128)(2,1)S(1)}, u32[]{:S(2)}, u32[]{:S(2)}) %collective-permute-start.10) | collective-permute-done | bytes 49184 | tf_op jit(solution)/shard_map/ppermute | solution.py:61
  137.8 3.7 %collective-permute-start.13 = (bf16[16,4,256]{2,1,0:T(4,128)(2,1)S(1)}, bf16[16,4,256]{2,1,0:T(4,128)(2,1)S(1)}, u32[]{:S(2)}, u32[]{:S(2)}) collective-permute-start(bf16[16,4,256]{2,1,0:T(4,128)(2,1)S(1)} %get-tuple-element.54), channel_id=1, source_target_pairs={{0,1},{1,2},{2,3},{3,32},{4,5},{5,6},{6,7},{7,36},{8,9},{9,10},{10... | collective-permute-start | bytes 98312 | tf_op jit(solution)/shard_map/ppermute | solution.py:49
  143.1 4.3 %collective-permute-start.16 = (bf16[1024,128]{1,0:T(8,128)(2,1)S(1)}, bf16[1024,128]{1,0:T(8,128)(2,1)S(1)}, u32[]{:S(2)}, u32[]{:S(2)}) collective-permute-start(bf16[1024,128]{1,0:T(8,128)(2,1)S(1)} %get-tuple-element.27), channel_id=1, source_target_pairs={{0,96},{32,0},{64,32},{96,64},{1,97},{33,1},{65,33},{97,65},{2,98}... | collective-permute-start | bytes 786440 | tf_op jit(solution)/shard_map/ppermute | solution.py:79
  149.3 3.8 %collective-permute-start.17 = (bf16[1024,128]{1,0:T(8,128)(2,1)S(1)}, bf16[1024,128]{1,0:T(8,128)(2,1)S(1)}, u32[]{:S(2)}, u32[]{:S(2)}) collective-permute-start(bf16[1024,128]{1,0:T(8,128)(2,1)S(1)} %get-tuple-element.29), channel_id=1, source_target_pairs={{0,64},{32,96},{64,0},{96,32},{1,65},{33,97},{65,1},{97,33},{2,66}... | collective-permute-start | bytes 786440 | tf_op jit(solution)/shard_map/ppermute | solution.py:79
  153.1 3.3 %collective-permute-done.18 = bf16[1024,128]{1,0:T(8,128)(2,1)S(1)} collective-permute-done((bf16[1024,128]{1,0:T(8,128)(2,1)S(1)}, bf16[1024,128]{1,0:T(8,128)(2,1)S(1)}, u32[]{:S(2)}, u32[]{:S(2)}) %collective-permute-start.18) | collective-permute-done | bytes 262176 | tf_op jit(solution)/shard_map/ppermute | solution.py:79
  156.4 4.3 %collective-permute-done.17 = bf16[1024,128]{1,0:T(8,128)(2,1)S(1)} collective-permute-done((bf16[1024,128]{1,0:T(8,128)(2,1)S(1)}, bf16[1024,128]{1,0:T(8,128)(2,1)S(1)}, u32[]{:S(2)}, u32[]{:S(2)}) %collective-permute-start.17) | collective-permute-done | bytes 262176 | tf_op jit(solution)/shard_map/ppermute | solution.py:79
  160.9 6.2 %collective-permute-start.19 = (bf16[8,64,128]{2,1,0:T(8,128)(2,1)S(1)}, bf16[8,64,128]{2,1,0:T(8,128)(2,1)S(1)}, u32[]{:S(2)}, u32[]{:S(2)}) collective-permute-start(bf16[8,64,128]{2,1,0:T(8,128)(2,1)S(1)} %fusion.33), channel_id=1, source_target_pairs={{0,1},{1,0},{2,3},{3,2},{4,5},{5,4},{6,7},{7,6},{8,9},{9,8},{10,11... | collective-permute-start | bytes 393224 | tf_op jit(solution)/shard_map/ppermute | solution.py:83
  168.1 10.1 %collective-permute-start.20 = (bf16[8,32,128]{2,1,0:T(8,128)(2,1)S(1)}, bf16[8,32,128]{2,1,0:T(8,128)(2,1)S(1)}, u32[]{:S(2)}, u32[]{:S(2)}) collective-permute-start(bf16[8,32,128]{2,1,0:T(8,128)(2,1)S(1)} %slice_bitcast_fusion.5), channel_id=1, source_target_pairs={{0,16},{16,0},{1,17},{17,1},{2,18},{18,2},{3,19},{19,3},{4,20},{20... | collective-permute-start | bytes 196616 | tf_op jit(solution)/shard_map/ppermute | solution.py:83
  180.3 14.1 %all_to_all.25 = bf16[8,2,32,128]{3,2,1,0:T(8,128)(2,1)S(1)} all-to-all(bf16[8,2,32,128]{3,2,1,0:T(8,128)(2,1)S(1)} %copy.250), channel_id=1, replica_groups=mesh['zl'=6,'x'=4,'zh'=2,'y'=8,'c'=2] {'y'}, dimensions={0} | all-to-all | bytes 262144 | tf_op jit(solution)/shard_map/all_to_all | solution.py:65
  195.3 9.6 %all-to-all-start.4 = ((bf16[6,8,32,128]{3,2,1,0:T(8,128)(2,1)}), bf16[6,8,32,128]{3,2,1,0:T(8,128)(2,1)S(1)}, u32[]{:S(2)}, u32[]{:S(2)}) async-start(bf16[6,8,32,128]{3,2,1,0:T(8,128)(2,1)} %broadcast_in_dim.43), calls=%async_computation.4 | async-start | bytes 786432 | tf_op jit(solution)/shard_map/all_to_all | solution.py:65
  207.0 14.8 %all-to-all-done.4 = bf16[6,8,32,128]{3,2,1,0:T(8,128)(2,1)S(1)} async-done(((bf16[6,8,32,128]{3,2,1,0:T(8,128)(2,1)}), bf16[6,8,32,128]{3,2,1,0:T(8,128)(2,1)S(1)}, u32[]{:S(2)}, u32[]{:S(2)}) %all-to-all-start.4) | async-done | bytes 393248 | tf_op jit(solution)/shard_map/all_to_all | solution.py:65
  221.8 3.6 %all-to-all-start.2 = ((bf16[8,128,512]{1,2,0:T(8,128)(2,1)}), bf16[8,128,512]{1,2,0:T(8,128)(2,1)S(1)}, u32[]{:S(2)}, u32[]{:S(2)}) async-start(bf16[8,128,512]{1,2,0:T(8,128)(2,1)} %copy_bitcast_fusion), calls=%async_computation.2 | async-start | bytes 2097152 | tf_op jit(solution)/shard_map/all_to_all | solution.py:65
  227.4 27.1 %all-to-all-done.2 = bf16[8,128,512]{1,2,0:T(8,128)(2,1)S(1)} async-done(((bf16[8,128,512]{1,2,0:T(8,128)(2,1)}), bf16[8,128,512]{1,2,0:T(8,128)(2,1)S(1)}, u32[]{:S(2)}, u32[]{:S(2)}) %all-to-all-start.2) | async-done | bytes 1048608 | tf_op jit(solution)/shard_map/all_to_all | solution.py:65
  255.1 6.2 %collective-permute-start.14 = (bf16[2,2,4,32,128]{4,2,3,0,1:T(4,128)(2,1)S(1)}, bf16[2,2,4,32,128]{4,2,3,0,1:T(4,128)(2,1)S(1)}, u32[]{:S(2)}, u32[]{:S(2)}) collective-permute-start(bf16[2,2,4,32,128]{4,2,3,0,1:T(4,128)(2,1)S(1)} %fusion.32), channel_id=1, source_target_pairs={{0,16},{16,0},{1,17},{17,1},{2,18},{18,2},{3,19},{19,3},{4,20},{20... | collective-permute-start | bytes 393224 | tf_op jit(solution)/shard_map/ppermute | solution.py:83
  263.7 8.4 %collective-permute-done.14 = bf16[2,2,4,32,128]{4,2,3,0,1:T(4,128)(2,1)S(1)} collective-permute-done((bf16[2,2,4,32,128]{4,2,3,0,1:T(4,128)(2,1)S(1)}, bf16[2,2,4,32,128]{4,2,3,0,1:T(4,128)(2,1)S(1)}, u32[]{:S(2)}, u32[]{:S(2)}) %collective-permute-start.14) | collective-permute-done | bytes 131104 | tf_op jit(solution)/shard_map/ppermute | solution.py:83
  272.2 3.3 %collective-permute-start.15 = (f32[2,4,32,128]{3,1,2,0:T(4,128)S(1)}, f32[2,4,32,128]{3,1,2,0:T(4,128)S(1)}, u32[]{:S(2)}, u32[]{:S(2)}) collective-permute-start(f32[2,4,32,128]{3,1,2,0:T(4,128)S(1)} %slice_bitcast_fusion.3), channel_id=1, source_target_pairs={{0,1},{1,0},{2,3},{3,2},{4,5},{5,4},{6,7},{7,6},{8,9},{9,8},{10,11... | collective-permute-start | bytes 393224 | tf_op jit(solution)/shard_map/ppermute | solution.py:83
  (114 shorter events, 40.1 us)
Async XLA Ops:
  0.6 18.1 %copy-start = (bf16[32,4,8,128]{3,2,1,0:T(8,128)(2,1)S(1)}, bf16[32,4,8,128]{3,2,1,0:T(8,128)(2,1)}, u32[]{:S(2)}) copy-start(bf16[32,4,8,128]{3,2,1,0:T(8,128)(2,1)} %param.5) | copy-start | bytes 786436
  3.1 27.1 %collective-permute-start = (bf16[2,2,4,32,128]{3,4,2,1,0:T(8,128)(2,1)S(1)}, bf16[2,2,4,32,128]{3,4,2,1,0:T(8,128)(2,1)S(1)}, u32[]{:S(2)}, u32[]{:S(2)}) collective-permute-start(bf16[2,2,4,32,128]{3,4,2,1,0:T(8,128)(2,1)S(1)} %get-tuple-element.37), channel_id=1, source_target_pairs={{0,16},{16,0},{1,17},{17,1},{2,18},{18,2},{3,19},{19,3},{4,20},{20... | collective-permute-start | bytes 393224 | tf_op jit(solution)/shard_map/ppermute | solution.py:83
  19.5 14.8 %all-to-all-start = ((bf16[8,2,32,128]{3,2,1,0:T(8,128)(2,1)}), bf16[8,2,32,128]{3,2,1,0:T(8,128)(2,1)S(1)}, u32[]{:S(2)}, u32[]{:S(2)}) async-start(bf16[8,2,32,128]{3,2,1,0:T(8,128)(2,1)} %bitcast.2), calls=%async_computation | async-start | bytes 262144 | tf_op jit(solution)/shard_map/all_to_all | solution.py:65
  34.3 5.4 %collective-permute-start.1 = (bf16[32,32,128]{2,1,0:T(8,128)(2,1)S(1)}, bf16[32,32,128]{2,1,0:T(8,128)(2,1)S(1)}, u32[]{:S(2)}, u32[]{:S(2)}) collective-permute-start(bf16[32,32,128]{2,1,0:T(8,128)(2,1)S(1)} %pad_maximum_fusion.7), channel_id=1, source_target_pairs={{0,1},{1,0},{2,3},{3,2},{4,5},{5,4},{6,7},{7,6},{8,9},{9,8},{10,11... | collective-permute-start | bytes 786440 | tf_op jit(solution)/shard_map/ppermute | solution.py:83
  41.2 55.0 %all-to-all-start.1 = ((bf16[8,128,512]{2,1,0:T(8,128)(2,1)}), bf16[8,128,512]{2,1,0:T(8,128)(2,1)S(1)}, u32[]{:S(2)}, u32[]{:S(2)}) async-start(bf16[8,128,512]{2,1,0:T(8,128)(2,1)} %bitcast.29), calls=%async_computation.1 | async-start | bytes 2097152 | tf_op jit(solution)/shard_map/all_to_all | solution.py:65
  44.8 33.4 %collective-permute-start.2 = (bf16[8,2,32,128]{3,2,1,0:T(8,128)(2,1)S(1)}, bf16[8,2,32,128]{3,2,1,0:T(8,128)(2,1)S(1)}, u32[]{:S(2)}, u32[]{:S(2)}) collective-permute-start(bf16[8,2,32,128]{3,2,1,0:T(8,128)(2,1)S(1)} %bitcast.204), channel_id=1, source_target_pairs={{0,16},{16,0},{1,17},{17,1},{2,18},{18,2},{3,19},{19,3},{4,20},{20... | collective-permute-start | bytes 393224 | tf_op jit(solution)/shard_map/ppermute | solution.py:83
  78.3 10.7 %collective-permute-start.5 = (bf16[1024,128]{1,0:T(8,128)(2,1)S(1)}, bf16[1024,128]{1,0:T(8,128)(2,1)S(1)}, u32[]{:S(2)}, u32[]{:S(2)}) collective-permute-start(bf16[1024,128]{1,0:T(8,128)(2,1)S(1)} %bitcast.179), channel_id=1, source_target_pairs={{0,32},{32,64},{64,96},{96,0},{1,33},{33,65},{65,97},{97,1},{2,34}... | collective-permute-start | bytes 786440 | tf_op jit(solution)/shard_map/ppermute | solution.py:79
  81.4 13.1 %collective-permute-start.4 = (bf16[1024,128]{1,0:T(8,128)(2,1)S(1)}, bf16[1024,128]{1,0:T(8,128)(2,1)S(1)}, u32[]{:S(2)}, u32[]{:S(2)}) collective-permute-start(bf16[1024,128]{1,0:T(8,128)(2,1)S(1)} %bitcast.180), channel_id=1, source_target_pairs={{0,64},{32,96},{64,0},{96,32},{1,65},{33,97},{65,1},{97,33},{2,66}... | collective-permute-start | bytes 786440 | tf_op jit(solution)/shard_map/ppermute | solution.py:79
  85.8 10.2 %collective-permute-start.3 = (bf16[1024,128]{1,0:T(8,128)(2,1)S(1)}, bf16[1024,128]{1,0:T(8,128)(2,1)S(1)}, u32[]{:S(2)}, u32[]{:S(2)}) collective-permute-start(bf16[1024,128]{1,0:T(8,128)(2,1)S(1)} %bitcast.181), channel_id=1, source_target_pairs={{0,96},{32,0},{64,32},{96,64},{1,97},{33,1},{65,33},{97,65},{2,98}... | collective-permute-start | bytes 786440 | tf_op jit(solution)/shard_map/ppermute | solution.py:79
  97.4 7.3 %collective-permute-start.6 = (bf16[16,4,256]{2,1,0:T(4,128)(2,1)}, bf16[16,4,256]{2,1,0:T(4,128)(2,1)S(1)}, u32[]{:S(2)}, u32[]{:S(2)}) collective-permute-start(bf16[16,4,256]{2,1,0:T(4,128)(2,1)} %get-tuple-element.59), channel_id=1, source_target_pairs={{0,1},{1,2},{2,3},{3,32},{4,5},{5,6},{6,7},{7,36},{8,9},{9,10},{10... | collective-permute-start | bytes 98312 | tf_op jit(solution)/shard_map/ppermute | solution.py:49
  102.6 5.4 %collective-permute-start.7 = (bf16[16,4,256]{2,1,0:T(4,128)(2,1)}, bf16[16,4,256]{2,1,0:T(4,128)(2,1)S(1)}, u32[]{:S(2)}, u32[]{:S(2)}) collective-permute-start(bf16[16,4,256]{2,1,0:T(4,128)(2,1)} %get-tuple-element.60), channel_id=1, source_target_pairs={{1,0},{2,1},{3,2},{32,3},{5,4},{6,5},{7,6},{36,7},{9,8},{10,9},{11... | collective-permute-start | bytes 98312 | tf_op jit(solution)/shard_map/ppermute | solution.py:53
  108.1 6.3 %collective-permute-start.8 = (bf16[4,24,256]{2,1,0:T(8,128)(2,1)S(1)}, bf16[4,24,256]{2,1,0:T(8,128)(2,1)S(1)}, u32[]{:S(2)}, u32[]{:S(2)}) collective-permute-start(bf16[4,24,256]{2,1,0:T(8,128)(2,1)S(1)} %get-tuple-element.55), channel_id=1, source_target_pairs={{0,64},{32,96},{64,128},{96,160},{128,192},{160,224},{192,256},{22... | collective-permute-start | bytes 147464 | tf_op jit(solution)/shard_map/ppermute | solution.py:57
  112.8 7.3 %collective-permute-start.9 = (bf16[4,24,256]{2,1,0:T(8,128)(2,1)S(1)}, bf16[4,24,256]{2,1,0:T(8,128)(2,1)S(1)}, u32[]{:S(2)}, u32[]{:S(2)}) collective-permute-start(bf16[4,24,256]{2,1,0:T(8,128)(2,1)S(1)} %get-tuple-element.56), channel_id=1, source_target_pairs={{64,0},{96,32},{128,64},{160,96},{192,128},{224,160},{256,192},{28... | collective-permute-start | bytes 147464 | tf_op jit(solution)/shard_map/ppermute | solution.py:61
  122.4 7.1 %collective-permute-start.11 = (bf16[4,24,256]{2,1,0:T(8,128)(2,1)S(1)}, bf16[4,24,256]{2,1,0:T(8,128)(2,1)S(1)}, u32[]{:S(2)}, u32[]{:S(2)}) collective-permute-start(bf16[4,24,256]{2,1,0:T(8,128)(2,1)S(1)} %bitcast.207), channel_id=1, source_target_pairs={{0,64},{32,96},{64,128},{96,160},{128,192},{160,224},{192,256},{22... | collective-permute-start | bytes 147464 | tf_op jit(solution)/shard_map/ppermute | solution.py:57
  128.2 7.1 %collective-permute-start.10 = (bf16[4,24,256]{2,1,0:T(8,128)(2,1)S(1)}, bf16[4,24,256]{2,1,0:T(8,128)(2,1)S(1)}, u32[]{:S(2)}, u32[]{:S(2)}) collective-permute-start(bf16[4,24,256]{2,1,0:T(8,128)(2,1)S(1)} %bitcast.206), channel_id=1, source_target_pairs={{64,0},{96,32},{128,64},{160,96},{192,128},{224,160},{256,192},{28... | collective-permute-start | bytes 147464 | tf_op jit(solution)/shard_map/ppermute | solution.py:61
  135.4 6.3 %collective-permute-start.12 = (bf16[16,4,256]{2,1,0:T(4,128)(2,1)S(1)}, bf16[16,4,256]{2,1,0:T(4,128)(2,1)S(1)}, u32[]{:S(2)}, u32[]{:S(2)}) collective-permute-start(bf16[16,4,256]{2,1,0:T(4,128)(2,1)S(1)} %get-tuple-element.53), channel_id=1, source_target_pairs={{1,0},{2,1},{3,2},{32,3},{5,4},{6,5},{7,6},{36,7},{9,8},{10,9},{11... | collective-permute-start | bytes 98312 | tf_op jit(solution)/shard_map/ppermute | solution.py:53
  137.8 4.7 %collective-permute-start.13 = (bf16[16,4,256]{2,1,0:T(4,128)(2,1)S(1)}, bf16[16,4,256]{2,1,0:T(4,128)(2,1)S(1)}, u32[]{:S(2)}, u32[]{:S(2)}) collective-permute-start(bf16[16,4,256]{2,1,0:T(4,128)(2,1)S(1)} %get-tuple-element.54), channel_id=1, source_target_pairs={{0,1},{1,2},{2,3},{3,32},{4,5},{5,6},{6,7},{7,36},{8,9},{9,10},{10... | collective-permute-start | bytes 98312 | tf_op jit(solution)/shard_map/ppermute | solution.py:49
  143.1 10.0 %collective-permute-start.16 = (bf16[1024,128]{1,0:T(8,128)(2,1)S(1)}, bf16[1024,128]{1,0:T(8,128)(2,1)S(1)}, u32[]{:S(2)}, u32[]{:S(2)}) collective-permute-start(bf16[1024,128]{1,0:T(8,128)(2,1)S(1)} %get-tuple-element.27), channel_id=1, source_target_pairs={{0,96},{32,0},{64,32},{96,64},{1,97},{33,1},{65,33},{97,65},{2,98}... | collective-permute-start | bytes 786440 | tf_op jit(solution)/shard_map/ppermute | solution.py:79
  147.4 9.0 %collective-permute-start.18 = (bf16[1024,128]{1,0:T(8,128)(2,1)S(1)}, bf16[1024,128]{1,0:T(8,128)(2,1)S(1)}, u32[]{:S(2)}, u32[]{:S(2)}) collective-permute-start(bf16[1024,128]{1,0:T(8,128)(2,1)S(1)} %get-tuple-element.28), channel_id=1, source_target_pairs={{0,32},{32,64},{64,96},{96,0},{1,33},{33,65},{65,97},{97,1},{2,34}... | collective-permute-start | bytes 786440 | tf_op jit(solution)/shard_map/ppermute | solution.py:79
  149.3 11.4 %collective-permute-start.17 = (bf16[1024,128]{1,0:T(8,128)(2,1)S(1)}, bf16[1024,128]{1,0:T(8,128)(2,1)S(1)}, u32[]{:S(2)}, u32[]{:S(2)}) collective-permute-start(bf16[1024,128]{1,0:T(8,128)(2,1)S(1)} %get-tuple-element.29), channel_id=1, source_target_pairs={{0,64},{32,96},{64,0},{96,32},{1,65},{33,97},{65,1},{97,33},{2,66}... | collective-permute-start | bytes 786440 | tf_op jit(solution)/shard_map/ppermute | solution.py:79
  160.9 7.2 %collective-permute-start.19 = (bf16[8,64,128]{2,1,0:T(8,128)(2,1)S(1)}, bf16[8,64,128]{2,1,0:T(8,128)(2,1)S(1)}, u32[]{:S(2)}, u32[]{:S(2)}) collective-permute-start(bf16[8,64,128]{2,1,0:T(8,128)(2,1)S(1)} %fusion.33), channel_id=1, source_target_pairs={{0,1},{1,0},{2,3},{3,2},{4,5},{5,4},{6,7},{7,6},{8,9},{9,8},{10,11... | collective-permute-start | bytes 393224 | tf_op jit(solution)/shard_map/ppermute | solution.py:83
  168.1 12.2 %collective-permute-start.20 = (bf16[8,32,128]{2,1,0:T(8,128)(2,1)S(1)}, bf16[8,32,128]{2,1,0:T(8,128)(2,1)S(1)}, u32[]{:S(2)}, u32[]{:S(2)}) collective-permute-start(bf16[8,32,128]{2,1,0:T(8,128)(2,1)S(1)} %slice_bitcast_fusion.5), channel_id=1, source_target_pairs={{0,16},{16,0},{1,17},{17,1},{2,18},{18,2},{3,19},{19,3},{4,20},{20... | collective-permute-start | bytes 196616 | tf_op jit(solution)/shard_map/ppermute | solution.py:83
  195.3 26.5 %all-to-all-start.4 = ((bf16[6,8,32,128]{3,2,1,0:T(8,128)(2,1)}), bf16[6,8,32,128]{3,2,1,0:T(8,128)(2,1)S(1)}, u32[]{:S(2)}, u32[]{:S(2)}) async-start(bf16[6,8,32,128]{3,2,1,0:T(8,128)(2,1)} %broadcast_in_dim.43), calls=%async_computation.4 | async-start | bytes 786432 | tf_op jit(solution)/shard_map/all_to_all | solution.py:65
  221.8 32.7 %all-to-all-start.2 = ((bf16[8,128,512]{1,2,0:T(8,128)(2,1)}), bf16[8,128,512]{1,2,0:T(8,128)(2,1)S(1)}, u32[]{:S(2)}, u32[]{:S(2)}) async-start(bf16[8,128,512]{1,2,0:T(8,128)(2,1)} %copy_bitcast_fusion), calls=%async_computation.2 | async-start | bytes 2097152 | tf_op jit(solution)/shard_map/all_to_all | solution.py:65
  225.5 35.8 %collective-permute-start.21 = (bf16[8,32,128]{2,1,0:T(8,128)(2,1)S(1)}, bf16[8,32,128]{2,1,0:T(8,128)(2,1)S(1)}, u32[]{:S(2)}, u32[]{:S(2)}) collective-permute-start(bf16[8,32,128]{2,1,0:T(8,128)(2,1)S(1)} %reduce_sum.55), channel_id=1, source_target_pairs={{0,32},{32,0},{64,96},{96,64},{1,33},{33,1},{65,97},{97,65},{2,34}... | collective-permute-start | bytes 196616 | tf_op jit(solution)/shard_map/ppermute | solution.py:83
  255.1 17.0 %collective-permute-start.14 = (bf16[2,2,4,32,128]{4,2,3,0,1:T(4,128)(2,1)S(1)}, bf16[2,2,4,32,128]{4,2,3,0,1:T(4,128)(2,1)S(1)}, u32[]{:S(2)}, u32[]{:S(2)}) collective-permute-start(bf16[2,2,4,32,128]{4,2,3,0,1:T(4,128)(2,1)S(1)} %fusion.32), channel_id=1, source_target_pairs={{0,16},{16,0},{1,17},{17,1},{2,18},{18,2},{3,19},{19,3},{4,20},{20... | collective-permute-start | bytes 393224 | tf_op jit(solution)/shard_map/ppermute | solution.py:83
  261.4 14.1 %collective-permute-start.22 = (bf16[2,8,32,128]{3,2,1,0:T(8,128)(2,1)S(1)}, bf16[2,8,32,128]{3,2,1,0:T(8,128)(2,1)S(1)}, u32[]{:S(2)}, u32[]{:S(2)}) collective-permute-start(bf16[2,8,32,128]{3,2,1,0:T(8,128)(2,1)S(1)} %pad_maximum_fusion.12), channel_id=1, source_target_pairs={{0,64},{32,96},{64,0},{96,32},{1,65},{33,97},{65,1},{97,33},{2,66}... | collective-permute-start | bytes 393224 | tf_op jit(solution)/shard_map/ppermute | solution.py:236
  272.2 4.5 %collective-permute-start.15 = (f32[2,4,32,128]{3,1,2,0:T(4,128)S(1)}, f32[2,4,32,128]{3,1,2,0:T(4,128)S(1)}, u32[]{:S(2)}, u32[]{:S(2)}) collective-permute-start(f32[2,4,32,128]{3,1,2,0:T(4,128)S(1)} %slice_bitcast_fusion.3), channel_id=1, source_target_pairs={{0,1},{1,0},{2,3},{3,2},{4,5},{5,4},{6,7},{7,6},{8,9},{9,8},{10,11... | collective-permute-start | bytes 393224 | tf_op jit(solution)/shard_map/ppermute | solution.py:83

commit v7 on v5

--- a/solution.py
+++ b/solution.py
@@ -126,21 +126,19 @@
     t_keep = pick(pairs, c, 1)
     t_give = pick(pairs, 1 - c, 1)
     w_keep = jnp.stack([w_keep, got[16:]], 1)
-    mine = jnp.concatenate([t_give.reshape(16, WIDTH, 128), w_keep.reshape(8, WIDTH, 128)])
-    got = swap(mine, "c")
-    t_mine = jnp.stack([t_keep, got[:16].reshape(2, 4, 2, WIDTH, 128)], 2)
+    got = swap(t_give, "c")
+    t_mine = jnp.stack([t_keep, got], 2)
     t_mine = t_mine.reshape(2, 4, 128, 128)
-    w_mine = jnp.stack([w_keep, got[16:].reshape(4, 2, WIDTH, 128)], 1).reshape(4, 128, 128)
     t_mine = t_mine.transpose(0, 2, 1, 3)
 
-    def gather(v, lead):
-        send = jnp.broadcast_to(v, lead + v.shape[2:]).reshape(8, 128, -1)
-        return a2a(send, "y").reshape(D, -1)
-
-    w_x = gather(w_mine[:, None], (4, 2))
-    both = gather(t_mine[None].reshape(1, 2, 128, 2 * TILE_TOKENS), (4, 2))
+    w_send = jnp.broadcast_to(w_keep.reshape(4, 1, 64, HEAD_DIM), (4, 2, 64, HEAD_DIM))
+    w_x = a2a(w_send.reshape(8, 64, HEAD_DIM), "y")
+    send = jnp.broadcast_to(t_mine.reshape(1, 2, 128, 512), (4, 2, 128, 512))
+    both = a2a(send.reshape(8, 128, 512), "y").reshape(D, 512)
     tokens, grads = both[:, :TILE_TOKENS], both[:, TILE_TOKENS:]
     w_list = jnp.stack([w_x] + [shift(w_x, "x", 4, 1, s) for s in (1, 2, 3)])
+    got = swap(w_list, "c")
+    w_list = jnp.stack([w_list, got], 2).reshape(4, D, HEAD_DIM)
     w_qkv = jnp.concatenate([pick(w_list, (m - x) % 4) for m in range(3)], 1)
     w_out = pick(w_list, (3 - x) % 4)
 
@@ -209,6 +207,9 @@
             dot(grads, attended, 1, 0),
         ]
     ).astype(bf16)
+    dw = dw.reshape(4, 8, 2, 64, HEAD_DIM)
+    got = swap(dw[:, :, 1], "c")
+    dw = (dw[:, :, 0].astype(f32) + got.astype(f32)).astype(bf16)
     total = pick(dw, x).astype(f32)
     for s in (1, 2, 3):
         got = shift(pick(dw, (x - s) % 4), "x", 4, 1, s)
@@ -224,19 +225,16 @@
     attention = join_tiles(back[:, :, :2].astype(bf16))
     token_grads = join_tiles(back[:, :, 2:])
 
-    total = total.reshape(8, 2, 64, 128)
-    got = swap(total[:, 1].astype(bf16), "c")
-    total = (total[:, 0] + got.astype(f32)).astype(bf16).reshape(8, 2, WIDTH, 128)
-    got = swap(total[:, 1], "zh")
-    total = jnp.stack(in_order(total[:, 0], got, zh), 1)
-    total = a2a(total, "y")
+    total = a2a(total.astype(bf16), "y")
     total = jnp.sum(total.reshape(4, 2, 2, WIDTH, 128).astype(f32), 1).astype(bf16)
-    total = total.transpose(1, 0, 2, 3).reshape(1, HEADS, WIDTH, 128)
-    total = jnp.broadcast_to(total, (6, HEADS, WIDTH, 128))
-    total = a2a(total, "zl")
-    total = jnp.sum(total.astype(f32), 0).astype(bf16)
-    total = jnp.stack(in_order(total, swap(total, "x"), x % 2))
-    total = jnp.concatenate(in_order(total, lax.ppermute(total, "x", SWAP_X2), x // 2))
+    total = jnp.stack(in_order(total[:, 0], total[:, 1], zh))
+    total = jnp.broadcast_to(total, (6, 2, 4, WIDTH, 128)).reshape(12, 4, WIDTH, 128)
+    total = a2a(total, ("zl", "zh"))
+    total = jnp.sum(total.reshape(6, HEADS, WIDTH, 128).astype(f32), 0).astype(bf16)
+    got = swap(total, "x")
+    total = jnp.stack(in_order(total, got, x % 2))
+    got = lax.ppermute(total, "x", SWAP_X2)
+    total = jnp.concatenate(in_order(total, got, x // 2))
     weight_grads = total.transpose(2, 0, 1, 3).astype(f32)
     return attention, token_grads, weight_grads
 

time: 259 us -> 241 us (0.931)
  waiting for transfers between devices: 111 us -> 97.7 us
  blocking collectives: 10.3 us -> 0 us
    all_to_all x4 -> x5, waiting for transfers between devices: 63.8 us -> 52.5 us  [a2a(): return lax.all_to_all(v, axes, 0, 0, tiled=True)]
    ppermute x7, starting transfers between devices: 54.7 us -> 43.6 us  [swap(): lax.ppermute(v, axis, [(i, i ^ 1) for i in range(lax.axis_size(axis))])]
    all_to_all x1 -> x0, blocking collectives: 10.3 us -> none  [a2a(): return lax.all_to_all(v, axes, 0, 0, tiled=True)]
    all_to_all x4 -> x5, starting transfers between devices: 16.8 us -> 26.1 us  [a2a(): return lax.all_to_all(v, axes, 0, 0, tiled=True)]
    ppermute x6, waiting for transfers between devices: 15.6 us -> 7.5 us  [shift(): return lax.ppermute(v, axis, pairs)]
    ppermute x7, waiting for transfers between devices: 13.1 us -> 16.8 us  [swap(): lax.ppermute(v, axis, [(i, i ^ 1) for i in range(lax.axis_size(axis))])]
    ppermute x6, starting transfers between devices: 20.8 us -> 23.7 us  [shift(): return lax.ppermute(v, axis, pairs)]
  transfers between devices with their start and end apart: 26 -> 27, of which waited for: 17 -> 18; matrix products, arithmetic and copies ran while one was open for 2% -> 4% of each run, Pallas kernels for 0% -> 0%
where the time goes in v7:
time: 241 us; the launch traced here: 240 us
  starting transfers between devices  120 us (50%)
  waiting for transfers between devices  97.7 us (41%)
  local copies, waits for them, and re-layouts  11.8 us (5%)
  other arithmetic  4.09 us (2%)
  matrix products  4.06 us (2%)
    all_to_all x5, waiting for transfers between devices, a2a(): return lax.all_to_all(v, axes, 0, 0, tiled=True)  52.5 us
    ppermute x7, starting transfers between devices, swap(): lax.ppermute(v, axis, [(i, i ^ 1) for i in range(lax.axis_size(axis))])  43.6 us
    all_to_all x5, starting transfers between devices, a2a(): return lax.all_to_all(v, axes, 0, 0, tiled=True)  26.1 us
    ppermute x6, starting transfers between devices, shift(): return lax.ppermute(v, axis, pairs)  23.7 us
    ppermute x7, waiting for transfers between devices, swap(): lax.ppermute(v, axis, [(i, i ^ 1) for i in range(lax.axis_size(axis))])  16.8 us
    ppermute x2, waiting for transfers between devices, to_up(): return lax.ppermute(v, ('zl', 'x'), UP)  14.5 us
    ppermute x2, starting transfers between devices, to_down(): return lax.ppermute(v, ('zl', 'x'), DOWN)  10.4 us
    ppermute x6, waiting for transfers between devices, shift(): return lax.ppermute(v, axis, pairs)  7.5 us
  transfers between devices with their start and end apart: 27, of which 18 were waited for; matrix products, arithmetic and copies ran while one was open for 4% of the time, Pallas kernels for 0%

profile of v7, /device:TPU:1, one launch (start us, length us, event | category | flops | bytes accessed | tf_op | source)
XLA Modules:
  0.0 239.7 jit_solution(13223200758623619090)
XLA Ops:
  3.4 15.7 %collective-permute-start = (bf16[20,32,128]{2,1,0:T(8,128)(2,1)S(1)}, bf16[20,32,128]{2,1,0:T(8,128)(2,1)S(1)}, u32[]{:S(2)}, u32[]{:S(2)}) collective-permute-start(bf16[20,32,128]{2,1,0:T(8,128)(2,1)S(1)} %pad_maximum_fusion.9), channel_id=1, source_target_pairs={{0,16},{16,0},{1,17},{17,1},{2,18},{18,2},{3,19},{19,3},{4,20},{20... | collective-permute-start | bytes 491528 | tf_op jit(solution)/shard_map/ppermute | solution.py:83
  19.1 5.7 %collective-permute-done = bf16[20,32,128]{2,1,0:T(8,128)(2,1)S(1)} collective-permute-done((bf16[20,32,128]{2,1,0:T(8,128)(2,1)S(1)}, bf16[20,32,128]{2,1,0:T(8,128)(2,1)S(1)}, u32[]{:S(2)}, u32[]{:S(2)}) %collective-permute-start) | collective-permute-done | bytes 163872 | tf_op jit(solution)/shard_map/ppermute | solution.py:83
  25.5 4.5 %collective-permute-start.5 = (bf16[2,4,2,32,128]{4,3,2,1,0:T(8,128)(2,1)S(1)}, bf16[2,4,2,32,128]{4,3,2,1,0:T(8,128)(2,1)S(1)}, u32[]{:S(2)}, u32[]{:S(2)}) collective-permute-start(bf16[2,4,2,32,128]{4,3,2,1,0:T(8,128)(2,1)S(1)} %bitcast.204), channel_id=1, source_target_pairs={{0,1},{1,0},{2,3},{3,2},{4,5},{5,4},{6,7},{7,6},{8,9},{9,8},{10,11... | collective-permute-start | bytes 393224 | tf_op jit(solution)/shard_map/ppermute | solution.py:83
  30.8 3.8 %all-to-all-start = ((bf16[8,64,128]{2,1,0:T(8,128)(2,1)}), bf16[8,64,128]{2,1,0:T(8,128)(2,1)S(1)}, u32[]{:S(2)}, u32[]{:S(2)}) async-start(bf16[8,64,128]{2,1,0:T(8,128)(2,1)} %bitcast.14), calls=%async_computation | async-start | bytes 262144 | tf_op jit(solution)/shard_map/all_to_all | solution.py:65
  35.2 7.8 %all-to-all-done = bf16[8,64,128]{2,1,0:T(8,128)(2,1)S(1)} async-done(((bf16[8,64,128]{2,1,0:T(8,128)(2,1)}), bf16[8,64,128]{2,1,0:T(8,128)(2,1)S(1)}, u32[]{:S(2)}, u32[]{:S(2)}) %all-to-all-start) | async-done | bytes 131104 | tf_op jit(solution)/shard_map/all_to_all | solution.py:65
  44.1 3.6 %all-to-all-start.1 = ((bf16[8,128,512]{2,1,0:T(8,128)(2,1)}), bf16[8,128,512]{2,1,0:T(8,128)(2,1)S(1)}, u32[]{:S(2)}, u32[]{:S(2)}) async-start(bf16[8,128,512]{2,1,0:T(8,128)(2,1)} %bitcast.32), calls=%async_computation.1 | async-start | bytes 2097152 | tf_op jit(solution)/shard_map/all_to_all | solution.py:65
  47.7 3.1 %collective-permute-start.3 = (bf16[8,64,128]{2,1,0:T(8,128)(2,1)S(1)}, bf16[8,64,128]{2,1,0:T(8,128)(2,1)S(1)}, u32[]{:S(2)}, u32[]{:S(2)}) collective-permute-start(bf16[8,64,128]{2,1,0:T(8,128)(2,1)S(1)} %all-to-all-done), channel_id=1, source_target_pairs={{0,32},{32,64},{64,96},{96,0},{1,33},{33,65},{65,97},{97,1},{2,34}... | collective-permute-start | bytes 393224 | tf_op jit(solution)/shard_map/ppermute | solution.py:79
  50.8 4.4 %collective-permute-start.2 = (bf16[8,64,128]{2,1,0:T(8,128)(2,1)S(1)}, bf16[8,64,128]{2,1,0:T(8,128)(2,1)S(1)}, u32[]{:S(2)}, u32[]{:S(2)}) collective-permute-start(bf16[8,64,128]{2,1,0:T(8,128)(2,1)S(1)} %all-to-all-done), channel_id=1, source_target_pairs={{0,64},{32,96},{64,0},{96,32},{1,65},{33,97},{65,1},{97,33},{2,66}... | collective-permute-start | bytes 393224 | tf_op jit(solution)/shard_map/ppermute | solution.py:79
  55.1 3.1 %collective-permute-start.1 = (bf16[8,64,128]{2,1,0:T(8,128)(2,1)S(1)}, bf16[8,64,128]{2,1,0:T(8,128)(2,1)S(1)}, u32[]{:S(2)}, u32[]{:S(2)}) collective-permute-start(bf16[8,64,128]{2,1,0:T(8,128)(2,1)S(1)} %all-to-all-done), channel_id=1, source_target_pairs={{0,96},{32,0},{64,32},{96,64},{1,97},{33,1},{65,33},{97,65},{2,98}... | collective-permute-start | bytes 393224 | tf_op jit(solution)/shard_map/ppermute | solution.py:79
  61.2 4.9 %collective-permute-start.4 = (bf16[4,8,64,128]{3,2,1,0:T(8,128)(2,1)S(1)}, bf16[4,8,64,128]{3,2,1,0:T(8,128)(2,1)S(1)}, u32[]{:S(2)}, u32[]{:S(2)}) collective-permute-start(bf16[4,8,64,128]{3,2,1,0:T(8,128)(2,1)S(1)} %get-tuple-element.34), channel_id=1, source_target_pairs={{0,1},{1,0},{2,3},{3,2},{4,5},{5,4},{6,7},{7,6},{8,9},{9,8},{10,11... | collective-permute-start | bytes 1572872 | tf_op jit(solution)/shard_map/ppermute | solution.py:83
  67.9 8.9 %all-to-all-done.1 = bf16[8,128,512]{2,1,0:T(8,128)(2,1)S(1)} async-done(((bf16[8,128,512]{2,1,0:T(8,128)(2,1)}), bf16[8,128,512]{2,1,0:T(8,128)(2,1)S(1)}, u32[]{:S(2)}, u32[]{:S(2)}) %all-to-all-start.1) | async-done | bytes 1048608 | tf_op jit(solution)/shard_map/all_to_all | solution.py:65
  77.3 2.6 %collective-permute-start.6 = (bf16[16,4,256]{2,1,0:T(4,128)(2,1)S(1)}, bf16[16,4,256]{2,1,0:T(4,128)(2,1)S(1)}, u32[]{:S(2)}, u32[]{:S(2)}) collective-permute-start(bf16[16,4,256]{2,1,0:T(4,128)(2,1)S(1)} %get-tuple-element.51), channel_id=1, source_target_pairs={{0,1},{1,2},{2,3},{3,32},{4,5},{5,6},{6,7},{7,36},{8,9},{9,10},{10... | collective-permute-start | bytes 98312 | tf_op jit(solution)/shard_map/ppermute | solution.py:49
  82.0 3.1 %collective-permute-done.7 = bf16[16,4,256]{2,1,0:T(4,128)(2,1)S(1)} collective-permute-done((bf16[16,4,256]{2,1,0:T(4,128)(2,1)S(1)}, bf16[16,4,256]{2,1,0:T(4,128)(2,1)S(1)}, u32[]{:S(2)}, u32[]{:S(2)}) %collective-permute-start.7) | collective-permute-done | bytes 32800 | tf_op jit(solution)/shard_map/ppermute | solution.py:53
  85.2 4.6 %collective-permute-start.8 = (bf16[4,24,256]{2,1,0:T(8,128)(2,1)S(1)}, bf16[4,24,256]{2,1,0:T(8,128)(2,1)S(1)}, u32[]{:S(2)}, u32[]{:S(2)}) collective-permute-start(bf16[4,24,256]{2,1,0:T(8,128)(2,1)S(1)} %get-tuple-element.47), channel_id=1, source_target_pairs={{0,64},{32,96},{64,128},{96,160},{128,192},{160,224},{192,256},{22... | collective-permute-start | bytes 147464 | tf_op jit(solution)/shard_map/ppermute | solution.py:57
  91.5 8.8 %collective-permute-done.9 = bf16[4,24,256]{2,1,0:T(8,128)(2,1)S(1)} collective-permute-done((bf16[4,24,256]{2,1,0:T(8,128)(2,1)S(1)}, bf16[4,24,256]{2,1,0:T(8,128)(2,1)S(1)}, u32[]{:S(2)}, u32[]{:S(2)}) %collective-permute-start.9) | collective-permute-done | bytes 49184 | tf_op jit(solution)/shard_map/ppermute | solution.py:61
  102.6 5.8 %collective-permute-start.11 = (bf16[4,24,256]{2,1,0:T(8,128)(2,1)S(1)}, bf16[4,24,256]{2,1,0:T(8,128)(2,1)S(1)}, u32[]{:S(2)}, u32[]{:S(2)}) collective-permute-start(bf16[4,24,256]{2,1,0:T(8,128)(2,1)S(1)} %bitcast.211), channel_id=1, source_target_pairs={{0,64},{32,96},{64,128},{96,160},{128,192},{160,224},{192,256},{22... | collective-permute-start | bytes 147464 | tf_op jit(solution)/shard_map/ppermute | solution.py:57
  109.8 5.8 %collective-permute-done.10 = bf16[4,24,256]{2,1,0:T(8,128)(2,1)S(1)} collective-permute-done((bf16[4,24,256]{2,1,0:T(8,128)(2,1)S(1)}, bf16[4,24,256]{2,1,0:T(8,128)(2,1)S(1)}, u32[]{:S(2)}, u32[]{:S(2)}) %collective-permute-start.10) | collective-permute-done | bytes 49184 | tf_op jit(solution)/shard_map/ppermute | solution.py:61
  118.0 3.6 %collective-permute-start.13 = (bf16[16,4,256]{2,1,0:T(4,128)(2,1)S(1)}, bf16[16,4,256]{2,1,0:T(4,128)(2,1)S(1)}, u32[]{:S(2)}, u32[]{:S(2)}) collective-permute-start(bf16[16,4,256]{2,1,0:T(4,128)(2,1)S(1)} %get-tuple-element.46), channel_id=1, source_target_pairs={{0,1},{1,2},{2,3},{3,32},{4,5},{5,6},{6,7},{7,36},{8,9},{9,10},{10... | collective-permute-start | bytes 98312 | tf_op jit(solution)/shard_map/ppermute | solution.py:49
  127.2 8.2 %collective-permute-start.17 = (bf16[8,64,128]{2,1,0:T(8,128)(2,1)S(1)}, bf16[8,64,128]{2,1,0:T(8,128)(2,1)S(1)}, u32[]{:S(2)}, u32[]{:S(2)}) collective-permute-start(bf16[8,64,128]{2,1,0:T(8,128)(2,1)S(1)} %get-tuple-element.26), channel_id=1, source_target_pairs={{0,96},{32,0},{64,32},{96,64},{1,97},{33,1},{65,33},{97,65},{2,98}... | collective-permute-start | bytes 393224 | tf_op jit(solution)/shard_map/ppermute | solution.py:79
  137.4 3.1 %collective-permute-start.18 = (bf16[8,64,128]{2,1,0:T(8,128)(2,1)S(1)}, bf16[8,64,128]{2,1,0:T(8,128)(2,1)S(1)}, u32[]{:S(2)}, u32[]{:S(2)}) collective-permute-start(bf16[8,64,128]{2,1,0:T(8,128)(2,1)S(1)} %get-tuple-element.28), channel_id=1, source_target_pairs={{0,64},{32,96},{64,0},{96,32},{1,65},{33,97},{65,1},{97,33},{2,66}... | collective-permute-start | bytes 393224 | tf_op jit(solution)/shard_map/ppermute | solution.py:79
  146.1 3.4 %all-to-all-start.3 = ((bf16[8,64,128]{2,1,0:T(8,128)(2,1)}), bf16[8,64,128]{2,1,0:T(8,128)(2,1)S(1)}, u32[]{:S(2)}, u32[]{:S(2)}) async-start(bf16[8,64,128]{2,1,0:T(8,128)(2,1)} %fusion.17), calls=%async_computation.3 | async-start | bytes 262144 | tf_op jit(solution)/shard_map/all_to_all | solution.py:65
  151.2 6.2 %all-to-all-done.3 = bf16[8,64,128]{2,1,0:T(8,128)(2,1)S(1)} async-done(((bf16[8,64,128]{2,1,0:T(8,128)(2,1)}), bf16[8,64,128]{2,1,0:T(8,128)(2,1)S(1)}, u32[]{:S(2)}, u32[]{:S(2)}) %all-to-all-start.3) | async-done | bytes 131104 | tf_op jit(solution)/shard_map/all_to_all | solution.py:65
  157.4 3.6 %all-to-all-start.2 = ((bf16[8,128,512]{1,2,0:T(8,128)(2,1)}), bf16[8,128,512]{1,2,0:T(8,128)(2,1)S(1)}, u32[]{:S(2)}, u32[]{:S(2)}) async-start(bf16[8,128,512]{1,2,0:T(8,128)(2,1)} %copy_bitcast_fusion), calls=%async_computation.2 | async-start | bytes 2097152 | tf_op jit(solution)/shard_map/all_to_all | solution.py:65
  161.0 26.9 %all-to-all-done.2 = bf16[8,128,512]{1,2,0:T(8,128)(2,1)S(1)} async-done(((bf16[8,128,512]{1,2,0:T(8,128)(2,1)}), bf16[8,128,512]{1,2,0:T(8,128)(2,1)S(1)}, u32[]{:S(2)}, u32[]{:S(2)}) %all-to-all-start.2) | async-done | bytes 1048608 | tf_op jit(solution)/shard_map/all_to_all | solution.py:65
  188.7 11.8 %all-to-all-start.4 = ((bf16[12,4,32,128]{3,2,1,0:T(8,128)(2,1)}), bf16[12,4,32,128]{3,2,1,0:T(8,128)(2,1)S(1)}, u32[]{:S(2)}, u32[]{:S(2)}) async-start(bf16[12,4,32,128]{3,2,1,0:T(8,128)(2,1)} %bitcast.73), calls=%async_computation.4 | async-start | bytes 786432 | tf_op jit(solution)/shard_map/all_to_all | solution.py:65
  201.2 9.6 %collective-permute-start.14 = (bf16[2,2,4,32,128]{4,2,3,0,1:T(4,128)(2,1)S(1)}, bf16[2,2,4,32,128]{4,2,3,0,1:T(4,128)(2,1)S(1)}, u32[]{:S(2)}, u32[]{:S(2)}) collective-permute-start(bf16[2,2,4,32,128]{4,2,3,0,1:T(4,128)(2,1)S(1)} %fusion.30), channel_id=1, source_target_pairs={{0,16},{16,0},{1,17},{17,1},{2,18},{18,2},{3,19},{19,3},{4,20},{20... | collective-permute-start | bytes 393224 | tf_op jit(solution)/shard_map/ppermute | solution.py:83
  210.8 2.7 %all-to-all-done.4 = bf16[12,4,32,128]{3,2,1,0:T(8,128)(2,1)S(1)} async-done(((bf16[12,4,32,128]{3,2,1,0:T(8,128)(2,1)}), bf16[12,4,32,128]{3,2,1,0:T(8,128)(2,1)S(1)}, u32[]{:S(2)}, u32[]{:S(2)}) %all-to-all-start.4) | async-done | bytes 393248 | tf_op jit(solution)/shard_map/all_to_all | solution.py:65
  213.5 2.5 %collective-permute-start.20 = (bf16[8,32,128]{2,1,0:T(8,128)(2,1)S(1)}, bf16[8,32,128]{2,1,0:T(8,128)(2,1)S(1)}, u32[]{:S(2)}, u32[]{:S(2)}) collective-permute-start(bf16[8,32,128]{2,1,0:T(8,128)(2,1)S(1)} %bitcast_reduce_fusion), channel_id=1, source_target_pairs={{0,32},{32,0},{64,96},{96,64},{1,33},{33,1},{65,97},{97,65},{2,34}... | collective-permute-start | bytes 196616 | tf_op jit(solution)/shard_map/ppermute | solution.py:83
  216.1 9.5 %collective-permute-done.14 = bf16[2,2,4,32,128]{4,2,3,0,1:T(4,128)(2,1)S(1)} collective-permute-done((bf16[2,2,4,32,128]{4,2,3,0,1:T(4,128)(2,1)S(1)}, bf16[2,2,4,32,128]{4,2,3,0,1:T(4,128)(2,1)S(1)}, u32[]{:S(2)}, u32[]{:S(2)}) %collective-permute-start.14) | collective-permute-done | bytes 131104 | tf_op jit(solution)/shard_map/ppermute | solution.py:83
  225.6 4.4 %collective-permute-start.15 = (f32[2,4,32,128]{3,1,2,0:T(4,128)S(1)}, f32[2,4,32,128]{3,1,2,0:T(4,128)S(1)}, u32[]{:S(2)}, u32[]{:S(2)}) collective-permute-start(f32[2,4,32,128]{3,1,2,0:T(4,128)S(1)} %slice_bitcast_fusion.3), channel_id=1, source_target_pairs={{0,1},{1,0},{2,3},{3,2},{4,5},{5,4},{6,7},{7,6},{8,9},{9,8},{10,11... | collective-permute-start | bytes 393224 | tf_op jit(solution)/shard_map/ppermute | solution.py:83
  230.1 3.5 %collective-permute-start.21 = (bf16[2,8,32,128]{3,2,1,0:T(8,128)(2,1)S(1)}, bf16[2,8,32,128]{3,2,1,0:T(8,128)(2,1)S(1)}, u32[]{:S(2)}, u32[]{:S(2)}) collective-permute-start(bf16[2,8,32,128]{3,2,1,0:T(8,128)(2,1)S(1)} %pad_maximum_fusion.11), channel_id=1, source_target_pairs={{0,64},{32,96},{64,0},{96,32},{1,65},{33,97},{65,1},{97,33},{2,66}... | collective-permute-start | bytes 393224 | tf_op jit(solution)/shard_map/ppermute | solution.py:236
  236.1 2.5 %collective-permute-done.21 = bf16[2,8,32,128]{3,2,1,0:T(8,128)(2,1)S(1)} collective-permute-done((bf16[2,8,32,128]{3,2,1,0:T(8,128)(2,1)S(1)}, bf16[2,8,32,128]{3,2,1,0:T(8,128)(2,1)S(1)}, u32[]{:S(2)}, u32[]{:S(2)}) %collective-permute-start.21) | collective-permute-done | bytes 131104 | tf_op jit(solution)/shard_map/ppermute | solution.py:236
  (127 shorter events, 40.5 us)
Async XLA Ops:
  3.4 21.4 %collective-permute-start = (bf16[20,32,128]{2,1,0:T(8,128)(2,1)S(1)}, bf16[20,32,128]{2,1,0:T(8,128)(2,1)S(1)}, u32[]{:S(2)}, u32[]{:S(2)}) collective-permute-start(bf16[20,32,128]{2,1,0:T(8,128)(2,1)S(1)} %pad_maximum_fusion.9), channel_id=1, source_target_pairs={{0,16},{16,0},{1,17},{17,1},{2,18},{18,2},{3,19},{19,3},{4,20},{20... | collective-permute-start | bytes 491528 | tf_op jit(solution)/shard_map/ppermute | solution.py:83
  25.5 9.3 %collective-permute-start.5 = (bf16[2,4,2,32,128]{4,3,2,1,0:T(8,128)(2,1)S(1)}, bf16[2,4,2,32,128]{4,3,2,1,0:T(8,128)(2,1)S(1)}, u32[]{:S(2)}, u32[]{:S(2)}) collective-permute-start(bf16[2,4,2,32,128]{4,3,2,1,0:T(8,128)(2,1)S(1)} %bitcast.204), channel_id=1, source_target_pairs={{0,1},{1,0},{2,3},{3,2},{4,5},{5,4},{6,7},{7,6},{8,9},{9,8},{10,11... | collective-permute-start | bytes 393224 | tf_op jit(solution)/shard_map/ppermute | solution.py:83
  30.8 12.3 %all-to-all-start = ((bf16[8,64,128]{2,1,0:T(8,128)(2,1)}), bf16[8,64,128]{2,1,0:T(8,128)(2,1)S(1)}, u32[]{:S(2)}, u32[]{:S(2)}) async-start(bf16[8,64,128]{2,1,0:T(8,128)(2,1)} %bitcast.14), calls=%async_computation | async-start | bytes 262144 | tf_op jit(solution)/shard_map/all_to_all | solution.py:65
  44.1 32.7 %all-to-all-start.1 = ((bf16[8,128,512]{2,1,0:T(8,128)(2,1)}), bf16[8,128,512]{2,1,0:T(8,128)(2,1)S(1)}, u32[]{:S(2)}, u32[]{:S(2)}) async-start(bf16[8,128,512]{2,1,0:T(8,128)(2,1)} %bitcast.32), calls=%async_computation.1 | async-start | bytes 2097152 | tf_op jit(solution)/shard_map/all_to_all | solution.py:65
  47.7 10.6 %collective-permute-start.3 = (bf16[8,64,128]{2,1,0:T(8,128)(2,1)S(1)}, bf16[8,64,128]{2,1,0:T(8,128)(2,1)S(1)}, u32[]{:S(2)}, u32[]{:S(2)}) collective-permute-start(bf16[8,64,128]{2,1,0:T(8,128)(2,1)S(1)} %all-to-all-done), channel_id=1, source_target_pairs={{0,32},{32,64},{64,96},{96,0},{1,33},{33,65},{65,97},{97,1},{2,34}... | collective-permute-start | bytes 393224 | tf_op jit(solution)/shard_map/ppermute | solution.py:79
  50.8 8.6 %collective-permute-start.2 = (bf16[8,64,128]{2,1,0:T(8,128)(2,1)S(1)}, bf16[8,64,128]{2,1,0:T(8,128)(2,1)S(1)}, u32[]{:S(2)}, u32[]{:S(2)}) collective-permute-start(bf16[8,64,128]{2,1,0:T(8,128)(2,1)S(1)} %all-to-all-done), channel_id=1, source_target_pairs={{0,64},{32,96},{64,0},{96,32},{1,65},{33,97},{65,1},{97,33},{2,66}... | collective-permute-start | bytes 393224 | tf_op jit(solution)/shard_map/ppermute | solution.py:79
  55.1 6.0 %collective-permute-start.1 = (bf16[8,64,128]{2,1,0:T(8,128)(2,1)S(1)}, bf16[8,64,128]{2,1,0:T(8,128)(2,1)S(1)}, u32[]{:S(2)}, u32[]{:S(2)}) collective-permute-start(bf16[8,64,128]{2,1,0:T(8,128)(2,1)S(1)} %all-to-all-done), channel_id=1, source_target_pairs={{0,96},{32,0},{64,32},{96,64},{1,97},{33,1},{65,33},{97,65},{2,98}... | collective-permute-start | bytes 393224 | tf_op jit(solution)/shard_map/ppermute | solution.py:79
  61.2 6.4 %collective-permute-start.4 = (bf16[4,8,64,128]{3,2,1,0:T(8,128)(2,1)S(1)}, bf16[4,8,64,128]{3,2,1,0:T(8,128)(2,1)S(1)}, u32[]{:S(2)}, u32[]{:S(2)}) collective-permute-start(bf16[4,8,64,128]{3,2,1,0:T(8,128)(2,1)S(1)} %get-tuple-element.34), channel_id=1, source_target_pairs={{0,1},{1,0},{2,3},{3,2},{4,5},{5,4},{6,7},{7,6},{8,9},{9,8},{10,11... | collective-permute-start | bytes 1572872 | tf_op jit(solution)/shard_map/ppermute | solution.py:83
  77.3 4.7 %collective-permute-start.6 = (bf16[16,4,256]{2,1,0:T(4,128)(2,1)S(1)}, bf16[16,4,256]{2,1,0:T(4,128)(2,1)S(1)}, u32[]{:S(2)}, u32[]{:S(2)}) collective-permute-start(bf16[16,4,256]{2,1,0:T(4,128)(2,1)S(1)} %get-tuple-element.51), channel_id=1, source_target_pairs={{0,1},{1,2},{2,3},{3,32},{4,5},{5,6},{6,7},{7,36},{8,9},{9,10},{10... | collective-permute-start | bytes 98312 | tf_op jit(solution)/shard_map/ppermute | solution.py:49
  79.9 5.2 %collective-permute-start.7 = (bf16[16,4,256]{2,1,0:T(4,128)(2,1)S(1)}, bf16[16,4,256]{2,1,0:T(4,128)(2,1)S(1)}, u32[]{:S(2)}, u32[]{:S(2)}) collective-permute-start(bf16[16,4,256]{2,1,0:T(4,128)(2,1)S(1)} %get-tuple-element.52), channel_id=1, source_target_pairs={{1,0},{2,1},{3,2},{32,3},{5,4},{6,5},{7,6},{36,7},{9,8},{10,9},{11... | collective-permute-start | bytes 98312 | tf_op jit(solution)/shard_map/ppermute | solution.py:53
  85.2 6.3 %collective-permute-start.8 = (bf16[4,24,256]{2,1,0:T(8,128)(2,1)S(1)}, bf16[4,24,256]{2,1,0:T(8,128)(2,1)S(1)}, u32[]{:S(2)}, u32[]{:S(2)}) collective-permute-start(bf16[4,24,256]{2,1,0:T(8,128)(2,1)S(1)} %get-tuple-element.47), channel_id=1, source_target_pairs={{0,64},{32,96},{64,128},{96,160},{128,192},{160,224},{192,256},{22... | collective-permute-start | bytes 147464 | tf_op jit(solution)/shard_map/ppermute | solution.py:57
  89.8 10.4 %collective-permute-start.9 = (bf16[4,24,256]{2,1,0:T(8,128)(2,1)S(1)}, bf16[4,24,256]{2,1,0:T(8,128)(2,1)S(1)}, u32[]{:S(2)}, u32[]{:S(2)}) collective-permute-start(bf16[4,24,256]{2,1,0:T(8,128)(2,1)S(1)} %get-tuple-element.48), channel_id=1, source_target_pairs={{64,0},{96,32},{128,64},{160,96},{192,128},{224,160},{256,192},{28... | collective-permute-start | bytes 147464 | tf_op jit(solution)/shard_map/ppermute | solution.py:61
  102.1 19.5 %copy-start.6 = (bf16[256,128]{0,1:T(8,128)(2,1)}, bf16[256,128]{0,1:T(8,128)(2,1)S(1)}, u32[]{:S(2)}) copy-start(bf16[256,128]{0,1:T(8,128)(2,1)S(1)} %convolution_convert_fusion.8) | copy-start | bytes 196612
  102.6 7.1 %collective-permute-start.11 = (bf16[4,24,256]{2,1,0:T(8,128)(2,1)S(1)}, bf16[4,24,256]{2,1,0:T(8,128)(2,1)S(1)}, u32[]{:S(2)}, u32[]{:S(2)}) collective-permute-start(bf16[4,24,256]{2,1,0:T(8,128)(2,1)S(1)} %bitcast.211), channel_id=1, source_target_pairs={{0,64},{32,96},{64,128},{96,160},{128,192},{160,224},{192,256},{22... | collective-permute-start | bytes 147464 | tf_op jit(solution)/shard_map/ppermute | solution.py:57
  108.4 7.1 %collective-permute-start.10 = (bf16[4,24,256]{2,1,0:T(8,128)(2,1)S(1)}, bf16[4,24,256]{2,1,0:T(8,128)(2,1)S(1)}, u32[]{:S(2)}, u32[]{:S(2)}) collective-permute-start(bf16[4,24,256]{2,1,0:T(8,128)(2,1)S(1)} %bitcast.210), channel_id=1, source_target_pairs={{64,0},{96,32},{128,64},{160,96},{192,128},{224,160},{256,192},{28... | collective-permute-start | bytes 147464 | tf_op jit(solution)/shard_map/ppermute | solution.py:61
  115.6 6.3 %collective-permute-start.12 = (bf16[16,4,256]{2,1,0:T(4,128)(2,1)S(1)}, bf16[16,4,256]{2,1,0:T(4,128)(2,1)S(1)}, u32[]{:S(2)}, u32[]{:S(2)}) collective-permute-start(bf16[16,4,256]{2,1,0:T(4,128)(2,1)S(1)} %get-tuple-element.45), channel_id=1, source_target_pairs={{1,0},{2,1},{3,2},{32,3},{5,4},{6,5},{7,6},{36,7},{9,8},{10,9},{11... | collective-permute-start | bytes 98312 | tf_op jit(solution)/shard_map/ppermute | solution.py:53
  118.0 4.6 %collective-permute-start.13 = (bf16[16,4,256]{2,1,0:T(4,128)(2,1)S(1)}, bf16[16,4,256]{2,1,0:T(4,128)(2,1)S(1)}, u32[]{:S(2)}, u32[]{:S(2)}) collective-permute-start(bf16[16,4,256]{2,1,0:T(4,128)(2,1)S(1)} %get-tuple-element.46), channel_id=1, source_target_pairs={{0,1},{1,2},{2,3},{3,32},{4,5},{5,6},{6,7},{7,36},{8,9},{9,10},{10... | collective-permute-start | bytes 98312 | tf_op jit(solution)/shard_map/ppermute | solution.py:49
  123.2 3.8 %collective-permute-start.16 = (bf16[4,8,64,128]{3,2,1,0:T(8,128)(2,1)S(1)}, bf16[4,8,64,128]{3,2,1,0:T(8,128)(2,1)S(1)}, u32[]{:S(2)}, u32[]{:S(2)}) collective-permute-start(bf16[4,8,64,128]{3,2,1,0:T(8,128)(2,1)S(1)} %slice_bitcast_fusion), channel_id=1, source_target_pairs={{0,1},{1,0},{2,3},{3,2},{4,5},{5,4},{6,7},{7,6},{8,9},{9,8},{10,11... | collective-permute-start | bytes 1572872 | tf_op jit(solution)/shard_map/ppermute | solution.py:83
  126.7 13.7 %copy-start.5 = (bf16[256,128]{1,0:T(8,128)(2,1)S(1)}, bf16[256,128]{1,0:T(8,128)(2,1)}, u32[]{:S(2)}) copy-start(bf16[256,128]{1,0:T(8,128)(2,1)} %copy-done.4) | copy-start | bytes 196612
  127.2 22.3 %copy-start.1 = (bf16[1024,128]{1,0:T(8,128)(2,1)S(1)}, bf16[1024,128]{1,0:T(8,128)(2,1)}, u32[]{:S(2)}) copy-start(bf16[1024,128]{1,0:T(8,128)(2,1)} %copy-done) | copy-start | bytes 786436
  127.2 22.3 %copy-start.3 = (bf16[1024,128]{1,0:T(8,128)(2,1)S(1)}, bf16[1024,128]{1,0:T(8,128)(2,1)}, u32[]{:S(2)}) copy-start(bf16[1024,128]{1,0:T(8,128)(2,1)} %copy-done.2) | copy-start | bytes 786436
  127.2 22.3 %copy-start.8 = (bf16[256,128]{1,0:T(8,128)(2,1)S(1)}, bf16[256,128]{1,0:T(8,128)(2,1)}, u32[]{:S(2)}) copy-start(bf16[256,128]{1,0:T(8,128)(2,1)} %copy.171) | copy-start | bytes 196612
  127.2 13.5 %collective-permute-start.17 = (bf16[8,64,128]{2,1,0:T(8,128)(2,1)S(1)}, bf16[8,64,128]{2,1,0:T(8,128)(2,1)S(1)}, u32[]{:S(2)}, u32[]{:S(2)}) collective-permute-start(bf16[8,64,128]{2,1,0:T(8,128)(2,1)S(1)} %get-tuple-element.26), channel_id=1, source_target_pairs={{0,96},{32,0},{64,32},{96,64},{1,97},{33,1},{65,33},{97,65},{2,98}... | collective-permute-start | bytes 393224 | tf_op jit(solution)/shard_map/ppermute | solution.py:79
  135.4 7.6 %collective-permute-start.19 = (bf16[8,64,128]{2,1,0:T(8,128)(2,1)S(1)}, bf16[8,64,128]{2,1,0:T(8,128)(2,1)S(1)}, u32[]{:S(2)}, u32[]{:S(2)}) collective-permute-start(bf16[8,64,128]{2,1,0:T(8,128)(2,1)S(1)} %get-tuple-element.27), channel_id=1, source_target_pairs={{0,32},{32,64},{64,96},{96,0},{1,33},{33,65},{65,97},{97,1},{2,34}... | collective-permute-start | bytes 393224 | tf_op jit(solution)/shard_map/ppermute | solution.py:79
  137.4 8.0 %collective-permute-start.18 = (bf16[8,64,128]{2,1,0:T(8,128)(2,1)S(1)}, bf16[8,64,128]{2,1,0:T(8,128)(2,1)S(1)}, u32[]{:S(2)}, u32[]{:S(2)}) collective-permute-start(bf16[8,64,128]{2,1,0:T(8,128)(2,1)S(1)} %get-tuple-element.28), channel_id=1, source_target_pairs={{0,64},{32,96},{64,0},{96,32},{1,65},{33,97},{65,1},{97,33},{2,66}... | collective-permute-start | bytes 393224 | tf_op jit(solution)/shard_map/ppermute | solution.py:79
  146.1 11.3 %all-to-all-start.3 = ((bf16[8,64,128]{2,1,0:T(8,128)(2,1)}), bf16[8,64,128]{2,1,0:T(8,128)(2,1)S(1)}, u32[]{:S(2)}, u32[]{:S(2)}) async-start(bf16[8,64,128]{2,1,0:T(8,128)(2,1)} %fusion.17), calls=%async_computation.3 | async-start | bytes 262144 | tf_op jit(solution)/shard_map/all_to_all | solution.py:65
  157.4 30.5 %all-to-all-start.2 = ((bf16[8,128,512]{1,2,0:T(8,128)(2,1)}), bf16[8,128,512]{1,2,0:T(8,128)(2,1)S(1)}, u32[]{:S(2)}, u32[]{:S(2)}) async-start(bf16[8,128,512]{1,2,0:T(8,128)(2,1)} %copy_bitcast_fusion), calls=%async_computation.2 | async-start | bytes 2097152 | tf_op jit(solution)/shard_map/all_to_all | solution.py:65
  188.7 24.8 %all-to-all-start.4 = ((bf16[12,4,32,128]{3,2,1,0:T(8,128)(2,1)}), bf16[12,4,32,128]{3,2,1,0:T(8,128)(2,1)S(1)}, u32[]{:S(2)}, u32[]{:S(2)}) async-start(bf16[12,4,32,128]{3,2,1,0:T(8,128)(2,1)} %bitcast.73), calls=%async_computation.4 | async-start | bytes 786432 | tf_op jit(solution)/shard_map/all_to_all | solution.py:65
  201.2 24.4 %collective-permute-start.14 = (bf16[2,2,4,32,128]{4,2,3,0,1:T(4,128)(2,1)S(1)}, bf16[2,2,4,32,128]{4,2,3,0,1:T(4,128)(2,1)S(1)}, u32[]{:S(2)}, u32[]{:S(2)}) collective-permute-start(bf16[2,2,4,32,128]{4,2,3,0,1:T(4,128)(2,1)S(1)} %fusion.30), channel_id=1, source_target_pairs={{0,16},{16,0},{1,17},{17,1},{2,18},{18,2},{3,19},{19,3},{4,20},{20... | collective-permute-start | bytes 393224 | tf_op jit(solution)/shard_map/ppermute | solution.py:83
  213.5 16.5 %collective-permute-start.20 = (bf16[8,32,128]{2,1,0:T(8,128)(2,1)S(1)}, bf16[8,32,128]{2,1,0:T(8,128)(2,1)S(1)}, u32[]{:S(2)}, u32[]{:S(2)}) collective-permute-start(bf16[8,32,128]{2,1,0:T(8,128)(2,1)S(1)} %bitcast_reduce_fusion), channel_id=1, source_target_pairs={{0,32},{32,0},{64,96},{96,64},{1,33},{33,1},{65,97},{97,65},{2,34}... | collective-permute-start | bytes 196616 | tf_op jit(solution)/shard_map/ppermute | solution.py:83
  225.6 7.9 %collective-permute-start.15 = (f32[2,4,32,128]{3,1,2,0:T(4,128)S(1)}, f32[2,4,32,128]{3,1,2,0:T(4,128)S(1)}, u32[]{:S(2)}, u32[]{:S(2)}) collective-permute-start(f32[2,4,32,128]{3,1,2,0:T(4,128)S(1)} %slice_bitcast_fusion.3), channel_id=1, source_target_pairs={{0,1},{1,0},{2,3},{3,2},{4,5},{5,4},{6,7},{7,6},{8,9},{9,8},{10,11... | collective-permute-start | bytes 393224 | tf_op jit(solution)/shard_map/ppermute | solution.py:83
  230.1 8.4 %collective-permute-start.21 = (bf16[2,8,32,128]{3,2,1,0:T(8,128)(2,1)S(1)}, bf16[2,8,32,128]{3,2,1,0:T(8,128)(2,1)S(1)}, u32[]{:S(2)}, u32[]{:S(2)}) collective-permute-start(bf16[2,8,32,128]{3,2,1,0:T(8,128)(2,1)S(1)} %pad_maximum_fusion.11), channel_id=1, source_target_pairs={{0,64},{32,96},{64,0},{96,32},{1,65},{33,97},{65,1},{97,33},{2,66}... | collective-permute-start | bytes 393224 | tf_op jit(solution)/shard_map/ppermute | solution.py:236
  (4 other events, 22.2 us)

commit v8 on v7

--- a/solution.py
+++ b/solution.py
@@ -42,7 +42,6 @@
 LEFT = [(b, a) for a, b in RIGHT]
 DOWN = [(t, t + 2) for t in range(22)]
 UP = [(t + 2, t) for t in range(22)]
-SWAP_X2 = [(i, i ^ 2) for i in range(4)]
 
 
 def to_right(v):
@@ -133,9 +132,13 @@
 
     w_send = jnp.broadcast_to(w_keep.reshape(4, 1, 64, HEAD_DIM), (4, 2, 64, HEAD_DIM))
     w_x = a2a(w_send.reshape(8, 64, HEAD_DIM), "y")
-    send = jnp.broadcast_to(t_mine.reshape(1, 2, 128, 512), (4, 2, 128, 512))
-    both = a2a(send.reshape(8, 128, 512), "y").reshape(D, 512)
-    tokens, grads = both[:, :TILE_TOKENS], both[:, TILE_TOKENS:]
+
+    def gather(v):
+        send = jnp.broadcast_to(v.reshape(1, 2, 128, TILE_TOKENS), (4, 2, 128, TILE_TOKENS))
+        return a2a(send.reshape(8, 128, TILE_TOKENS), "y").reshape(D, TILE_TOKENS)
+
+    tokens = gather(t_mine[:, :, :2])
+    grads = gather(t_mine[:, :, 2:])
     w_list = jnp.stack([w_x] + [shift(w_x, "x", 4, 1, s) for s in (1, 2, 3)])
     got = swap(w_list, "c")
     w_list = jnp.stack([w_list, got], 2).reshape(4, D, HEAD_DIM)
@@ -228,13 +231,14 @@
     total = a2a(total.astype(bf16), "y")
     total = jnp.sum(total.reshape(4, 2, 2, WIDTH, 128).astype(f32), 1).astype(bf16)
     total = jnp.stack(in_order(total[:, 0], total[:, 1], zh))
-    total = jnp.broadcast_to(total, (6, 2, 4, WIDTH, 128)).reshape(12, 4, WIDTH, 128)
+    total = jnp.pad(total.reshape(2, 128, 128), ((0, 0), (0, 16), (0, 0)))
+    total = total.reshape(2, 6, 24, 128).transpose(1, 0, 2, 3).reshape(12, 24, 128)
     total = a2a(total, ("zl", "zh"))
-    total = jnp.sum(total.reshape(6, HEADS, WIDTH, 128).astype(f32), 0).astype(bf16)
-    got = swap(total, "x")
-    total = jnp.stack(in_order(total, got, x % 2))
-    got = lax.ppermute(total, "x", SWAP_X2)
-    total = jnp.concatenate(in_order(total, got, x // 2))
+    total = jnp.sum(total.reshape(6, 1, 48, 128).astype(f32), 0).astype(bf16)
+    total = jnp.broadcast_to(total, (24, 48, 128))
+    total = a2a(total, ("zl", "x"))
+    total = total.reshape(6, 4, 2, 24, 128).transpose(1, 2, 0, 3, 4).reshape(4, 2, 144, 128)
+    total = total[:, :, :128].reshape(4, HEADS, WIDTH, 128)
     weight_grads = total.transpose(2, 0, 1, 3).astype(f32)
     return attention, token_grads, weight_grads
 

time: 241 us -> 252 us (1.046)
  starting transfers between devices: 120 us -> 131 us
    all_to_all x5 -> x7, starting transfers between devices: 26.1 us -> 39.1 us  [a2a(): return lax.all_to_all(v, axes, 0, 0, tiled=True)]
    all_to_all x5 -> x7, waiting for transfers between devices: 52.5 us -> 62.1 us  [a2a(): return lax.all_to_all(v, axes, 0, 0, tiled=True)]
    ppermute x7 -> x6, waiting for transfers between devices: 16.8 us -> 10.4 us  [swap(): lax.ppermute(v, axis, [(i, i ^ 1) for i in range(lax.axis_size(axis))])]
    ppermute x2, starting transfers between devices: 6.15 us -> 11.1 us  [to_right(): return lax.ppermute(v, ('x', 'y', 'c'), RIGHT)]
    ppermute x6, waiting for transfers between devices: 7.5 us -> 3.64 us  [shift(): return lax.ppermute(v, axis, pairs)]
    ppermute x6, starting transfers between devices: 23.7 us -> 19.9 us  [shift(): return lax.ppermute(v, axis, pairs)]
    ppermute x1 -> x0, starting transfers between devices: 3.48 us -> none  [work(): got = lax.ppermute(total, 'x', SWAP_X2)]
    ppermute x7 -> x6, starting transfers between devices: 43.6 us -> 46 us  [swap(): lax.ppermute(v, axis, [(i, i ^ 1) for i in range(lax.axis_size(axis))])]
  transfers between devices with their start and end apart: 27 -> 27, of which waited for: 18 -> 16; matrix products, arithmetic and copies ran while one was open for 4% -> 4% of each run, Pallas kernels for 0% -> 0%
where the time goes in v8:
time: 252 us; the launch traced here: 251 us
  starting transfers between devices  131 us (52%)
  waiting for transfers between devices  97.6 us (39%)
  local copies, waits for them, and re-layouts  12.9 us (5%)
  matrix products  4.06 us (2%)
  other arithmetic  3.99 us (2%)
    all_to_all x7, waiting for transfers between devices, a2a(): return lax.all_to_all(v, axes, 0, 0, tiled=True)  62.1 us
    ppermute x6, starting transfers between devices, swap(): lax.ppermute(v, axis, [(i, i ^ 1) for i in range(lax.axis_size(axis))])  46 us
    all_to_all x7, starting transfers between devices, a2a(): return lax.all_to_all(v, axes, 0, 0, tiled=True)  39.1 us
    ppermute x6, starting transfers between devices, shift(): return lax.ppermute(v, axis, pairs)  19.9 us
    ppermute x2, waiting for transfers between devices, to_up(): return lax.ppermute(v, ('zl', 'x'), UP)  15.9 us
    ppermute x2, starting transfers between devices, to_right(): return lax.ppermute(v, ('x', 'y', 'c'), RIGHT)  11.1 us
    ppermute x6, waiting for transfers between devices, swap(): lax.ppermute(v, axis, [(i, i ^ 1) for i in range(lax.axis_size(axis))])  10.4 us
    ppermute x2, starting transfers between devices, to_down(): return lax.ppermute(v, ('zl', 'x'), DOWN)  7.9 us
  transfers between devices with their start and end apart: 27, of which 16 were waited for; matrix products, arithmetic and copies ran while one was open for 4% of the time, Pallas kernels for 0%

profile of v8, /device:TPU:1, one launch (start us, length us, event | category | flops | bytes accessed | tf_op | source)
XLA Modules:
  0.0 250.7 jit_solution(9068498543572745207)
XLA Ops:
  3.4 15.7 %collective-permute-start = (bf16[20,32,128]{2,1,0:T(8,128)(2,1)S(1)}, bf16[20,32,128]{2,1,0:T(8,128)(2,1)S(1)}, u32[]{:S(2)}, u32[]{:S(2)}) collective-permute-start(bf16[20,32,128]{2,1,0:T(8,128)(2,1)S(1)} %pad_maximum_fusion.9), channel_id=1, source_target_pairs={{0,16},{16,0},{1,17},{17,1},{2,18},{18,2},{3,19},{19,3},{4,20},{20... | collective-permute-start | bytes 491528 | tf_op jit(solution)/shard_map/ppermute | solution.py:82
  19.1 5.7 %collective-permute-done = bf16[20,32,128]{2,1,0:T(8,128)(2,1)S(1)} collective-permute-done((bf16[20,32,128]{2,1,0:T(8,128)(2,1)S(1)}, bf16[20,32,128]{2,1,0:T(8,128)(2,1)S(1)}, u32[]{:S(2)}, u32[]{:S(2)}) %collective-permute-start) | collective-permute-done | bytes 163872 | tf_op jit(solution)/shard_map/ppermute | solution.py:82
  25.5 4.5 %collective-permute-start.5 = (bf16[2,4,2,32,128]{4,3,2,1,0:T(8,128)(2,1)S(1)}, bf16[2,4,2,32,128]{4,3,2,1,0:T(8,128)(2,1)S(1)}, u32[]{:S(2)}, u32[]{:S(2)}) collective-permute-start(bf16[2,4,2,32,128]{4,3,2,1,0:T(8,128)(2,1)S(1)} %bitcast.218), channel_id=1, source_target_pairs={{0,1},{1,0},{2,3},{3,2},{4,5},{5,4},{6,7},{7,6},{8,9},{9,8},{10,11... | collective-permute-start | bytes 393224 | tf_op jit(solution)/shard_map/ppermute | solution.py:82
  30.8 3.8 %all-to-all-start = ((bf16[8,64,128]{2,1,0:T(8,128)(2,1)}), bf16[8,64,128]{2,1,0:T(8,128)(2,1)S(1)}, u32[]{:S(2)}, u32[]{:S(2)}) async-start(bf16[8,64,128]{2,1,0:T(8,128)(2,1)} %bitcast.14), calls=%async_computation | async-start | bytes 262144 | tf_op jit(solution)/shard_map/all_to_all | solution.py:64
  34.8 8.2 %all-to-all-done = bf16[8,64,128]{2,1,0:T(8,128)(2,1)S(1)} async-done(((bf16[8,64,128]{2,1,0:T(8,128)(2,1)}), bf16[8,64,128]{2,1,0:T(8,128)(2,1)S(1)}, u32[]{:S(2)}, u32[]{:S(2)}) %all-to-all-start) | async-done | bytes 131104 | tf_op jit(solution)/shard_map/all_to_all | solution.py:64
  43.0 3.1 %collective-permute-start.3 = (bf16[8,64,128]{2,1,0:T(8,128)(2,1)S(1)}, bf16[8,64,128]{2,1,0:T(8,128)(2,1)S(1)}, u32[]{:S(2)}, u32[]{:S(2)}) collective-permute-start(bf16[8,64,128]{2,1,0:T(8,128)(2,1)S(1)} %all-to-all-done), channel_id=1, source_target_pairs={{0,32},{32,64},{64,96},{96,0},{1,33},{33,65},{65,97},{97,1},{2,34}... | collective-permute-start | bytes 393224 | tf_op jit(solution)/shard_map/ppermute | solution.py:78
  46.1 4.4 %collective-permute-start.2 = (bf16[8,64,128]{2,1,0:T(8,128)(2,1)S(1)}, bf16[8,64,128]{2,1,0:T(8,128)(2,1)S(1)}, u32[]{:S(2)}, u32[]{:S(2)}) collective-permute-start(bf16[8,64,128]{2,1,0:T(8,128)(2,1)S(1)} %all-to-all-done), channel_id=1, source_target_pairs={{0,64},{32,96},{64,0},{96,32},{1,65},{33,97},{65,1},{97,33},{2,66}... | collective-permute-start | bytes 393224 | tf_op jit(solution)/shard_map/ppermute | solution.py:78
  50.5 3.1 %collective-permute-start.1 = (bf16[8,64,128]{2,1,0:T(8,128)(2,1)S(1)}, bf16[8,64,128]{2,1,0:T(8,128)(2,1)S(1)}, u32[]{:S(2)}, u32[]{:S(2)}) collective-permute-start(bf16[8,64,128]{2,1,0:T(8,128)(2,1)S(1)} %all-to-all-done), channel_id=1, source_target_pairs={{0,96},{32,0},{64,32},{96,64},{1,97},{33,1},{65,33},{97,65},{2,98}... | collective-permute-start | bytes 393224 | tf_op jit(solution)/shard_map/ppermute | solution.py:78
  54.7 3.5 %all-to-all-start.1 = ((bf16[8,128,256]{2,1,0:T(8,128)(2,1)}), bf16[8,128,256]{2,1,0:T(8,128)(2,1)S(1)}, u32[]{:S(2)}, u32[]{:S(2)}) async-start(bf16[8,128,256]{2,1,0:T(8,128)(2,1)} %bitcast.32), calls=%async_computation.1 | async-start | bytes 1048576 | tf_op jit(solution)/shard_map/all_to_all | solution.py:64
  58.3 4.3 %collective-permute-start.4 = (bf16[4,8,64,128]{3,2,1,0:T(8,128)(2,1)S(1)}, bf16[4,8,64,128]{3,2,1,0:T(8,128)(2,1)S(1)}, u32[]{:S(2)}, u32[]{:S(2)}) collective-permute-start(bf16[4,8,64,128]{3,2,1,0:T(8,128)(2,1)S(1)} %get-tuple-element.31), channel_id=1, source_target_pairs={{0,1},{1,0},{2,3},{3,2},{4,5},{5,4},{6,7},{7,6},{8,9},{9,8},{10,11... | collective-permute-start | bytes 1572872 | tf_op jit(solution)/shard_map/ppermute | solution.py:82
  64.2 9.1 %all-to-all-done.1 = bf16[8,128,256]{2,1,0:T(8,128)(2,1)S(1)} async-done(((bf16[8,128,256]{2,1,0:T(8,128)(2,1)}), bf16[8,128,256]{2,1,0:T(8,128)(2,1)S(1)}, u32[]{:S(2)}, u32[]{:S(2)}) %all-to-all-start.1) | async-done | bytes 524320 | tf_op jit(solution)/shard_map/all_to_all | solution.py:64
  74.2 3.5 %all-to-all-start.2 = ((bf16[8,128,256]{2,1,0:T(8,128)(2,1)}), bf16[8,128,256]{2,1,0:T(8,128)(2,1)S(1)}, u32[]{:S(2)}, u32[]{:S(2)}) async-start(bf16[8,128,256]{2,1,0:T(8,128)(2,1)} %bitcast.41), calls=%async_computation.2 | async-start | bytes 1048576 | tf_op jit(solution)/shard_map/all_to_all | solution.py:64
  78.6 6.6 %collective-permute-start.6 = (bf16[16,4,256]{2,1,0:T(4,128)(2,1)S(1)}, bf16[16,4,256]{2,1,0:T(4,128)(2,1)S(1)}, u32[]{:S(2)}, u32[]{:S(2)}) collective-permute-start(bf16[16,4,256]{2,1,0:T(4,128)(2,1)S(1)} %get-tuple-element.46), channel_id=1, source_target_pairs={{0,1},{1,2},{2,3},{3,32},{4,5},{5,6},{6,7},{7,36},{8,9},{9,10},{10... | collective-permute-start | bytes 98312 | tf_op jit(solution)/shard_map/ppermute | solution.py:48
  87.3 4.8 %collective-permute-done.7 = bf16[16,4,256]{2,1,0:T(4,128)(2,1)S(1)} collective-permute-done((bf16[16,4,256]{2,1,0:T(4,128)(2,1)S(1)}, bf16[16,4,256]{2,1,0:T(4,128)(2,1)S(1)}, u32[]{:S(2)}, u32[]{:S(2)}) %collective-permute-start.7) | collective-permute-done | bytes 32800 | tf_op jit(solution)/shard_map/ppermute | solution.py:52
  92.2 2.1 collective-permute-start.8
  96.0 11.3 %collective-permute-done.9 = bf16[4,24,256]{2,1,0:T(8,128)(2,1)S(1)} collective-permute-done((bf16[4,24,256]{2,1,0:T(8,128)(2,1)S(1)}, bf16[4,24,256]{2,1,0:T(8,128)(2,1)S(1)}, u32[]{:S(2)}, u32[]{:S(2)}) %collective-permute-start.9) | collective-permute-done | bytes 49184 | tf_op jit(solution)/shard_map/ppermute | solution.py:60
  109.3 5.8 %collective-permute-start.11 = (bf16[4,24,256]{2,1,0:T(8,128)(2,1)S(1)}, bf16[4,24,256]{2,1,0:T(8,128)(2,1)S(1)}, u32[]{:S(2)}, u32[]{:S(2)}) collective-permute-start(bf16[4,24,256]{2,1,0:T(8,128)(2,1)S(1)} %bitcast.225), channel_id=1, source_target_pairs={{0,64},{32,96},{64,128},{96,160},{128,192},{160,224},{192,256},{22... | collective-permute-start | bytes 147464 | tf_op jit(solution)/shard_map/ppermute | solution.py:56
  116.7 4.7 %collective-permute-done.10 = bf16[4,24,256]{2,1,0:T(8,128)(2,1)S(1)} collective-permute-done((bf16[4,24,256]{2,1,0:T(8,128)(2,1)S(1)}, bf16[4,24,256]{2,1,0:T(8,128)(2,1)S(1)}, u32[]{:S(2)}, u32[]{:S(2)}) %collective-permute-start.10) | collective-permute-done | bytes 49184 | tf_op jit(solution)/shard_map/ppermute | solution.py:60
  123.4 4.5 %collective-permute-start.13 = (bf16[16,4,256]{2,1,0:T(4,128)(2,1)S(1)}, bf16[16,4,256]{2,1,0:T(4,128)(2,1)S(1)}, u32[]{:S(2)}, u32[]{:S(2)}) collective-permute-start(bf16[16,4,256]{2,1,0:T(4,128)(2,1)S(1)} %get-tuple-element.43), channel_id=1, source_target_pairs={{0,1},{1,2},{2,3},{3,32},{4,5},{5,6},{6,7},{7,36},{8,9},{9,10},{10... | collective-permute-start | bytes 98312 | tf_op jit(solution)/shard_map/ppermute | solution.py:48
  133.6 4.2 %collective-permute-start.17 = (bf16[8,64,128]{2,1,0:T(8,128)(2,1)S(1)}, bf16[8,64,128]{2,1,0:T(8,128)(2,1)S(1)}, u32[]{:S(2)}, u32[]{:S(2)}) collective-permute-start(bf16[8,64,128]{2,1,0:T(8,128)(2,1)S(1)} %get-tuple-element.23), channel_id=1, source_target_pairs={{0,96},{32,0},{64,32},{96,64},{1,97},{33,1},{65,33},{97,65},{2,98}... | collective-permute-start | bytes 393224 | tf_op jit(solution)/shard_map/ppermute | solution.py:78
  139.7 3.3 %collective-permute-start.18 = (bf16[8,64,128]{2,1,0:T(8,128)(2,1)S(1)}, bf16[8,64,128]{2,1,0:T(8,128)(2,1)S(1)}, u32[]{:S(2)}, u32[]{:S(2)}) collective-permute-start(bf16[8,64,128]{2,1,0:T(8,128)(2,1)S(1)} %get-tuple-element.25), channel_id=1, source_target_pairs={{0,64},{32,96},{64,0},{96,32},{1,65},{33,97},{65,1},{97,33},{2,66}... | collective-permute-start | bytes 393224 | tf_op jit(solution)/shard_map/ppermute | solution.py:78
  145.3 2.3 collective-permute-done.18
  148.3 7.2 %all-to-all-start.4 = ((bf16[8,64,128]{2,1,0:T(8,128)(2,1)}), bf16[8,64,128]{2,1,0:T(8,128)(2,1)S(1)}, u32[]{:S(2)}, u32[]{:S(2)}) async-start(bf16[8,64,128]{2,1,0:T(8,128)(2,1)} %fusion.14), calls=%async_computation.4 | async-start | bytes 262144 | tf_op jit(solution)/shard_map/all_to_all | solution.py:64
  155.9 7.7 %all-to-all-done.4 = bf16[8,64,128]{2,1,0:T(8,128)(2,1)S(1)} async-done(((bf16[8,64,128]{2,1,0:T(8,128)(2,1)}), bf16[8,64,128]{2,1,0:T(8,128)(2,1)S(1)}, u32[]{:S(2)}, u32[]{:S(2)}) %all-to-all-start.4) | async-done | bytes 131104 | tf_op jit(solution)/shard_map/all_to_all | solution.py:64
  164.3 12.3 %all-to-all-start.5 = ((bf16[12,24,128]{2,1,0:T(8,128)(2,1)}), bf16[12,24,128]{2,1,0:T(8,128)(2,1)S(1)}, u32[]{:S(2)}, u32[]{:S(2)}) async-start(bf16[12,24,128]{2,1,0:T(8,128)(2,1)} %bitcast.81), calls=%async_computation.5 | async-start | bytes 147456 | tf_op jit(solution)/shard_map/all_to_all | solution.py:64
  178.3 7.6 %all-to-all-done.5 = bf16[12,24,128]{2,1,0:T(8,128)(2,1)S(1)} async-done(((bf16[12,24,128]{2,1,0:T(8,128)(2,1)}), bf16[12,24,128]{2,1,0:T(8,128)(2,1)S(1)}, u32[]{:S(2)}, u32[]{:S(2)}) %all-to-all-start.5) | async-done | bytes 73760 | tf_op jit(solution)/shard_map/all_to_all | solution.py:64
  185.9 3.6 %all-to-all-start.3 = ((bf16[8,128,512]{1,2,0:T(8,128)(2,1)}), bf16[8,128,512]{1,2,0:T(8,128)(2,1)S(1)}, u32[]{:S(2)}, u32[]{:S(2)}) async-start(bf16[8,128,512]{1,2,0:T(8,128)(2,1)} %copy_bitcast_fusion), calls=%async_computation.3 | async-start | bytes 2097152 | tf_op jit(solution)/shard_map/all_to_all | solution.py:64
  189.5 25.2 %all-to-all-done.3 = bf16[8,128,512]{1,2,0:T(8,128)(2,1)S(1)} async-done(((bf16[8,128,512]{1,2,0:T(8,128)(2,1)}), bf16[8,128,512]{1,2,0:T(8,128)(2,1)S(1)}, u32[]{:S(2)}, u32[]{:S(2)}) %all-to-all-start.3) | async-done | bytes 1048608 | tf_op jit(solution)/shard_map/all_to_all | solution.py:64
  215.5 5.2 %all-to-all-start.6 = ((bf16[24,48,128]{2,1,0:T(8,128)(2,1)}), bf16[24,48,128]{2,1,0:T(8,128)(2,1)S(1)}, u32[]{:S(2)}, u32[]{:S(2)}) async-start(bf16[24,48,128]{2,1,0:T(8,128)(2,1)} %broadcast_in_dim.51), calls=%async_computation.6 | async-start | bytes 589824 | tf_op jit(solution)/shard_map/all_to_all | solution.py:64
  221.2 7.3 %collective-permute-start.14 = (bf16[2,2,4,32,128]{4,2,3,0,1:T(4,128)(2,1)S(1)}, bf16[2,2,4,32,128]{4,2,3,0,1:T(4,128)(2,1)S(1)}, u32[]{:S(2)}, u32[]{:S(2)}) collective-permute-start(bf16[2,2,4,32,128]{4,2,3,0,1:T(4,128)(2,1)S(1)} %fusion.29), channel_id=1, source_target_pairs={{0,16},{16,0},{1,17},{17,1},{2,18},{18,2},{3,19},{19,3},{4,20},{20... | collective-permute-start | bytes 393224 | tf_op jit(solution)/shard_map/ppermute | solution.py:82
  228.5 4.3 %all-to-all-done.6 = bf16[24,48,128]{2,1,0:T(8,128)(2,1)S(1)} async-done(((bf16[24,48,128]{2,1,0:T(8,128)(2,1)}), bf16[24,48,128]{2,1,0:T(8,128)(2,1)S(1)}, u32[]{:S(2)}, u32[]{:S(2)}) %all-to-all-start.6) | async-done | bytes 294944 | tf_op jit(solution)/shard_map/all_to_all | solution.py:64
  234.8 12.3 %collective-permute-start.15 = (f32[2,4,32,128]{3,1,2,0:T(4,128)S(1)}, f32[2,4,32,128]{3,1,2,0:T(4,128)S(1)}, u32[]{:S(2)}, u32[]{:S(2)}) collective-permute-start(f32[2,4,32,128]{3,1,2,0:T(4,128)S(1)} %slice_bitcast_fusion.3), channel_id=1, source_target_pairs={{0,1},{1,0},{2,3},{3,2},{4,5},{5,4},{6,7},{7,6},{8,9},{9,8},{10,11... | collective-permute-start | bytes 393224 | tf_op jit(solution)/shard_map/ppermute | solution.py:82
  (128 shorter events, 37.9 us)
Async XLA Ops:
  3.4 21.4 %collective-permute-start = (bf16[20,32,128]{2,1,0:T(8,128)(2,1)S(1)}, bf16[20,32,128]{2,1,0:T(8,128)(2,1)S(1)}, u32[]{:S(2)}, u32[]{:S(2)}) collective-permute-start(bf16[20,32,128]{2,1,0:T(8,128)(2,1)S(1)} %pad_maximum_fusion.9), channel_id=1, source_target_pairs={{0,16},{16,0},{1,17},{17,1},{2,18},{18,2},{3,19},{19,3},{4,20},{20... | collective-permute-start | bytes 491528 | tf_op jit(solution)/shard_map/ppermute | solution.py:82
  25.5 9.3 %collective-permute-start.5 = (bf16[2,4,2,32,128]{4,3,2,1,0:T(8,128)(2,1)S(1)}, bf16[2,4,2,32,128]{4,3,2,1,0:T(8,128)(2,1)S(1)}, u32[]{:S(2)}, u32[]{:S(2)}) collective-permute-start(bf16[2,4,2,32,128]{4,3,2,1,0:T(8,128)(2,1)S(1)} %bitcast.218), channel_id=1, source_target_pairs={{0,1},{1,0},{2,3},{3,2},{4,5},{5,4},{6,7},{7,6},{8,9},{9,8},{10,11... | collective-permute-start | bytes 393224 | tf_op jit(solution)/shard_map/ppermute | solution.py:82
  30.8 12.3 %all-to-all-start = ((bf16[8,64,128]{2,1,0:T(8,128)(2,1)}), bf16[8,64,128]{2,1,0:T(8,128)(2,1)S(1)}, u32[]{:S(2)}, u32[]{:S(2)}) async-start(bf16[8,64,128]{2,1,0:T(8,128)(2,1)} %bitcast.14), calls=%async_computation | async-start | bytes 262144 | tf_op jit(solution)/shard_map/all_to_all | solution.py:64
  43.0 15.2 %collective-permute-start.3 = (bf16[8,64,128]{2,1,0:T(8,128)(2,1)S(1)}, bf16[8,64,128]{2,1,0:T(8,128)(2,1)S(1)}, u32[]{:S(2)}, u32[]{:S(2)}) collective-permute-start(bf16[8,64,128]{2,1,0:T(8,128)(2,1)S(1)} %all-to-all-done), channel_id=1, source_target_pairs={{0,32},{32,64},{64,96},{96,0},{1,33},{33,65},{65,97},{97,1},{2,34}... | collective-permute-start | bytes 393224 | tf_op jit(solution)/shard_map/ppermute | solution.py:78
  46.1 12.1 %collective-permute-start.2 = (bf16[8,64,128]{2,1,0:T(8,128)(2,1)S(1)}, bf16[8,64,128]{2,1,0:T(8,128)(2,1)S(1)}, u32[]{:S(2)}, u32[]{:S(2)}) collective-permute-start(bf16[8,64,128]{2,1,0:T(8,128)(2,1)S(1)} %all-to-all-done), channel_id=1, source_target_pairs={{0,64},{32,96},{64,0},{96,32},{1,65},{33,97},{65,1},{97,33},{2,66}... | collective-permute-start | bytes 393224 | tf_op jit(solution)/shard_map/ppermute | solution.py:78
  50.5 7.7 %collective-permute-start.1 = (bf16[8,64,128]{2,1,0:T(8,128)(2,1)S(1)}, bf16[8,64,128]{2,1,0:T(8,128)(2,1)S(1)}, u32[]{:S(2)}, u32[]{:S(2)}) collective-permute-start(bf16[8,64,128]{2,1,0:T(8,128)(2,1)S(1)} %all-to-all-done), channel_id=1, source_target_pairs={{0,96},{32,0},{64,32},{96,64},{1,97},{33,1},{65,33},{97,65},{2,98}... | collective-permute-start | bytes 393224 | tf_op jit(solution)/shard_map/ppermute | solution.py:78
  54.7 18.6 %all-to-all-start.1 = ((bf16[8,128,256]{2,1,0:T(8,128)(2,1)}), bf16[8,128,256]{2,1,0:T(8,128)(2,1)S(1)}, u32[]{:S(2)}, u32[]{:S(2)}) async-start(bf16[8,128,256]{2,1,0:T(8,128)(2,1)} %bitcast.32), calls=%async_computation.1 | async-start | bytes 1048576 | tf_op jit(solution)/shard_map/all_to_all | solution.py:64
  58.3 5.8 %collective-permute-start.4 = (bf16[4,8,64,128]{3,2,1,0:T(8,128)(2,1)S(1)}, bf16[4,8,64,128]{3,2,1,0:T(8,128)(2,1)S(1)}, u32[]{:S(2)}, u32[]{:S(2)}) collective-permute-start(bf16[4,8,64,128]{3,2,1,0:T(8,128)(2,1)S(1)} %get-tuple-element.31), channel_id=1, source_target_pairs={{0,1},{1,0},{2,3},{3,2},{4,5},{5,4},{6,7},{7,6},{8,9},{9,8},{10,11... | collective-permute-start | bytes 1572872 | tf_op jit(solution)/shard_map/ppermute | solution.py:82
  74.2 21.5 %all-to-all-start.2 = ((bf16[8,128,256]{2,1,0:T(8,128)(2,1)}), bf16[8,128,256]{2,1,0:T(8,128)(2,1)S(1)}, u32[]{:S(2)}, u32[]{:S(2)}) async-start(bf16[8,128,256]{2,1,0:T(8,128)(2,1)} %bitcast.41), calls=%async_computation.2 | async-start | bytes 1048576 | tf_op jit(solution)/shard_map/all_to_all | solution.py:64
  78.6 8.8 %collective-permute-start.6 = (bf16[16,4,256]{2,1,0:T(4,128)(2,1)S(1)}, bf16[16,4,256]{2,1,0:T(4,128)(2,1)S(1)}, u32[]{:S(2)}, u32[]{:S(2)}) collective-permute-start(bf16[16,4,256]{2,1,0:T(4,128)(2,1)S(1)} %get-tuple-element.46), channel_id=1, source_target_pairs={{0,1},{1,2},{2,3},{3,32},{4,5},{5,6},{6,7},{7,36},{8,9},{9,10},{10... | collective-permute-start | bytes 98312 | tf_op jit(solution)/shard_map/ppermute | solution.py:48
  85.2 6.9 %collective-permute-start.7 = (bf16[16,4,256]{2,1,0:T(4,128)(2,1)S(1)}, bf16[16,4,256]{2,1,0:T(4,128)(2,1)S(1)}, u32[]{:S(2)}, u32[]{:S(2)}) collective-permute-start(bf16[16,4,256]{2,1,0:T(4,128)(2,1)S(1)} %get-tuple-element.47), channel_id=1, source_target_pairs={{1,0},{2,1},{3,2},{32,3},{5,4},{6,5},{7,6},{36,7},{9,8},{10,9},{11... | collective-permute-start | bytes 98312 | tf_op jit(solution)/shard_map/ppermute | solution.py:52
  92.2 3.8 %collective-permute-start.8 = (bf16[4,24,256]{2,1,0:T(8,128)(2,1)S(1)}, bf16[4,24,256]{2,1,0:T(8,128)(2,1)S(1)}, u32[]{:S(2)}, u32[]{:S(2)}) collective-permute-start(bf16[4,24,256]{2,1,0:T(8,128)(2,1)S(1)} %get-tuple-element.44), channel_id=1, source_target_pairs={{0,64},{32,96},{64,128},{96,160},{128,192},{160,224},{192,256},{22... | collective-permute-start | bytes 147464 | tf_op jit(solution)/shard_map/ppermute | solution.py:56
  94.3 12.9 %collective-permute-start.9 = (bf16[4,24,256]{2,1,0:T(8,128)(2,1)S(1)}, bf16[4,24,256]{2,1,0:T(8,128)(2,1)S(1)}, u32[]{:S(2)}, u32[]{:S(2)}) collective-permute-start(bf16[4,24,256]{2,1,0:T(8,128)(2,1)S(1)} %get-tuple-element.45), channel_id=1, source_target_pairs={{64,0},{96,32},{128,64},{160,96},{192,128},{224,160},{256,192},{28... | collective-permute-start | bytes 147464 | tf_op jit(solution)/shard_map/ppermute | solution.py:60
  108.0 8.3 %copy-start.4 = (bf16[256,128]{1,0:T(8,128)(2,1)}, bf16[256,128]{1,0:T(8,128)(2,1)S(1)}, u32[]{:S(2)}) copy-start(bf16[256,128]{1,0:T(8,128)(2,1)S(1)} %convolution_convert_fusion.10) | copy-start | bytes 196612
  109.0 18.9 %copy-start.6 = (bf16[256,128]{0,1:T(8,128)(2,1)}, bf16[256,128]{0,1:T(8,128)(2,1)S(1)}, u32[]{:S(2)}) copy-start(bf16[256,128]{0,1:T(8,128)(2,1)S(1)} %convolution_convert_fusion.8) | copy-start | bytes 196612
  109.3 7.4 %collective-permute-start.11 = (bf16[4,24,256]{2,1,0:T(8,128)(2,1)S(1)}, bf16[4,24,256]{2,1,0:T(8,128)(2,1)S(1)}, u32[]{:S(2)}, u32[]{:S(2)}) collective-permute-start(bf16[4,24,256]{2,1,0:T(8,128)(2,1)S(1)} %bitcast.225), channel_id=1, source_target_pairs={{0,64},{32,96},{64,128},{96,160},{128,192},{160,224},{192,256},{22... | collective-permute-start | bytes 147464 | tf_op jit(solution)/shard_map/ppermute | solution.py:56
  115.1 6.3 %collective-permute-start.10 = (bf16[4,24,256]{2,1,0:T(8,128)(2,1)S(1)}, bf16[4,24,256]{2,1,0:T(8,128)(2,1)S(1)}, u32[]{:S(2)}, u32[]{:S(2)}) collective-permute-start(bf16[4,24,256]{2,1,0:T(8,128)(2,1)S(1)} %bitcast.224), channel_id=1, source_target_pairs={{64,0},{96,32},{128,64},{160,96},{192,128},{224,160},{256,192},{28... | collective-permute-start | bytes 147464 | tf_op jit(solution)/shard_map/ppermute | solution.py:60
  121.5 6.7 %collective-permute-start.12 = (bf16[16,4,256]{2,1,0:T(4,128)(2,1)S(1)}, bf16[16,4,256]{2,1,0:T(4,128)(2,1)S(1)}, u32[]{:S(2)}, u32[]{:S(2)}) collective-permute-start(bf16[16,4,256]{2,1,0:T(4,128)(2,1)S(1)} %get-tuple-element.42), channel_id=1, source_target_pairs={{1,0},{2,1},{3,2},{32,3},{5,4},{6,5},{7,6},{36,7},{9,8},{10,9},{11... | collective-permute-start | bytes 98312 | tf_op jit(solution)/shard_map/ppermute | solution.py:52
  123.4 5.5 %collective-permute-start.13 = (bf16[16,4,256]{2,1,0:T(4,128)(2,1)S(1)}, bf16[16,4,256]{2,1,0:T(4,128)(2,1)S(1)}, u32[]{:S(2)}, u32[]{:S(2)}) collective-permute-start(bf16[16,4,256]{2,1,0:T(4,128)(2,1)S(1)} %get-tuple-element.43), channel_id=1, source_target_pairs={{0,1},{1,2},{2,3},{3,32},{4,5},{5,6},{6,7},{7,36},{8,9},{9,10},{10... | collective-permute-start | bytes 98312 | tf_op jit(solution)/shard_map/ppermute | solution.py:48
  129.5 3.8 %collective-permute-start.16 = (bf16[4,8,64,128]{3,2,1,0:T(8,128)(2,1)S(1)}, bf16[4,8,64,128]{3,2,1,0:T(8,128)(2,1)S(1)}, u32[]{:S(2)}, u32[]{:S(2)}) collective-permute-start(bf16[4,8,64,128]{3,2,1,0:T(8,128)(2,1)S(1)} %slice_bitcast_fusion), channel_id=1, source_target_pairs={{0,1},{1,0},{2,3},{3,2},{4,5},{5,4},{6,7},{7,6},{8,9},{9,8},{10,11... | collective-permute-start | bytes 1572872 | tf_op jit(solution)/shard_map/ppermute | solution.py:82
  133.5 22.1 %copy-start.5 = (bf16[256,128]{1,0:T(8,128)(2,1)S(1)}, bf16[256,128]{1,0:T(8,128)(2,1)}, u32[]{:S(2)}) copy-start(bf16[256,128]{1,0:T(8,128)(2,1)} %copy-done.4) | copy-start | bytes 196612
  133.6 10.4 %collective-permute-start.17 = (bf16[8,64,128]{2,1,0:T(8,128)(2,1)S(1)}, bf16[8,64,128]{2,1,0:T(8,128)(2,1)S(1)}, u32[]{:S(2)}, u32[]{:S(2)}) collective-permute-start(bf16[8,64,128]{2,1,0:T(8,128)(2,1)S(1)} %get-tuple-element.23), channel_id=1, source_target_pairs={{0,96},{32,0},{64,32},{96,64},{1,97},{33,1},{65,33},{97,65},{2,98}... | collective-permute-start | bytes 393224 | tf_op jit(solution)/shard_map/ppermute | solution.py:78
  137.8 7.5 %collective-permute-start.19 = (bf16[8,64,128]{2,1,0:T(8,128)(2,1)S(1)}, bf16[8,64,128]{2,1,0:T(8,128)(2,1)S(1)}, u32[]{:S(2)}, u32[]{:S(2)}) collective-permute-start(bf16[8,64,128]{2,1,0:T(8,128)(2,1)S(1)} %get-tuple-element.24), channel_id=1, source_target_pairs={{0,32},{32,64},{64,96},{96,0},{1,33},{33,65},{65,97},{97,1},{2,34}... | collective-permute-start | bytes 393224 | tf_op jit(solution)/shard_map/ppermute | solution.py:78
  139.7 7.9 %collective-permute-start.18 = (bf16[8,64,128]{2,1,0:T(8,128)(2,1)S(1)}, bf16[8,64,128]{2,1,0:T(8,128)(2,1)S(1)}, u32[]{:S(2)}, u32[]{:S(2)}) collective-permute-start(bf16[8,64,128]{2,1,0:T(8,128)(2,1)S(1)} %get-tuple-element.25), channel_id=1, source_target_pairs={{0,64},{32,96},{64,0},{96,32},{1,65},{33,97},{65,1},{97,33},{2,66}... | collective-permute-start | bytes 393224 | tf_op jit(solution)/shard_map/ppermute | solution.py:78
  148.3 28.3 %copy-start.1 = (bf16[1024,128]{1,0:T(8,128)(2,1)S(1)}, bf16[1024,128]{1,0:T(8,128)(2,1)}, u32[]{:S(2)}) copy-start(bf16[1024,128]{1,0:T(8,128)(2,1)} %copy-done) | copy-start | bytes 786436
  148.3 28.3 %copy-start.3 = (bf16[1024,128]{1,0:T(8,128)(2,1)S(1)}, bf16[1024,128]{1,0:T(8,128)(2,1)}, u32[]{:S(2)}) copy-start(bf16[1024,128]{1,0:T(8,128)(2,1)} %copy-done.2) | copy-start | bytes 786436
  148.3 15.3 %all-to-all-start.4 = ((bf16[8,64,128]{2,1,0:T(8,128)(2,1)}), bf16[8,64,128]{2,1,0:T(8,128)(2,1)S(1)}, u32[]{:S(2)}, u32[]{:S(2)}) async-start(bf16[8,64,128]{2,1,0:T(8,128)(2,1)} %fusion.14), calls=%async_computation.4 | async-start | bytes 262144 | tf_op jit(solution)/shard_map/all_to_all | solution.py:64
  164.3 21.6 %all-to-all-start.5 = ((bf16[12,24,128]{2,1,0:T(8,128)(2,1)}), bf16[12,24,128]{2,1,0:T(8,128)(2,1)S(1)}, u32[]{:S(2)}, u32[]{:S(2)}) async-start(bf16[12,24,128]{2,1,0:T(8,128)(2,1)} %bitcast.81), calls=%async_computation.5 | async-start | bytes 147456 | tf_op jit(solution)/shard_map/all_to_all | solution.py:64
  185.9 28.8 %all-to-all-start.3 = ((bf16[8,128,512]{1,2,0:T(8,128)(2,1)}), bf16[8,128,512]{1,2,0:T(8,128)(2,1)S(1)}, u32[]{:S(2)}, u32[]{:S(2)}) async-start(bf16[8,128,512]{1,2,0:T(8,128)(2,1)} %copy_bitcast_fusion), calls=%async_computation.3 | async-start | bytes 2097152 | tf_op jit(solution)/shard_map/all_to_all | solution.py:64
  215.5 17.4 %all-to-all-start.6 = ((bf16[24,48,128]{2,1,0:T(8,128)(2,1)}), bf16[24,48,128]{2,1,0:T(8,128)(2,1)S(1)}, u32[]{:S(2)}, u32[]{:S(2)}) async-start(bf16[24,48,128]{2,1,0:T(8,128)(2,1)} %broadcast_in_dim.51), calls=%async_computation.6 | async-start | bytes 589824 | tf_op jit(solution)/shard_map/all_to_all | solution.py:64
  221.2 13.4 %collective-permute-start.14 = (bf16[2,2,4,32,128]{4,2,3,0,1:T(4,128)(2,1)S(1)}, bf16[2,2,4,32,128]{4,2,3,0,1:T(4,128)(2,1)S(1)}, u32[]{:S(2)}, u32[]{:S(2)}) collective-permute-start(bf16[2,2,4,32,128]{4,2,3,0,1:T(4,128)(2,1)S(1)} %fusion.29), channel_id=1, source_target_pairs={{0,16},{16,0},{1,17},{17,1},{2,18},{18,2},{3,19},{19,3},{4,20},{20... | collective-permute-start | bytes 393224 | tf_op jit(solution)/shard_map/ppermute | solution.py:82
  234.8 13.5 %collective-permute-start.15 = (f32[2,4,32,128]{3,1,2,0:T(4,128)S(1)}, f32[2,4,32,128]{3,1,2,0:T(4,128)S(1)}, u32[]{:S(2)}, u32[]{:S(2)}) collective-permute-start(f32[2,4,32,128]{3,1,2,0:T(4,128)S(1)} %slice_bitcast_fusion.3), channel_id=1, source_target_pairs={{0,1},{1,0},{2,3},{3,2},{4,5},{5,4},{6,7},{7,6},{8,9},{9,8},{10,11... | collective-permute-start | bytes 393224 | tf_op jit(solution)/shard_map/ppermute | solution.py:82
  (3 other events, 3.6 us)

commit v9 on v8

--- a/solution.py
+++ b/solution.py
@@ -132,13 +132,9 @@
 
     w_send = jnp.broadcast_to(w_keep.reshape(4, 1, 64, HEAD_DIM), (4, 2, 64, HEAD_DIM))
     w_x = a2a(w_send.reshape(8, 64, HEAD_DIM), "y")
-
-    def gather(v):
-        send = jnp.broadcast_to(v.reshape(1, 2, 128, TILE_TOKENS), (4, 2, 128, TILE_TOKENS))
-        return a2a(send.reshape(8, 128, TILE_TOKENS), "y").reshape(D, TILE_TOKENS)
-
-    tokens = gather(t_mine[:, :, :2])
-    grads = gather(t_mine[:, :, 2:])
+    send = jnp.broadcast_to(t_mine.reshape(1, 2, 128, 512), (4, 2, 128, 512))
+    both = a2a(send.reshape(8, 128, 512), "y").reshape(D, 512)
+    tokens, grads = both[:, :TILE_TOKENS], both[:, TILE_TOKENS:]
     w_list = jnp.stack([w_x] + [shift(w_x, "x", 4, 1, s) for s in (1, 2, 3)])
     got = swap(w_list, "c")
     w_list = jnp.stack([w_list, got], 2).reshape(4, D, HEAD_DIM)

time: 252 us -> 245 us (0.972)
  starting transfers between devices: 131 us -> 125 us
    all_to_all x7 -> x6, starting transfers between devices: 39.1 us -> 31.3 us  [a2a(): return lax.all_to_all(v, axes, 0, 0, tiled=True)]
    ppermute x2, starting transfers between devices: 11.1 us -> 6.15 us  [to_right(): return lax.ppermute(v, ('x', 'y', 'c'), RIGHT)]
    ppermute x6, starting transfers between devices: 19.9 us -> 23.5 us  [shift(): return lax.ppermute(v, axis, pairs)]
    ppermute x6, waiting for transfers between devices: 3.64 us -> 6.75 us  [shift(): return lax.ppermute(v, axis, pairs)]
    all_to_all x7 -> x6, waiting for transfers between devices: 62.1 us -> 61.9 us  [a2a(): return lax.all_to_all(v, axes, 0, 0, tiled=True)]
  transfers between devices with their start and end apart: 27 -> 26, of which waited for: 16 -> 18; matrix products, arithmetic and copies ran while one was open for 4% -> 3% of each run, Pallas kernels for 0% -> 0%
where the time goes in v9:
time: 245 us; the launch traced here: 244 us
  starting transfers between devices  125 us (51%)
  waiting for transfers between devices  97.6 us (40%)
  local copies, waits for them, and re-layouts  11.8 us (5%)
  matrix products  4.06 us (2%)
  other arithmetic  3.99 us (2%)
    all_to_all x6, waiting for transfers between devices, a2a(): return lax.all_to_all(v, axes, 0, 0, tiled=True)  61.9 us
    ppermute x6, starting transfers between devices, swap(): lax.ppermute(v, axis, [(i, i ^ 1) for i in range(lax.axis_size(axis))])  46.4 us
    all_to_all x6, starting transfers between devices, a2a(): return lax.all_to_all(v, axes, 0, 0, tiled=True)  31.3 us
    ppermute x6, starting transfers between devices, shift(): return lax.ppermute(v, axis, pairs)  23.5 us
    ppermute x2, waiting for transfers between devices, to_up(): return lax.ppermute(v, ('zl', 'x'), UP)  14.5 us
    ppermute x6, waiting for transfers between devices, swap(): lax.ppermute(v, axis, [(i, i ^ 1) for i in range(lax.axis_size(axis))])  10.6 us
    ppermute x2, starting transfers between devices, to_down(): return lax.ppermute(v, ('zl', 'x'), DOWN)  10.4 us
    ppermute x6, waiting for transfers between devices, shift(): return lax.ppermute(v, axis, pairs)  6.75 us
  transfers between devices with their start and end apart: 26, of which 18 were waited for; matrix products, arithmetic and copies ran while one was open for 3% of the time, Pallas kernels for 0%

profile of v9, /device:TPU:1, one launch (start us, length us, event | category | flops | bytes accessed | tf_op | source)
XLA Modules:
  0.0 243.8 jit_solution(2531778042735160155)
XLA Ops:
  3.4 15.7 %collective-permute-start = (bf16[20,32,128]{2,1,0:T(8,128)(2,1)S(1)}, bf16[20,32,128]{2,1,0:T(8,128)(2,1)S(1)}, u32[]{:S(2)}, u32[]{:S(2)}) collective-permute-start(bf16[20,32,128]{2,1,0:T(8,128)(2,1)S(1)} %pad_maximum_fusion.9), channel_id=1, source_target_pairs={{0,16},{16,0},{1,17},{17,1},{2,18},{18,2},{3,19},{19,3},{4,20},{20... | collective-permute-start | bytes 491528 | tf_op jit(solution)/shard_map/ppermute | solution.py:82
  19.1 5.7 %collective-permute-done = bf16[20,32,128]{2,1,0:T(8,128)(2,1)S(1)} collective-permute-done((bf16[20,32,128]{2,1,0:T(8,128)(2,1)S(1)}, bf16[20,32,128]{2,1,0:T(8,128)(2,1)S(1)}, u32[]{:S(2)}, u32[]{:S(2)}) %collective-permute-start) | collective-permute-done | bytes 163872 | tf_op jit(solution)/shard_map/ppermute | solution.py:82
  25.5 4.5 %collective-permute-start.5 = (bf16[2,4,2,32,128]{4,3,2,1,0:T(8,128)(2,1)S(1)}, bf16[2,4,2,32,128]{4,3,2,1,0:T(8,128)(2,1)S(1)}, u32[]{:S(2)}, u32[]{:S(2)}) collective-permute-start(bf16[2,4,2,32,128]{4,3,2,1,0:T(8,128)(2,1)S(1)} %bitcast.199), channel_id=1, source_target_pairs={{0,1},{1,0},{2,3},{3,2},{4,5},{5,4},{6,7},{7,6},{8,9},{9,8},{10,11... | collective-permute-start | bytes 393224 | tf_op jit(solution)/shard_map/ppermute | solution.py:82
  30.8 3.8 %all-to-all-start = ((bf16[8,64,128]{2,1,0:T(8,128)(2,1)}), bf16[8,64,128]{2,1,0:T(8,128)(2,1)S(1)}, u32[]{:S(2)}, u32[]{:S(2)}) async-start(bf16[8,64,128]{2,1,0:T(8,128)(2,1)} %bitcast.14), calls=%async_computation | async-start | bytes 262144 | tf_op jit(solution)/shard_map/all_to_all | solution.py:64
  35.2 7.8 %all-to-all-done = bf16[8,64,128]{2,1,0:T(8,128)(2,1)S(1)} async-done(((bf16[8,64,128]{2,1,0:T(8,128)(2,1)}), bf16[8,64,128]{2,1,0:T(8,128)(2,1)S(1)}, u32[]{:S(2)}, u32[]{:S(2)}) %all-to-all-start) | async-done | bytes 131104 | tf_op jit(solution)/shard_map/all_to_all | solution.py:64
  44.1 3.6 %all-to-all-start.1 = ((bf16[8,128,512]{2,1,0:T(8,128)(2,1)}), bf16[8,128,512]{2,1,0:T(8,128)(2,1)S(1)}, u32[]{:S(2)}, u32[]{:S(2)}) async-start(bf16[8,128,512]{2,1,0:T(8,128)(2,1)} %bitcast.32), calls=%async_computation.1 | async-start | bytes 2097152 | tf_op jit(solution)/shard_map/all_to_all | solution.py:64
  47.7 3.1 %collective-permute-start.3 = (bf16[8,64,128]{2,1,0:T(8,128)(2,1)S(1)}, bf16[8,64,128]{2,1,0:T(8,128)(2,1)S(1)}, u32[]{:S(2)}, u32[]{:S(2)}) collective-permute-start(bf16[8,64,128]{2,1,0:T(8,128)(2,1)S(1)} %all-to-all-done), channel_id=1, source_target_pairs={{0,32},{32,64},{64,96},{96,0},{1,33},{33,65},{65,97},{97,1},{2,34}... | collective-permute-start | bytes 393224 | tf_op jit(solution)/shard_map/ppermute | solution.py:78
  50.8 4.4 %collective-permute-start.2 = (bf16[8,64,128]{2,1,0:T(8,128)(2,1)S(1)}, bf16[8,64,128]{2,1,0:T(8,128)(2,1)S(1)}, u32[]{:S(2)}, u32[]{:S(2)}) collective-permute-start(bf16[8,64,128]{2,1,0:T(8,128)(2,1)S(1)} %all-to-all-done), channel_id=1, source_target_pairs={{0,64},{32,96},{64,0},{96,32},{1,65},{33,97},{65,1},{97,33},{2,66}... | collective-permute-start | bytes 393224 | tf_op jit(solution)/shard_map/ppermute | solution.py:78
  55.1 3.1 %collective-permute-start.1 = (bf16[8,64,128]{2,1,0:T(8,128)(2,1)S(1)}, bf16[8,64,128]{2,1,0:T(8,128)(2,1)S(1)}, u32[]{:S(2)}, u32[]{:S(2)}) collective-permute-start(bf16[8,64,128]{2,1,0:T(8,128)(2,1)S(1)} %all-to-all-done), channel_id=1, source_target_pairs={{0,96},{32,0},{64,32},{96,64},{1,97},{33,1},{65,33},{97,65},{2,98}... | collective-permute-start | bytes 393224 | tf_op jit(solution)/shard_map/ppermute | solution.py:78
  61.2 4.9 %collective-permute-start.4 = (bf16[4,8,64,128]{3,2,1,0:T(8,128)(2,1)S(1)}, bf16[4,8,64,128]{3,2,1,0:T(8,128)(2,1)S(1)}, u32[]{:S(2)}, u32[]{:S(2)}) collective-permute-start(bf16[4,8,64,128]{3,2,1,0:T(8,128)(2,1)S(1)} %get-tuple-element.34), channel_id=1, source_target_pairs={{0,1},{1,0},{2,3},{3,2},{4,5},{5,4},{6,7},{7,6},{8,9},{9,8},{10,11... | collective-permute-start | bytes 1572872 | tf_op jit(solution)/shard_map/ppermute | solution.py:82
  67.8 8.9 %all-to-all-done.1 = bf16[8,128,512]{2,1,0:T(8,128)(2,1)S(1)} async-done(((bf16[8,128,512]{2,1,0:T(8,128)(2,1)}), bf16[8,128,512]{2,1,0:T(8,128)(2,1)S(1)}, u32[]{:S(2)}, u32[]{:S(2)}) %all-to-all-start.1) | async-done | bytes 1048608 | tf_op jit(solution)/shard_map/all_to_all | solution.py:64
  77.3 2.6 %collective-permute-start.6 = (bf16[16,4,256]{2,1,0:T(4,128)(2,1)S(1)}, bf16[16,4,256]{2,1,0:T(4,128)(2,1)S(1)}, u32[]{:S(2)}, u32[]{:S(2)}) collective-permute-start(bf16[16,4,256]{2,1,0:T(4,128)(2,1)S(1)} %get-tuple-element.47), channel_id=1, source_target_pairs={{0,1},{1,2},{2,3},{3,32},{4,5},{5,6},{6,7},{7,36},{8,9},{9,10},{10... | collective-permute-start | bytes 98312 | tf_op jit(solution)/shard_map/ppermute | solution.py:48
  82.0 3.1 %collective-permute-done.7 = bf16[16,4,256]{2,1,0:T(4,128)(2,1)S(1)} collective-permute-done((bf16[16,4,256]{2,1,0:T(4,128)(2,1)S(1)}, bf16[16,4,256]{2,1,0:T(4,128)(2,1)S(1)}, u32[]{:S(2)}, u32[]{:S(2)}) %collective-permute-start.7) | collective-permute-done | bytes 32800 | tf_op jit(solution)/shard_map/ppermute | solution.py:52
  85.2 4.6 %collective-permute-start.8 = (bf16[4,24,256]{2,1,0:T(8,128)(2,1)S(1)}, bf16[4,24,256]{2,1,0:T(8,128)(2,1)S(1)}, u32[]{:S(2)}, u32[]{:S(2)}) collective-permute-start(bf16[4,24,256]{2,1,0:T(8,128)(2,1)S(1)} %get-tuple-element.45), channel_id=1, source_target_pairs={{0,64},{32,96},{64,128},{96,160},{128,192},{160,224},{192,256},{22... | collective-permute-start | bytes 147464 | tf_op jit(solution)/shard_map/ppermute | solution.py:56
  91.5 8.8 %collective-permute-done.9 = bf16[4,24,256]{2,1,0:T(8,128)(2,1)S(1)} collective-permute-done((bf16[4,24,256]{2,1,0:T(8,128)(2,1)S(1)}, bf16[4,24,256]{2,1,0:T(8,128)(2,1)S(1)}, u32[]{:S(2)}, u32[]{:S(2)}) %collective-permute-start.9) | collective-permute-done | bytes 49184 | tf_op jit(solution)/shard_map/ppermute | solution.py:60
  102.6 5.8 %collective-permute-start.11 = (bf16[4,24,256]{2,1,0:T(8,128)(2,1)S(1)}, bf16[4,24,256]{2,1,0:T(8,128)(2,1)S(1)}, u32[]{:S(2)}, u32[]{:S(2)}) collective-permute-start(bf16[4,24,256]{2,1,0:T(8,128)(2,1)S(1)} %bitcast.208), channel_id=1, source_target_pairs={{0,64},{32,96},{64,128},{96,160},{128,192},{160,224},{192,256},{22... | collective-permute-start | bytes 147464 | tf_op jit(solution)/shard_map/ppermute | solution.py:56
  109.8 5.8 %collective-permute-done.10 = bf16[4,24,256]{2,1,0:T(8,128)(2,1)S(1)} collective-permute-done((bf16[4,24,256]{2,1,0:T(8,128)(2,1)S(1)}, bf16[4,24,256]{2,1,0:T(8,128)(2,1)S(1)}, u32[]{:S(2)}, u32[]{:S(2)}) %collective-permute-start.10) | collective-permute-done | bytes 49184 | tf_op jit(solution)/shard_map/ppermute | solution.py:60
  115.6 2.4 collective-permute-start.12
  118.0 3.6 %collective-permute-start.13 = (bf16[16,4,256]{2,1,0:T(4,128)(2,1)S(1)}, bf16[16,4,256]{2,1,0:T(4,128)(2,1)S(1)}, u32[]{:S(2)}, u32[]{:S(2)}) collective-permute-start(bf16[16,4,256]{2,1,0:T(4,128)(2,1)S(1)} %get-tuple-element.44), channel_id=1, source_target_pairs={{0,1},{1,2},{2,3},{3,32},{4,5},{5,6},{6,7},{7,36},{8,9},{9,10},{10... | collective-permute-start | bytes 98312 | tf_op jit(solution)/shard_map/ppermute | solution.py:48
  127.2 7.9 %collective-permute-start.17 = (bf16[8,64,128]{2,1,0:T(8,128)(2,1)S(1)}, bf16[8,64,128]{2,1,0:T(8,128)(2,1)S(1)}, u32[]{:S(2)}, u32[]{:S(2)}) collective-permute-start(bf16[8,64,128]{2,1,0:T(8,128)(2,1)S(1)} %get-tuple-element.26), channel_id=1, source_target_pairs={{0,96},{32,0},{64,32},{96,64},{1,97},{33,1},{65,33},{97,65},{2,98}... | collective-permute-start | bytes 393224 | tf_op jit(solution)/shard_map/ppermute | solution.py:78
  137.1 3.1 %collective-permute-start.18 = (bf16[8,64,128]{2,1,0:T(8,128)(2,1)S(1)}, bf16[8,64,128]{2,1,0:T(8,128)(2,1)S(1)}, u32[]{:S(2)}, u32[]{:S(2)}) collective-permute-start(bf16[8,64,128]{2,1,0:T(8,128)(2,1)S(1)} %get-tuple-element.28), channel_id=1, source_target_pairs={{0,64},{32,96},{64,0},{96,32},{1,65},{33,97},{65,1},{97,33},{2,66}... | collective-permute-start | bytes 393224 | tf_op jit(solution)/shard_map/ppermute | solution.py:78
  142.6 2.3 collective-permute-done.18
  145.7 3.5 %all-to-all-start.3 = ((bf16[8,64,128]{2,1,0:T(8,128)(2,1)}), bf16[8,64,128]{2,1,0:T(8,128)(2,1)S(1)}, u32[]{:S(2)}, u32[]{:S(2)}) async-start(bf16[8,64,128]{2,1,0:T(8,128)(2,1)} %fusion.17), calls=%async_computation.3 | async-start | bytes 262144 | tf_op jit(solution)/shard_map/all_to_all | solution.py:64
  149.5 7.6 %all-to-all-done.3 = bf16[8,64,128]{2,1,0:T(8,128)(2,1)S(1)} async-done(((bf16[8,64,128]{2,1,0:T(8,128)(2,1)}), bf16[8,64,128]{2,1,0:T(8,128)(2,1)S(1)}, u32[]{:S(2)}, u32[]{:S(2)}) %all-to-all-start.3) | async-done | bytes 131104 | tf_op jit(solution)/shard_map/all_to_all | solution.py:64
  157.9 11.8 %all-to-all-start.4 = ((bf16[12,24,128]{2,1,0:T(8,128)(2,1)}), bf16[12,24,128]{2,1,0:T(8,128)(2,1)S(1)}, u32[]{:S(2)}, u32[]{:S(2)}) async-start(bf16[12,24,128]{2,1,0:T(8,128)(2,1)} %bitcast.72), calls=%async_computation.4 | async-start | bytes 147456 | tf_op jit(solution)/shard_map/all_to_all | solution.py:64
  171.4 7.6 %all-to-all-done.4 = bf16[12,24,128]{2,1,0:T(8,128)(2,1)S(1)} async-done(((bf16[12,24,128]{2,1,0:T(8,128)(2,1)}), bf16[12,24,128]{2,1,0:T(8,128)(2,1)S(1)}, u32[]{:S(2)}, u32[]{:S(2)}) %all-to-all-start.4) | async-done | bytes 73760 | tf_op jit(solution)/shard_map/all_to_all | solution.py:64
  179.0 3.6 %all-to-all-start.2 = ((bf16[8,128,512]{1,2,0:T(8,128)(2,1)}), bf16[8,128,512]{1,2,0:T(8,128)(2,1)S(1)}, u32[]{:S(2)}, u32[]{:S(2)}) async-start(bf16[8,128,512]{1,2,0:T(8,128)(2,1)} %copy_bitcast_fusion), calls=%async_computation.2 | async-start | bytes 2097152 | tf_op jit(solution)/shard_map/all_to_all | solution.py:64
  182.6 25.4 %all-to-all-done.2 = bf16[8,128,512]{1,2,0:T(8,128)(2,1)S(1)} async-done(((bf16[8,128,512]{1,2,0:T(8,128)(2,1)}), bf16[8,128,512]{1,2,0:T(8,128)(2,1)S(1)}, u32[]{:S(2)}, u32[]{:S(2)}) %all-to-all-start.2) | async-done | bytes 1048608 | tf_op jit(solution)/shard_map/all_to_all | solution.py:64
  208.7 5.1 %all-to-all-start.5 = ((bf16[24,48,128]{2,1,0:T(8,128)(2,1)}), bf16[24,48,128]{2,1,0:T(8,128)(2,1)S(1)}, u32[]{:S(2)}, u32[]{:S(2)}) async-start(bf16[24,48,128]{2,1,0:T(8,128)(2,1)} %broadcast_in_dim.42), calls=%async_computation.5 | async-start | bytes 589824 | tf_op jit(solution)/shard_map/all_to_all | solution.py:64
  214.4 7.1 %collective-permute-start.14 = (bf16[2,2,4,32,128]{4,2,3,0,1:T(4,128)(2,1)S(1)}, bf16[2,2,4,32,128]{4,2,3,0,1:T(4,128)(2,1)S(1)}, u32[]{:S(2)}, u32[]{:S(2)}) collective-permute-start(bf16[2,2,4,32,128]{4,2,3,0,1:T(4,128)(2,1)S(1)} %fusion.32), channel_id=1, source_target_pairs={{0,16},{16,0},{1,17},{17,1},{2,18},{18,2},{3,19},{19,3},{4,20},{20... | collective-permute-start | bytes 393224 | tf_op jit(solution)/shard_map/ppermute | solution.py:82
  221.5 4.5 %all-to-all-done.5 = bf16[24,48,128]{2,1,0:T(8,128)(2,1)S(1)} async-done(((bf16[24,48,128]{2,1,0:T(8,128)(2,1)}), bf16[24,48,128]{2,1,0:T(8,128)(2,1)S(1)}, u32[]{:S(2)}, u32[]{:S(2)}) %all-to-all-start.5) | async-done | bytes 294944 | tf_op jit(solution)/shard_map/all_to_all | solution.py:64
  227.9 12.3 %collective-permute-start.15 = (f32[2,4,32,128]{3,1,2,0:T(4,128)S(1)}, f32[2,4,32,128]{3,1,2,0:T(4,128)S(1)}, u32[]{:S(2)}, u32[]{:S(2)}) collective-permute-start(f32[2,4,32,128]{3,1,2,0:T(4,128)S(1)} %slice_bitcast_fusion.3), channel_id=1, source_target_pairs={{0,1},{1,0},{2,3},{3,2},{4,5},{5,4},{6,7},{7,6},{8,9},{9,8},{10,11... | collective-permute-start | bytes 393224 | tf_op jit(solution)/shard_map/ppermute | solution.py:82
  (122 shorter events, 38.3 us)
Async XLA Ops:
  3.4 21.4 %collective-permute-start = (bf16[20,32,128]{2,1,0:T(8,128)(2,1)S(1)}, bf16[20,32,128]{2,1,0:T(8,128)(2,1)S(1)}, u32[]{:S(2)}, u32[]{:S(2)}) collective-permute-start(bf16[20,32,128]{2,1,0:T(8,128)(2,1)S(1)} %pad_maximum_fusion.9), channel_id=1, source_target_pairs={{0,16},{16,0},{1,17},{17,1},{2,18},{18,2},{3,19},{19,3},{4,20},{20... | collective-permute-start | bytes 491528 | tf_op jit(solution)/shard_map/ppermute | solution.py:82
  25.5 9.3 %collective-permute-start.5 = (bf16[2,4,2,32,128]{4,3,2,1,0:T(8,128)(2,1)S(1)}, bf16[2,4,2,32,128]{4,3,2,1,0:T(8,128)(2,1)S(1)}, u32[]{:S(2)}, u32[]{:S(2)}) collective-permute-start(bf16[2,4,2,32,128]{4,3,2,1,0:T(8,128)(2,1)S(1)} %bitcast.199), channel_id=1, source_target_pairs={{0,1},{1,0},{2,3},{3,2},{4,5},{5,4},{6,7},{7,6},{8,9},{9,8},{10,11... | collective-permute-start | bytes 393224 | tf_op jit(solution)/shard_map/ppermute | solution.py:82
  30.8 12.3 %all-to-all-start = ((bf16[8,64,128]{2,1,0:T(8,128)(2,1)}), bf16[8,64,128]{2,1,0:T(8,128)(2,1)S(1)}, u32[]{:S(2)}, u32[]{:S(2)}) async-start(bf16[8,64,128]{2,1,0:T(8,128)(2,1)} %bitcast.14), calls=%async_computation | async-start | bytes 262144 | tf_op jit(solution)/shard_map/all_to_all | solution.py:64
  44.1 32.7 %all-to-all-start.1 = ((bf16[8,128,512]{2,1,0:T(8,128)(2,1)}), bf16[8,128,512]{2,1,0:T(8,128)(2,1)S(1)}, u32[]{:S(2)}, u32[]{:S(2)}) async-start(bf16[8,128,512]{2,1,0:T(8,128)(2,1)} %bitcast.32), calls=%async_computation.1 | async-start | bytes 2097152 | tf_op jit(solution)/shard_map/all_to_all | solution.py:64
  47.7 10.6 %collective-permute-start.3 = (bf16[8,64,128]{2,1,0:T(8,128)(2,1)S(1)}, bf16[8,64,128]{2,1,0:T(8,128)(2,1)S(1)}, u32[]{:S(2)}, u32[]{:S(2)}) collective-permute-start(bf16[8,64,128]{2,1,0:T(8,128)(2,1)S(1)} %all-to-all-done), channel_id=1, source_target_pairs={{0,32},{32,64},{64,96},{96,0},{1,33},{33,65},{65,97},{97,1},{2,34}... | collective-permute-start | bytes 393224 | tf_op jit(solution)/shard_map/ppermute | solution.py:78
  50.8 8.6 %collective-permute-start.2 = (bf16[8,64,128]{2,1,0:T(8,128)(2,1)S(1)}, bf16[8,64,128]{2,1,0:T(8,128)(2,1)S(1)}, u32[]{:S(2)}, u32[]{:S(2)}) collective-permute-start(bf16[8,64,128]{2,1,0:T(8,128)(2,1)S(1)} %all-to-all-done), channel_id=1, source_target_pairs={{0,64},{32,96},{64,0},{96,32},{1,65},{33,97},{65,1},{97,33},{2,66}... | collective-permute-start | bytes 393224 | tf_op jit(solution)/shard_map/ppermute | solution.py:78
  55.1 6.0 %collective-permute-start.1 = (bf16[8,64,128]{2,1,0:T(8,128)(2,1)S(1)}, bf16[8,64,128]{2,1,0:T(8,128)(2,1)S(1)}, u32[]{:S(2)}, u32[]{:S(2)}) collective-permute-start(bf16[8,64,128]{2,1,0:T(8,128)(2,1)S(1)} %all-to-all-done), channel_id=1, source_target_pairs={{0,96},{32,0},{64,32},{96,64},{1,97},{33,1},{65,33},{97,65},{2,98}... | collective-permute-start | bytes 393224 | tf_op jit(solution)/shard_map/ppermute | solution.py:78
  61.2 6.4 %collective-permute-start.4 = (bf16[4,8,64,128]{3,2,1,0:T(8,128)(2,1)S(1)}, bf16[4,8,64,128]{3,2,1,0:T(8,128)(2,1)S(1)}, u32[]{:S(2)}, u32[]{:S(2)}) collective-permute-start(bf16[4,8,64,128]{3,2,1,0:T(8,128)(2,1)S(1)} %get-tuple-element.34), channel_id=1, source_target_pairs={{0,1},{1,0},{2,3},{3,2},{4,5},{5,4},{6,7},{7,6},{8,9},{9,8},{10,11... | collective-permute-start | bytes 1572872 | tf_op jit(solution)/shard_map/ppermute | solution.py:82
  67.8 9.4 %copy-start = (bf16[1024,128]{1,0:T(8,128)(2,1)}, bf16[1024,128]{1,0:T(8,128)(2,1)S(1)}, u32[]{:S(2)}) copy-start(bf16[1024,128]{1,0:T(8,128)(2,1)S(1)} %get-tuple-element.24) | copy-start | bytes 786436
  67.8 9.4 %copy-start.2 = (bf16[1024,128]{1,0:T(8,128)(2,1)}, bf16[1024,128]{1,0:T(8,128)(2,1)S(1)}, u32[]{:S(2)}) copy-start(bf16[1024,128]{1,0:T(8,128)(2,1)S(1)} %get-tuple-element.25) | copy-start | bytes 786436
  77.3 4.7 %collective-permute-start.6 = (bf16[16,4,256]{2,1,0:T(4,128)(2,1)S(1)}, bf16[16,4,256]{2,1,0:T(4,128)(2,1)S(1)}, u32[]{:S(2)}, u32[]{:S(2)}) collective-permute-start(bf16[16,4,256]{2,1,0:T(4,128)(2,1)S(1)} %get-tuple-element.47), channel_id=1, source_target_pairs={{0,1},{1,2},{2,3},{3,32},{4,5},{5,6},{6,7},{7,36},{8,9},{9,10},{10... | collective-permute-start | bytes 98312 | tf_op jit(solution)/shard_map/ppermute | solution.py:48
  79.9 5.2 %collective-permute-start.7 = (bf16[16,4,256]{2,1,0:T(4,128)(2,1)S(1)}, bf16[16,4,256]{2,1,0:T(4,128)(2,1)S(1)}, u32[]{:S(2)}, u32[]{:S(2)}) collective-permute-start(bf16[16,4,256]{2,1,0:T(4,128)(2,1)S(1)} %get-tuple-element.48), channel_id=1, source_target_pairs={{1,0},{2,1},{3,2},{32,3},{5,4},{6,5},{7,6},{36,7},{9,8},{10,9},{11... | collective-permute-start | bytes 98312 | tf_op jit(solution)/shard_map/ppermute | solution.py:52
  85.2 6.3 %collective-permute-start.8 = (bf16[4,24,256]{2,1,0:T(8,128)(2,1)S(1)}, bf16[4,24,256]{2,1,0:T(8,128)(2,1)S(1)}, u32[]{:S(2)}, u32[]{:S(2)}) collective-permute-start(bf16[4,24,256]{2,1,0:T(8,128)(2,1)S(1)} %get-tuple-element.45), channel_id=1, source_target_pairs={{0,64},{32,96},{64,128},{96,160},{128,192},{160,224},{192,256},{22... | collective-permute-start | bytes 147464 | tf_op jit(solution)/shard_map/ppermute | solution.py:56
  89.8 10.4 %collective-permute-start.9 = (bf16[4,24,256]{2,1,0:T(8,128)(2,1)S(1)}, bf16[4,24,256]{2,1,0:T(8,128)(2,1)S(1)}, u32[]{:S(2)}, u32[]{:S(2)}) collective-permute-start(bf16[4,24,256]{2,1,0:T(8,128)(2,1)S(1)} %get-tuple-element.46), channel_id=1, source_target_pairs={{64,0},{96,32},{128,64},{160,96},{192,128},{224,160},{256,192},{28... | collective-permute-start | bytes 147464 | tf_op jit(solution)/shard_map/ppermute | solution.py:60
  102.1 19.5 %copy-start.6 = (bf16[256,128]{0,1:T(8,128)(2,1)}, bf16[256,128]{0,1:T(8,128)(2,1)S(1)}, u32[]{:S(2)}) copy-start(bf16[256,128]{0,1:T(8,128)(2,1)S(1)} %convolution_convert_fusion.8) | copy-start | bytes 196612
  102.6 7.1 %collective-permute-start.11 = (bf16[4,24,256]{2,1,0:T(8,128)(2,1)S(1)}, bf16[4,24,256]{2,1,0:T(8,128)(2,1)S(1)}, u32[]{:S(2)}, u32[]{:S(2)}) collective-permute-start(bf16[4,24,256]{2,1,0:T(8,128)(2,1)S(1)} %bitcast.208), channel_id=1, source_target_pairs={{0,64},{32,96},{64,128},{96,160},{128,192},{160,224},{192,256},{22... | collective-permute-start | bytes 147464 | tf_op jit(solution)/shard_map/ppermute | solution.py:56
  108.4 7.1 %collective-permute-start.10 = (bf16[4,24,256]{2,1,0:T(8,128)(2,1)S(1)}, bf16[4,24,256]{2,1,0:T(8,128)(2,1)S(1)}, u32[]{:S(2)}, u32[]{:S(2)}) collective-permute-start(bf16[4,24,256]{2,1,0:T(8,128)(2,1)S(1)} %bitcast.207), channel_id=1, source_target_pairs={{64,0},{96,32},{128,64},{160,96},{192,128},{224,160},{256,192},{28... | collective-permute-start | bytes 147464 | tf_op jit(solution)/shard_map/ppermute | solution.py:60
  115.6 6.3 %collective-permute-start.12 = (bf16[16,4,256]{2,1,0:T(4,128)(2,1)S(1)}, bf16[16,4,256]{2,1,0:T(4,128)(2,1)S(1)}, u32[]{:S(2)}, u32[]{:S(2)}) collective-permute-start(bf16[16,4,256]{2,1,0:T(4,128)(2,1)S(1)} %get-tuple-element.43), channel_id=1, source_target_pairs={{1,0},{2,1},{3,2},{32,3},{5,4},{6,5},{7,6},{36,7},{9,8},{10,9},{11... | collective-permute-start | bytes 98312 | tf_op jit(solution)/shard_map/ppermute | solution.py:52
  118.0 4.6 %collective-permute-start.13 = (bf16[16,4,256]{2,1,0:T(4,128)(2,1)S(1)}, bf16[16,4,256]{2,1,0:T(4,128)(2,1)S(1)}, u32[]{:S(2)}, u32[]{:S(2)}) collective-permute-start(bf16[16,4,256]{2,1,0:T(4,128)(2,1)S(1)} %get-tuple-element.44), channel_id=1, source_target_pairs={{0,1},{1,2},{2,3},{3,32},{4,5},{5,6},{6,7},{7,36},{8,9},{9,10},{10... | collective-permute-start | bytes 98312 | tf_op jit(solution)/shard_map/ppermute | solution.py:48
  123.2 3.8 %collective-permute-start.16 = (bf16[4,8,64,128]{3,2,1,0:T(8,128)(2,1)S(1)}, bf16[4,8,64,128]{3,2,1,0:T(8,128)(2,1)S(1)}, u32[]{:S(2)}, u32[]{:S(2)}) collective-permute-start(bf16[4,8,64,128]{3,2,1,0:T(8,128)(2,1)S(1)} %slice_bitcast_fusion), channel_id=1, source_target_pairs={{0,1},{1,0},{2,3},{3,2},{4,5},{5,4},{6,7},{7,6},{8,9},{9,8},{10,11... | collective-permute-start | bytes 1572872 | tf_op jit(solution)/shard_map/ppermute | solution.py:82
  127.2 22.1 %copy-start.5 = (bf16[256,128]{1,0:T(8,128)(2,1)S(1)}, bf16[256,128]{1,0:T(8,128)(2,1)}, u32[]{:S(2)}) copy-start(bf16[256,128]{1,0:T(8,128)(2,1)} %copy-done.4) | copy-start | bytes 196612
  127.2 13.9 %collective-permute-start.17 = (bf16[8,64,128]{2,1,0:T(8,128)(2,1)S(1)}, bf16[8,64,128]{2,1,0:T(8,128)(2,1)S(1)}, u32[]{:S(2)}, u32[]{:S(2)}) collective-permute-start(bf16[8,64,128]{2,1,0:T(8,128)(2,1)S(1)} %get-tuple-element.26), channel_id=1, source_target_pairs={{0,96},{32,0},{64,32},{96,64},{1,97},{33,1},{65,33},{97,65},{2,98}... | collective-permute-start | bytes 393224 | tf_op jit(solution)/shard_map/ppermute | solution.py:78
  135.1 7.5 %collective-permute-start.19 = (bf16[8,64,128]{2,1,0:T(8,128)(2,1)S(1)}, bf16[8,64,128]{2,1,0:T(8,128)(2,1)S(1)}, u32[]{:S(2)}, u32[]{:S(2)}) collective-permute-start(bf16[8,64,128]{2,1,0:T(8,128)(2,1)S(1)} %get-tuple-element.27), channel_id=1, source_target_pairs={{0,32},{32,64},{64,96},{96,0},{1,33},{33,65},{65,97},{97,1},{2,34}... | collective-permute-start | bytes 393224 | tf_op jit(solution)/shard_map/ppermute | solution.py:78
  137.1 7.9 %collective-permute-start.18 = (bf16[8,64,128]{2,1,0:T(8,128)(2,1)S(1)}, bf16[8,64,128]{2,1,0:T(8,128)(2,1)S(1)}, u32[]{:S(2)}, u32[]{:S(2)}) collective-permute-start(bf16[8,64,128]{2,1,0:T(8,128)(2,1)S(1)} %get-tuple-element.28), channel_id=1, source_target_pairs={{0,64},{32,96},{64,0},{96,32},{1,65},{33,97},{65,1},{97,33},{2,66}... | collective-permute-start | bytes 393224 | tf_op jit(solution)/shard_map/ppermute | solution.py:78
  145.7 24.0 %copy-start.1 = (bf16[1024,128]{1,0:T(8,128)(2,1)S(1)}, bf16[1024,128]{1,0:T(8,128)(2,1)}, u32[]{:S(2)}) copy-start(bf16[1024,128]{1,0:T(8,128)(2,1)} %copy-done) | copy-start | bytes 786436
  145.7 24.0 %copy-start.3 = (bf16[1024,128]{1,0:T(8,128)(2,1)S(1)}, bf16[1024,128]{1,0:T(8,128)(2,1)}, u32[]{:S(2)}) copy-start(bf16[1024,128]{1,0:T(8,128)(2,1)} %copy-done.2) | copy-start | bytes 786436
  145.7 11.4 %all-to-all-start.3 = ((bf16[8,64,128]{2,1,0:T(8,128)(2,1)}), bf16[8,64,128]{2,1,0:T(8,128)(2,1)S(1)}, u32[]{:S(2)}, u32[]{:S(2)}) async-start(bf16[8,64,128]{2,1,0:T(8,128)(2,1)} %fusion.17), calls=%async_computation.3 | async-start | bytes 262144 | tf_op jit(solution)/shard_map/all_to_all | solution.py:64
  157.9 21.1 %all-to-all-start.4 = ((bf16[12,24,128]{2,1,0:T(8,128)(2,1)}), bf16[12,24,128]{2,1,0:T(8,128)(2,1)S(1)}, u32[]{:S(2)}, u32[]{:S(2)}) async-start(bf16[12,24,128]{2,1,0:T(8,128)(2,1)} %bitcast.72), calls=%async_computation.4 | async-start | bytes 147456 | tf_op jit(solution)/shard_map/all_to_all | solution.py:64
  179.0 28.9 %all-to-all-start.2 = ((bf16[8,128,512]{1,2,0:T(8,128)(2,1)}), bf16[8,128,512]{1,2,0:T(8,128)(2,1)S(1)}, u32[]{:S(2)}, u32[]{:S(2)}) async-start(bf16[8,128,512]{1,2,0:T(8,128)(2,1)} %copy_bitcast_fusion), calls=%async_computation.2 | async-start | bytes 2097152 | tf_op jit(solution)/shard_map/all_to_all | solution.py:64
  208.7 17.3 %all-to-all-start.5 = ((bf16[24,48,128]{2,1,0:T(8,128)(2,1)}), bf16[24,48,128]{2,1,0:T(8,128)(2,1)S(1)}, u32[]{:S(2)}, u32[]{:S(2)}) async-start(bf16[24,48,128]{2,1,0:T(8,128)(2,1)} %broadcast_in_dim.42), calls=%async_computation.5 | async-start | bytes 589824 | tf_op jit(solution)/shard_map/all_to_all | solution.py:64
  214.4 13.4 %collective-permute-start.14 = (bf16[2,2,4,32,128]{4,2,3,0,1:T(4,128)(2,1)S(1)}, bf16[2,2,4,32,128]{4,2,3,0,1:T(4,128)(2,1)S(1)}, u32[]{:S(2)}, u32[]{:S(2)}) collective-permute-start(bf16[2,2,4,32,128]{4,2,3,0,1:T(4,128)(2,1)S(1)} %fusion.32), channel_id=1, source_target_pairs={{0,16},{16,0},{1,17},{17,1},{2,18},{18,2},{3,19},{19,3},{4,20},{20... | collective-permute-start | bytes 393224 | tf_op jit(solution)/shard_map/ppermute | solution.py:82
  227.9 13.4 %collective-permute-start.15 = (f32[2,4,32,128]{3,1,2,0:T(4,128)S(1)}, f32[2,4,32,128]{3,1,2,0:T(4,128)S(1)}, u32[]{:S(2)}, u32[]{:S(2)}) collective-permute-start(f32[2,4,32,128]{3,1,2,0:T(4,128)S(1)} %slice_bitcast_fusion.3), channel_id=1, source_target_pairs={{0,1},{1,0},{2,3},{3,2},{4,5},{5,4},{6,7},{7,6},{8,9},{9,8},{10,11... | collective-permute-start | bytes 393224 | tf_op jit(solution)/shard_map/ppermute | solution.py:82
  (2 other events, 3.4 us)

commit v10 on v9

--- a/solution.py
+++ b/solution.py
@@ -224,18 +224,16 @@
     attention = join_tiles(back[:, :, :2].astype(bf16))
     token_grads = join_tiles(back[:, :, 2:])
 
-    total = a2a(total.astype(bf16), "y")
-    total = jnp.sum(total.reshape(4, 2, 2, WIDTH, 128).astype(f32), 1).astype(bf16)
+    total = total.astype(bf16).reshape(8, 2, WIDTH, 128)
     total = jnp.stack(in_order(total[:, 0], total[:, 1], zh))
-    total = jnp.pad(total.reshape(2, 128, 128), ((0, 0), (0, 16), (0, 0)))
-    total = total.reshape(2, 6, 24, 128).transpose(1, 0, 2, 3).reshape(12, 24, 128)
-    total = a2a(total, ("zl", "zh"))
-    total = jnp.sum(total.reshape(6, 1, 48, 128).astype(f32), 0).astype(bf16)
-    total = jnp.broadcast_to(total, (24, 48, 128))
+    total = jnp.pad(total, ((0, 0), (0, 0), (0, 16), (0, 0))).reshape(2, 8, 6, 8, 128)
+    total = total.transpose(2, 0, 1, 3, 4).reshape(96, 8, 128)
+    total = a2a(total, ("zl", "zh", "y"))
+    total = jnp.sum(total.reshape(6, 8, 2, 8, 128).astype(f32), (0, 2))
+    total = jnp.broadcast_to(total.astype(bf16).reshape(1, 64, 128), (24, 64, 128))
     total = a2a(total, ("zl", "x"))
-    total = total.reshape(6, 4, 2, 24, 128).transpose(1, 2, 0, 3, 4).reshape(4, 2, 144, 128)
-    total = total[:, :, :128].reshape(4, HEADS, WIDTH, 128)
-    weight_grads = total.transpose(2, 0, 1, 3).astype(f32)
+    total = total.reshape(6, 4, HEADS, 8, 128)[:4].transpose(0, 3, 1, 2, 4)
+    weight_grads = total.reshape(WIDTH, 4, HEADS, HEAD_DIM).astype(f32)
     return attention, token_grads, weight_grads
 
 

time: 245 us -> 223 us (0.910)
  the two profiles are of different devices: /device:TPU:1 before, /device:TPU:8 now
where the time goes in v10:
time: 223 us; the launch traced here: 222 us
  starting transfers between devices  122 us (55%)
  waiting for transfers between devices  76.7 us (34%)
  local copies, waits for them, and re-layouts  13.2 us (6%)
  other arithmetic  4.1 us (2%)
  matrix products  4.06 us (2%)
    all_to_all x5, waiting for transfers between devices, a2a(): return lax.all_to_all(v, axes, 0, 0, tiled=True)  41.2 us
    all_to_all x5, starting transfers between devices, a2a(): return lax.all_to_all(v, axes, 0, 0, tiled=True)  41.2 us
    ppermute x6, starting transfers between devices, swap(): lax.ppermute(v, axis, [(i, i ^ 1) for i in range(lax.axis_size(axis))])  33.7 us
    ppermute x6, starting transfers between devices, shift(): return lax.ppermute(v, axis, pairs)  23.3 us
    ppermute x2, waiting for transfers between devices, to_up(): return lax.ppermute(v, ('zl', 'x'), UP)  15.3 us
    ppermute x2, starting transfers between devices, to_down(): return lax.ppermute(v, ('zl', 'x'), DOWN)  11.3 us
    ppermute x6, waiting for transfers between devices, shift(): return lax.ppermute(v, axis, pairs)  9.44 us
    ppermute x6, waiting for transfers between devices, swap(): lax.ppermute(v, axis, [(i, i ^ 1) for i in range(lax.axis_size(axis))])  7.44 us
  transfers between devices with their start and end apart: 25, of which 17 were waited for; matrix products, arithmetic and copies ran while one was open for 4% of the time, Pallas kernels for 0%

profile of v10, /device:TPU:8, one launch (start us, length us, event | category | flops | bytes accessed | tf_op | source)
XLA Modules:
  0.0 221.6 jit_solution(10930175716379547375)
XLA Ops:
  3.4 15.1 %collective-permute-start = (bf16[20,32,128]{2,1,0:T(8,128)(2,1)S(1)}, bf16[20,32,128]{2,1,0:T(8,128)(2,1)S(1)}, u32[]{:S(2)}, u32[]{:S(2)}) collective-permute-start(bf16[20,32,128]{2,1,0:T(8,128)(2,1)S(1)} %pad_maximum_fusion.9), channel_id=1, source_target_pairs={{0,16},{16,0},{1,17},{17,1},{2,18},{18,2},{3,19},{19,3},{4,20},{20... | collective-permute-start | bytes 491528 | tf_op jit(solution)/shard_map/ppermute | solution.py:82
  18.5 4.4 %collective-permute-done = bf16[20,32,128]{2,1,0:T(8,128)(2,1)S(1)} collective-permute-done((bf16[20,32,128]{2,1,0:T(8,128)(2,1)S(1)}, bf16[20,32,128]{2,1,0:T(8,128)(2,1)S(1)}, u32[]{:S(2)}, u32[]{:S(2)}) %collective-permute-start) | collective-permute-done | bytes 163872 | tf_op jit(solution)/shard_map/ppermute | solution.py:82
  23.6 1.9 collective-permute-start.5
  26.2 7.5 %all-to-all-start = ((bf16[8,64,128]{2,1,0:T(8,128)(2,1)}), bf16[8,64,128]{2,1,0:T(8,128)(2,1)S(1)}, u32[]{:S(2)}, u32[]{:S(2)}) async-start(bf16[8,64,128]{2,1,0:T(8,128)(2,1)} %bitcast.14), calls=%async_computation | async-start | bytes 262144 | tf_op jit(solution)/shard_map/all_to_all | solution.py:64
  34.4 7.6 %all-to-all-done = bf16[8,64,128]{2,1,0:T(8,128)(2,1)S(1)} async-done(((bf16[8,64,128]{2,1,0:T(8,128)(2,1)}), bf16[8,64,128]{2,1,0:T(8,128)(2,1)S(1)}, u32[]{:S(2)}, u32[]{:S(2)}) %all-to-all-start) | async-done | bytes 131104 | tf_op jit(solution)/shard_map/all_to_all | solution.py:64
  43.0 5.0 %all-to-all-start.1 = ((bf16[8,128,512]{2,1,0:T(8,128)(2,1)}), bf16[8,128,512]{2,1,0:T(8,128)(2,1)S(1)}, u32[]{:S(2)}, u32[]{:S(2)}) async-start(bf16[8,128,512]{2,1,0:T(8,128)(2,1)} %bitcast.32), calls=%async_computation.1 | async-start | bytes 2097152 | tf_op jit(solution)/shard_map/all_to_all | solution.py:64
  48.1 3.4 %collective-permute-start.3 = (bf16[8,64,128]{2,1,0:T(8,128)(2,1)S(1)}, bf16[8,64,128]{2,1,0:T(8,128)(2,1)S(1)}, u32[]{:S(2)}, u32[]{:S(2)}) collective-permute-start(bf16[8,64,128]{2,1,0:T(8,128)(2,1)S(1)} %all-to-all-done), channel_id=1, source_target_pairs={{0,32},{32,64},{64,96},{96,0},{1,33},{33,65},{65,97},{97,1},{2,34}... | collective-permute-start | bytes 393224 | tf_op jit(solution)/shard_map/ppermute | solution.py:78
  51.5 4.6 %collective-permute-start.2 = (bf16[8,64,128]{2,1,0:T(8,128)(2,1)S(1)}, bf16[8,64,128]{2,1,0:T(8,128)(2,1)S(1)}, u32[]{:S(2)}, u32[]{:S(2)}) collective-permute-start(bf16[8,64,128]{2,1,0:T(8,128)(2,1)S(1)} %all-to-all-done), channel_id=1, source_target_pairs={{0,64},{32,96},{64,0},{96,32},{1,65},{33,97},{65,1},{97,33},{2,66}... | collective-permute-start | bytes 393224 | tf_op jit(solution)/shard_map/ppermute | solution.py:78
  56.1 3.3 %collective-permute-start.1 = (bf16[8,64,128]{2,1,0:T(8,128)(2,1)S(1)}, bf16[8,64,128]{2,1,0:T(8,128)(2,1)S(1)}, u32[]{:S(2)}, u32[]{:S(2)}) collective-permute-start(bf16[8,64,128]{2,1,0:T(8,128)(2,1)S(1)} %all-to-all-done), channel_id=1, source_target_pairs={{0,96},{32,0},{64,32},{96,64},{1,97},{33,1},{65,33},{97,65},{2,98}... | collective-permute-start | bytes 393224 | tf_op jit(solution)/shard_map/ppermute | solution.py:78
  59.9 3.0 %collective-permute-done.1 = bf16[8,64,128]{2,1,0:T(8,128)(2,1)S(1)} collective-permute-done((bf16[8,64,128]{2,1,0:T(8,128)(2,1)S(1)}, bf16[8,64,128]{2,1,0:T(8,128)(2,1)S(1)}, u32[]{:S(2)}, u32[]{:S(2)}) %collective-permute-start.1) | collective-permute-done | bytes 131104 | tf_op jit(solution)/shard_map/ppermute | solution.py:78
  63.1 1.9 collective-permute-start.4
  67.1 7.7 %all-to-all-done.1 = bf16[8,128,512]{2,1,0:T(8,128)(2,1)S(1)} async-done(((bf16[8,128,512]{2,1,0:T(8,128)(2,1)}), bf16[8,128,512]{2,1,0:T(8,128)(2,1)S(1)}, u32[]{:S(2)}, u32[]{:S(2)}) %all-to-all-start.1) | async-done | bytes 1048608 | tf_op jit(solution)/shard_map/all_to_all | solution.py:64
  75.3 1.9 collective-permute-start.6
  77.2 3.6 %collective-permute-start.7 = (bf16[16,4,256]{2,1,0:T(4,128)(2,1)S(1)}, bf16[16,4,256]{2,1,0:T(4,128)(2,1)S(1)}, u32[]{:S(2)}, u32[]{:S(2)}) collective-permute-start(bf16[16,4,256]{2,1,0:T(4,128)(2,1)S(1)} %get-tuple-element.48), channel_id=1, source_target_pairs={{1,0},{2,1},{3,2},{32,3},{5,4},{6,5},{7,6},{36,7},{9,8},{10,9},{11... | collective-permute-start | bytes 98312 | tf_op jit(solution)/shard_map/ppermute | solution.py:52
  82.5 4.9 %collective-permute-start.8 = (bf16[4,24,256]{2,1,0:T(8,128)(2,1)S(1)}, bf16[4,24,256]{2,1,0:T(8,128)(2,1)S(1)}, u32[]{:S(2)}, u32[]{:S(2)}) collective-permute-start(bf16[4,24,256]{2,1,0:T(8,128)(2,1)S(1)} %get-tuple-element.45), channel_id=1, source_target_pairs={{0,64},{32,96},{64,128},{96,160},{128,192},{160,224},{192,256},{22... | collective-permute-start | bytes 147464 | tf_op jit(solution)/shard_map/ppermute | solution.py:56
  89.2 9.6 %collective-permute-done.9 = bf16[4,24,256]{2,1,0:T(8,128)(2,1)S(1)} collective-permute-done((bf16[4,24,256]{2,1,0:T(8,128)(2,1)S(1)}, bf16[4,24,256]{2,1,0:T(8,128)(2,1)S(1)}, u32[]{:S(2)}, u32[]{:S(2)}) %collective-permute-start.9) | collective-permute-done | bytes 49184 | tf_op jit(solution)/shard_map/ppermute | solution.py:60
  101.1 6.3 %collective-permute-start.11 = (bf16[4,24,256]{2,1,0:T(8,128)(2,1)S(1)}, bf16[4,24,256]{2,1,0:T(8,128)(2,1)S(1)}, u32[]{:S(2)}, u32[]{:S(2)}) collective-permute-start(bf16[4,24,256]{2,1,0:T(8,128)(2,1)S(1)} %bitcast.219), channel_id=1, source_target_pairs={{0,64},{32,96},{64,128},{96,160},{128,192},{160,224},{192,256},{22... | collective-permute-start | bytes 147464 | tf_op jit(solution)/shard_map/ppermute | solution.py:56
  109.2 5.8 %collective-permute-done.10 = bf16[4,24,256]{2,1,0:T(8,128)(2,1)S(1)} collective-permute-done((bf16[4,24,256]{2,1,0:T(8,128)(2,1)S(1)}, bf16[4,24,256]{2,1,0:T(8,128)(2,1)S(1)}, u32[]{:S(2)}, u32[]{:S(2)}) %collective-permute-start.10) | collective-permute-done | bytes 49184 | tf_op jit(solution)/shard_map/ppermute | solution.py:60
  117.5 2.4 %collective-permute-start.13 = (bf16[16,4,256]{2,1,0:T(4,128)(2,1)}, bf16[16,4,256]{2,1,0:T(4,128)(2,1)}, u32[]{:S(2)}, u32[]{:S(2)}) collective-permute-start(bf16[16,4,256]{2,1,0:T(4,128)(2,1)} %get-tuple-element.44), channel_id=1, source_target_pairs={{0,1},{1,2},{2,3},{3,32},{4,5},{5,6},{6,7},{7,36},{8,9},{9,10},{10... | collective-permute-start | bytes 98312 | tf_op jit(solution)/shard_map/ppermute | solution.py:48
  125.7 3.1 %collective-permute-start.16 = (bf16[4,8,64,128]{3,2,1,0:T(8,128)(2,1)}, bf16[4,8,64,128]{3,2,1,0:T(8,128)(2,1)S(1)}, u32[]{:S(2)}, u32[]{:S(2)}) collective-permute-start(bf16[4,8,64,128]{3,2,1,0:T(8,128)(2,1)} %slice_bitcast_fusion), channel_id=1, source_target_pairs={{0,1},{1,0},{2,3},{3,2},{4,5},{5,4},{6,7},{7,6},{8,9},{9,8},{10,11... | collective-permute-start | bytes 1572872 | tf_op jit(solution)/shard_map/ppermute | solution.py:82
  130.0 3.5 %all-to-all-start.2 = ((bf16[8,128,512]{1,2,0:T(8,128)(2,1)}), bf16[8,128,512]{1,2,0:T(8,128)(2,1)S(1)}, u32[]{:S(2)}, u32[]{:S(2)}) async-start(bf16[8,128,512]{1,2,0:T(8,128)(2,1)} %copy_bitcast_fusion), calls=%async_computation.2 | async-start | bytes 2097152 | tf_op jit(solution)/shard_map/all_to_all | solution.py:64
  133.8 6.6 %collective-permute-start.17 = (bf16[8,64,128]{2,1,0:T(8,128)(2,1)S(1)}, bf16[8,64,128]{2,1,0:T(8,128)(2,1)S(1)}, u32[]{:S(2)}, u32[]{:S(2)}) collective-permute-start(bf16[8,64,128]{2,1,0:T(8,128)(2,1)S(1)} %get-tuple-element.26), channel_id=1, source_target_pairs={{0,96},{32,0},{64,32},{96,64},{1,97},{33,1},{65,33},{97,65},{2,98}... | collective-permute-start | bytes 393224 | tf_op jit(solution)/shard_map/ppermute | solution.py:78
  140.5 1.9 collective-permute-start.19
  142.4 3.4 %collective-permute-start.18 = (bf16[8,64,128]{2,1,0:T(8,128)(2,1)S(1)}, bf16[8,64,128]{2,1,0:T(8,128)(2,1)S(1)}, u32[]{:S(2)}, u32[]{:S(2)}) collective-permute-start(bf16[8,64,128]{2,1,0:T(8,128)(2,1)S(1)} %get-tuple-element.28), channel_id=1, source_target_pairs={{0,64},{32,96},{64,0},{96,32},{1,65},{33,97},{65,1},{97,33},{2,66}... | collective-permute-start | bytes 393224 | tf_op jit(solution)/shard_map/ppermute | solution.py:78
  145.8 5.9 %collective-permute-done.19 = bf16[8,64,128]{2,1,0:T(8,128)(2,1)S(1)} collective-permute-done((bf16[8,64,128]{2,1,0:T(8,128)(2,1)S(1)}, bf16[8,64,128]{2,1,0:T(8,128)(2,1)S(1)}, u32[]{:S(2)}, u32[]{:S(2)}) %collective-permute-start.19) | collective-permute-done | bytes 131104 | tf_op jit(solution)/shard_map/ppermute | solution.py:78
  152.6 8.2 %all-to-all-done.2 = bf16[8,128,512]{1,2,0:T(8,128)(2,1)S(1)} async-done(((bf16[8,128,512]{1,2,0:T(8,128)(2,1)}), bf16[8,128,512]{1,2,0:T(8,128)(2,1)S(1)}, u32[]{:S(2)}, u32[]{:S(2)}) %all-to-all-start.2) | async-done | bytes 1048608 | tf_op jit(solution)/shard_map/all_to_all | solution.py:64
  160.7 15.2 %all-to-all-start.3 = ((bf16[96,8,128]{2,1,0:T(8,128)(2,1)}), bf16[96,8,128]{2,1,0:T(8,128)(2,1)S(1)}, u32[]{:S(2)}, u32[]{:S(2)}) async-start(bf16[96,8,128]{2,1,0:T(8,128)(2,1)} %bitcast.75), calls=%async_computation.3 | async-start | bytes 393216 | tf_op jit(solution)/shard_map/all_to_all | solution.py:64
  176.5 9.7 %collective-permute-start.14 = (bf16[2,2,4,32,128]{4,2,3,0,1:T(4,128)(2,1)S(1)}, bf16[2,2,4,32,128]{4,2,3,0,1:T(4,128)(2,1)S(1)}, u32[]{:S(2)}, u32[]{:S(2)}) collective-permute-start(bf16[2,2,4,32,128]{4,2,3,0,1:T(4,128)(2,1)S(1)} %fusion.34), channel_id=1, source_target_pairs={{0,16},{16,0},{1,17},{17,1},{2,18},{18,2},{3,19},{19,3},{4,20},{20... | collective-permute-start | bytes 393224 | tf_op jit(solution)/shard_map/ppermute | solution.py:82
  186.2 8.9 %all-to-all-done.3 = bf16[96,8,128]{2,1,0:T(8,128)(2,1)S(1)} async-done(((bf16[96,8,128]{2,1,0:T(8,128)(2,1)}), bf16[96,8,128]{2,1,0:T(8,128)(2,1)S(1)}, u32[]{:S(2)}, u32[]{:S(2)}) %all-to-all-start.3) | async-done | bytes 196640 | tf_op jit(solution)/shard_map/all_to_all | solution.py:64
  196.1 9.9 %all-to-all-start.4 = ((bf16[24,64,128]{2,1,0:T(8,128)(2,1)}), bf16[24,64,128]{2,1,0:T(8,128)(2,1)S(1)}, u32[]{:S(2)}, u32[]{:S(2)}) async-start(bf16[24,64,128]{2,1,0:T(8,128)(2,1)} %broadcast_in_dim.45), calls=%async_computation.4 | async-start | bytes 786432 | tf_op jit(solution)/shard_map/all_to_all | solution.py:64
  206.1 1.9 collective-permute-start.15
  211.8 8.9 %all-to-all-done.4 = bf16[24,64,128]{2,1,0:T(8,128)(2,1)S(1)} async-done(((bf16[24,64,128]{2,1,0:T(8,128)(2,1)}), bf16[24,64,128]{2,1,0:T(8,128)(2,1)S(1)}, u32[]{:S(2)}, u32[]{:S(2)}) %all-to-all-start.4) | async-done | bytes 393248 | tf_op jit(solution)/shard_map/all_to_all | solution.py:64
  (119 shorter events, 32.7 us)
Async XLA Ops:
  3.4 19.5 %collective-permute-start = (bf16[20,32,128]{2,1,0:T(8,128)(2,1)S(1)}, bf16[20,32,128]{2,1,0:T(8,128)(2,1)S(1)}, u32[]{:S(2)}, u32[]{:S(2)}) collective-permute-start(bf16[20,32,128]{2,1,0:T(8,128)(2,1)S(1)} %pad_maximum_fusion.9), channel_id=1, source_target_pairs={{0,16},{16,0},{1,17},{17,1},{2,18},{18,2},{3,19},{19,3},{4,20},{20... | collective-permute-start | bytes 491528 | tf_op jit(solution)/shard_map/ppermute | solution.py:82
  23.6 10.4 %collective-permute-start.5 = (bf16[2,4,2,32,128]{4,3,2,1,0:T(8,128)(2,1)S(1)}, bf16[2,4,2,32,128]{4,3,2,1,0:T(8,128)(2,1)S(1)}, u32[]{:S(2)}, u32[]{:S(2)}) collective-permute-start(bf16[2,4,2,32,128]{4,3,2,1,0:T(8,128)(2,1)S(1)} %bitcast.211), channel_id=1, source_target_pairs={{0,1},{1,0},{2,3},{3,2},{4,5},{5,4},{6,7},{7,6},{8,9},{9,8},{10,11... | collective-permute-start | bytes 393224 | tf_op jit(solution)/shard_map/ppermute | solution.py:82
  26.2 15.7 %all-to-all-start = ((bf16[8,64,128]{2,1,0:T(8,128)(2,1)}), bf16[8,64,128]{2,1,0:T(8,128)(2,1)S(1)}, u32[]{:S(2)}, u32[]{:S(2)}) async-start(bf16[8,64,128]{2,1,0:T(8,128)(2,1)} %bitcast.14), calls=%async_computation | async-start | bytes 262144 | tf_op jit(solution)/shard_map/all_to_all | solution.py:64
  43.0 31.7 %all-to-all-start.1 = ((bf16[8,128,512]{2,1,0:T(8,128)(2,1)}), bf16[8,128,512]{2,1,0:T(8,128)(2,1)S(1)}, u32[]{:S(2)}, u32[]{:S(2)}) async-start(bf16[8,128,512]{2,1,0:T(8,128)(2,1)} %bitcast.32), calls=%async_computation.1 | async-start | bytes 2097152 | tf_op jit(solution)/shard_map/all_to_all | solution.py:64
  48.1 11.4 %collective-permute-start.3 = (bf16[8,64,128]{2,1,0:T(8,128)(2,1)S(1)}, bf16[8,64,128]{2,1,0:T(8,128)(2,1)S(1)}, u32[]{:S(2)}, u32[]{:S(2)}) collective-permute-start(bf16[8,64,128]{2,1,0:T(8,128)(2,1)S(1)} %all-to-all-done), channel_id=1, source_target_pairs={{0,32},{32,64},{64,96},{96,0},{1,33},{33,65},{65,97},{97,1},{2,34}... | collective-permute-start | bytes 393224 | tf_op jit(solution)/shard_map/ppermute | solution.py:78
  51.5 8.5 %collective-permute-start.2 = (bf16[8,64,128]{2,1,0:T(8,128)(2,1)S(1)}, bf16[8,64,128]{2,1,0:T(8,128)(2,1)S(1)}, u32[]{:S(2)}, u32[]{:S(2)}) collective-permute-start(bf16[8,64,128]{2,1,0:T(8,128)(2,1)S(1)} %all-to-all-done), channel_id=1, source_target_pairs={{0,64},{32,96},{64,0},{96,32},{1,65},{33,97},{65,1},{97,33},{2,66}... | collective-permute-start | bytes 393224 | tf_op jit(solution)/shard_map/ppermute | solution.py:78
  56.1 6.9 %collective-permute-start.1 = (bf16[8,64,128]{2,1,0:T(8,128)(2,1)S(1)}, bf16[8,64,128]{2,1,0:T(8,128)(2,1)S(1)}, u32[]{:S(2)}, u32[]{:S(2)}) collective-permute-start(bf16[8,64,128]{2,1,0:T(8,128)(2,1)S(1)} %all-to-all-done), channel_id=1, source_target_pairs={{0,96},{32,0},{64,32},{96,64},{1,97},{33,1},{65,33},{97,65},{2,98}... | collective-permute-start | bytes 393224 | tf_op jit(solution)/shard_map/ppermute | solution.py:78
  63.1 3.8 %collective-permute-start.4 = (bf16[4,8,64,128]{3,2,1,0:T(8,128)(2,1)S(1)}, bf16[4,8,64,128]{3,2,1,0:T(8,128)(2,1)S(1)}, u32[]{:S(2)}, u32[]{:S(2)}) collective-permute-start(bf16[4,8,64,128]{3,2,1,0:T(8,128)(2,1)S(1)} %get-tuple-element.34), channel_id=1, source_target_pairs={{0,1},{1,0},{2,3},{3,2},{4,5},{5,4},{6,7},{7,6},{8,9},{9,8},{10,11... | collective-permute-start | bytes 1572872 | tf_op jit(solution)/shard_map/ppermute | solution.py:82
  67.0 7.7 %copy-start = (bf16[1024,128]{1,0:T(8,128)(2,1)}, bf16[1024,128]{1,0:T(8,128)(2,1)S(1)}, u32[]{:S(2)}) copy-start(bf16[1024,128]{1,0:T(8,128)(2,1)S(1)} %get-tuple-element.23) | copy-start | bytes 786436
  67.0 8.2 %copy-start.2 = (bf16[1024,128]{1,0:T(8,128)(2,1)}, bf16[1024,128]{1,0:T(8,128)(2,1)S(1)}, u32[]{:S(2)}) copy-start(bf16[1024,128]{1,0:T(8,128)(2,1)S(1)} %get-tuple-element.24) | copy-start | bytes 786436
  67.1 8.2 %copy-start.4 = (bf16[1024,128]{1,0:T(8,128)(2,1)}, bf16[1024,128]{1,0:T(8,128)(2,1)S(1)}, u32[]{:S(2)}) copy-start(bf16[1024,128]{1,0:T(8,128)(2,1)S(1)} %get-tuple-element.25) | copy-start | bytes 786436
  75.3 5.8 %collective-permute-start.6 = (bf16[16,4,256]{2,1,0:T(4,128)(2,1)S(1)}, bf16[16,4,256]{2,1,0:T(4,128)(2,1)S(1)}, u32[]{:S(2)}, u32[]{:S(2)}) collective-permute-start(bf16[16,4,256]{2,1,0:T(4,128)(2,1)S(1)} %get-tuple-element.47), channel_id=1, source_target_pairs={{0,1},{1,2},{2,3},{3,32},{4,5},{5,6},{6,7},{7,36},{8,9},{9,10},{10... | collective-permute-start | bytes 98312 | tf_op jit(solution)/shard_map/ppermute | solution.py:48
  77.2 5.2 %collective-permute-start.7 = (bf16[16,4,256]{2,1,0:T(4,128)(2,1)S(1)}, bf16[16,4,256]{2,1,0:T(4,128)(2,1)S(1)}, u32[]{:S(2)}, u32[]{:S(2)}) collective-permute-start(bf16[16,4,256]{2,1,0:T(4,128)(2,1)S(1)} %get-tuple-element.48), channel_id=1, source_target_pairs={{1,0},{2,1},{3,2},{32,3},{5,4},{6,5},{7,6},{36,7},{9,8},{10,9},{11... | collective-permute-start | bytes 98312 | tf_op jit(solution)/shard_map/ppermute | solution.py:52
  82.5 6.7 %collective-permute-start.8 = (bf16[4,24,256]{2,1,0:T(8,128)(2,1)S(1)}, bf16[4,24,256]{2,1,0:T(8,128)(2,1)S(1)}, u32[]{:S(2)}, u32[]{:S(2)}) collective-permute-start(bf16[4,24,256]{2,1,0:T(8,128)(2,1)S(1)} %get-tuple-element.45), channel_id=1, source_target_pairs={{0,64},{32,96},{64,128},{96,160},{128,192},{160,224},{192,256},{22... | collective-permute-start | bytes 147464 | tf_op jit(solution)/shard_map/ppermute | solution.py:56
  87.4 11.3 %collective-permute-start.9 = (bf16[4,24,256]{2,1,0:T(8,128)(2,1)S(1)}, bf16[4,24,256]{2,1,0:T(8,128)(2,1)S(1)}, u32[]{:S(2)}, u32[]{:S(2)}) collective-permute-start(bf16[4,24,256]{2,1,0:T(8,128)(2,1)S(1)} %get-tuple-element.46), channel_id=1, source_target_pairs={{64,0},{96,32},{128,64},{160,96},{192,128},{224,160},{256,192},{28... | collective-permute-start | bytes 147464 | tf_op jit(solution)/shard_map/ppermute | solution.py:60
  100.5 8.2 %copy-start.6 = (bf16[256,128]{0,1:T(8,128)(2,1)}, bf16[256,128]{0,1:T(8,128)(2,1)S(1)}, u32[]{:S(2)}) copy-start(bf16[256,128]{0,1:T(8,128)(2,1)S(1)} %convolution_convert_fusion.8) | copy-start | bytes 196612
  101.1 8.1 %collective-permute-start.11 = (bf16[4,24,256]{2,1,0:T(8,128)(2,1)S(1)}, bf16[4,24,256]{2,1,0:T(8,128)(2,1)S(1)}, u32[]{:S(2)}, u32[]{:S(2)}) collective-permute-start(bf16[4,24,256]{2,1,0:T(8,128)(2,1)S(1)} %bitcast.219), channel_id=1, source_target_pairs={{0,64},{32,96},{64,128},{96,160},{128,192},{160,224},{192,256},{22... | collective-permute-start | bytes 147464 | tf_op jit(solution)/shard_map/ppermute | solution.py:56
  107.4 7.5 %collective-permute-start.10 = (bf16[4,24,256]{2,1,0:T(8,128)(2,1)S(1)}, bf16[4,24,256]{2,1,0:T(8,128)(2,1)S(1)}, u32[]{:S(2)}, u32[]{:S(2)}) collective-permute-start(bf16[4,24,256]{2,1,0:T(8,128)(2,1)S(1)} %bitcast.218), channel_id=1, source_target_pairs={{64,0},{96,32},{128,64},{160,96},{192,128},{224,160},{256,192},{28... | collective-permute-start | bytes 147464 | tf_op jit(solution)/shard_map/ppermute | solution.py:60
  115.6 5.7 %collective-permute-start.12 = (bf16[16,4,256]{2,1,0:T(4,128)(2,1)}, bf16[16,4,256]{2,1,0:T(4,128)(2,1)}, u32[]{:S(2)}, u32[]{:S(2)}) collective-permute-start(bf16[16,4,256]{2,1,0:T(4,128)(2,1)} %get-tuple-element.43), channel_id=1, source_target_pairs={{1,0},{2,1},{3,2},{32,3},{5,4},{6,5},{7,6},{36,7},{9,8},{10,9},{11... | collective-permute-start | bytes 98312 | tf_op jit(solution)/shard_map/ppermute | solution.py:52
  117.5 5.6 %collective-permute-start.13 = (bf16[16,4,256]{2,1,0:T(4,128)(2,1)}, bf16[16,4,256]{2,1,0:T(4,128)(2,1)}, u32[]{:S(2)}, u32[]{:S(2)}) collective-permute-start(bf16[16,4,256]{2,1,0:T(4,128)(2,1)} %get-tuple-element.44), channel_id=1, source_target_pairs={{0,1},{1,2},{2,3},{3,32},{4,5},{5,6},{6,7},{7,36},{8,9},{9,10},{10... | collective-permute-start | bytes 98312 | tf_op jit(solution)/shard_map/ppermute | solution.py:48
  120.3 3.9 %copy-start.1 = (bf16[1024,128]{1,0:T(8,128)(2,1)S(1)}, bf16[1024,128]{1,0:T(8,128)(2,1)}, u32[]{:S(2)}) copy-start(bf16[1024,128]{1,0:T(8,128)(2,1)} %copy-done) | copy-start | bytes 786436
  121.3 2.9 %copy-start.3 = (bf16[1024,128]{1,0:T(8,128)(2,1)S(1)}, bf16[1024,128]{1,0:T(8,128)(2,1)}, u32[]{:S(2)}) copy-start(bf16[1024,128]{1,0:T(8,128)(2,1)} %copy-done.2) | copy-start | bytes 786436
  121.3 2.9 %copy-start.5 = (bf16[1024,128]{1,0:T(8,128)(2,1)S(1)}, bf16[1024,128]{1,0:T(8,128)(2,1)}, u32[]{:S(2)}) copy-start(bf16[1024,128]{1,0:T(8,128)(2,1)} %copy-done.4) | copy-start | bytes 786436
  125.7 7.8 %collective-permute-start.16 = (bf16[4,8,64,128]{3,2,1,0:T(8,128)(2,1)}, bf16[4,8,64,128]{3,2,1,0:T(8,128)(2,1)S(1)}, u32[]{:S(2)}, u32[]{:S(2)}) collective-permute-start(bf16[4,8,64,128]{3,2,1,0:T(8,128)(2,1)} %slice_bitcast_fusion), channel_id=1, source_target_pairs={{0,1},{1,0},{2,3},{3,2},{4,5},{5,4},{6,7},{7,6},{8,9},{9,8},{10,11... | collective-permute-start | bytes 1572872 | tf_op jit(solution)/shard_map/ppermute | solution.py:82
  130.0 30.7 %all-to-all-start.2 = ((bf16[8,128,512]{1,2,0:T(8,128)(2,1)}), bf16[8,128,512]{1,2,0:T(8,128)(2,1)S(1)}, u32[]{:S(2)}, u32[]{:S(2)}) async-start(bf16[8,128,512]{1,2,0:T(8,128)(2,1)} %copy_bitcast_fusion), calls=%async_computation.2 | async-start | bytes 2097152 | tf_op jit(solution)/shard_map/all_to_all | solution.py:64
  133.8 12.0 %collective-permute-start.17 = (bf16[8,64,128]{2,1,0:T(8,128)(2,1)S(1)}, bf16[8,64,128]{2,1,0:T(8,128)(2,1)S(1)}, u32[]{:S(2)}, u32[]{:S(2)}) collective-permute-start(bf16[8,64,128]{2,1,0:T(8,128)(2,1)S(1)} %get-tuple-element.26), channel_id=1, source_target_pairs={{0,96},{32,0},{64,32},{96,64},{1,97},{33,1},{65,33},{97,65},{2,98}... | collective-permute-start | bytes 393224 | tf_op jit(solution)/shard_map/ppermute | solution.py:78
  140.5 11.3 %collective-permute-start.19 = (bf16[8,64,128]{2,1,0:T(8,128)(2,1)S(1)}, bf16[8,64,128]{2,1,0:T(8,128)(2,1)S(1)}, u32[]{:S(2)}, u32[]{:S(2)}) collective-permute-start(bf16[8,64,128]{2,1,0:T(8,128)(2,1)S(1)} %get-tuple-element.27), channel_id=1, source_target_pairs={{0,32},{32,64},{64,96},{96,0},{1,33},{33,65},{65,97},{97,1},{2,34}... | collective-permute-start | bytes 393224 | tf_op jit(solution)/shard_map/ppermute | solution.py:78
  142.4 9.3 %collective-permute-start.18 = (bf16[8,64,128]{2,1,0:T(8,128)(2,1)S(1)}, bf16[8,64,128]{2,1,0:T(8,128)(2,1)S(1)}, u32[]{:S(2)}, u32[]{:S(2)}) collective-permute-start(bf16[8,64,128]{2,1,0:T(8,128)(2,1)S(1)} %get-tuple-element.28), channel_id=1, source_target_pairs={{0,64},{32,96},{64,0},{96,32},{1,65},{33,97},{65,1},{97,33},{2,66}... | collective-permute-start | bytes 393224 | tf_op jit(solution)/shard_map/ppermute | solution.py:78
  160.7 34.4 %all-to-all-start.3 = ((bf16[96,8,128]{2,1,0:T(8,128)(2,1)}), bf16[96,8,128]{2,1,0:T(8,128)(2,1)S(1)}, u32[]{:S(2)}, u32[]{:S(2)}) async-start(bf16[96,8,128]{2,1,0:T(8,128)(2,1)} %bitcast.75), calls=%async_computation.3 | async-start | bytes 393216 | tf_op jit(solution)/shard_map/all_to_all | solution.py:64
  176.5 29.4 %collective-permute-start.14 = (bf16[2,2,4,32,128]{4,2,3,0,1:T(4,128)(2,1)S(1)}, bf16[2,2,4,32,128]{4,2,3,0,1:T(4,128)(2,1)S(1)}, u32[]{:S(2)}, u32[]{:S(2)}) collective-permute-start(bf16[2,2,4,32,128]{4,2,3,0,1:T(4,128)(2,1)S(1)} %fusion.34), channel_id=1, source_target_pairs={{0,16},{16,0},{1,17},{17,1},{2,18},{18,2},{3,19},{19,3},{4,20},{20... | collective-permute-start | bytes 393224 | tf_op jit(solution)/shard_map/ppermute | solution.py:82
  196.1 24.6 %all-to-all-start.4 = ((bf16[24,64,128]{2,1,0:T(8,128)(2,1)}), bf16[24,64,128]{2,1,0:T(8,128)(2,1)S(1)}, u32[]{:S(2)}, u32[]{:S(2)}) async-start(bf16[24,64,128]{2,1,0:T(8,128)(2,1)} %broadcast_in_dim.45), calls=%async_computation.4 | async-start | bytes 786432 | tf_op jit(solution)/shard_map/all_to_all | solution.py:64
  206.1 3.2 %collective-permute-start.15 = (f32[2,4,32,128]{3,1,2,0:T(4,128)S(1)}, f32[2,4,32,128]{3,1,2,0:T(4,128)S(1)}, u32[]{:S(2)}, u32[]{:S(2)}) collective-permute-start(f32[2,4,32,128]{3,1,2,0:T(4,128)S(1)} %slice_bitcast_fusion.3), channel_id=1, source_target_pairs={{0,1},{1,0},{2,3},{3,2},{4,5},{5,4},{6,7},{7,6},{8,9},{9,8},{10,11... | collective-permute-start | bytes 393224 | tf_op jit(solution)/shard_map/ppermute | solution.py:82
  (1 other events, 2.1 us)
